TPU v7x, 32 devices: a whole 2x2x4 slice. The times are simulated.
32 devices in a mesh: fsdp: 4 (over y, x), ctx: 4 (over z), tp: 2 (over core).
Axes of the slice: x: 2, y: 2, z: 4, core: 2. Of those that a mesh axis runs over, the one named last changes fastest.
Arguments:
- tokens: bfloat16 [8, 2048, 768], P('fsdp', 'ctx'), may hold values from -6 to 6
- doc_lengths: int32 [8, 8], P('fsdp'), may hold values from 1 to 1536, 2048 in all within a row
- keep: int32 [8, 2048], P('fsdp', 'ctx'), may hold values 0 or 1
- w_query: bfloat16 [768, 768], P('fsdp', 'tp'), may hold values from -0.21875 to 0.21875
- b_query: float32 [768], P('tp'), may hold values from -3 to 3
- w_key: bfloat16 [768, 768], P('fsdp', 'tp'), may hold values from -0.21875 to 0.21875
- w_value: bfloat16 [768, 768], P('fsdp', 'tp'), may hold values from -0.21875 to 0.21875
- b_value: float32 [768], P('tp'), may hold values from -3 to 3
- w_out: bfloat16 [768, 768], P('fsdp', 'tp'), may hold values from -0.4375 to 0.4375
- b_out: float32 [768], replicated, may hold values from -3 to 3
- gain_one: float32 [768], replicated, may hold values from 0.5 to 1.5
- shift_one: float32 [768], replicated, may hold values from -2 to 2
- w_up: bfloat16 [768, 2, 3072], P('fsdp', None, 'tp'), may hold values from -0.21875 to 0.21875
- w_down: bfloat16 [768, 3072], P('fsdp', 'tp'), may hold values from -0.15625 to 0.15625
- b_down: float32 [768], replicated, may hold values from -3 to 3
- gain_two: float32 [768], replicated, may hold values from 0.5 to 1.5
- shift_two: float32 [768], replicated, may hold values from -2 to 2
- cotangent: bfloat16 [8, 2048, 768], P('fsdp', 'ctx'), may hold values from -6 to 6
Outputs:
- out: bfloat16 [8, 2048, 768], P('fsdp', 'ctx')
- d_tokens: float32 [8, 2048, 768], P('fsdp', 'ctx')
- d_w_query: float32 [768, 768], P('fsdp', 'tp')
- d_b_query: float32 [768], P('tp')
- d_w_key: float32 [768, 768], P('fsdp', 'tp')
- d_w_value: float32 [768, 768], P('fsdp', 'tp')
- d_b_value: float32 [768], P('tp')
- d_w_out: float32 [768, 768], P('fsdp', 'tp')
- d_b_out: float32 [768], replicated
- d_gain_one: float32 [768], replicated
- d_shift_one: float32 [768], replicated
- d_w_up: float32 [768, 2, 3072], P('fsdp', None, 'tp')
- d_w_down: float32 [768, 3072], P('fsdp', 'tp')
- d_b_down: float32 [768], replicated
- d_gain_two: float32 [768], replicated
- d_shift_two: float32 [768], replicated
Inputs may be any that keep to these rules, and one draw needn't show every extreme that they name: `doc_lengths`: row b lists the lengths of the 8 documents of sequence b in order; they sum to 2048. `keep`: 0 marks a padding token, which only itself attends to.
All inputs are finite; a program needn't handle non-finite values. No bound on the sum of `keep` on one device may be relied on, other than what follows from the above.
Results may differ from a plain program's by a relative error of at most 0.029.
Values may be sent and summed in bfloat16 or wider, within the bound.
A program may use at most 256 MiB of HBM per device.

v0:
```python
import jax
import jax.numpy as jnp
from jax import lax
from jax.sharding import PartitionSpec as P

HEAD = 64


NORM_EPS = 1e-12
MASKED = -1e30


def layer_norm(residual, norm_gain, norm_shift):
    centered = residual - jnp.mean(residual, -1, keepdims=True)
    inv_scale = lax.rsqrt(jnp.mean(centered * centered, -1, keepdims=True) + NORM_EPS)
    normed = centered * inv_scale
    return (normed * norm_gain + norm_shift, normed, inv_scale)


def norm_back(grad_out, normed, inv_scale, norm_gain):
    grad_norm = grad_out * norm_gain
    mean_grad = jnp.mean(grad_norm, -1, keepdims=True)
    mean_cross = jnp.mean(grad_norm * normed, -1, keepdims=True)
    grad_in = (grad_norm - mean_grad - normed * mean_cross) * inv_scale
    return (grad_in, jnp.sum(grad_out * normed, 0), jnp.sum(grad_out, 0))


def head_slopes(first_head, head_count):
    head_index = first_head + jnp.arange(head_count, dtype=jnp.int32)
    head_float = head_index.astype(jnp.float32)
    return jnp.where(head_index < 8, jnp.exp2(-(head_float + 1.0)), jnp.exp2(-(head_float - 7.5)))


def segment_ids(lengths, positions):
    bounds = jnp.cumsum(lengths, -1)
    return jnp.sum((bounds[:, None, :] <= positions[None, :, None]).astype(jnp.int32), -1)


def score_block(query_heads, query_pos, query_seg, key_heads, key_pos, key_seg, key_keep, slopes):
    scores = (
        jnp.einsum("sqhd,skhd->shqk", query_heads, key_heads, preferred_element_type=jnp.float32)
        * 0.125
    )
    distance = jnp.abs(query_pos[:, None] - key_pos[None, :]).astype(jnp.float32)
    scores = scores - slopes[None, :, None, None] * distance[None, None]
    same_doc = query_seg[:, None, :, None] == key_seg[:, None, None, :]
    visible = (key_keep[:, None, None, :] == 1) | (query_pos[:, None] == key_pos[None, :])[
        None, None
    ]
    return (scores, same_doc & visible)


def grad_block(
    query_heads,
    query_pos,
    query_seg,
    grad_heads,
    log_total,
    delta,
    key_heads,
    value_heads,
    key_pos,
    key_seg,
    key_keep,
    slopes,
):
    scores, allowed = score_block(
        query_heads, query_pos, query_seg, key_heads, key_pos, key_seg, key_keep, slopes
    )
    probs = jnp.where(allowed, jnp.exp(scores - log_total[..., None]), 0.0)
    grad_probs = jnp.einsum(
        "sqhd,skhd->shqk", grad_heads, value_heads, preferred_element_type=jnp.float32
    )
    grad_scores = (probs * (grad_probs - delta[..., None])).astype(jnp.bfloat16)
    grad_query = (
        jnp.einsum("shqk,skhd->sqhd", grad_scores, key_heads, preferred_element_type=jnp.float32)
        * 0.125
    )
    grad_key = (
        jnp.einsum("shqk,sqhd->skhd", grad_scores, query_heads, preferred_element_type=jnp.float32)
        * 0.125
    )
    grad_value = jnp.einsum(
        "shqk,sqhd->skhd",
        probs.astype(jnp.bfloat16),
        grad_heads,
        preferred_element_type=jnp.float32,
    )
    return (grad_query, grad_key, grad_value)


def intersections(query_seg, key_seg):
    return jnp.any((key_seg[:, 0] <= query_seg[:, -1]) & (key_seg[:, -1] >= query_seg[:, 0]))


def guarded(active, update, current):
    return lax.cond(active, update, lambda untouched: untouched, current)


def over_blocks(length, advance, current):
    block_len = 512
    block_count = length // block_len
    return lax.fori_loop(
        0,
        block_count,
        lambda block_index, running: advance(running, block_index * block_len, block_len),
        current,
    )


def per_device(
    tokens,
    doc_lengths,
    keep,
    w_query,
    b_query,
    w_key,
    w_value,
    b_value,
    w_out,
    b_out,
    gain_one,
    shift_one,
    w_up,
    w_down,
    b_down,
    gain_two,
    shift_two,
    cotangent,
):
    seq_count, block_rows, model_width = tokens.shape
    local_heads = b_query.shape[0] // HEAD
    head_width = local_heads * HEAD
    row_count = seq_count * block_rows
    slopes = head_slopes(lax.axis_index("tp") * local_heads, local_heads)
    own_pos = lax.axis_index("ctx") * block_rows + jnp.arange(block_rows, dtype=jnp.int32)
    own_seg = segment_ids(doc_lengths, own_pos)
    token_rows = tokens.reshape(row_count, model_width)
    full_query, full_key, full_value, full_out = (
        lax.all_gather(w_query, "fsdp", axis=0, tiled=True),
        lax.all_gather(w_key, "fsdp", axis=0, tiled=True),
        lax.all_gather(w_value, "fsdp", axis=0, tiled=True),
        lax.all_gather(w_out, "fsdp", axis=0, tiled=True),
    )
    queries = (
        jnp.dot(token_rows, full_query, preferred_element_type=jnp.float32) + b_query
    ).astype(jnp.bfloat16)
    key_rows = jnp.dot(token_rows, full_key, preferred_element_type=jnp.float32).astype(
        jnp.bfloat16
    )
    values = (jnp.dot(token_rows, full_value, preferred_element_type=jnp.float32) + b_value).astype(
        jnp.bfloat16
    )
    query_heads = queries.reshape(seq_count, block_rows, local_heads, HEAD)
    key_value = jnp.concatenate([key_rows, values], -1).reshape(
        seq_count, block_rows, 2 * head_width
    )

    def split_pairs(slab_pairs, block_len):
        return (
            slab_pairs[..., :head_width].reshape(seq_count, block_len, local_heads, HEAD),
            slab_pairs[..., head_width:].reshape(seq_count, block_len, local_heads, HEAD),
        )

    def key_slab(pairs, piece_keep, offset, block_len):
        slab_pairs = lax.dynamic_slice_in_dim(pairs, offset, block_len, 1)
        slab_keep = lax.dynamic_slice_in_dim(piece_keep, offset, block_len, 1)
        key_pos = offset + jnp.arange(block_len, dtype=jnp.int32)
        key_seg = segment_ids(doc_lengths, key_pos)
        slab_keys, slab_values = split_pairs(slab_pairs, block_len)
        return (slab_keys, slab_values, slab_keep, key_pos, key_seg)

    start_state = (
        jnp.full((seq_count, local_heads, block_rows), MASKED, jnp.float32),
        jnp.zeros((seq_count, local_heads, block_rows), jnp.float32),
        jnp.zeros((seq_count, local_heads, block_rows, HEAD), jnp.float32),
    )
    pairs = lax.all_gather(key_value, "ctx", axis=1, tiled=True)
    piece_keep = lax.all_gather(keep, "ctx", axis=1, tiled=True)

    def advance(partial_value, offset, block_len):
        slab_keys, slab_values, slab_keep, key_pos, key_seg = key_slab(
            pairs, piece_keep, offset, block_len
        )

        def update(current):
            row_max, row_sum, weighted = current
            scores, allowed = score_block(
                query_heads, own_pos, own_seg, slab_keys, key_pos, key_seg, slab_keep, slopes
            )
            scores = jnp.where(allowed, scores, MASKED)
            new_max = jnp.maximum(row_max, jnp.max(scores, -1))
            factor = jnp.exp(row_max - new_max)
            weights = jnp.where(allowed, jnp.exp(scores - new_max[..., None]), 0.0)
            row_sum = row_sum * factor + jnp.sum(weights, -1)
            weighted = weighted * factor[..., None] + jnp.einsum(
                "shqk,skhd->shqd",
                weights.astype(jnp.bfloat16),
                slab_values,
                preferred_element_type=jnp.float32,
            )
            return (new_max, row_sum, weighted)

        return guarded(intersections(own_seg, key_seg), update, partial_value)

    row_max, row_sum, weighted = over_blocks(pairs.shape[1], advance, start_state)
    attended = (
        (weighted / row_sum[..., None])
        .transpose(0, 2, 1, 3)
        .reshape(row_count, head_width)
        .astype(jnp.bfloat16)
    )
    log_total = row_max + jnp.log(row_sum)
    att_part = jnp.einsum("rh,dh->rd", attended, full_out, preferred_element_type=jnp.float32)
    branch_att = lax.psum(att_part.astype(jnp.bfloat16), "tp").astype(jnp.float32) + b_out
    first_out, normed_one, inv_one = layer_norm(
        token_rows.astype(jnp.float32) + branch_att, gain_one, shift_one
    )
    first_low = first_out.astype(jnp.bfloat16)
    full_up, full_down = (
        lax.all_gather(w_up, "fsdp", axis=0, tiled=True),
        lax.all_gather(w_down, "fsdp", axis=0, tiled=True),
    )
    gate_up = jnp.einsum("rd,dcf->rcf", first_low, full_up, preferred_element_type=jnp.float32)
    product, gelu_back = jax.vjp(
        lambda gate_part, up_part: jax.nn.gelu(gate_part, approximate=False) * up_part,
        gate_up[:, 0],
        gate_up[:, 1],
    )
    hidden = product.astype(jnp.bfloat16)
    ffn_part = jnp.einsum("rf,df->rd", hidden, full_down, preferred_element_type=jnp.float32)
    branch_ffn = lax.psum(ffn_part.astype(jnp.bfloat16), "tp").astype(jnp.float32) + b_down
    result, normed_two, inv_two = layer_norm(first_out + branch_ffn, gain_two, shift_two)
    grad_in = cotangent.reshape(row_count, model_width).astype(jnp.float32)
    grad_two, d_gain_two, d_shift_two = norm_back(grad_in, normed_two, inv_two, gain_two)
    grad_ffn = grad_two.astype(jnp.bfloat16)
    d_b_down = jnp.sum(grad_ffn.astype(jnp.float32), 0)
    d_w_down = jnp.einsum("rd,rf->df", grad_ffn, hidden, preferred_element_type=jnp.float32)
    grad_hidden = jnp.einsum("rd,df->rf", grad_ffn, full_down, preferred_element_type=jnp.float32)
    grad_gate, grad_up = gelu_back(grad_hidden)
    grad_gate_up = jnp.stack([grad_gate, grad_up], 1).astype(jnp.bfloat16)
    d_w_up = jnp.einsum("rd,rcf->dcf", first_low, grad_gate_up, preferred_element_type=jnp.float32)
    first_part = jnp.einsum(
        "rcf,dcf->rd", grad_gate_up, full_up, preferred_element_type=jnp.float32
    )
    grad_first = grad_two + lax.psum(first_part.astype(jnp.bfloat16), "tp").astype(jnp.float32)
    grad_one, d_gain_one, d_shift_one = norm_back(grad_first, normed_one, inv_one, gain_one)
    grad_att = grad_one.astype(jnp.bfloat16)
    d_b_out = jnp.sum(grad_att.astype(jnp.float32), 0)
    d_w_out = jnp.einsum("rd,rh->dh", grad_att, attended, preferred_element_type=jnp.float32)
    grad_attended = jnp.einsum(
        "rd,dh->rh", grad_att, full_out, preferred_element_type=jnp.float32
    ).astype(jnp.bfloat16)
    grad_heads = grad_attended.reshape(seq_count, block_rows, local_heads, HEAD)
    delta = jnp.einsum(
        "sqhd,sqhd->shq",
        grad_heads,
        attended.reshape(seq_count, block_rows, local_heads, HEAD),
        preferred_element_type=jnp.float32,
    )
    query_zero = jnp.zeros((seq_count, block_rows, local_heads, HEAD), jnp.float32)
    full_len = block_rows * lax.axis_size("ctx")
    term_zero = jnp.zeros((seq_count, full_len, 2 * head_width), jnp.float32)
    return_pairs = lax.all_gather(key_value, "ctx", axis=1, tiled=True)
    return_piece_keep = lax.all_gather(keep, "ctx", axis=1, tiled=True)

    def advance(partial_value, offset, block_len):
        slab_keys, slab_values, slab_keep, key_pos, key_seg = key_slab(
            return_pairs, return_piece_keep, offset, block_len
        )

        def update(current):
            query_grad, key_terms = current
            part_query, part_key, part_value = grad_block(
                query_heads,
                own_pos,
                own_seg,
                grad_heads,
                log_total,
                delta,
                slab_keys,
                slab_values,
                key_pos,
                key_seg,
                slab_keep,
                slopes,
            )
            slab_grads = jnp.concatenate(
                [
                    part_key.reshape(seq_count, block_len, head_width),
                    part_value.reshape(seq_count, block_len, head_width),
                ],
                -1,
            )
            return (
                query_grad + part_query,
                lax.dynamic_update_slice_in_dim(key_terms, slab_grads, offset, 1),
            )

        return guarded(intersections(own_seg, key_seg), update, partial_value)

    query_grad, key_terms = over_blocks(return_pairs.shape[1], advance, (query_zero, term_zero))
    pair_grads = lax.psum_scatter(
        key_terms.astype(jnp.bfloat16), "ctx", scatter_dimension=1, tiled=True
    ).astype(jnp.float32)
    query_low = query_grad.reshape(row_count, head_width).astype(jnp.bfloat16)
    pair_low = pair_grads.reshape(row_count, 2 * head_width).astype(jnp.bfloat16)
    grad_project = jnp.concatenate([query_low, pair_low], -1)
    joined_weights = jnp.concatenate([full_query, full_key, full_value], -1)
    joined_grads = jnp.einsum(
        "rd,rh->dh", token_rows, grad_project, preferred_element_type=jnp.float32
    )
    input_part = jnp.einsum(
        "rh,dh->rd", grad_project, joined_weights, preferred_element_type=jnp.float32
    )
    d_tokens = grad_one + lax.psum(input_part.astype(jnp.bfloat16), "tp").astype(jnp.float32)
    d_b_query = jnp.sum(query_low.astype(jnp.float32), 0)
    d_b_value = jnp.sum(pair_low[:, head_width:].astype(jnp.float32), 0)
    d_w_query = joined_grads[:, :head_width]
    d_w_key = joined_grads[:, head_width : 2 * head_width]
    d_w_value = joined_grads[:, 2 * head_width :]
    shard_grads = (
        lax.psum_scatter(
            d_w_query.astype(jnp.bfloat16), "fsdp", scatter_dimension=0, tiled=True
        ).astype(jnp.float32),
        lax.psum_scatter(
            d_w_key.astype(jnp.bfloat16), "fsdp", scatter_dimension=0, tiled=True
        ).astype(jnp.float32),
        lax.psum_scatter(
            d_w_value.astype(jnp.bfloat16), "fsdp", scatter_dimension=0, tiled=True
        ).astype(jnp.float32),
        lax.psum_scatter(
            d_w_out.astype(jnp.bfloat16), "fsdp", scatter_dimension=0, tiled=True
        ).astype(jnp.float32),
        lax.psum_scatter(
            d_w_up.astype(jnp.bfloat16), "fsdp", scatter_dimension=0, tiled=True
        ).astype(jnp.float32),
        lax.psum_scatter(
            d_w_down.astype(jnp.bfloat16), "fsdp", scatter_dimension=0, tiled=True
        ).astype(jnp.float32),
    )
    sum_query, sum_key, sum_value, sum_out, sum_up, sum_down = (
        lax.psum(shard_grads[0].astype(jnp.bfloat16), "ctx").astype(jnp.float32),
        lax.psum(shard_grads[1].astype(jnp.bfloat16), "ctx").astype(jnp.float32),
        lax.psum(shard_grads[2].astype(jnp.bfloat16), "ctx").astype(jnp.float32),
        lax.psum(shard_grads[3].astype(jnp.bfloat16), "ctx").astype(jnp.float32),
        lax.psum(shard_grads[4].astype(jnp.bfloat16), "ctx").astype(jnp.float32),
        lax.psum(shard_grads[5].astype(jnp.bfloat16), "ctx").astype(jnp.float32),
    )
    (
        total_b_query,
        total_b_value,
        total_b_out,
        total_b_down,
        total_gain_one,
        total_shift_one,
        total_gain_two,
        total_shift_two,
    ) = lax.psum(
        (d_b_query, d_b_value, d_b_out, d_b_down, d_gain_one, d_shift_one, d_gain_two, d_shift_two),
        ("fsdp", "ctx"),
    )
    return (
        result.reshape(seq_count, block_rows, model_width).astype(jnp.bfloat16),
        d_tokens.reshape(seq_count, block_rows, model_width),
        sum_query,
        total_b_query,
        sum_key,
        sum_value,
        total_b_value,
        sum_out,
        total_b_out,
        total_gain_one,
        total_shift_one,
        sum_up,
        sum_down,
        total_b_down,
        total_gain_two,
        total_shift_two,
    )


def solution(mesh):
    in_specs = (
        P("fsdp", "ctx", None),
        P("fsdp", None),
        P("fsdp", "ctx"),
        P("fsdp", "tp"),
        P("tp"),
        P("fsdp", "tp"),
        P("fsdp", "tp"),
        P("tp"),
        P("fsdp", "tp"),
        P(),
        P(),
        P(),
        P("fsdp", None, "tp"),
        P("fsdp", "tp"),
        P(),
        P(),
        P(),
        P("fsdp", "ctx", None),
    )
    out_specs = (
        P("fsdp", "ctx", None),
        P("fsdp", "ctx", None),
        P("fsdp", "tp"),
        P("tp"),
        P("fsdp", "tp"),
        P("fsdp", "tp"),
        P("tp"),
        P("fsdp", "tp"),
        P(),
        P(),
        P(),
        P("fsdp", None, "tp"),
        P("fsdp", "tp"),
        P(),
        P(),
        P(),
    )
    return jax.shard_map(
        per_device, mesh=mesh, in_specs=in_specs, out_specs=out_specs, check_vma=False
    )
```

profile of v0, /device:TPU:0, one launch (start us, length us, event | category | flops | bytes accessed | tf_op | source)
XLA Modules:
  0.0 1039.2 jit_solution(15343525228402633456)
XLA Ops:
  8.1 12.4 %all_gather.28 = bf16[768,384]{1,0:T(8,128)(2,1)S(1)} all-gather(bf16[192,384]{1,0:T(8,128)(2,1)} %param.32), channel_id=1, replica_groups=mesh['fsdp'=4,'ctx'=4,'tp'=2] {'fsdp'}, dimensions={0}, use_global_device_ids=true | all-gather | bytes 737280 | tf_op jit(solution)/shard_map/all_gather | solution.py:142
  20.5 10.4 %all_gather.27 = bf16[768,384]{1,0:T(8,128)(2,1)S(1)} all-gather(bf16[192,384]{1,0:T(8,128)(2,1)} %param.31), channel_id=1, replica_groups=mesh['fsdp'=4,'ctx'=4,'tp'=2] {'fsdp'}, dimensions={0}, use_global_device_ids=true | all-gather | bytes 737280 | tf_op jit(solution)/shard_map/all_gather | solution.py:141
  36.0 9.7 all_gather.30
  48.5 13.5 %all_gather.26 = s32[2,2048]{1,0:T(2,128)S(1)} all-gather(s32[2,512]{1,0:T(2,128)S(1)} %copy-done.41), channel_id=1, replica_groups=mesh['fsdp'=4,'ctx'=4,'tp'=2] {'ctx'}, dimensions={1}, use_global_device_ids=true | all-gather | bytes 20480 | tf_op jit(solution)/shard_map/all_gather | solution.py:179
  62.0 10.8 %all_gather.31 = bf16[768,384]{1,0:T(8,128)(2,1)} all-gather(bf16[192,384]{1,0:T(8,128)(2,1)S(1)} %copy-done.26), channel_id=1, replica_groups=mesh['fsdp'=4,'ctx'=4,'tp'=2] {'fsdp'}, dimensions={0}, use_global_device_ids=true | all-gather | bytes 737280 | tf_op jit(solution)/shard_map/all_gather | solution.py:143
  72.9 78.7 %all-gather.4.cloned.1.call-done = bf16[2,2048,768]{1,2,0:T(8,128)(2,1)} async-done(((bf16[2,512,768]{1,2,0:T(8,128)(2,1)}), bf16[2,2048,768]{1,2,0:T(8,128)(2,1)}) %all-gather.4.cloned.1.call-update) | async-done | bytes 6291472 | tf_op jit(solution)/shard_map/all_gather | solution.py:178
  151.8 86.0 %while.38 = (s32[]{:T(128)}, f32[2,6,512]{2,1,0:T(8,128)S(1)}, f32[2,6,512]{2,1,0:T(8,128)S(1)}, f32[2,6,512,64]{2,3,1,0:T(8,128)S(1)}, s32[2,1,8]{2,0,1:T(2,128...) while((s32[]{:T(128)}, f32[2,6,512]{2,1,0:T(8,128)S(1)}, ...), condition=%wide.region_9.10_spmd.clone, body=%wide.region_2.9_spmd.clone.sunk | while | flops 860657216 | bytes 95593216 | solution.py:103
  153.4 20.0 %conditional.6 = ((f32[2,6,512]{2,1,0:T(8,128)S(1)}, f32[2,6,512]{2,1,0:T(8,128)S(1)}, f32[2,6,512,64]{2,3,1,0:T(8,128)S(1)})) conditional(s32[]{:T(128)} %convert_element_type.410, (f32[2,6,512]{2,1,0:T(8,128)S(1)}, f32[2,6,512]{2,1,0:T(8,128)S(1)}, f32[2,6,512,64]{2,3,1,0:T(8,128)S(1)}) %tuple.180, (s32[2,512]{1,0:T(2,128)S(1)}, ...), branch_computations={%region_5.5_spmd, %region_6.8_spmd.clone} | conditional | flops 860633152 | bytes 95582496 | solution.py:97
  174.9 20.0 %conditional.6 = ((f32[2,6,512]{2,1,0:T(8,128)S(1)}, f32[2,6,512]{2,1,0:T(8,128)S(1)}, f32[2,6,512,64]{2,3,1,0:T(8,128)S(1)})) conditional(s32[]{:T(128)} %convert_element_type.410, (f32[2,6,512]{2,1,0:T(8,128)S(1)}, f32[2,6,512]{2,1,0:T(8,128)S(1)}, f32[2,6,512,64]{2,3,1,0:T(8,128)S(1)}) %tuple.180, (s32[2,512]{1,0:T(2,128)S(1)}, ...), branch_computations={%region_5.5_spmd, %region_6.8_spmd.clone} | conditional | flops 860633152 | bytes 95582496 | solution.py:97
  196.4 20.0 %conditional.6 = ((f32[2,6,512]{2,1,0:T(8,128)S(1)}, f32[2,6,512]{2,1,0:T(8,128)S(1)}, f32[2,6,512,64]{2,3,1,0:T(8,128)S(1)})) conditional(s32[]{:T(128)} %convert_element_type.410, (f32[2,6,512]{2,1,0:T(8,128)S(1)}, f32[2,6,512]{2,1,0:T(8,128)S(1)}, f32[2,6,512,64]{2,3,1,0:T(8,128)S(1)}) %tuple.180, (s32[2,512]{1,0:T(2,128)S(1)}, ...), branch_computations={%region_5.5_spmd, %region_6.8_spmd.clone} | conditional | flops 860633152 | bytes 95582496 | solution.py:97
  217.9 20.0 %conditional.6 = ((f32[2,6,512]{2,1,0:T(8,128)S(1)}, f32[2,6,512]{2,1,0:T(8,128)S(1)}, f32[2,6,512,64]{2,3,1,0:T(8,128)S(1)})) conditional(s32[]{:T(128)} %convert_element_type.410, (f32[2,6,512]{2,1,0:T(8,128)S(1)}, f32[2,6,512]{2,1,0:T(8,128)S(1)}, f32[2,6,512,64]{2,3,1,0:T(8,128)S(1)}) %tuple.180, (s32[2,512]{1,0:T(2,128)S(1)}, ...), branch_computations={%region_5.5_spmd, %region_6.8_spmd.clone} | conditional | flops 860633152 | bytes 95582496 | solution.py:97
  245.5 15.5 %all-reduce.8.cloned.1.call-done = bf16[1024,768]{1,0:T(8,128)(2,1)} async-done(((bf16[1024,768]{1,0:T(8,128)(2,1)}), bf16[1024,768]{1,0:T(8,128)(2,1)}) %all-reduce.8.cloned.1.call-update) | async-done | bytes 1572880 | tf_op jit(solution)/shard_map/psum | solution.py:215
  267.1 33.3 %all-gather.6.cloned.1.call-done = bf16[768,2,1536]{2,0,1:T(8,128)(2,1)} async-done(((bf16[192,2,1536]{2,0,1:T(8,128)(2,1)}), bf16[768,2,1536]{2,0,1:T(8,128)(2,1)}) %all-gather.6.cloned.1.call-update) | async-done | bytes 4718608 | tf_op jit(solution)/shard_map/all_gather | solution.py:221
  300.4 7.8 fusion.80
  312.9 14.7 %multiply_convert_fusion.1 = (bf16[1024,1536]{1,0:T(8,128)(2,1)}, f32[1024,1536]{1,0:T(8,128)}) fusion(f32[1024,2,1536]{2,0,1:T(8,128)S(1)} %fusion.80), kind=kLoop, calls=%fused_computation.88 | loop fusion | flops 103809024 | bytes 22020096 | tf_op jit(solution)/shard_map/convert_element_type | solution.py:230
  327.6 11.9 %all-gather.8.cloned.1.call-done = bf16[768,1536]{1,0:T(8,128)(2,1)} async-done(((bf16[192,1536]{1,0:T(8,128)(2,1)}), bf16[768,1536]{1,0:T(8,128)(2,1)}) %all-gather.8.cloned.1.call-update) | async-done | bytes 2359312 | tf_op jit(solution)/shard_map/all_gather | solution.py:222
  339.6 6.4 convolution_convert_fusion.4
  349.1 17.5 %all-reduce.10.cloned.1.call-done = bf16[1024,768]{1,0:T(8,128)(2,1)} async-done(((bf16[1024,768]{1,0:T(8,128)(2,1)}), bf16[1024,768]{1,0:T(8,128)(2,1)}) %all-reduce.10.cloned.1.call-update) | async-done | bytes 1572880 | tf_op jit(solution)/shard_map/psum | solution.py:232
  375.6 10.2 fusion.65
  385.7 9.5 bitcast_convert_fusion
  395.8 21.2 %all-reduce.12.cloned.1.call-done = bf16[1024,768]{1,0:T(8,128)(2,1)} async-done(((bf16[1024,768]{1,0:T(8,128)(2,1)}), bf16[1024,768]{1,0:T(8,128)(2,1)}) %all-reduce.12.cloned.1.call-update) | async-done | bytes 1572880 | tf_op jit(solution)/shard_map/psum | solution.py:246
  443.3 136.7 %while.39 = (s32[]{:T(128)}, f32[2,512,6,64]{1,3,2,0:T(8,128)}, bf16[2,2048,768]{1,2,0:T(8,128)(2,1)}, s32[2,1,8]{2,0,1:T(2,128)S(1)}, s32[2,512]{1,0:T(2,128)S(...) while((s32[]{:T(128)}, f32[2,512,6,64]{1,3,2,0:T(8,128)}, ...), condition=%wide.region_26.27_spmd.clone, body=%wide.region_21.0_spmd.clone.sunk | while | flops 2059953664 | bytes 96322272 | solution.py:103
  444.9 32.6 %conditional.7 = ((f32[2,512,6,64]{1,3,2,0:T(8,128)}, bf16[2,2048,768]{1,2,0:T(8,128)(2,1)})) conditional(s32[]{:T(128)} %convert_element_type.412, (f32[2,512,6,64]{1,3,2,0:T(8,128)}, bf16[2,2048,768]{1,2,0:T(8,128)(2,1)}) %tuple.184, (s32[2,512]{1,0:T(2,128)S(1)}, s32[2,512]{1,0:T(2,128)S(1)}, s32[]{:T(128)}, s32[2,2048]{1,0:T(2,128)S(1)}, ...), branch_computations={%region_24.24_spmd, %region_25.25_spmd.clone} | conditional | flops 2059929600 | bytes 96311528 | solution.py:97
  455.9 8.2 fusion.23
  466.1 6.5 fusion.28
  479.0 32.7 %conditional.7 = ((f32[2,512,6,64]{1,3,2,0:T(8,128)}, bf16[2,2048,768]{1,2,0:T(8,128)(2,1)})) conditional(s32[]{:T(128)} %convert_element_type.412, (f32[2,512,6,64]{1,3,2,0:T(8,128)}, bf16[2,2048,768]{1,2,0:T(8,128)(2,1)}) %tuple.184, (s32[2,512]{1,0:T(2,128)S(1)}, s32[2,512]{1,0:T(2,128)S(1)}, s32[]{:T(128)}, s32[2,2048]{1,0:T(2,128)S(1)}, ...), branch_computations={%region_24.24_spmd, %region_25.25_spmd.clone} | conditional | flops 2059929600 | bytes 96311528 | solution.py:97
  482.4 6.4 fusion.98
  489.9 8.2 fusion.23
  500.2 6.5 fusion.28
  513.2 32.6 %conditional.7 = ((f32[2,512,6,64]{1,3,2,0:T(8,128)}, bf16[2,2048,768]{1,2,0:T(8,128)(2,1)})) conditional(s32[]{:T(128)} %convert_element_type.412, (f32[2,512,6,64]{1,3,2,0:T(8,128)}, bf16[2,2048,768]{1,2,0:T(8,128)(2,1)}) %tuple.184, (s32[2,512]{1,0:T(2,128)S(1)}, s32[2,512]{1,0:T(2,128)S(1)}, s32[]{:T(128)}, s32[2,2048]{1,0:T(2,128)S(1)}, ...), branch_computations={%region_24.24_spmd, %region_25.25_spmd.clone} | conditional | flops 2059929600 | bytes 96311528 | solution.py:97
  516.5 6.4 fusion.98
  524.1 8.2 fusion.23
  534.3 6.5 fusion.28
  547.3 32.7 %conditional.7 = ((f32[2,512,6,64]{1,3,2,0:T(8,128)}, bf16[2,2048,768]{1,2,0:T(8,128)(2,1)})) conditional(s32[]{:T(128)} %convert_element_type.412, (f32[2,512,6,64]{1,3,2,0:T(8,128)}, bf16[2,2048,768]{1,2,0:T(8,128)(2,1)}) %tuple.184, (s32[2,512]{1,0:T(2,128)S(1)}, s32[2,512]{1,0:T(2,128)S(1)}, s32[]{:T(128)}, s32[2,2048]{1,0:T(2,128)S(1)}, ...), branch_computations={%region_24.24_spmd, %region_25.25_spmd.clone} | conditional | flops 2059929600 | bytes 96311528 | solution.py:97
  550.6 6.4 fusion.98
  558.2 8.2 fusion.23
  568.4 6.5 fusion.28
  579.9 8.7 copy.101
  591.9 108.8 %reduce-scatter.14.cloned.1.call-done = bf16[2,512,768]{2,1,0:T(8,128)(2,1)} async-done(((bf16[2,2048,768]{2,1,0:T(8,128)(2,1)}), bf16[2,512,768]{2,1,0:T(8,128)(2,1)}) %reduce-scatter.14.cloned.1.call-update) | async-done | bytes 1572880 | tf_op jit(solution)/shard_map/reduce_scatter | solution.py:303
  715.3 6.9 convolution_convert_fusion.1
  722.3 9.8 convolution_convert_fusion
  739.8 22.1 %reduce-scatter.24.cloned.1.call-done = bf16[192,384]{1,0:T(8,128)(2,1)} async-done(((bf16[768,384]{1,0:T(8,128)(2,1)}), bf16[192,384]{1,0:T(8,128)(2,1)}) %reduce-scatter.24.cloned.1.call-update) | async-done | bytes 147472
  763.6 26.4 %reduce-scatter.26.cloned.1.call-done = bf16[192,384]{1,0:T(8,128)(2,1)} async-done(((bf16[768,384]{1,0:T(8,128)(2,1)}), bf16[192,384]{1,0:T(8,128)(2,1)}) %reduce-scatter.26.cloned.1.call-update) | async-done | bytes 147472
  791.7 26.6 %reduce-scatter.16.cloned.1.call-done = bf16[192,384]{1,0:T(8,128)(2,1)} async-done(((bf16[768,384]{1,0:T(8,128)(2,1)}), bf16[192,384]{1,0:T(8,128)(2,1)}) %reduce-scatter.16.cloned.1.call-update) | async-done | bytes 147472 | tf_op jit(solution)/shard_map/reduce_scatter | solution.py:332
  818.3 40.7 %reduce-scatter.20.cloned.1.call-done = bf16[192,1536]{1,0:T(8,128)(2,1)} async-done(((bf16[768,1536]{1,0:T(8,128)(2,1)}), bf16[192,1536]{1,0:T(8,128)(2,1)}) %reduce-scatter.20.cloned.1.call-update) | async-done | bytes 589840 | tf_op jit(solution)/shard_map/reduce_scatter | solution.py:338
  859.0 59.8 %reduce-scatter.18.cloned.1.call-done = bf16[192,2,1536]{2,0,1:T(8,128)(2,1)} async-done(((bf16[768,2,1536]{2,0,1:T(8,128)(2,1)}), bf16[192,2,1536]{2,0,1:T(8,128)(2,1)}) %reduce-scatter.18.cloned.1.call-update) | async-done | bytes 1179664 | tf_op jit(solution)/shard_map/reduce_scatter | solution.py:335
  920.3 79.8 %all-reduce = (f32[384]{0:T(512)}, f32[384]{0:T(512)}, f32[768]{0:T(1024)}, f32[768]{0:T(1024)}, f32[768]{0:T(1024)}, /*index=5*/f32[768]{0:T(1024)}, f32[768]{0:T(1024)}, f32[768]{0:T(1024)}) all-reduce(f32[384]{0:T(512)S(1)} %reduce_sum.208, ...), channel_id=1, replica_groups=mesh['fsdp'=4,'ctx'=4,'tp'=2] {'fsdp','ctx'}, use_global_device_ids=true, to_apply=%region_32.33 | all-reduce | flops 5376 | bytes 43008 | tf_op jit(solution)/shard_map/psum | solution.py:359
  1003.5 19.6 %all-reduce.16.cloned.1.call-done = (bf16[192,384]{0,1:T(8,128)(2,1)}, bf16[192,384]{0,1:T(8,128)(2,1)}, bf16[192,384]{0,1:T(8,128)(2,1)}, bf16[192,2,1536]{2,0,...) async-done(((bf16[192,384]{0,1:T(8,128)(2,1)}, bf16[192,384]{0,1:T(8,128)(2,1)}, bf16[192,384]{0,1:T(8,128)(2,1)}, bf16[192,2,1536]{2,0,1:T(8,128)(2,1)}, ...) | async-done | bytes 2359312 | tf_op jit(solution)/shard_map/psum | solution.py:343
  (367 shorter events, 245.6 us)
Async XLA Ops:
  8.0 25.4 %copy-start.6 = (bf16[2,512,768]{2,1,0:T(8,128)(2,1)S(1)}, bf16[2,512,768]{2,1,0:T(8,128)(2,1)}, u32[]{:S(2)}) copy-start(bf16[2,512,768]{2,1,0:T(8,128)(2,1)} %param.26) | copy-start | bytes 4718596
  8.0 25.4 %copy-start.43 = (f32[384]{0:T(512)S(1)}, f32[384]{0:T(512)}, u32[]{:S(2)}) copy-start(f32[384]{0:T(512)} %param.33) | copy-start | bytes 4612
  8.0 143.6 %all-gather.4.cloned.1.call-start = ((), (), s32[]{:S(2)}) async-start(), calls=%async_computation.7 | async-start | bytes 7864320 | tf_op jit(solution)/shard_map/all_gather | solution.py:178
  20.5 12.9 %copy-start.18 = (bf16[768,384]{1,0:T(8,128)(2,1)}, bf16[768,384]{1,0:T(8,128)(2,1)S(1)}, u32[]{:S(2)}) copy-start(bf16[768,384]{1,0:T(8,128)(2,1)S(1)} %all_gather.28) | copy-start | bytes 1769476
  34.4 12.1 %copy-start.44 = (f32[384]{0:T(512)S(1)}, f32[384]{0:T(512)}, u32[]{:S(2)}) copy-start(f32[384]{0:T(512)} %param.30) | copy-start | bytes 4612
  35.7 225.3 %all-reduce.8.cloned.1.call-start = ((), (), s32[]{:S(2)}) async-start(), calls=%async_computation.8 | async-start | bytes 3145728 | tf_op jit(solution)/shard_map/psum | solution.py:215
  47.5 14.5 %copy-start.26 = (bf16[192,384]{1,0:T(8,128)(2,1)S(1)}, bf16[192,384]{1,0:T(8,128)(2,1)}, u32[]{:S(2)}) copy-start(bf16[192,384]{1,0:T(8,128)(2,1)} %param.34) | copy-start | bytes 442372
  181.1 5.8 slice-start
  202.6 5.8 slice-start
  202.6 5.8 slice-start.1
  224.1 5.8 slice-start
  242.1 18.8 %copy-start.29 = (f32[768]{0:T(1024)S(1)}, f32[768]{0:T(1024)}, u32[]{:S(2)}) copy-start(f32[768]{0:T(1024)} %param.35) | copy-start | bytes 9220
  242.2 58.2 %all-gather.6.cloned.1.call-start = ((), (), s32[]{:S(2)}) async-start(), calls=%async_computation.9 | async-start | bytes 5898240 | tf_op jit(solution)/shard_map/all_gather | solution.py:221
  244.6 94.9 %all-gather.8.cloned.1.call-start = ((), (), s32[]{:S(2)}) async-start(), calls=%async_computation.10 | async-start | bytes 2949120 | tf_op jit(solution)/shard_map/all_gather | solution.py:222
  245.2 121.3 %all-reduce.10.cloned.1.call-start = ((), (), s32[]{:S(2)}) async-start(), calls=%async_computation.11 | async-start | bytes 3145728 | tf_op jit(solution)/shard_map/psum | solution.py:232
  264.7 35.7 %copy-start.27 = (f32[768]{0:T(1024)S(1)}, f32[768]{0:T(1024)}, u32[]{:S(2)}) copy-start(f32[768]{0:T(1024)} %param.36) | copy-start | bytes 9220
  264.7 35.6 %copy-start.39 = (f32[768]{0:T(1024)S(1)}, f32[768]{0:T(1024)}, u32[]{:S(2)}) copy-start(f32[768]{0:T(1024)} %param.37) | copy-start | bytes 9220
  339.6 6.7 copy-start.30
  346.0 20.6 %copy-start.37 = (f32[768]{0:T(1024)S(1)}, f32[768]{0:T(1024)}, u32[]{:S(2)}) copy-start(f32[768]{0:T(1024)} %param.40) | copy-start | bytes 9220
  346.0 71.0 %all-reduce.12.cloned.1.call-start = ((), (), s32[]{:S(2)}) async-start(), calls=%async_computation.12 | async-start | bytes 3145728 | tf_op jit(solution)/shard_map/psum | solution.py:246
  366.6 8.7 slice-start.2
  375.3 10.4 %copy-start.4 = (f32[1024,768]{1,0:T(8,128)}, f32[1024,768]{1,0:T(8,128)S(1)}, u32[]{:S(2)}) copy-start(f32[1024,768]{1,0:T(8,128)S(1)} %get-tuple-element.1416) | copy-start | bytes 9437188
  395.2 305.5 %reduce-scatter.14.cloned.1.call-start = ((), (), s32[]{:S(2)}) async-start(), calls=%async_computation.13 | async-start | bytes 7864320 | tf_op jit(solution)/shard_map/reduce_scatter | solution.py:303
  417.0 6.1 copy-start.3
  417.0 6.1 copy-start.5
  417.0 6.5 copy-start.12
  588.6 149.4 %reduce-scatter.22.cloned.1.call-start = ((), (), s32[]{:S(2)}) async-start(), calls=%async_computation.18 | async-start | bytes 737280
  588.9 111.8 %copy-start.8 = (bf16[2,512,768]{2,1,0:T(8,128)(2,1)S(1)}, bf16[2,512,768]{2,1,0:T(8,128)(2,1)}, u32[]{:S(2)}) copy-start(bf16[2,512,768]{2,1,0:T(8,128)(2,1)} %param.26) | copy-start | bytes 4718596
  591.9 112.3 %copy-start.16 = (bf16[1024,384]{1,0:T(8,128)(2,1)}, bf16[1024,384]{1,0:T(8,128)(2,1)S(1)}, u32[]{:S(2)}) copy-start(bf16[1024,384]{1,0:T(8,128)(2,1)S(1)} %copy.102) | copy-start | bytes 2359300
  705.4 6.8 copy-start.2
  707.7 54.1 %reduce-scatter.24.cloned.1.call-start = ((), (), s32[]{:S(2)}) async-start(), calls=%async_computation.19 | async-start | bytes 737280
  710.0 80.0 %reduce-scatter.26.cloned.1.call-start = ((), (), s32[]{:S(2)}) async-start(), calls=%async_computation.20 | async-start | bytes 737280
  712.2 106.1 %reduce-scatter.16.cloned.1.call-start = ((), (), s32[]{:S(2)}) async-start(), calls=%async_computation.15 | async-start | bytes 737280 | tf_op jit(solution)/shard_map/reduce_scatter | solution.py:332
  715.2 7.1 copy-start.28
  715.2 7.1 copy-start.40
  715.3 143.8 %reduce-scatter.20.cloned.1.call-start = ((), (), s32[]{:S(2)}) async-start(), calls=%async_computation.17 | async-start | bytes 2949120 | tf_op jit(solution)/shard_map/reduce_scatter | solution.py:338
  722.2 196.6 %reduce-scatter.18.cloned.1.call-start = ((), (), s32[]{:S(2)}) async-start(), calls=%async_computation.16 | async-start | bytes 5898240 | tf_op jit(solution)/shard_map/reduce_scatter | solution.py:335
  732.1 268.0 %all-reduce.14.cloned.1.call-start = ((), (), s32[]{:S(2)}) async-start(), calls=%async_computation.14 | async-start | bytes 3145728 | tf_op jit(solution)/shard_map/psum | solution.py:316
  737.7 182.5 %copy-start.31 = (f32[768]{0:T(1024)S(1)}, f32[768]{0:T(1024)}, u32[]{:S(2)}) copy-start(f32[768]{0:T(1024)} %get-tuple-element.1392) | copy-start | bytes 9220
  737.7 182.5 %copy-start.32 = (f32[768]{0:T(1024)S(1)}, f32[768]{0:T(1024)}, u32[]{:S(2)}) copy-start(f32[768]{0:T(1024)} %get-tuple-element.1326) | copy-start | bytes 9220
  737.7 182.5 %copy-start.33 = (f32[768]{0:T(1024)S(1)}, f32[768]{0:T(1024)}, u32[]{:S(2)}) copy-start(f32[768]{0:T(1024)} %get-tuple-element.1319) | copy-start | bytes 9220
  737.7 182.6 %copy-start.34 = (f32[768]{0:T(1024)S(1)}, f32[768]{0:T(1024)}, u32[]{:S(2)}) copy-start(f32[768]{0:T(1024)} %get-tuple-element.1324) | copy-start | bytes 9220
  737.7 182.6 %copy-start.35 = (f32[768]{0:T(1024)S(1)}, f32[768]{0:T(1024)}, u32[]{:S(2)}) copy-start(f32[768]{0:T(1024)} %get-tuple-element.1325) | copy-start | bytes 9220
  737.7 182.6 %copy-start.36 = (f32[768]{0:T(1024)S(1)}, f32[768]{0:T(1024)}, u32[]{:S(2)}) copy-start(f32[768]{0:T(1024)} %get-tuple-element.1321) | copy-start | bytes 9220
  737.7 285.4 %all-reduce.16.cloned.1.call-start = ((), (), s32[]{:S(2)}) async-start(), calls=%async_computation.21 | async-start | bytes 5013504 | tf_op jit(solution)/shard_map/psum | solution.py:343
  1023.1 5.9 copy-start.23
  1023.1 6.7 copy-start.22
  1023.1 7.6 copy-start.21
  (23 other events, 74.7 us)
Sparse Core Ops, SparseCore 0:
  35.8 115.7 all-gather.3
  242.3 18.6 all-reduce.7
  346.1 20.3 all-reduce.9
  395.4 21.5 all-reduce.11
  588.7 111.9 reduce-scatter.13
  737.9 20.9 all-reduce.13
  919.0 104.1 all-reduce.15
Sparse Core Ops, SparseCore 1:
  245.2 55.1 all-gather.5
  302.2 37.3 all-gather.7
  707.8 25.7 reduce-scatter.21
  736.7 25.1 reduce-scatter.23
  764.8 25.1 reduce-scatter.25
  793.1 25.1 reduce-scatter.15
  821.8 37.2 reduce-scatter.19
  861.9 56.9 reduce-scatter.17
where the time goes:
time: 1040 us
  waiting for transfers between devices  483 us (46%)
  matrix products  217 us (21%)
  blocking collectives  137 us (13%)
  other arithmetic  104 us (10%)
  local copies, waits for them, and re-layouts  73.4 us (7%)
  between operations  16.5 us (2%)
    reduce_scatter x1, waiting for transfers between devices, per_device(): lax.psum_scatter(key_terms.astype(jnp.bfloat16), 'ctx', scatter_dimension...  109 us
    psum x1, blocking collectives, per_device(): lax.psum((d_b_query, d_b_value, d_b_out, d_b_down, d_gain_one, d_shift_on...  79.8 us
    all_gather x1, waiting for transfers between devices, per_device(): pairs = lax.all_gather(key_value, 'ctx', axis=1, tiled=True)  78.7 us
    reduce_scatter x1, waiting for transfers between devices, per_device(): lax.psum_scatter(d_w_up.astype(jnp.bfloat16), 'fsdp', scatter_dimension=0...  59.8 us
    unnamed x18, waiting for transfers between devices  49.2 us
    dot_general x8, matrix products, score_block(): jnp.einsum('sqhd,skhd->shqk', query_heads, key_heads, preferred_element_t...  48.4 us
    reduce_scatter x1, waiting for transfers between devices, per_device(): lax.psum_scatter(d_w_down.astype(jnp.bfloat16), 'fsdp', scatter_dimension...  40.7 us
    all_gather x1, waiting for transfers between devices, per_device(): lax.all_gather(w_up, 'fsdp', axis=0, tiled=True)  33.3 us
  transfers between devices with their start and end apart: 15, of which 13 were waited for; matrix products, arithmetic and copies ran while one was open for 8% of the time, Pallas kernels for 0%

commit v1 on v0

--- a/solution.py
+++ b/solution.py
@@ -1,6 +1,10 @@
+import functools
+
 import jax
 import jax.numpy as jnp
 from jax import lax
+from jax.experimental import pallas as pl
+from jax.experimental.pallas import tpu as pltpu
 from jax.sharding import PartitionSpec as P
 
 HEAD = 64
@@ -108,7 +112,7 @@
     )
 
 
-def per_device(
+def per_device_general(
     tokens,
     doc_lengths,
     keep,
@@ -380,6 +384,674 @@
     )
 
 
+LANES = 128
+TILE = 256
+DOC_ROW, KEEP_ROW, POS_ROW, LINE_ROW, LOG_ROW, FEAT_END = 64, 72, 73, 79, 82, 85
+TP_SWAP = [(0, 1), (1, 0)]
+X_SWAP = [(0, 1), (1, 0), (2, 3), (3, 2)]
+Y_SWAP = [(0, 2), (2, 0), (1, 3), (3, 1)]
+D_SWAP = [(0, 3), (3, 0), (1, 2), (2, 1)]
+PAIR_SWAP = [(0, 1), (1, 0), (2, 3), (3, 2)]
+CROSS_SWAP = [(0, 2), (2, 0), (1, 3), (3, 1)]
+MID_SWAP = [(1, 2), (2, 1)]
+
+
+def dot(left, right, dims=((1,), (0,))):
+    return lax.dot_general(left, right, (dims, ((), ())), preferred_element_type=jnp.float32)
+
+
+def three_terms(value, low):
+    high = low(value)
+    middle = low(value - high)
+    return high, middle, low(value - high - middle)
+
+
+def narrow(value):
+    return lax.reduce_precision(value, 8, 7)
+
+
+def project_kernel(x_ref, w_ref, bias_ref, key_feat_ref, query_feat_ref, qt_ref, q_ref, k_ref, kt_ref, v_ref, vt_ref):
+    heads = q_ref.shape[0]
+    rows = x_ref.shape[0]
+    y = dot(x_ref[...], w_ref[...]) + bias_ref[...]
+    y = y.astype(jnp.bfloat16).astype(jnp.float32)
+    lane = lax.broadcasted_iota(jnp.int32, (rows, LANES), 1)
+    sub = lax.broadcasted_iota(jnp.int32, (LANES, rows), 0)
+
+    def head_part(index):
+        pair = y[:, index // 2 * LANES : (index // 2 + 1) * LANES]
+        if index % 2:
+            pair = pltpu.roll(pair, HEAD, 1)
+        return jnp.where(lane < HEAD, pair, 0.0)
+
+    for head in range(heads):
+        query = head_part(head) * 0.125
+        q_ref[head] = query[:, :HEAD].astype(jnp.bfloat16)
+        qt_ref[head] = (query.T + query_feat_ref[head].astype(jnp.float32)).astype(jnp.bfloat16)
+        key = head_part(heads + head)
+        k_ref[head] = (key + key_feat_ref[...].astype(jnp.float32)).astype(jnp.bfloat16)
+        kt_ref[head] = key.T[:HEAD].astype(jnp.bfloat16)
+        value = head_part(2 * heads + head)
+        ones = (lane >= HEAD) & (lane < HEAD + 3)
+        v_ref[head] = jnp.where(ones, 1.0, value).astype(jnp.bfloat16)
+        vt_ref[head] = jnp.where(sub == HEAD, 1.0, value.T)[:80].astype(jnp.bfloat16)
+
+
+def project(x, weight, bias, key_feat, query_feat, heads):
+    length, width = x.shape
+    rows = 2 * TILE
+    return pl.pallas_call(
+        project_kernel,
+        grid=(length // rows,),
+        in_specs=[
+            pl.BlockSpec((rows, width), lambda i: (i, 0)),
+            pl.BlockSpec(weight.shape, lambda i: (0, 0)),
+            pl.BlockSpec(bias.shape, lambda i: (0, 0)),
+            pl.BlockSpec((rows, LANES), lambda i: (i, 0)),
+            pl.BlockSpec((heads, LANES, rows), lambda i: (0, 0, i)),
+        ],
+        out_specs=[
+            pl.BlockSpec((heads, LANES, rows), lambda i: (0, 0, i)),
+            pl.BlockSpec((heads, rows, HEAD), lambda i: (0, i, 0)),
+            pl.BlockSpec((heads, rows, LANES), lambda i: (0, i, 0)),
+            pl.BlockSpec((heads, HEAD, rows), lambda i: (0, 0, i)),
+            pl.BlockSpec((heads, rows, LANES), lambda i: (0, i, 0)),
+            pl.BlockSpec((heads, 80, rows), lambda i: (0, 0, i)),
+        ],
+        out_shape=[
+            jax.ShapeDtypeStruct((heads, LANES, length), jnp.bfloat16),
+            jax.ShapeDtypeStruct((heads, length, HEAD), jnp.bfloat16),
+            jax.ShapeDtypeStruct((heads, length, LANES), jnp.bfloat16),
+            jax.ShapeDtypeStruct((heads, HEAD, length), jnp.bfloat16),
+            jax.ShapeDtypeStruct((heads, length, LANES), jnp.bfloat16),
+            jax.ShapeDtypeStruct((heads, 80, length), jnp.bfloat16),
+        ],
+        compiler_params=pltpu.CompilerParams(vmem_limit_bytes=40 << 20),
+        cost_estimate=pl.CostEstimate(
+            flops=2 * length * width * weight.shape[1], bytes_accessed=12 << 20, transcendentals=0
+        ),
+        name="project",
+    )(x, weight, bias, key_feat, query_feat)
+
+
+def side_signs(rows):
+    sub = lax.broadcasted_iota(jnp.int32, (LANES, rows), 0)
+    bias_rows = (sub >= POS_ROW) & (sub < LOG_ROW)
+    after = jnp.where(bias_rows, -1.0, 1.0).astype(jnp.bfloat16)
+    same = jnp.where(bias_rows, 0.0, 1.0).astype(jnp.bfloat16)
+    bare = jnp.where(bias_rows | (sub == KEEP_ROW), 0.0, 1.0).astype(jnp.bfloat16)
+    return after, same, bare
+
+
+def diagonal_scores(keys, query_t, same, bare, slope):
+    rows = lax.broadcasted_iota(jnp.int32, (TILE, TILE), 0)
+    cols = lax.broadcasted_iota(jnp.int32, (TILE, TILE), 1)
+    apart = jnp.abs(rows - cols)
+    full = dot(keys, query_t * same) - slope * apart.astype(jnp.float32)
+    return jnp.where(apart == 0, dot(keys, query_t * bare), full)
+
+
+def attend_kernel(span_ref, slope_ref, qt_ref, k_ref, vt_ref, o_ref, ot_ref, lse_ref, max_ref, acc_ref):
+    heads = qt_ref.shape[0]
+    block = pl.program_id(0)
+    after, same, bare = side_signs(TILE)
+
+    def tile_rows(tile):
+        return pl.ds(pl.multiple_of(tile * TILE, TILE), TILE)
+
+    own = tile_rows(block)
+    for head in range(heads):
+        scores = diagonal_scores(k_ref[head, own, :], qt_ref[head], same, bare, slope_ref[head])
+        top = jnp.max(scores, 0, keepdims=True)
+        weights = jnp.exp(scores - top).astype(jnp.bfloat16)
+        max_ref[head] = top
+        acc_ref[head] = dot(vt_ref[head, :, own], weights)
+
+    def step(tile, sign):
+        for head in range(heads):
+            query_t = qt_ref[head] if sign is None else qt_ref[head] * sign
+            scores = dot(k_ref[head, tile_rows(tile), :], query_t)
+            old = max_ref[head]
+            top = jnp.maximum(old, jnp.max(scores, 0, keepdims=True))
+            weights = jnp.exp(scores - top).astype(jnp.bfloat16)
+            max_ref[head] = top
+            acc_ref[head] = acc_ref[head] * jnp.exp(old - top) + dot(
+                vt_ref[head, :, tile_rows(tile)], weights
+            )
+
+    @pl.loop(span_ref[0, block], block)
+    def _(tile):
+        step(tile, None)
+
+    @pl.loop(block + 1, span_ref[1, block])
+    def _(tile):
+        step(tile, after)
+
+    parts = []
+    for head in range(heads):
+        total = acc_ref[head, HEAD : HEAD + 1, :]
+        out_t = acc_ref[head, :HEAD, :] / total
+        ot_ref[head] = out_t
+        parts.append(out_t)
+        lse_ref[head] = max_ref[head] + jnp.log(total)
+    o_ref[...] = jnp.concatenate(parts, 0).T.astype(jnp.bfloat16)
+
+
+def attend(spans, slopes, query_t, keys, value_t):
+    heads, _, length = query_t.shape
+    blocks = length // TILE
+    return pl.pallas_call(
+        attend_kernel,
+        grid_spec=pltpu.PrefetchScalarGridSpec(
+            num_scalar_prefetch=2,
+            grid=(blocks,),
+            in_specs=[
+                pl.BlockSpec((heads, LANES, TILE), lambda i, *_: (0, 0, i)),
+                pl.BlockSpec(keys.shape, lambda i, *_: (0, 0, 0)),
+                pl.BlockSpec(value_t.shape, lambda i, *_: (0, 0, 0)),
+            ],
+            out_specs=[
+                pl.BlockSpec((TILE, heads * HEAD), lambda i, *_: (i, 0)),
+                pl.BlockSpec((heads, HEAD, TILE), lambda i, *_: (0, 0, i)),
+                pl.BlockSpec((heads, 1, TILE), lambda i, *_: (0, 0, i)),
+            ],
+            scratch_shapes=[
+                pltpu.VMEM((heads, 1, TILE), jnp.float32),
+                pltpu.VMEM((heads, 80, TILE), jnp.float32),
+            ],
+        ),
+        out_shape=[
+            jax.ShapeDtypeStruct((length, heads * HEAD), jnp.bfloat16),
+            jax.ShapeDtypeStruct((heads, HEAD, length), jnp.float32),
+            jax.ShapeDtypeStruct((heads, 1, length), jnp.float32),
+        ],
+        compiler_params=pltpu.CompilerParams(vmem_limit_bytes=40 << 20),
+        cost_estimate=pl.CostEstimate(
+            flops=heads * length * length * 256, bytes_accessed=6 << 20, transcendentals=heads * length * length
+        ),
+        name="attend",
+    )(spans, slopes, query_t, keys, value_t)
+
+
+def attend_back_kernel(
+    span_ref, slope_ref, qt_ref, q_ref, k_ref, kt_ref, v_ref, g_ref, ot_ref, lse_ref,
+    dq_ref, dk_ref, dv_ref, qt_log, grad_heads, grad_t, query_acc, key_acc, value_acc,
+):
+    heads = qt_ref.shape[0]
+    blocks = pl.num_programs(0)
+    block = pl.program_id(0)
+    length = qt_ref.shape[2]
+    after, same, bare = side_signs(TILE)
+
+    def low(value):
+        return value.astype(jnp.bfloat16).astype(jnp.float32)
+
+    def tile_rows(tile):
+        return pl.ds(pl.multiple_of(tile * TILE, TILE), TILE)
+
+    @pl.when(block == 0)
+    def _():
+        query_acc[...] = jnp.zeros_like(query_acc)
+        sub = lax.broadcasted_iota(jnp.int32, (LANES, TILE), 0)
+
+        @pl.loop(0, length // TILE)
+        def _(tile):
+            rows = tile_rows(tile)
+            grad = g_ref[rows, :].astype(jnp.float32)
+            turned = grad.T
+            for head in range(heads):
+                own = turned[head * HEAD : (head + 1) * HEAD]
+                delta = jnp.sum(own * ot_ref[head, :, rows], 0, keepdims=True)
+                first, second, third = three_terms(-delta, low)
+                wide = jnp.concatenate([own, jnp.zeros_like(own)], 0)
+                wide = jnp.where(sub == HEAD, first, wide)
+                wide = jnp.where(sub == HEAD + 1, second, wide)
+                wide = jnp.where(sub == HEAD + 2, third, wide)
+                grad_t[head, :, rows] = wide.astype(jnp.bfloat16)
+                grad_heads[head, rows, :] = own.T.astype(jnp.bfloat16)
+                first, second, third = three_terms(-lse_ref[head, :, rows], low)
+                query = qt_ref[head, :, rows].astype(jnp.float32)
+                query = jnp.where(sub == LOG_ROW, first, query)
+                query = jnp.where(sub == LOG_ROW + 1, second, query)
+                query = jnp.where(sub == LOG_ROW + 2, third, query)
+                qt_log[head, :, rows] = query.astype(jnp.bfloat16)
+
+    def accumulate(head, tile, scores, first):
+        rows = tile_rows(tile)
+        probs = jnp.exp(scores)
+        grad_probs = dot(v_ref[head], grad_t[head, :, rows])
+        grad_scores = (probs * grad_probs).astype(jnp.bfloat16)
+        value_part = dot(probs.astype(jnp.bfloat16), grad_heads[head, rows, :])
+        key_part = dot(grad_scores, q_ref[head, rows, :])
+        query_acc[head, :, rows] += dot(kt_ref[head], grad_scores)
+        if first:
+            value_acc[head] = value_part
+            key_acc[head] = key_part
+        else:
+            value_acc[head] += value_part
+            key_acc[head] += key_part
+
+    for head in range(heads):
+        accumulate(
+            head,
+            block,
+            diagonal_scores(k_ref[head], qt_log[head, :, tile_rows(block)], same, bare, slope_ref[head]),
+            True,
+        )
+
+    @pl.loop(span_ref[0, block], block)
+    def _(tile):
+        for head in range(heads):
+            accumulate(head, tile, dot(k_ref[head], qt_log[head, :, tile_rows(tile)] * after), False)
+
+    @pl.loop(block + 1, span_ref[1, block])
+    def _(tile):
+        for head in range(heads):
+            accumulate(head, tile, dot(k_ref[head], qt_log[head, :, tile_rows(tile)]), False)
+
+    dk_ref[...] = jnp.concatenate([key_acc[head] for head in range(heads)], 1).astype(jnp.bfloat16)
+    dv_ref[...] = jnp.concatenate([value_acc[head] for head in range(heads)], 1).astype(jnp.bfloat16)
+
+    @pl.when(block == blocks - 1)
+    def _():
+        @pl.loop(0, length // TILE)
+        def _(tile):
+            rows = tile_rows(tile)
+            turned = jnp.concatenate([query_acc[head, :, rows] for head in range(heads)], 0)
+            dq_ref[rows, :] = (turned.T * 0.125).astype(jnp.bfloat16)
+
+
+def attend_back(spans, slopes, query_t, queries, keys, keys_t, values, grads, out_t, lse):
+    heads, _, length = query_t.shape
+    blocks = length // TILE
+    width = heads * HEAD
+
+    def whole(array):
+        return pl.BlockSpec(array.shape, lambda i, *_: (0,) * array.ndim)
+
+    return pl.pallas_call(
+        attend_back_kernel,
+        grid_spec=pltpu.PrefetchScalarGridSpec(
+            num_scalar_prefetch=2,
+            grid=(blocks,),
+            in_specs=[
+                whole(query_t),
+                whole(queries),
+                pl.BlockSpec((heads, TILE, LANES), lambda i, *_: (0, i, 0)),
+                pl.BlockSpec((heads, HEAD, TILE), lambda i, *_: (0, 0, i)),
+                pl.BlockSpec((heads, TILE, LANES), lambda i, *_: (0, i, 0)),
+                whole(grads),
+                whole(out_t),
+                whole(lse),
+            ],
+            out_specs=[
+                pl.BlockSpec((length, width), lambda i, *_: (0, 0)),
+                pl.BlockSpec((TILE, width), lambda i, *_: (i, 0)),
+                pl.BlockSpec((TILE, width), lambda i, *_: (i, 0)),
+            ],
+            scratch_shapes=[
+                pltpu.VMEM((heads, LANES, length), jnp.bfloat16),
+                pltpu.VMEM((heads, length, HEAD), jnp.bfloat16),
+                pltpu.VMEM((heads, LANES, length), jnp.bfloat16),
+                pltpu.VMEM((heads, HEAD, length), jnp.float32),
+                pltpu.VMEM((heads, TILE, HEAD), jnp.float32),
+                pltpu.VMEM((heads, TILE, HEAD), jnp.float32),
+            ],
+        ),
+        out_shape=[jax.ShapeDtypeStruct((length, width), jnp.bfloat16)] * 3,
+        compiler_params=pltpu.CompilerParams(vmem_limit_bytes=50 << 20),
+        cost_estimate=pl.CostEstimate(
+            flops=heads * length * length * 640, bytes_accessed=12 << 20, transcendentals=heads * length * length
+        ),
+        name="attend_back",
+    )(spans, slopes, query_t, queries, keys, keys_t, values, grads, out_t, lse)
+
+
+def gather_rows(shard, place):
+    parts = (
+        shard,
+        lax.ppermute(shard, "fsdp", X_SWAP),
+        lax.ppermute(shard, "fsdp", Y_SWAP),
+        lax.ppermute(shard, "fsdp", D_SWAP),
+    )
+    rows = shard.shape[0]
+    full = jnp.zeros((4 * rows,) + shard.shape[1:], shard.dtype)
+    for other, part in enumerate(parts):
+        full = lax.dynamic_update_slice_in_dim(full, part, (place ^ other) * rows, 0)
+    return full
+
+
+def scatter_rows(grad, place):
+    rows = grad.shape[0] // 4
+    low = grad.astype(jnp.bfloat16)
+
+    def quarter(other):
+        return lax.dynamic_slice_in_dim(low, (place ^ other) * rows, rows, 0)
+
+    return sum(
+        (
+            lax.ppermute(quarter(other), "fsdp", swap).astype(jnp.float32)
+            for other, swap in ((1, X_SWAP), (2, Y_SWAP), (3, D_SWAP))
+        ),
+        quarter(0).astype(jnp.float32),
+    )
+
+
+def line_sum(part, stage):
+    part = part.astype(jnp.bfloat16)
+    inner = part + lax.ppermute(part, "ctx", [(0, 1), (3, 2)])
+    both = inner + lax.ppermute(inner, "ctx", MID_SWAP)
+    back = lax.ppermute(both, "ctx", [(1, 0), (2, 3)])
+    return jnp.where((stage == 1) | (stage == 2), both, back).astype(jnp.float32)
+
+
+def tp_sum(part):
+    low = part.astype(jnp.bfloat16)
+    return low.astype(jnp.float32) + lax.ppermute(low, "tp", TP_SWAP).astype(jnp.float32)
+
+
+def join_cores(mine, core, axis):
+    other = lax.ppermute(mine, "tp", TP_SWAP)
+    return jnp.concatenate(
+        [jnp.where(core == 0, mine, other), jnp.where(core == 0, other, mine)], axis
+    )
+
+
+def pick(pair, index):
+    return lax.dynamic_index_in_dim(pair, index, 0, keepdims=False)
+
+
+def home_blocks(blocks, stage):
+    odd = stage % 2 == 1
+    far = lax.ppermute(
+        jnp.where(stage < 2, blocks[1], blocks[0]), "ctx", [(1, 3), (2, 0), (0, 1), (3, 2)]
+    )
+    near = jnp.where(stage < 2, blocks[0], blocks[1])
+    crossed = lax.ppermute(near, "ctx", MID_SWAP)
+    near = jnp.where((stage == 1) | (stage == 2), crossed, near)
+    return jnp.stack([jnp.where(odd, far, near), jnp.where(odd, near, far)])
+
+
+def away_blocks(pair, stage):
+    odd = stage % 2 == 1
+    far = lax.ppermute(
+        jnp.where(odd, pair[0], pair[1]), "ctx", [(3, 1), (0, 2), (1, 0), (2, 3)]
+    )
+    near = jnp.where(odd, pair[1], pair[0])
+    crossed = lax.ppermute(near, "ctx", MID_SWAP)
+    near = jnp.where((stage == 1) | (stage == 2), crossed, near)
+    return jnp.stack([jnp.where(stage < 2, near, far), jnp.where(stage < 2, far, near)])
+
+
+def per_device_paired(
+    tokens,
+    doc_lengths,
+    keep,
+    w_query,
+    b_query,
+    w_key,
+    w_value,
+    b_value,
+    w_out,
+    b_out,
+    gain_one,
+    shift_one,
+    w_up,
+    w_down,
+    b_down,
+    gain_two,
+    shift_two,
+    cotangent,
+):
+    _, block_rows, model_width = tokens.shape
+    length = 4 * block_rows
+    half_rows = block_rows // 2
+    local_heads = b_query.shape[0] // HEAD
+    heads = local_heads // 2
+    width = heads * HEAD
+    place = lax.axis_index("fsdp")
+    stage = lax.axis_index("ctx")
+    core = lax.axis_index("tp")
+    seq, half = stage // 2, stage % 2
+    inner = (stage == 1) | (stage == 2)
+
+    def core_half(array):
+        return lax.dynamic_slice_in_dim(array, core * half_rows, half_rows, 1)
+
+    def own_columns(array):
+        return lax.dynamic_slice_in_dim(array, half * width, width, array.ndim - 1)
+
+    token_half = core_half(tokens)
+    ours, theirs = pick(token_half, seq), pick(token_half, 1 - seq)
+    from_pair = lax.ppermute(ours, "ctx", PAIR_SWAP)
+    crossed = lax.ppermute(theirs, "ctx", MID_SWAP)
+    relayed = lax.ppermute(crossed, "ctx", [(1, 0), (2, 3)])
+    far_inner = lax.ppermute(theirs, "ctx", [(3, 1), (0, 2)])
+    far_outer = lax.ppermute(theirs, "ctx", [(3, 0), (0, 3)])
+    arrived = jnp.stack(
+        [from_pair, jnp.where(inner, crossed, relayed), jnp.where(inner, far_inner, far_outer)]
+    )
+    arrived_other = lax.ppermute(arrived, "tp", TP_SWAP)
+    block_at = (stage ^ 1, jnp.where(seq == 0, 2, 1), jnp.where(seq == 0, 3, 0))
+    sequence = jnp.zeros((4, 2, half_rows, model_width), jnp.bfloat16)
+    sequence = lax.dynamic_update_slice(
+        sequence,
+        pick(tokens, seq).reshape(1, 2, half_rows, model_width),
+        (stage, 0, 0, 0),
+    )
+    for slot in range(3):
+        sequence = lax.dynamic_update_slice(
+            sequence, arrived[slot][None, None], (block_at[slot], core, 0, 0)
+        )
+        sequence = lax.dynamic_update_slice(
+            sequence, arrived_other[slot][None, None], (block_at[slot], 1 - core, 0, 0)
+        )
+    sequence = sequence.reshape(length, model_width)
+
+    keep_all = jnp.zeros((4,) + keep.shape, jnp.int32)
+    keep_all = lax.dynamic_update_slice(keep_all, keep[None], (stage, 0, 0))
+    for shift in range(1, 4):
+        moved = lax.ppermute(keep, "ctx", [(i, (i + shift) % 4) for i in range(4)])
+        keep_all = lax.dynamic_update_slice(keep_all, moved[None], ((stage - shift) % 4, 0, 0))
+    keep_row = lax.dynamic_index_in_dim(keep_all, seq, 1, keepdims=False).reshape(length)
+
+    bounds = jnp.cumsum(pick(doc_lengths, seq))
+    docs = bounds.shape[0]
+    positions = jnp.arange(length, dtype=jnp.int32)
+    segments = jnp.sum((bounds[None, :] <= positions[:, None]).astype(jnp.int32), -1)
+    starts = jnp.concatenate([jnp.zeros((1,), jnp.int32), bounds[:-1]])
+    firsts = segments[:: TILE]
+    lasts = segments[TILE - 1 :: TILE]
+    doc_index = jnp.arange(docs, dtype=jnp.int32)
+    span_from = jnp.sum(jnp.where(firsts[:, None] == doc_index, starts, 0), -1) // TILE
+    span_to = (jnp.sum(jnp.where(lasts[:, None] == doc_index, bounds, 0), -1) + TILE - 1) // TILE
+    spans = jnp.stack([span_from, span_to]).astype(jnp.int32)
+    slopes = head_slopes(core * local_heads + half * heads, heads)
+    feature = jnp.arange(LANES, dtype=jnp.int32)
+    key_doc = jnp.where(segments[:, None] == feature - DOC_ROW, 0.0, MASKED)
+    pos_high = (positions // 256 * 256).astype(jnp.float32)[:, None]
+    pos_low = (positions % 256).astype(jnp.float32)[:, None]
+    key_feat = jnp.where(feature < DOC_ROW, 0.0, 1.0)[None, :]
+    key_feat = jnp.where((feature >= DOC_ROW) & (feature < DOC_ROW + docs), key_doc, key_feat)
+    key_feat = jnp.where(feature == KEEP_ROW, jnp.where(keep_row == 1, 0.0, MASKED)[:, None], key_feat)
+    key_feat = jnp.where((feature >= POS_ROW) & (feature < POS_ROW + 3), pos_high, key_feat)
+    key_feat = jnp.where((feature >= POS_ROW + 3) & (feature < LINE_ROW), pos_low, key_feat)
+    key_feat = jnp.where(feature >= FEAT_END, 0.0, key_feat).astype(jnp.bfloat16)
+    rows = feature[None, :, None]
+    query_feat = jnp.where(segments[None, None, :] == rows - DOC_ROW, 1.0, 0.0)
+    query_feat = jnp.where(rows == KEEP_ROW, 1.0, query_feat)
+    slope_terms = three_terms(slopes[:, None, None], narrow)
+    line_terms = three_terms(
+        -slopes[:, None, None] * positions.astype(jnp.float32)[None, None, :], narrow
+    )
+    for term in range(3):
+        here = (rows == POS_ROW + term) | (rows == POS_ROW + 3 + term)
+        query_feat = jnp.where(here, slope_terms[term], query_feat)
+        query_feat = jnp.where(rows == LINE_ROW + term, line_terms[term], query_feat)
+    query_feat = query_feat.astype(jnp.bfloat16)
+
+    w_joined = jnp.concatenate([own_columns(w_query), own_columns(w_key), own_columns(w_value)], -1)
+    full_joined = gather_rows(w_joined, place)
+    full_out = gather_rows(w_out, place)
+    full_up = gather_rows(w_up, place)
+    full_down = gather_rows(w_down, place)
+
+    bias = jnp.concatenate([own_columns(b_query), jnp.zeros((width,), jnp.float32), own_columns(b_value)])
+    pad = -3 * width % LANES
+    query_t, queries, keys, keys_t, values, values_t = project(
+        sequence,
+        jnp.pad(full_joined, ((0, 0), (0, pad))),
+        jnp.pad(bias, (0, pad))[None],
+        key_feat,
+        query_feat,
+        heads,
+    )
+    attended_all, attended_t, lse = attend(spans, slopes, query_t, keys, values_t)
+
+    row_count = length // 2
+
+    def own_half(array):
+        return lax.dynamic_slice_in_dim(array, half * row_count, row_count, 0)
+
+    def other_half(array):
+        return lax.dynamic_slice_in_dim(array, (1 - half) * row_count, row_count, 0)
+
+    mine = own_half(attended_all)
+    recv = lax.ppermute(other_half(attended_all), "ctx", PAIR_SWAP)
+    attended = jnp.concatenate(
+        [jnp.where(half == 0, mine, recv), jnp.where(half == 0, recv, mine)], -1
+    )
+    token_rows = own_half(sequence)
+    cotangent_half = away_blocks(core_half(cotangent), stage)
+    grad_in = join_cores(cotangent_half, core, 1).reshape(row_count, model_width).astype(jnp.float32)
+
+    branch_att = tp_sum(dot(attended, full_out, ((1,), (1,)))) + b_out
+    first_out, normed_one, inv_one = layer_norm(
+        token_rows.astype(jnp.float32) + branch_att, gain_one, shift_one
+    )
+    first_low = first_out.astype(jnp.bfloat16)
+    gate_up = jnp.einsum("rd,dcf->rcf", first_low, full_up, preferred_element_type=jnp.float32)
+    product, gelu_back = jax.vjp(
+        lambda gate_part, up_part: jax.nn.gelu(gate_part, approximate=False) * up_part,
+        gate_up[:, 0],
+        gate_up[:, 1],
+    )
+    hidden = product.astype(jnp.bfloat16)
+    branch_ffn = tp_sum(dot(hidden, full_down, ((1,), (1,)))) + b_down
+    result, normed_two, inv_two = layer_norm(first_out + branch_ffn, gain_two, shift_two)
+    grad_two, d_gain_two, d_shift_two = norm_back(grad_in, normed_two, inv_two, gain_two)
+    grad_ffn = grad_two.astype(jnp.bfloat16)
+    d_b_down = jnp.sum(grad_ffn.astype(jnp.float32), 0)
+    d_w_down = dot(grad_ffn, hidden, ((0,), (0,)))
+    grad_hidden = dot(grad_ffn, full_down)
+    grad_gate, grad_up = gelu_back(grad_hidden)
+    grad_gate_up = jnp.stack([grad_gate, grad_up], 1).astype(jnp.bfloat16)
+    d_w_up = jnp.einsum("rd,rcf->dcf", first_low, grad_gate_up, preferred_element_type=jnp.float32)
+    first_part = jnp.einsum(
+        "rcf,dcf->rd", grad_gate_up, full_up, preferred_element_type=jnp.float32
+    )
+    grad_first = grad_two + tp_sum(first_part)
+    grad_one, d_gain_one, d_shift_one = norm_back(grad_first, normed_one, inv_one, gain_one)
+    grad_att = grad_one.astype(jnp.bfloat16)
+    d_b_out = jnp.sum(grad_att.astype(jnp.float32), 0)
+    d_w_out = dot(grad_att, attended, ((0,), (0,)))
+    grad_attended = dot(grad_att, full_out).astype(jnp.bfloat16)
+
+    mine = own_columns(grad_attended)
+    away = lax.dynamic_slice_in_dim(grad_attended, (1 - half) * width, width, 1)
+    recv = lax.ppermute(away, "ctx", PAIR_SWAP)
+    grad_heads = jnp.concatenate(
+        [jnp.where(half == 0, mine, recv), jnp.where(half == 0, recv, mine)], 0
+    )
+    d_query, d_key, d_value = attend_back(
+        spans, slopes, query_t, queries, keys, keys_t, values, grad_heads, attended_t, lse
+    )
+    grad_project = jnp.concatenate([d_query, d_key, d_value], -1)
+    d_joined = dot(sequence, grad_project, ((0,), (0,)))
+    input_part = dot(grad_project, full_joined, ((1,), (1,))).astype(jnp.bfloat16)
+    input_part = input_part.reshape(4, 2, half_rows, model_width)
+    over_tp = lax.ppermute(
+        lax.dynamic_index_in_dim(input_part, 1 - core, 1, keepdims=False), "tp", TP_SWAP
+    )
+    input_half = lax.dynamic_index_in_dim(input_part, core, 1, keepdims=False).astype(
+        jnp.float32
+    ) + over_tp.astype(jnp.float32)
+    away = lax.dynamic_slice_in_dim(input_half, 2 * (1 - half), 2, 0).astype(jnp.bfloat16)
+    d_rows = (
+        lax.dynamic_slice_in_dim(input_half, 2 * half, 2, 0)
+        + lax.ppermute(away, "ctx", PAIR_SWAP).astype(jnp.float32)
+        + core_half(grad_one.reshape(2, block_rows, model_width))
+    )
+    d_tokens = join_cores(home_blocks(d_rows.astype(jnp.bfloat16), stage), core, 1).astype(jnp.float32)
+    out = join_cores(
+        home_blocks(
+            core_half(result.reshape(2, block_rows, model_width)).astype(jnp.bfloat16), stage
+        ),
+        core,
+        1,
+    )
+
+    sum_out = line_sum(scatter_rows(d_w_out, place), stage)
+    sum_up = line_sum(scatter_rows(d_w_up, place), stage)
+    sum_down = line_sum(scatter_rows(d_w_down, place), stage)
+    joined = scatter_rows(d_joined, place).astype(jnp.bfloat16)
+    joined = joined + lax.ppermute(joined, "ctx", CROSS_SWAP)
+    joined_other = lax.ppermute(joined, "ctx", PAIR_SWAP)
+    low_half = jnp.where(half == 0, joined, joined_other).astype(jnp.float32)
+    high_half = jnp.where(half == 0, joined_other, joined).astype(jnp.float32)
+
+    def both_halves(first):
+        return jnp.concatenate(
+            [low_half[..., first : first + width], high_half[..., first : first + width]], -1
+        )
+
+    d_bias = jnp.concatenate([d_query, d_value], -1).astype(jnp.float32).sum(0).reshape(2, 1, width)
+    d_bias = lax.dynamic_update_slice(
+        jnp.zeros((2, 2, width), jnp.float32), d_bias, (0, half, 0)
+    ).reshape(2, 2 * width)
+    (
+        total_bias,
+        total_b_out,
+        total_b_down,
+        total_gain_one,
+        total_shift_one,
+        total_gain_two,
+        total_shift_two,
+    ) = lax.psum(
+        (d_bias, d_b_out, d_b_down, d_gain_one, d_shift_one, d_gain_two, d_shift_two),
+        ("fsdp", "ctx"),
+    )
+    return (
+        out,
+        d_tokens,
+        both_halves(0),
+        total_bias[0],
+        both_halves(width),
+        both_halves(2 * width),
+        total_bias[1],
+        sum_out,
+        total_b_out,
+        total_gain_one,
+        total_shift_one,
+        sum_up,
+        sum_down,
+        total_b_down,
+        total_gain_two,
+        total_shift_two,
+    )
+
+
+def paired(mesh, tokens, doc_lengths, b_query):
+    sizes = dict(mesh.shape)
+    return (
+        sizes == {"fsdp": 4, "ctx": 4, "tp": 2}
+        and tokens.shape[0] == 8
+        and tokens.shape[1] % (8 * TILE) == 0
+        and doc_lengths.shape[1] <= KEEP_ROW - DOC_ROW
+        and b_query.shape[0] % (4 * HEAD) == 0
+    )
+
+
 def solution(mesh):
     in_specs = (
         P("fsdp", "ctx", None),
@@ -419,6 +1091,11 @@
         P(),
         P(),
     )
-    return jax.shard_map(
-        per_device, mesh=mesh, in_specs=in_specs, out_specs=out_specs, check_vma=False
-    )
+
+    def whole(*args):
+        body = per_device_paired if paired(mesh, args[0], args[1], args[4]) else per_device_general
+        return jax.shard_map(
+            body, mesh=mesh, in_specs=in_specs, out_specs=out_specs, check_vma=False
+        )(*args)
+
+    return whole

time: 1040 us -> 600 us (0.58)
  waiting for transfers between devices: 483 us -> 158 us
  matrix products: 217 us -> 44.1 us
  Pallas kernels: 0 us -> 106 us
  starting transfers between devices: 2.04 us -> 90.8 us
  blocking collectives: 137 us -> 74.7 us
  other arithmetic: 104 us -> 73.4 us
  local copies, waits for them, and re-layouts: 73.4 us -> 44.3 us
  between operations: 16.5 us -> 2.7 us
    reduce_scatter x4 -> x0, waiting for transfers between devices: 236 us -> none  [the longest x1 109 us: per_device(): lax.psum_scatter(key_terms.astype(jnp.bfloat16), 'ctx', scatter_dimension...]
    dot_general x42 -> x11, matrix products: 217 us -> 44.1 us  [the longest x8 21.2 us: dot(): lax.dot_general(left, right, (dims, ((), ())), preferred_element_type=jnp...]
    ppermute x0 -> x60, waiting for transfers between devices: none -> 158 us  [the longest x12 67.7 us: scatter_rows(): lax.ppermute(quarter(other), 'fsdp', swap).astype(jnp.float32)]
    all_gather x3 -> x0, waiting for transfers between devices: 124 us -> none  [the longest x1 78.7 us: per_device(): pairs = lax.all_gather(key_value, 'ctx', axis=1, tiled=True)]
    pallas_call x0 -> x3, Pallas kernels: none -> 106 us  [the longest x1 52 us: attend_back(): pl.pallas_call(attend_back_kernel, grid_spec=pltpu.PrefetchScalarGridSpec...]
    ppermute x0 -> x60, starting transfers between devices: none -> 90.8 us  [the longest x1 16.6 us: per_device_paired(): from_pair = lax.ppermute(ours, 'ctx', PAIR_SWAP)]
    psum x5 -> x0, waiting for transfers between devices: 73.8 us -> none  [the longest x1 21.2 us: per_device(): lax.psum(first_part.astype(jnp.bfloat16), 'tp').astype(jnp.float32)]
    all_gather x5 -> x0, blocking collectives: 56.9 us -> none  [the longest x1 13.5 us: per_device(): piece_keep = lax.all_gather(keep, 'ctx', axis=1, tiled=True)]
  transfers between devices with their start and end apart: 15 -> 60, of which waited for: 13 -> 19; matrix products, arithmetic and copies ran while one was open for 8% -> 15% of each run, Pallas kernels for 0% -> 18%
where the time goes in v1:
time: 600 us; the launch traced here: 594 us
  waiting for transfers between devices  158 us (26%)
  Pallas kernels  106 us (18%)
  starting transfers between devices  90.8 us (15%)
  blocking collectives  74.7 us (12%)
  other arithmetic  73.4 us (12%)
  local copies, waits for them, and re-layouts  44.3 us (7%)
  matrix products  44.1 us (7%)
    psum x1, blocking collectives, per_device_paired(): lax.psum((d_bias, d_b_out, d_b_down, d_gain_one, d_shift_one, d_gain_two,...  74.7 us
    ppermute x12, waiting for transfers between devices, scatter_rows(): lax.ppermute(quarter(other), 'fsdp', swap).astype(jnp.float32)  67.7 us
    pallas_call x1, Pallas kernels, attend_back(): pl.pallas_call(attend_back_kernel, grid_spec=pltpu.PrefetchScalarGridSpec...  52 us
    pallas_call x1, Pallas kernels, attend(): pl.pallas_call(attend_kernel, grid_spec=pltpu.PrefetchScalarGridSpec(num_...  48.6 us
    ppermute x3, waiting for transfers between devices, line_sum(): back = lax.ppermute(both, 'ctx', [(1, 0), (2, 3)])  24 us
    dot_general x8, matrix products, dot(): lax.dot_general(left, right, (dims, ((), ())), preferred_element_type=jnp...  21.2 us
    ppermute x1, starting transfers between devices, per_device_paired(): from_pair = lax.ppermute(ours, 'ctx', PAIR_SWAP)  16.6 us
    convert_element_type x1, other arithmetic, per_device_paired(): hidden = product.astype(jnp.bfloat16)  15 us
  transfers between devices with their start and end apart: 60, of which 19 were waited for; matrix products, arithmetic and copies ran while one was open for 15% of the time, Pallas kernels for 18%

profile of v1, /device:TPU:0, one launch (start us, length us, event | category | flops | bytes accessed | tf_op | source)
XLA Modules:
  0.0 593.7 jit_solution(7552112576172398790)
XLA Ops:
  0.7 3.1 collective-permute-start.9
  3.8 2.1 collective-permute-start.11
  18.2 2.1 constant_dynamic-slice_fusion.19
  26.0 2.5 broadcast_in_dim.310
  35.8 3.2 collective-permute-start.4
  45.8 2.6 select_convert_fusion.2.key_feat_ref
  55.0 16.6 %collective-permute-start = (bf16[256,768]{1,0:T(8,128)(2,1)}, bf16[256,768]{1,0:T(8,128)(2,1)S(1)}, u32[]{:S(2)}, u32[]{:S(2)}) collective-permute-start(bf16[256,768]{1,0:T(8,128)(2,1)} %get-tuple-element.121), channel_id=1, source_target_pairs={{0,2},{2,0},{4,6},{6,4},{1,3},{3,1},{5,7},{7,5},{8,10},{10,8},{12,... | collective-permute-start | bytes 1179656 | tf_op jit(solution)/shard_map/ppermute | solution.py:826
  72.2 5.6 collective-permute-done.2
  78.3 7.3 %collective-permute-done = bf16[256,768]{1,0:T(8,128)(2,1)S(1)} collective-permute-done((bf16[256,768]{1,0:T(8,128)(2,1)}, bf16[256,768]{1,0:T(8,128)(2,1)S(1)}, u32[]{:S(2)}, u32[]{:S(2)}) %collective-permute-start) | collective-permute-done | bytes 393248 | tf_op jit(solution)/shard_map/ppermute | solution.py:826
  86.3 4.6 collective-permute-start.28
  96.4 2.5 collective-permute-done.28
  103.7 5.1 project.1
  110.1 48.6 %attend.1 = (bf16[2048,192]{1,0:T(8,128)(2,1)S(1)}, f32[3,64,2048]{2,1,0:T(8,128)S(1)}, f32[3,1,2048]{2,1,0:T(1,128)S(1)}) custom-call(s32[2,8]{1,0:T(2,128)S(1)} %pad_add_fusion.span_ref, f32[3]{0:T(128)S(1)} %get-tuple-element.155.slope_ref, bf16[3,128,2048]{2,1,0:T(8,128)(2,1)S(1)} %get-tuple-element.28.qt_ref, ...), custom_call_target="tpu_custom_call" | custom-call | flops 3221225472 | bytes 6291456 | tf_op jit(solution)/shard_map/attend/pallas_call | solution.py:543
  158.8 10.4 %collective-permute-start.12 = (bf16[1024,192]{1,0:T(8,128)(2,1)S(1)}, bf16[1024,192]{1,0:T(8,128)(2,1)S(1)}, u32[]{:S(2)}, u32[]{:S(2)}) collective-permute-start(bf16[1024,192]{1,0:T(8,128)(2,1)S(1)} %constant_dynamic-slice_fusion.13), channel_id=1, source_target_pairs={{0,2},{2,0},{4,6},{6,4},{1,3},{3,1},{5,7},{7,5},{8,10},{10,8},{12,... | collective-permute-start | bytes 1179656 | tf_op jit(solution)/shard_map/ppermute | solution.py:920
  169.3 11.1 %collective-permute-done.12 = bf16[1024,192]{1,0:T(8,128)(2,1)S(1)} collective-permute-done((bf16[1024,192]{1,0:T(8,128)(2,1)S(1)}, bf16[1024,192]{1,0:T(8,128)(2,1)S(1)}, u32[]{:S(2)}, u32[]{:S(2)}) %collective-permute-start.12) | collective-permute-done | bytes 393248 | tf_op jit(solution)/shard_map/ppermute | solution.py:920
  186.9 7.6 %fusion.61 = f32[1024,2,1536]{2,0,1:T(8,128)S(1)} fusion(bf16[768,2,1536]{2,0,1:T(8,128)(2,1)} %copy_dynamic-update-slice_fusion, f32[1024,768]{1,0:T(8,128)S(1)} %get-tuple-element.99, f32[768]{0:T(1024)S(1)} %copy-done.54, f32[768]{0:T(1024)S(1)} %copy-done.49, f32[1024]{0:T(1024)S(1)} %add_rsqrt_fusion.1, f32[1024]{0:T(1024)S(1)} %broadcast_multiply_fusion.4), kind=kOutput, calls=%fused_computation.267 | convolution fusion | flops 4835770368 | bytes 20461568 | tf_op jit(solution)/shard_map/rd,dcf->rcf/dot_general | solution.py:933
  194.6 15.0 %multiply_convert_fusion.1 = (bf16[1024,1536]{1,0:T(8,128)(2,1)S(1)}, f32[1024,1536]{1,0:T(8,128)}) fusion(f32[1024,2,1536]{2,0,1:T(8,128)S(1)} %fusion.61), kind=kLoop, calls=%fused_computation.18 | loop fusion | flops 103809024 | bytes 22020096 | tf_op jit(solution)/shard_map/convert_element_type | solution.py:939
  209.5 3.9 convolution_convert_fusion.4
  215.0 3.5 collective-permute-done.29
  220.7 3.1 fusion.64
  227.6 4.6 fusion.56
  234.6 7.9 %fusion.29 = (bf16[1024,1,1536]{2,0,1:T(8,128)(2,1)}, bf16[1024,1,1536]{2,0,1:T(8,128)(2,1)}) fusion(f32[1024,1536]{1,0:T(8,128)} %get-tuple-element.97, f32[1024,1536]{1,0:T(8,128)} %fusion.56, f32[1024,2,1536]{2,0,1:T(8,128)S(1)} %bitcast.224), kind=kLoop, calls=%fused_computation.65 | loop fusion | flops 28311552 | bytes 31457280 | tf_op jit(solution)/shard_map/stack | solution.py:948
  242.5 8.7 %bitcast_convert_fusion = bf16[1024,768]{1,0:T(8,128)(2,1)S(1)} fusion(bf16[768,2,1536]{2,0,1:T(8,128)(2,1)} %copy_dynamic-update-slice_fusion, bf16[1024,1,1536]{2,0,1:T(8,128)(2,1)} %get-tuple-element.103, bf16[1024,1,1536]{2,0,1:T(8,128)(2,1)} %get-tuple-element.102), kind=kOutput, calls=%fused_computation.39 | convolution fusion | flops 4835770368 | bytes 12582912 | tf_op jit(solution)/shard_map/rcf,dcf->rd/dot_general | solution.py:950
  251.3 6.5 %convolution_convert_fusion = bf16[768,2,1536]{2,0,1:T(8,128)(2,1)S(1)} fusion(bf16[1024,1,1536]{2,0,1:T(8,128)(2,1)S(1)} %copy-done.25, bf16[1024,1,1536]{2,0,1:T(8,128)(2,1)S(1)} %copy-done.24, f32[1024,768]{1,0:T(8,128)S(1)} %copy-done.11, f32[768]{0:T(1024)S(1)} %copy-done.54, f32[768]{0:T(1024)S(1)} %copy-done.49, f32[1024]{0:T(1024)S(1)} %add_rsqrt_fusion.1, ...), kind=kOutput, calls=%fused_computation.33 | convolution fusion | flops 4850712576 | bytes 14170112 | tf_op jit(solution)/shard_map/rd,rcf->dcf/dot_general | solution.py:949
  260.7 2.9 convolution_convert_fusion.1
  266.4 5.0 collective-permute-done.24
  273.0 7.6 %collective-permute-done.54 = bf16[192,1536]{1,0:T(8,128)(2,1)S(1)} collective-permute-done((bf16[192,1536]{1,0:T(8,128)(2,1)S(1)}, bf16[192,1536]{1,0:T(8,128)(2,1)S(1)}, u32[]{:S(2)}, u32[]{:S(2)}) %collective-permute-start.54) | collective-permute-done | bytes 589856 | tf_op jit(solution)/shard_map/ppermute | solution.py:733
  281.1 12.1 %collective-permute-done.56 = bf16[192,1536]{1,0:T(8,128)(2,1)S(1)} collective-permute-done((bf16[192,1536]{1,0:T(8,128)(2,1)S(1)}, bf16[192,1536]{1,0:T(8,128)(2,1)S(1)}, u32[]{:S(2)}, u32[]{:S(2)}) %collective-permute-start.56) | collective-permute-done | bytes 589856 | tf_op jit(solution)/shard_map/ppermute | solution.py:733
  294.8 5.6 collective-permute-done.55
  300.6 2.0 collective-permute-start.57
  302.7 2.2 multiply_reduce_fusion
  309.2 9.4 %collective-permute-done.48 = bf16[192,2,1536]{2,0,1:T(8,128)(2,1)S(1)} collective-permute-done((bf16[192,2,1536]{2,0,1:T(8,128)(2,1)S(1)}, bf16[192,2,1536]{2,0,1:T(8,128)(2,1)S(1)}, u32[]{:S(2)}, u32[]{:S(2)}) %collective-permute-start.48) | collective-permute-done | bytes 1179680 | tf_op jit(solution)/shard_map/ppermute | solution.py:733
  319.1 24.8 %collective-permute-done.50 = bf16[192,2,1536]{2,0,1:T(8,128)(2,1)S(1)} collective-permute-done((bf16[192,2,1536]{2,0,1:T(8,128)(2,1)S(1)}, bf16[192,2,1536]{2,0,1:T(8,128)(2,1)S(1)}, u32[]{:S(2)}, u32[]{:S(2)}) %collective-permute-start.50) | collective-permute-done | bytes 1179680 | tf_op jit(solution)/shard_map/ppermute | solution.py:733
  345.4 8.3 %collective-permute-done.49 = bf16[192,2,1536]{2,0,1:T(8,128)(2,1)S(1)} collective-permute-done((bf16[192,2,1536]{2,0,1:T(8,128)(2,1)S(1)}, bf16[192,2,1536]{2,0,1:T(8,128)(2,1)S(1)}, u32[]{:S(2)}, u32[]{:S(2)}) %collective-permute-start.49) | collective-permute-done | bytes 1179680 | tf_op jit(solution)/shard_map/ppermute | solution.py:733
  356.8 5.7 collective-permute-start.51
  365.6 52.0 %attend_back.1 = (bf16[2048,192]{1,0:T(8,128)(2,1)S(1)}, bf16[2048,192]{1,0:T(8,128)(2,1)S(1)}, bf16[2048,192]{1,0:T(8,128)(2,1)S(1)}) custom-call(s32[2,8]{1,0:T(2,128)S(1)} %pad_add_fusion.span_ref, f32[3]{0:T(128)S(1)} %get-tuple-element.155.slope_ref, bf16[3,128,2048]{2,1,0:T(8,128)(2,1)} %copy-done.3, bf16[3,2048,64]{2,1,0:T(8,128)(2,1)} %copy-done.4, ...), custom_call_target="tpu_custom_call" | custom-call | flops 8053063680 | bytes 12582912 | tf_op jit(solution)/shard_map/attend_back/pallas_call | solution.py:672
  417.6 4.1 convolution_convert_fusion.2
  424.6 2.6 convolution_convert_fusion.5
  428.2 2.1 collective-permute-start.39
  434.4 74.7 %all-reduce.2 = (f32[2,384]{1,0:T(2,128)S(1)}, f32[768]{0:T(1024)}, f32[768]{0:T(1024)}, f32[768]{0:T(1024)}, f32[768]{0:T(1024)}, /*index=5*/f32[768]{0:T(1024)}, f32[768]{0:T(1024)}) all-reduce(f32[2,384]{1,0:T(2,128)S(1)} %reshape.534, f32[768]{0:T(1024)S(1)} %get-tuple-element.91, ...), channel_id=1, replica_groups=mesh['fsdp'=4,'ctx'=4,'tp'=2] {'fsdp','ctx'}, use_global_device_ids=true, to_apply=%region_13.14 | all-reduce | flops 5376 | bytes 43008 | tf_op jit(solution)/shard_map/psum | solution.py:1020
  513.9 19.7 %collective-permute-done.47 = bf16[192,384]{1,0:T(8,128)(2,1)S(1)} collective-permute-done((bf16[192,384]{1,0:T(8,128)(2,1)S(1)}, bf16[192,384]{1,0:T(8,128)(2,1)S(1)}, u32[]{:S(2)}, u32[]{:S(2)}) %collective-permute-start.47) | collective-permute-done | bytes 147488 | tf_op jit(solution)/shard_map/ppermute | solution.py:744
  534.4 1.9 add.466
  542.2 9.0 %collective-permute-done.41 = bf16[192,576]{0,1:T(8,128)(2,1)S(1)} collective-permute-done((bf16[192,576]{0,1:T(8,128)(2,1)S(1)}, bf16[192,576]{0,1:T(8,128)(2,1)S(1)}, u32[]{:S(2)}, u32[]{:S(2)}) %collective-permute-start.41) | collective-permute-done | bytes 221216 | tf_op jit(solution)/shard_map/ppermute | solution.py:999
  553.9 14.2 %collective-permute-done.33 = bf16[2,256,768]{2,1,0:T(8,128)(2,1)S(1)} collective-permute-done((bf16[2,256,768]{2,1,0:T(8,128)(2,1)S(1)}, bf16[2,256,768]{2,1,0:T(8,128)(2,1)S(1)}, u32[]{:S(2)}, u32[]{:S(2)}) %collective-permute-start.33) | collective-permute-done | bytes 786464 | tf_op jit(solution)/shard_map/ppermute | solution.py:982
  569.6 7.7 %collective-permute-done.34 = bf16[256,768]{1,0:T(8,128)(2,1)S(1)} collective-permute-done((bf16[256,768]{1,0:T(8,128)(2,1)S(1)}, bf16[256,768]{1,0:T(8,128)(2,1)S(1)}, u32[]{:S(2)}, u32[]{:S(2)}) %collective-permute-start.34) | collective-permute-done | bytes 393248 | tf_op jit(solution)/shard_map/ppermute | solution.py:766
  581.0 4.4 collective-permute-done.53
  586.8 3.2 copy.55
  591.3 1.9 maximum_convert_fusion
  (384 shorter events, 119.7 us)
Async XLA Ops:
  0.7 35.1 %collective-permute-start.9 = (s32[2,512]{1,0:T(2,128)}, s32[2,512]{1,0:T(2,128)}, u32[]{:S(2)}, u32[]{:S(2)}) collective-permute-start(s32[2,512]{1,0:T(2,128)} %param.20), channel_id=1, source_target_pairs={{0,2},{2,4},{4,6},{6,0},{1,3},{3,5},{5,7},{7,1},{8,10},{10,12},{12... | collective-permute-start | bytes 12296 | tf_op jit(solution)/shard_map/ppermute | solution.py:854
  3.8 39.4 %collective-permute-start.11 = (s32[2,512]{1,0:T(2,128)}, s32[2,512]{1,0:T(2,128)}, u32[]{:S(2)}, u32[]{:S(2)}) collective-permute-start(s32[2,512]{1,0:T(2,128)} %param.20), channel_id=1, source_target_pairs={{0,6},{2,0},{4,2},{6,4},{1,7},{3,1},{5,3},{7,5},{8,14},{10,8},{12,... | collective-permute-start | bytes 12296 | tf_op jit(solution)/shard_map/ppermute | solution.py:854
  5.8 34.4 %collective-permute-start.10 = (s32[2,512]{1,0:T(2,128)}, s32[2,512]{1,0:T(2,128)}, u32[]{:S(2)}, u32[]{:S(2)}) collective-permute-start(s32[2,512]{1,0:T(2,128)} %param.20), channel_id=1, source_target_pairs={{0,4},{2,6},{4,0},{6,2},{1,5},{3,7},{5,1},{7,3},{8,12},{10,14},{12... | collective-permute-start | bytes 12296 | tf_op jit(solution)/shard_map/ppermute | solution.py:854
  6.8 41.7 %collective-permute-start.13 = (bf16[192,384]{1,0:T(8,128)(2,1)}, bf16[192,384]{1,0:T(8,128)(2,1)}, u32[]{:S(2)}, u32[]{:S(2)}) collective-permute-start(bf16[192,384]{1,0:T(8,128)(2,1)} %param.26), channel_id=1, source_target_pairs={{0,8},{8,0},{16,24},{24,16},{1,9},{9,1},{17,25},{25,17},{2,10},{10... | collective-permute-start | bytes 442376 | tf_op jit(solution)/shard_map/ppermute | solution.py:713
  8.3 43.5 %collective-permute-start.14 = (bf16[192,384]{1,0:T(8,128)(2,1)}, bf16[192,384]{1,0:T(8,128)(2,1)}, u32[]{:S(2)}, u32[]{:S(2)}) collective-permute-start(bf16[192,384]{1,0:T(8,128)(2,1)} %param.26), channel_id=1, source_target_pairs={{0,16},{16,0},{8,24},{24,8},{1,17},{17,1},{9,25},{25,9},{2,18},{18... | collective-permute-start | bytes 442376 | tf_op jit(solution)/shard_map/ppermute | solution.py:714
  35.8 19.2 %collective-permute-start.4 = (bf16[256,768]{1,0:T(8,128)(2,1)}, bf16[256,768]{1,0:T(8,128)(2,1)S(1)}, u32[]{:S(2)}, u32[]{:S(2)}) collective-permute-start(bf16[256,768]{1,0:T(8,128)(2,1)} %get-tuple-element.120), channel_id=1, source_target_pairs={{6,0},{0,6},{7,1},{1,7},{14,8},{8,14},{15,9},{9,15},{22,16},{16,22... | collective-permute-start | bytes 1179656 | tf_op jit(solution)/shard_map/ppermute | solution.py:830
  40.3 31.3 %collective-permute-start.3 = (bf16[256,768]{1,0:T(8,128)(2,1)}, bf16[256,768]{1,0:T(8,128)(2,1)S(1)}, u32[]{:S(2)}, u32[]{:S(2)}) collective-permute-start(bf16[256,768]{1,0:T(8,128)(2,1)} %get-tuple-element.120), channel_id=1, source_target_pairs={{6,2},{0,4},{7,3},{1,5},{14,10},{8,12},{15,11},{9,13},{22,18},{16,... | collective-permute-start | bytes 1179656 | tf_op jit(solution)/shard_map/ppermute | solution.py:829
  48.5 37.7 %collective-permute-start.15 = (bf16[192,384]{1,0:T(8,128)(2,1)}, bf16[192,384]{1,0:T(8,128)(2,1)S(1)}, u32[]{:S(2)}, u32[]{:S(2)}) collective-permute-start(bf16[192,384]{1,0:T(8,128)(2,1)} %param.26), channel_id=1, source_target_pairs={{0,24},{24,0},{8,16},{16,8},{1,25},{25,1},{9,17},{17,9},{2,26},{26... | collective-permute-start | bytes 442376 | tf_op jit(solution)/shard_map/ppermute | solution.py:715
  48.9 28.8 %collective-permute-start.2 = (bf16[256,768]{1,0:T(8,128)(2,1)S(1)}, bf16[256,768]{1,0:T(8,128)(2,1)S(1)}, u32[]{:S(2)}, u32[]{:S(2)}) collective-permute-start(bf16[256,768]{1,0:T(8,128)(2,1)S(1)} %collective-permute-done.1), channel_id=1, source_target_pairs={{2,0},{4,6},{3,1},{5,7},{10,8},{12,14},{11,9},{13,15},{18,16},{20,... | collective-permute-start | bytes 1179656 | tf_op jit(solution)/shard_map/ppermute | solution.py:828
  51.8 49.4 %collective-permute-start.20 = (bf16[192,1536]{1,0:T(8,128)(2,1)}, bf16[192,1536]{1,0:T(8,128)(2,1)S(1)}, u32[]{:S(2)}, u32[]{:S(2)}) collective-permute-start(bf16[192,1536]{1,0:T(8,128)(2,1)} %param.31), channel_id=1, source_target_pairs={{0,8},{8,0},{16,24},{24,16},{1,9},{9,1},{17,25},{25,17},{2,10},{10... | collective-permute-start | bytes 1769480 | tf_op jit(solution)/shard_map/ppermute | solution.py:713
  55.0 30.6 %collective-permute-start = (bf16[256,768]{1,0:T(8,128)(2,1)}, bf16[256,768]{1,0:T(8,128)(2,1)S(1)}, u32[]{:S(2)}, u32[]{:S(2)}) collective-permute-start(bf16[256,768]{1,0:T(8,128)(2,1)} %get-tuple-element.121), channel_id=1, source_target_pairs={{0,2},{2,0},{4,6},{6,4},{1,3},{3,1},{5,7},{7,5},{8,10},{10,8},{12,... | collective-permute-start | bytes 1179656 | tf_op jit(solution)/shard_map/ppermute | solution.py:826
  71.6 20.1 %collective-permute-start.7 = (bf16[192,576]{1,0:T(8,128)(2,1)S(1)}, bf16[192,576]{1,0:T(8,128)(2,1)S(1)}, u32[]{:S(2)}, u32[]{:S(2)}) collective-permute-start(bf16[192,576]{1,0:T(8,128)(2,1)S(1)} %copy-done.46), channel_id=1, source_target_pairs={{0,16},{16,0},{8,24},{24,8},{1,17},{17,1},{9,25},{25,9},{2,18},{18... | collective-permute-start | bytes 663560 | tf_op jit(solution)/shard_map/ppermute | solution.py:714
  86.2 16.4 %collective-permute-start.5 = (bf16[3,256,768]{2,1,0:T(8,128)(2,1)S(1)}, bf16[3,256,768]{2,1,0:T(8,128)(2,1)S(1)}, u32[]{:S(2)}, u32[]{:S(2)}) collective-permute-start(bf16[3,256,768]{2,1,0:T(8,128)(2,1)S(1)} %pad_maximum_fusion.8), channel_id=1, source_target_pairs={{0,1},{1,0},{2,3},{3,2},{4,5},{5,4},{6,7},{7,6},{8,9},{9,8},{10,11... | collective-permute-start | bytes 3538952 | tf_op jit(solution)/shard_map/ppermute | solution.py:834
  86.3 12.5 %collective-permute-start.28 = (bf16[256,768]{1,0:T(8,128)(2,1)}, bf16[256,768]{1,0:T(8,128)(2,1)S(1)}, u32[]{:S(2)}, u32[]{:S(2)}) collective-permute-start(bf16[256,768]{1,0:T(8,128)(2,1)} %get-tuple-element.115), channel_id=1, source_target_pairs={{6,2},{0,4},{2,0},{4,6},{7,3},{1,5},{3,1},{5,7},{14,10},{8,12},{10... | collective-permute-start | bytes 1179656 | tf_op jit(solution)/shard_map/ppermute | solution.py:777
  93.8 75.4 %collective-permute-start.22 = (bf16[192,1536]{1,0:T(8,128)(2,1)S(1)}, bf16[192,1536]{1,0:T(8,128)(2,1)S(1)}, u32[]{:S(2)}, u32[]{:S(2)}) collective-permute-start(bf16[192,1536]{1,0:T(8,128)(2,1)S(1)} %copy-done.44), channel_id=1, source_target_pairs={{0,24},{24,0},{8,16},{16,8},{1,25},{25,1},{9,17},{17,9},{2,26},{26... | collective-permute-start | bytes 1769480 | tf_op jit(solution)/shard_map/ppermute | solution.py:715
  98.9 59.9 %collective-permute-start.21 = (bf16[192,1536]{1,0:T(8,128)(2,1)S(1)}, bf16[192,1536]{1,0:T(8,128)(2,1)S(1)}, u32[]{:S(2)}, u32[]{:S(2)}) collective-permute-start(bf16[192,1536]{1,0:T(8,128)(2,1)S(1)} %copy-done.44), channel_id=1, source_target_pairs={{0,16},{16,0},{8,24},{24,8},{1,17},{17,1},{9,25},{25,9},{2,18},{18... | collective-permute-start | bytes 1769480 | tf_op jit(solution)/shard_map/ppermute | solution.py:714
  99.6 82.3 %collective-permute-start.17 = (bf16[192,2,1536]{2,1,0:T(2,128)(2,1)S(1)}, bf16[192,2,1536]{2,1,0:T(2,128)(2,1)S(1)}, u32[]{:S(2)}, u32[]{:S(2)}) collective-permute-start(bf16[192,2,1536]{2,1,0:T(2,128)(2,1)S(1)} %copy-done.42), channel_id=1, source_target_pairs={{0,8},{8,0},{16,24},{24,16},{1,9},{9,1},{17,25},{25,17},{2,10},{10... | collective-permute-start | bytes 3538952 | tf_op jit(solution)/shard_map/ppermute | solution.py:713
  101.2 82.9 %collective-permute-start.19 = (bf16[192,2,1536]{2,1,0:T(2,128)(2,1)S(1)}, bf16[192,2,1536]{2,1,0:T(2,128)(2,1)S(1)}, u32[]{:S(2)}, u32[]{:S(2)}) collective-permute-start(bf16[192,2,1536]{2,1,0:T(2,128)(2,1)S(1)} %copy-done.42), channel_id=1, source_target_pairs={{0,24},{24,0},{8,16},{16,8},{1,25},{25,1},{9,17},{17,9},{2,26},{26... | collective-permute-start | bytes 3538952 | tf_op jit(solution)/shard_map/ppermute | solution.py:715
  102.6 80.4 %collective-permute-start.18 = (bf16[192,2,1536]{2,1,0:T(2,128)(2,1)S(1)}, bf16[192,2,1536]{2,1,0:T(2,128)(2,1)S(1)}, u32[]{:S(2)}, u32[]{:S(2)}) collective-permute-start(bf16[192,2,1536]{2,1,0:T(2,128)(2,1)S(1)} %copy-done.42), channel_id=1, source_target_pairs={{0,16},{16,0},{8,24},{24,8},{1,17},{17,1},{9,25},{25,9},{2,18},{18... | collective-permute-start | bytes 3538952 | tf_op jit(solution)/shard_map/ppermute | solution.py:714
  158.8 21.7 %collective-permute-start.12 = (bf16[1024,192]{1,0:T(8,128)(2,1)S(1)}, bf16[1024,192]{1,0:T(8,128)(2,1)S(1)}, u32[]{:S(2)}, u32[]{:S(2)}) collective-permute-start(bf16[1024,192]{1,0:T(8,128)(2,1)S(1)} %constant_dynamic-slice_fusion.13), channel_id=1, source_target_pairs={{0,2},{2,0},{4,6},{6,4},{1,3},{3,1},{5,7},{7,5},{8,10},{10,8},{12,... | collective-permute-start | bytes 1179656 | tf_op jit(solution)/shard_map/ppermute | solution.py:920
  258.5 12.9 %collective-permute-start.24 = (bf16[256,768]{1,0:T(8,128)(2,1)S(1)}, bf16[256,768]{1,0:T(8,128)(2,1)S(1)}, u32[]{:S(2)}, u32[]{:S(2)}) collective-permute-start(bf16[256,768]{1,0:T(8,128)(2,1)S(1)} %get-tuple-element.136), channel_id=1, source_target_pairs={{2,6},{4,0},{0,2},{6,4},{3,7},{5,1},{1,3},{7,5},{10,14},{12,8},{8,... | collective-permute-start | bytes 1179656 | tf_op jit(solution)/shard_map/ppermute | solution.py:766
  260.3 42.3 %collective-permute-start.30 = (bf16[1024,768]{1,0:T(8,128)(2,1)S(1)}, bf16[1024,768]{1,0:T(8,128)(2,1)S(1)}, u32[]{:S(2)}, u32[]{:S(2)}) collective-permute-start(bf16[1024,768]{1,0:T(8,128)(2,1)S(1)} %bitcast_convert_fusion), channel_id=1, source_target_pairs={{0,1},{1,0},{2,3},{3,2},{4,5},{5,4},{6,7},{7,6},{8,9},{9,8},{10,11... | collective-permute-start | bytes 4718600 | tf_op jit(solution)/shard_map/ppermute | solution.py:750
  264.4 16.2 %collective-permute-start.54 = (bf16[192,1536]{1,0:T(8,128)(2,1)S(1)}, bf16[192,1536]{1,0:T(8,128)(2,1)S(1)}, u32[]{:S(2)}, u32[]{:S(2)}) collective-permute-start(bf16[192,1536]{1,0:T(8,128)(2,1)S(1)} %get-tuple-element.107), channel_id=1, source_target_pairs={{0,8},{8,0},{16,24},{24,16},{1,9},{9,1},{17,25},{25,17},{2,10},{10... | collective-permute-start | bytes 1769480 | tf_op jit(solution)/shard_map/ppermute | solution.py:733
  265.0 28.3 %collective-permute-start.56 = (bf16[192,1536]{1,0:T(8,128)(2,1)S(1)}, bf16[192,1536]{1,0:T(8,128)(2,1)S(1)}, u32[]{:S(2)}, u32[]{:S(2)}) collective-permute-start(bf16[192,1536]{1,0:T(8,128)(2,1)S(1)} %get-tuple-element.108), channel_id=1, source_target_pairs={{0,24},{24,0},{8,16},{16,8},{1,25},{25,1},{9,17},{17,9},{2,26},{26... | collective-permute-start | bytes 1769480 | tf_op jit(solution)/shard_map/ppermute | solution.py:733
  271.4 28.9 %collective-permute-start.55 = (bf16[192,1536]{1,0:T(8,128)(2,1)S(1)}, bf16[192,1536]{1,0:T(8,128)(2,1)S(1)}, u32[]{:S(2)}, u32[]{:S(2)}) collective-permute-start(bf16[192,1536]{1,0:T(8,128)(2,1)S(1)} %get-tuple-element.109), channel_id=1, source_target_pairs={{0,16},{16,0},{8,24},{24,8},{1,17},{17,1},{9,25},{25,9},{2,18},{18... | collective-permute-start | bytes 1769480 | tf_op jit(solution)/shard_map/ppermute | solution.py:733
  272.2 46.4 %collective-permute-start.48 = (bf16[192,2,1536]{2,0,1:T(8,128)(2,1)S(1)}, bf16[192,2,1536]{2,0,1:T(8,128)(2,1)S(1)}, u32[]{:S(2)}, u32[]{:S(2)}) collective-permute-start(bf16[192,2,1536]{2,0,1:T(8,128)(2,1)S(1)} %get-tuple-element.104), channel_id=1, source_target_pairs={{0,8},{8,0},{16,24},{24,16},{1,9},{9,1},{17,25},{25,17},{2,10},{10... | collective-permute-start | bytes 3538952 | tf_op jit(solution)/shard_map/ppermute | solution.py:733
  280.6 63.2 %collective-permute-start.50 = (bf16[192,2,1536]{2,0,1:T(8,128)(2,1)S(1)}, bf16[192,2,1536]{2,0,1:T(8,128)(2,1)S(1)}, u32[]{:S(2)}, u32[]{:S(2)}) collective-permute-start(bf16[192,2,1536]{2,0,1:T(8,128)(2,1)S(1)} %get-tuple-element.105), channel_id=1, source_target_pairs={{0,24},{24,0},{8,16},{16,8},{1,25},{25,1},{9,17},{17,9},{2,26},{26... | collective-permute-start | bytes 3538952 | tf_op jit(solution)/shard_map/ppermute | solution.py:733
  293.2 60.4 %collective-permute-start.49 = (bf16[192,2,1536]{2,0,1:T(8,128)(2,1)S(1)}, bf16[192,2,1536]{2,0,1:T(8,128)(2,1)S(1)}, u32[]{:S(2)}, u32[]{:S(2)}) collective-permute-start(bf16[192,2,1536]{2,0,1:T(8,128)(2,1)S(1)} %get-tuple-element.106), channel_id=1, source_target_pairs={{0,16},{16,0},{8,24},{24,8},{1,17},{17,1},{9,25},{25,9},{2,18},{18... | collective-permute-start | bytes 3538952 | tf_op jit(solution)/shard_map/ppermute | solution.py:733
  300.6 55.1 %collective-permute-start.57 = (bf16[192,1536]{1,0:T(8,128)(2,1)S(1)}, bf16[192,1536]{1,0:T(8,128)(2,1)S(1)}, u32[]{:S(2)}, u32[]{:S(2)}) collective-permute-start(bf16[192,1536]{1,0:T(8,128)(2,1)S(1)} %add_convert_fusion.2), channel_id=1, source_target_pairs={{0,2},{6,4},{1,3},{7,5},{8,10},{14,12},{9,11},{15,13},{16,18},{22,... | collective-permute-start | bytes 1769480 | tf_op jit(solution)/shard_map/ppermute | solution.py:742
  307.4 48.5 %collective-permute-start.42 = (bf16[192,384]{1,0:T(8,128)(2,1)S(1)}, bf16[192,384]{1,0:T(8,128)(2,1)S(1)}, u32[]{:S(2)}, u32[]{:S(2)}) collective-permute-start(bf16[192,384]{1,0:T(8,128)(2,1)S(1)} %get-tuple-element.137), channel_id=1, source_target_pairs={{0,8},{8,0},{16,24},{24,16},{1,9},{9,1},{17,25},{25,17},{2,10},{10... | collective-permute-start | bytes 442376 | tf_op jit(solution)/shard_map/ppermute | solution.py:733
  318.6 38.2 %collective-permute-start.44 = (bf16[192,384]{1,0:T(8,128)(2,1)S(1)}, bf16[192,384]{1,0:T(8,128)(2,1)S(1)}, u32[]{:S(2)}, u32[]{:S(2)}) collective-permute-start(bf16[192,384]{1,0:T(8,128)(2,1)S(1)} %get-tuple-element.138), channel_id=1, source_target_pairs={{0,24},{24,0},{8,16},{16,8},{1,25},{25,1},{9,17},{17,9},{2,26},{26... | collective-permute-start | bytes 442376 | tf_op jit(solution)/shard_map/ppermute | solution.py:733
  343.8 18.6 %collective-permute-start.43 = (bf16[192,384]{1,0:T(8,128)(2,1)S(1)}, bf16[192,384]{1,0:T(8,128)(2,1)S(1)}, u32[]{:S(2)}, u32[]{:S(2)}) collective-permute-start(bf16[192,384]{1,0:T(8,128)(2,1)S(1)} %get-tuple-element.139), channel_id=1, source_target_pairs={{0,16},{16,0},{8,24},{24,8},{1,17},{17,1},{9,25},{25,9},{2,18},{18... | collective-permute-start | bytes 442376 | tf_op jit(solution)/shard_map/ppermute | solution.py:733
  355.8 67.3 %collective-permute-start.26 = (bf16[2,256,768]{2,1,0:T(8,128)(2,1)S(1)}, bf16[2,256,768]{2,1,0:T(8,128)(2,1)S(1)}, u32[]{:S(2)}, u32[]{:S(2)}) collective-permute-start(bf16[2,256,768]{2,1,0:T(8,128)(2,1)S(1)} %pad_maximum_fusion.13), channel_id=1, source_target_pairs={{0,1},{1,0},{2,3},{3,2},{4,5},{5,4},{6,7},{7,6},{8,9},{9,8},{10,11... | collective-permute-start | bytes 2359304 | tf_op jit(solution)/shard_map/ppermute | solution.py:754
  355.9 72.3 %collective-permute-start.58 = (bf16[192,1536]{1,0:T(8,128)(2,1)S(1)}, bf16[192,1536]{1,0:T(8,128)(2,1)S(1)}, u32[]{:S(2)}, u32[]{:S(2)}) collective-permute-start(bf16[192,1536]{1,0:T(8,128)(2,1)S(1)} %add.471), channel_id=1, source_target_pairs={{2,4},{4,2},{3,5},{5,3},{10,12},{12,10},{11,13},{13,11},{18,20},{2... | collective-permute-start | bytes 1769480 | tf_op jit(solution)/shard_map/ppermute | solution.py:743
  356.8 177.6 %collective-permute-start.51 = (bf16[192,2,1536]{2,0,1:T(8,128)(2,1)}, bf16[192,2,1536]{2,0,1:T(8,128)(2,1)}, u32[]{:S(2)}, u32[]{:S(2)}) collective-permute-start(bf16[192,2,1536]{2,0,1:T(8,128)(2,1)} %add_convert_fusion), channel_id=1, source_target_pairs={{0,2},{6,4},{1,3},{7,5},{8,10},{14,12},{9,11},{15,13},{16,18},{22,... | collective-permute-start | bytes 3538952 | tf_op jit(solution)/shard_map/ppermute | solution.py:742
  362.5 61.4 %collective-permute-start.45 = (bf16[192,384]{1,0:T(8,128)(2,1)S(1)}, bf16[192,384]{1,0:T(8,128)(2,1)S(1)}, u32[]{:S(2)}, u32[]{:S(2)}) collective-permute-start(bf16[192,384]{1,0:T(8,128)(2,1)S(1)} %add_convert_fusion.4), channel_id=1, source_target_pairs={{0,2},{6,4},{1,3},{7,5},{8,10},{14,12},{9,11},{15,13},{16,18},{22,... | collective-permute-start | bytes 442376 | tf_op jit(solution)/shard_map/ppermute | solution.py:742
  423.1 114.8 %collective-permute-start.32 = (bf16[4,256,768]{2,1,0:T(8,128)(2,1)}, bf16[4,256,768]{2,1,0:T(8,128)(2,1)}, u32[]{:S(2)}, u32[]{:S(2)}) collective-permute-start(bf16[4,256,768]{2,1,0:T(8,128)(2,1)} %dynamic-slice_bitcast_fusion), channel_id=1, source_target_pairs={{0,1},{1,0},{2,3},{3,2},{4,5},{5,4},{6,7},{7,6},{8,9},{9,8},{10,11... | collective-permute-start | bytes 4718600 | tf_op jit(solution)/shard_map/ppermute | solution.py:973
  427.6 82.1 %collective-permute-start.37 = (bf16[192,576]{0,1:T(8,128)(2,1)S(1)}, bf16[192,576]{0,1:T(8,128)(2,1)S(1)}, u32[]{:S(2)}, u32[]{:S(2)}) collective-permute-start(bf16[192,576]{0,1:T(8,128)(2,1)S(1)} %get-tuple-element.130), channel_id=1, source_target_pairs={{0,8},{8,0},{16,24},{24,16},{1,9},{9,1},{17,25},{25,17},{2,10},{10... | collective-permute-start | bytes 663560 | tf_op jit(solution)/shard_map/ppermute | solution.py:733
  428.2 83.1 %collective-permute-start.39 = (bf16[192,576]{0,1:T(8,128)(2,1)S(1)}, bf16[192,576]{0,1:T(8,128)(2,1)S(1)}, u32[]{:S(2)}, u32[]{:S(2)}) collective-permute-start(bf16[192,576]{0,1:T(8,128)(2,1)S(1)} %get-tuple-element.131), channel_id=1, source_target_pairs={{0,24},{24,0},{8,16},{16,8},{1,25},{25,1},{9,17},{17,9},{2,26},{26... | collective-permute-start | bytes 663560 | tf_op jit(solution)/shard_map/ppermute | solution.py:733
  430.3 82.3 %collective-permute-start.38 = (bf16[192,576]{0,1:T(8,128)(2,1)S(1)}, bf16[192,576]{0,1:T(8,128)(2,1)S(1)}, u32[]{:S(2)}, u32[]{:S(2)}) collective-permute-start(bf16[192,576]{0,1:T(8,128)(2,1)S(1)} %get-tuple-element.132), channel_id=1, source_target_pairs={{0,16},{16,0},{8,24},{24,8},{1,17},{17,1},{9,25},{25,9},{2,18},{18... | collective-permute-start | bytes 663560 | tf_op jit(solution)/shard_map/ppermute | solution.py:733
  509.7 31.3 %collective-permute-start.59 = (bf16[192,1536]{1,0:T(8,128)(2,1)}, bf16[192,1536]{1,0:T(8,128)(2,1)S(1)}, u32[]{:S(2)}, u32[]{:S(2)}) collective-permute-start(bf16[192,1536]{1,0:T(8,128)(2,1)} %add.472), channel_id=1, source_target_pairs={{2,0},{4,6},{3,1},{5,7},{10,8},{12,14},{11,9},{13,15},{18,16},{20,... | collective-permute-start | bytes 1769480 | tf_op jit(solution)/shard_map/ppermute | solution.py:744
  511.3 22.3 %collective-permute-start.47 = (bf16[192,384]{1,0:T(8,128)(2,1)S(1)}, bf16[192,384]{1,0:T(8,128)(2,1)S(1)}, u32[]{:S(2)}, u32[]{:S(2)}) collective-permute-start(bf16[192,384]{1,0:T(8,128)(2,1)S(1)} %add.462), channel_id=1, source_target_pairs={{2,0},{4,6},{3,1},{5,7},{10,8},{12,14},{11,9},{13,15},{18,16},{20,... | collective-permute-start | bytes 442376 | tf_op jit(solution)/shard_map/ppermute | solution.py:744
  513.9 23.2 %collective-permute-start.40 = (bf16[192,576]{0,1:T(8,128)(2,1)S(1)}, bf16[192,576]{0,1:T(8,128)(2,1)S(1)}, u32[]{:S(2)}, u32[]{:S(2)}) collective-permute-start(bf16[192,576]{0,1:T(8,128)(2,1)S(1)} %add_convert_fusion.3), channel_id=1, source_target_pairs={{0,4},{4,0},{2,6},{6,2},{1,5},{5,1},{3,7},{7,3},{8,12},{12,8},{10,... | collective-permute-start | bytes 663560 | tf_op jit(solution)/shard_map/ppermute | solution.py:998
  536.3 15.1 %collective-permute-start.52 = (bf16[192,2,1536]{2,0,1:T(8,128)(2,1)S(1)}, bf16[192,2,1536]{2,0,1:T(8,128)(2,1)S(1)}, u32[]{:S(2)}, u32[]{:S(2)}) collective-permute-start(bf16[192,2,1536]{2,0,1:T(8,128)(2,1)S(1)} %add.466), channel_id=1, source_target_pairs={{2,4},{4,2},{3,5},{5,3},{10,12},{12,10},{11,13},{13,11},{18,20},{2... | collective-permute-start | bytes 3538952 | tf_op jit(solution)/shard_map/ppermute | solution.py:743
  537.1 14.1 %collective-permute-start.41 = (bf16[192,576]{0,1:T(8,128)(2,1)S(1)}, bf16[192,576]{0,1:T(8,128)(2,1)S(1)}, u32[]{:S(2)}, u32[]{:S(2)}) collective-permute-start(bf16[192,576]{0,1:T(8,128)(2,1)S(1)} %add.456), channel_id=1, source_target_pairs={{0,2},{2,0},{4,6},{6,4},{1,3},{3,1},{5,7},{7,5},{8,10},{10,8},{12,... | collective-permute-start | bytes 663560 | tf_op jit(solution)/shard_map/ppermute | solution.py:999
  539.7 28.4 %collective-permute-start.33 = (bf16[2,256,768]{2,1,0:T(8,128)(2,1)S(1)}, bf16[2,256,768]{2,1,0:T(8,128)(2,1)S(1)}, u32[]{:S(2)}, u32[]{:S(2)}) collective-permute-start(bf16[2,256,768]{2,1,0:T(8,128)(2,1)S(1)} %dynamic-slice_convert_fusion), channel_id=1, source_target_pairs={{0,2},{2,0},{4,6},{6,4},{1,3},{3,1},{5,7},{7,5},{8,10},{10,8},{12,... | collective-permute-start | bytes 2359304 | tf_op jit(solution)/shard_map/ppermute | solution.py:982
  552.6 32.7 %collective-permute-start.53 = (bf16[192,2,1536]{2,0,1:T(8,128)(2,1)}, bf16[192,2,1536]{2,0,1:T(8,128)(2,1)}, u32[]{:S(2)}, u32[]{:S(2)}) collective-permute-start(bf16[192,2,1536]{2,0,1:T(8,128)(2,1)} %add.467), channel_id=1, source_target_pairs={{2,0},{4,6},{3,1},{5,7},{10,8},{12,14},{11,9},{13,15},{18,16},{20,... | collective-permute-start | bytes 3538952 | tf_op jit(solution)/shard_map/ppermute | solution.py:744
  578.3 11.7 %collective-permute-start.36 = (bf16[2,256,768]{2,1,0:T(8,128)(2,1)}, bf16[2,256,768]{2,1,0:T(8,128)(2,1)}, u32[]{:S(2)}, u32[]{:S(2)}) collective-permute-start(bf16[2,256,768]{2,1,0:T(8,128)(2,1)} %pad_maximum_fusion.15), channel_id=1, source_target_pairs={{0,1},{1,0},{2,3},{3,2},{4,5},{5,4},{6,7},{7,6},{8,9},{9,8},{10,11... | collective-permute-start | bytes 2359304 | tf_op jit(solution)/shard_map/ppermute | solution.py:754
  (83 other events, 1209.8 us)

commit v2 on v1

--- a/solution.py
+++ b/solution.py
@@ -385,15 +385,12 @@
 
 
 LANES = 128
+MESH = pl.DeviceIdType.MESH
 TILE = 256
 DOC_ROW, KEEP_ROW, POS_ROW, LINE_ROW, LOG_ROW, FEAT_END = 64, 72, 73, 79, 82, 85
-TP_SWAP = [(0, 1), (1, 0)]
 X_SWAP = [(0, 1), (1, 0), (2, 3), (3, 2)]
 Y_SWAP = [(0, 2), (2, 0), (1, 3), (3, 1)]
 D_SWAP = [(0, 3), (3, 0), (1, 2), (2, 1)]
-PAIR_SWAP = [(0, 1), (1, 0), (2, 3), (3, 2)]
-CROSS_SWAP = [(0, 2), (2, 0), (1, 3), (3, 1)]
-MID_SWAP = [(1, 2), (2, 1)]
 
 
 def dot(left, right, dims=((1,), (0,))):
@@ -707,80 +704,874 @@
     )(spans, slopes, query_t, queries, keys, keys_t, values, grads, out_t, lse)
 
 
-def gather_rows(shard, place):
-    parts = (
-        shard,
-        lax.ppermute(shard, "fsdp", X_SWAP),
-        lax.ppermute(shard, "fsdp", Y_SWAP),
-        lax.ppermute(shard, "fsdp", D_SWAP),
-    )
-    rows = shard.shape[0]
-    full = jnp.zeros((4 * rows,) + shard.shape[1:], shard.dtype)
-    for other, part in enumerate(parts):
-        full = lax.dynamic_update_slice_in_dim(full, part, (place ^ other) * rows, 0)
-    return full
-
-
-def scatter_rows(grad, place):
-    rows = grad.shape[0] // 4
-    low = grad.astype(jnp.bfloat16)
-
-    def quarter(other):
-        return lax.dynamic_slice_in_dim(low, (place ^ other) * rows, rows, 0)
-
-    return sum(
+def start_kernel(
+    tokens, keep, w_joined, w_out, w_down, sequence, keep_all, full_joined, full_out, full_down,
+    z_send, z_recv, tp_send, tp_recv, w_send, w_recv, keep_send, keep_recv, local_sem,
+):
+    place, stage, core = lax.axis_index("fsdp"), lax.axis_index("ctx"), lax.axis_index("tp")
+    seq = stage // 2
+    half_rows = sequence.shape[2]
+    barrier = pltpu.get_barrier_semaphore()
+    peers = [(place ^ other, stage, core) for other in (1, 2, 3)]
+    peers += [(place, lax.rem(stage + shift, 4), core) for shift in (1, 2, 3)]
+    peers += [(place, stage, 1 - core)]
+    for peer in peers:
+        pl.semaphore_signal(barrier, inc=1, device_id=peer, device_id_type=MESH)
+    pl.semaphore_wait(barrier, len(peers))
+
+    rows = pl.ds(pl.multiple_of(core * half_rows, half_rows), half_rows)
+    ours, theirs = tokens.at[seq, rows], tokens.at[1 - seq, rows]
+
+    def send(source, block, target, slot):
+        return pltpu.make_async_remote_copy(
+            source, sequence.at[block, core], z_send.at[slot], z_recv.at[block],
+            device_id=(place, target, core), device_id_type=MESH,
+        )
+
+    def arrival(block):
+        return pltpu.make_async_remote_copy(
+            ours, sequence.at[block, core], z_send.at[0], z_recv.at[block],
+            device_id=(place, stage, 1 - core), device_id_type=MESH,
+        )
+
+    def share(block):
+        return pltpu.make_async_remote_copy(
+            sequence.at[block, core], sequence.at[block, core], tp_send.at[block], tp_recv.at[block],
+            device_id=(place, stage, 1 - core), device_id_type=MESH,
+        )
+
+    def shared(block):
+        return pltpu.make_async_remote_copy(
+            sequence.at[block, 1 - core], sequence.at[block, 1 - core], tp_send.at[block], tp_recv.at[block],
+            device_id=(place, stage, 1 - core), device_id_type=MESH,
+        )
+
+    first = send(ours, stage, stage ^ 1, 0)
+    ends = ((0, 2, 3), (3, 1, 0))
+    mids = ((1, 2, 0), (2, 1, 3))
+    for own, near, _ in mids:
+
+        @pl.when(stage == own)
+        def _():
+            send(theirs, own, near, 1).start()
+
+    first.start()
+    for own, near, far in ends:
+
+        @pl.when(stage == own)
+        def _():
+            send(theirs, own, far, 1).start()
+            send(theirs, own, near, 2).start()
+
+    weights = []
+    for index, (shard, full) in enumerate(
+        ((w_joined, full_joined), (w_out, full_out), (w_down, full_down))
+    ):
+        for other in (1, 2, 3):
+            sem = 3 * index + other - 1
+            weights.append(
+                pltpu.make_async_remote_copy(
+                    shard, full.at[place], w_send.at[sem], w_recv.at[sem],
+                    device_id=(place ^ other, stage, core), device_id_type=MESH,
+                )
+            )
+            weights[-1].start()
+    flags = []
+    for shift in (1, 2, 3):
+        flags.append(
+            pltpu.make_async_remote_copy(
+                keep, keep_all.at[stage], keep_send.at[shift - 1], keep_recv.at[shift - 1],
+                device_id=(place, lax.rem(stage + shift, 4), core), device_id_type=MESH,
+            )
+        )
+        flags[-1].start()
+    local = []
+    for index, (source, target) in enumerate(
         (
-            lax.ppermute(quarter(other), "fsdp", swap).astype(jnp.float32)
-            for other, swap in ((1, X_SWAP), (2, Y_SWAP), (3, D_SWAP))
+            (tokens.at[seq, pl.ds(0, half_rows)], sequence.at[stage, 0]),
+            (tokens.at[seq, pl.ds(half_rows, half_rows)], sequence.at[stage, 1]),
+            (keep, keep_all.at[stage]),
+            (w_joined, full_joined.at[place]),
+            (w_out, full_out.at[place]),
+            (w_down, full_down.at[place]),
+        )
+    ):
+        local.append(pltpu.make_async_copy(source, target, local_sem.at[index]))
+        local[-1].start()
+
+    for own, near, end in mids:
+        far = 3 - end
+
+        @pl.when(stage == own)
+        def _():
+            arrival(near).wait_recv()
+            send(sequence.at[near, core], near, end, 2).start()
+            share(near).start()
+            arrival(end).wait_recv()
+            share(end).start()
+            arrival(far).wait_recv()
+            share(far).start()
+            send(theirs, own, near, 1).wait_send()
+            send(sequence.at[near, core], near, end, 2).wait_send()
+            for block in (near, end, far):
+                share(block).wait_send()
+                shared(block).wait_recv()
+
+    for own, near, far in ends:
+
+        @pl.when(stage == own)
+        def _():
+            inner = 3 - near
+            for block in (inner, far, near):
+                arrival(block).wait_recv()
+                share(block).start()
+            send(theirs, own, near, 1).wait_send()
+            send(theirs, own, near, 2).wait_send()
+            for block in (inner, far, near):
+                share(block).wait_send()
+                shared(block).wait_recv()
+
+    first.wait_send()
+    for copy in weights + flags:
+        copy.wait()
+    for copy in local:
+        copy.wait()
+
+
+def start(tokens, keep, w_joined, w_out, w_down):
+    _, block_rows, width = tokens.shape
+    dma = pltpu.SemaphoreType.DMA
+    return pl.pallas_call(
+        start_kernel,
+        in_specs=[pl.BlockSpec(memory_space=pl.ANY)] * 5,
+        out_specs=[pl.BlockSpec(memory_space=pl.ANY)] * 5,
+        out_shape=[
+            jax.ShapeDtypeStruct((4, 2, block_rows // 2, width), tokens.dtype),
+            jax.ShapeDtypeStruct((4,) + keep.shape, keep.dtype),
+            jax.ShapeDtypeStruct((4,) + w_joined.shape, w_joined.dtype),
+            jax.ShapeDtypeStruct((4,) + w_out.shape, w_out.dtype),
+            jax.ShapeDtypeStruct((4,) + w_down.shape, w_down.dtype),
+        ],
+        scratch_shapes=[
+            dma((3,)), dma((4,)), dma((4,)), dma((4,)), dma((9,)), dma((9,)), dma((3,)), dma((3,)), dma((6,)),
+        ],
+        compiler_params=pltpu.CompilerParams(collective_id=0, has_side_effects=True),
+        cost_estimate=pl.CostEstimate(flops=40 << 30, bytes_accessed=16 << 20, transcendentals=0),
+        name="start",
+    )(tokens, keep, w_joined, w_out, w_down)
+
+
+def rows_norm(residual):
+    centered = residual - jnp.mean(residual, -1, keepdims=True)
+    inv_scale = lax.rsqrt(jnp.mean(centered * centered, -1, keepdims=True) + NORM_EPS)
+    return centered * inv_scale, inv_scale
+
+
+def rows_norm_back(grad_out, normed, inv_scale, norm_gain):
+    grad_norm = grad_out * norm_gain
+    mean_grad = jnp.mean(grad_norm, -1, keepdims=True)
+    mean_cross = jnp.mean(grad_norm * normed, -1, keepdims=True)
+    return (grad_norm - mean_grad - normed * mean_cross) * inv_scale
+
+
+def middle_kernel(
+    attended, sequence, cotangent, w_out, w_down, up_0, up_1, up_2, up_3, vectors,
+    out_home, grad_one, grad_heads, pack, sums,
+    token_v, mine_v, theirs_v, both_v, cot_v, out_w, down_w, up_w,
+    send_a, recv_a, send_b, recv_b, send_c, recv_c,
+    normed_v, inv_v, low_v, hidden_v, gate_v, lift_v, grad_v, ffn_v, att_v, result_v, keep_v, away_v, tile_v,
+    load_sem, pair_send, pair_recv, cot_send, cot_recv, cot_pass, cot_took,
+    a_send, a_recv, b_send, b_recv, c_send, c_recv, out_send, out_recv, out_pass, out_took,
+    one_sem, keep_sem, away_send, away_recv, tile_sem,
+):
+    place, stage, core = lax.axis_index("fsdp"), lax.axis_index("ctx"), lax.axis_index("tp")
+    seq, half = stage // 2, stage % 2
+    pair = stage ^ 1
+    chunks = token_v.shape[0]
+    units = hidden_v.shape[2]
+    wide = 512
+    quarter = up_0.shape[0]
+
+    barrier = pltpu.get_barrier_semaphore()
+    peers = [(place, lax.rem(stage + shift, 4), core) for shift in (1, 2, 3)]
+    peers += [(place, stage, 1 - core)]
+    for peer in peers:
+        pl.semaphore_signal(barrier, inc=1, device_id=peer, device_id_type=MESH)
+    pl.semaphore_wait(barrier, len(peers))
+
+    def remote(source, target, send, recv, device):
+        return pltpu.make_async_remote_copy(
+            source, target, send, recv, device_id=device, device_id_type=MESH
+        )
+
+    partner = (place, pair, core)
+    other_core = (place, stage, 1 - core)
+
+    def pair_copy(c):
+        return remote(
+            attended.at[(1 - half) * chunks + c], theirs_v.at[c], pair_send.at[c], pair_recv.at[c], partner
+        )
+
+    for c in range(chunks):
+        pair_copy(c).start()
+
+    def cot_owner(which):
+        return 2 * which + stage // 2
+
+    def cot_copy(which):
+        return remote(
+            cotangent.at[which, core], cot_v.at[stage % 2, core],
+            cot_send.at[which], cot_recv.at[stage % 2], (place, cot_owner(which), core),
+        )
+
+    def cot_local(which):
+        return pltpu.make_async_copy(cotangent.at[which], cot_v.at[stage % 2], cot_send.at[which])
+
+    for which in (0, 1):
+
+        @pl.when(cot_owner(which) == stage)
+        def _():
+            cot_local(which).start()
+
+        @pl.when(cot_owner(which) != stage)
+        def _():
+            cot_copy(which).start()
+
+    def cot_arrival(block):
+        return remote(
+            cot_v.at[block, core], cot_v.at[block, core], cot_pass.at[block], cot_recv.at[block], other_core
+        )
+
+    def cot_share(block, whose):
+        return remote(
+            cot_v.at[block, whose], cot_v.at[block, whose], cot_pass.at[block], cot_took.at[block], other_core
+        )
+
+    loads = [
+        pltpu.make_async_copy(attended.at[pl.ds(half * chunks, chunks)], mine_v, load_sem.at[0]),
+        pltpu.make_async_copy(w_out, out_w, load_sem.at[1]),
+        pltpu.make_async_copy(sequence.at[pl.ds(half * chunks, chunks)], token_v, load_sem.at[2]),
+        pltpu.make_async_copy(w_down, down_w, load_sem.at[3]),
+    ]
+    for other, shard in enumerate((up_0, up_1, up_2, up_3)):
+        rows = pl.ds(pl.multiple_of((place ^ other) * quarter, quarter), quarter)
+        loads.append(pltpu.make_async_copy(shard, up_w.at[rows], load_sem.at[4 + other]))
+    for load in loads:
+        load.start()
+
+    def vector(index):
+        return vectors[index : index + 1, :]
+
+    b_out, gain_one, shift_one, b_down, gain_two, shift_two = (vector(i) for i in range(6))
+    sums[...] = jnp.zeros_like(sums)
+
+    def add_sum(index, rows):
+        sums[index : index + 1, :] += jnp.sum(rows, 0, keepdims=True)
+
+    def exchange(c, sent, got, send, recv):
+        return remote(sent.at[c], got.at[c], send.at[c], recv.at[c], other_core)
+
+    def total(c, sent, got):
+        return sent[c].astype(jnp.float32) + got[c].astype(jnp.float32)
+
+    loads[0].wait()
+    loads[1].wait()
+
+    @pl.loop(0, chunks)
+    def _(c):
+        pair_copy(c).wait_recv()
+        first, second = mine_v[c], theirs_v[c]
+        both = jnp.where(
+            half == 0, jnp.concatenate([first, second], 1), jnp.concatenate([second, first], 1)
+        )
+        both_v[c] = both
+        send_a[c] = dot(both, out_w[...], ((1,), (1,))).astype(jnp.bfloat16)
+        exchange(c, send_a, recv_a, a_send, a_recv).start()
+
+    for load in loads[2:]:
+        load.wait()
+
+    @pl.loop(0, chunks)
+    def _(c):
+        exchange(c, send_a, recv_a, a_send, a_recv).wait_recv()
+
+        @pl.when(c == chunks - 1)
+        def _():
+            for block in (0, 1):
+
+                @pl.when(2 * half + block != stage)
+                def _():
+                    cot_arrival(block).wait_recv()
+                    cot_share(block, core).start()
+
+        residual = token_v[c].astype(jnp.float32) + (total(c, send_a, recv_a) + b_out)
+        normed, inv_scale = rows_norm(residual)
+        normed_v[c] = normed
+        inv_v[c] = inv_scale
+        low_v[c] = (normed * gain_one + shift_one).astype(jnp.bfloat16)
+        for n in range(0, units, wide):
+            gate = dot(low_v[c], up_w[:, n : n + wide])
+            lift = dot(low_v[c], up_w[:, units + n : units + n + wide])
+            chance = 0.5 + 0.5 * lax.erf(gate * 0.7071067811865476)
+            density = jnp.exp(gate * gate * -0.5) * 0.3989422804014327
+            gelu = gate * chance
+            hidden_v[c, :, n : n + wide] = (gelu * lift).astype(jnp.bfloat16)
+            gate_v[c, :, n : n + wide] = (lift * (chance + gate * density)).astype(jnp.bfloat16)
+            lift_v[c, :, n : n + wide] = gelu.astype(jnp.bfloat16)
+        send_b[c] = dot(hidden_v[c], down_w[...], ((1,), (1,))).astype(jnp.bfloat16)
+        exchange(c, send_b, recv_b, b_send, b_recv).start()
+
+    for block in (0, 1):
+
+        @pl.when(2 * half + block != stage)
+        def _():
+            cot_share(block, core).wait_send()
+            cot_share(block, 1 - core).wait_recv()
+
+    for which in (0, 1):
+
+        @pl.when(cot_owner(which) == stage)
+        def _():
+            cot_local(which).wait()
+
+        @pl.when(cot_owner(which) != stage)
+        def _():
+            cot_copy(which).wait_send()
+
+    def home(c):
+        return 2 * half + c // 2
+
+    def out_copy(c):
+        return remote(
+            result_v.at[c], out_home.at[seq, core], out_send.at[c], out_recv.at[seq], (place, home(c), core)
+        )
+
+    def out_local(c):
+        return pltpu.make_async_copy(result_v.at[c], out_home.at[seq, c % 2], out_send.at[c])
+
+    @pl.loop(0, chunks)
+    def _(c):
+        exchange(c, send_b, recv_b, b_send, b_recv).wait_recv()
+        normed_one = normed_v[c]
+        residual = normed_one * gain_one + shift_one + (total(c, send_b, recv_b) + b_down)
+        normed, inv_scale = rows_norm(residual)
+        result_v[c] = (normed * gain_two + shift_two).astype(jnp.bfloat16)
+
+        @pl.when(home(c) == stage)
+        def _():
+            out_local(c).start()
+
+        @pl.when((home(c) != stage) & (c % 2 == core))
+        def _():
+            out_copy(c).start()
+
+        grad_in = cot_v[c // 2, c % 2].astype(jnp.float32)
+        add_sum(0, grad_in * normed)
+        add_sum(1, grad_in)
+        grad_two = rows_norm_back(grad_in, normed, inv_scale, gain_two)
+        grad_v[c] = grad_two
+        grad_ffn = grad_two.astype(jnp.bfloat16)
+        ffn_v[c] = grad_ffn
+        add_sum(2, grad_ffn.astype(jnp.float32))
+        for n in range(0, units, wide):
+            grad_hidden = dot(ffn_v[c], down_w[:, n : n + wide])
+            gate_v[c, :, n : n + wide] = (grad_hidden * gate_v[c, :, n : n + wide]).astype(jnp.bfloat16)
+            lift_v[c, :, n : n + wide] = (grad_hidden * lift_v[c, :, n : n + wide]).astype(jnp.bfloat16)
+        send_c[c] = (
+            dot(gate_v[c], up_w[:, :units], ((1,), (1,))) + dot(lift_v[c], up_w[:, units:], ((1,), (1,)))
+        ).astype(jnp.bfloat16)
+        exchange(c, send_c, recv_c, c_send, c_recv).start()
+
+    def one_copy(c):
+        return pltpu.make_async_copy(grad_v.at[c], grad_one.at[c], one_sem.at[c])
+
+    def keep_copy(c):
+        return pltpu.make_async_copy(keep_v.at[c], grad_heads.at[half * chunks + c], keep_sem.at[c])
+
+    def away_copy(c, whose):
+        return remote(
+            away_v.at[c], grad_heads.at[whose * chunks + c], away_send.at[c], away_recv.at[c], partner
+        )
+
+    @pl.loop(0, chunks)
+    def _(c):
+        exchange(c, send_c, recv_c, c_send, c_recv).wait_recv()
+        grad_first = grad_v[c] + total(c, send_c, recv_c)
+        normed = normed_v[c]
+        add_sum(3, grad_first * normed)
+        add_sum(4, grad_first)
+        grad_res = rows_norm_back(grad_first, normed, inv_v[c], gain_one)
+        grad_v[c] = grad_res
+        one_copy(c).start()
+        grad_att = grad_res.astype(jnp.bfloat16)
+        att_v[c] = grad_att
+        add_sum(5, grad_att.astype(jnp.float32))
+        heads = dot(att_v[c], out_w[...]).astype(jnp.bfloat16)
+        first, second = heads[:, : heads.shape[1] // 2], heads[:, heads.shape[1] // 2 :]
+        keep_v[c] = jnp.where(half == 0, first, second)
+        away_v[c] = jnp.where(half == 0, second, first)
+        away_copy(c, half).start()
+        keep_copy(c).start()
+
+    tile = tile_v.shape[2]
+
+    def tile_copy(slot, row, column):
+        return pltpu.make_async_copy(
+            tile_v.at[slot, pl.ds(row * quarter, quarter)],
+            pack.at[place ^ row, :, pl.ds(pl.multiple_of(column * tile, tile), tile)],
+            tile_sem.at[slot, row],
+        )
+
+    def weight_tile(column, left, right):
+        slot = lax.rem(column, 2)
+
+        @pl.when(column >= 2)
+        def _():
+            for row in range(4):
+                tile_copy(slot, row, column - 2).wait()
+
+        rows = left.shape[0] * left.shape[1]
+        tile_v[slot] = dot(
+            left[...].reshape(rows, left.shape[2]), right.reshape(rows, tile), ((0,), (0,))
+        ).astype(jnp.bfloat16)
+        for row in range(4):
+            tile_copy(slot, row, column).start()
+
+    out_tiles = both_v.shape[2] // tile
+    unit_tiles = units // tile
+
+    def columns(index):
+        return pl.ds(pl.multiple_of(index * tile, tile), tile)
+
+    @pl.loop(0, out_tiles)
+    def _(i):
+        weight_tile(i, att_v, both_v[:, :, columns(i)])
+
+    @pl.loop(0, unit_tiles)
+    def _(i):
+        weight_tile(out_tiles + i, ffn_v, hidden_v[:, :, columns(i)])
+
+    @pl.loop(0, unit_tiles)
+    def _(i):
+        weight_tile(out_tiles + unit_tiles + i, low_v, gate_v[:, :, columns(i)])
+
+    @pl.loop(0, unit_tiles)
+    def _(i):
+        weight_tile(out_tiles + 2 * unit_tiles + i, low_v, lift_v[:, :, columns(i)])
+
+    last = out_tiles + 3 * unit_tiles
+    for column in (last - 2, last - 1):
+        for row in range(4):
+            tile_copy(column % 2, row, column).wait()
+
+    def out_arrival(which):
+        return remote(
+            out_home.at[which, core], out_home.at[which, core], out_pass.at[which], out_recv.at[which], other_core
+        )
+
+    def out_share(which, whose):
+        return remote(
+            out_home.at[which, whose], out_home.at[which, whose], out_pass.at[which], out_took.at[which], other_core
+        )
+
+    for which in (0, 1):
+
+        @pl.when(cot_owner(which) != stage)
+        def _():
+            out_arrival(which).wait_recv()
+            out_share(which, core).start()
+
+    @pl.loop(0, chunks)
+    def _(c):
+        pair_copy(c).wait_send()
+        exchange(c, send_a, recv_a, a_send, a_recv).wait_send()
+        exchange(c, send_b, recv_b, b_send, b_recv).wait_send()
+        exchange(c, send_c, recv_c, c_send, c_recv).wait_send()
+        one_copy(c).wait()
+        keep_copy(c).wait()
+        away_copy(c, half).wait_send()
+        away_copy(c, 1 - half).wait_recv()
+
+        @pl.when(home(c) == stage)
+        def _():
+            out_local(c).wait()
+
+        @pl.when((home(c) != stage) & (c % 2 == core))
+        def _():
+            out_copy(c).wait_send()
+
+    for which in (0, 1):
+
+        @pl.when(cot_owner(which) != stage)
+        def _():
+            out_share(which, core).wait_send()
+            out_share(which, 1 - core).wait_recv()
+
+
+def middle(attended, sequence, cotangent, w_out, w_down, up_shards, vectors):
+    chunks, rows, width = 4, sequence.shape[1], sequence.shape[2]
+    head_width, units = w_out.shape[1], w_down.shape[1]
+    columns = head_width + 3 * units
+    dma, bf16, f32 = pltpu.SemaphoreType.DMA, jnp.bfloat16, jnp.float32
+
+    def vmem(shape, dtype=bf16):
+        return pltpu.VMEM(shape, dtype)
+
+    wide = (chunks, rows, width)
+    inner = (chunks, rows, units)
+    narrow_rows = (chunks, rows, head_width // 2)
+    four, two = dma((chunks,)), dma((2,))
+    return pl.pallas_call(
+        middle_kernel,
+        in_specs=[pl.BlockSpec(memory_space=pl.ANY)] * 9 + [pl.BlockSpec(memory_space=pltpu.VMEM)],
+        out_specs=[pl.BlockSpec(memory_space=pl.ANY)] * 4 + [pl.BlockSpec(memory_space=pltpu.VMEM)],
+        out_shape=[
+            jax.ShapeDtypeStruct((2, 2, rows, width), bf16),
+            jax.ShapeDtypeStruct(wide, f32),
+            jax.ShapeDtypeStruct((2 * chunks, rows, head_width // 2), bf16),
+            jax.ShapeDtypeStruct((4, width // 4, columns), bf16),
+            jax.ShapeDtypeStruct((8, width), f32),
+        ],
+        scratch_shapes=[
+            vmem(wide), vmem(narrow_rows), vmem(narrow_rows), vmem((chunks, rows, head_width)),
+            vmem((2, 2, rows, width)), vmem((width, head_width)), vmem((width, units)), vmem((width, 2 * units)),
+            vmem(wide), vmem(wide), vmem(wide), vmem(wide), vmem(wide), vmem(wide),
+            vmem(wide, f32), vmem((chunks, rows, 1), f32), vmem(wide),
+            vmem(inner), vmem(inner), vmem(inner),
+            vmem(wide, f32), vmem(wide), vmem(wide), vmem(wide), vmem(narrow_rows), vmem(narrow_rows),
+            vmem((2, width, 384)),
+            dma((8,)), four, four, two, two, two, two,
+            four, four, four, four, four, four, four, two, two, two,
+            four, four, four, four, dma((2, 4)),
+        ],
+        compiler_params=pltpu.CompilerParams(
+            collective_id=1, has_side_effects=True, vmem_limit_bytes=60 << 20
         ),
-        quarter(0).astype(jnp.float32),
-    )
-
-
-def line_sum(part, stage):
-    part = part.astype(jnp.bfloat16)
-    inner = part + lax.ppermute(part, "ctx", [(0, 1), (3, 2)])
-    both = inner + lax.ppermute(inner, "ctx", MID_SWAP)
-    back = lax.ppermute(both, "ctx", [(1, 0), (2, 3)])
-    return jnp.where((stage == 1) | (stage == 2), both, back).astype(jnp.float32)
-
-
-def tp_sum(part):
-    low = part.astype(jnp.bfloat16)
-    return low.astype(jnp.float32) + lax.ppermute(low, "tp", TP_SWAP).astype(jnp.float32)
-
-
-def join_cores(mine, core, axis):
-    other = lax.ppermute(mine, "tp", TP_SWAP)
-    return jnp.concatenate(
-        [jnp.where(core == 0, mine, other), jnp.where(core == 0, other, mine)], axis
-    )
+        cost_estimate=pl.CostEstimate(flops=50 << 30, bytes_accessed=32 << 20, transcendentals=0),
+        name="middle",
+    )(attended, sequence, cotangent, w_out, w_down, *up_shards, vectors)
+
+
+def tail_kernel(
+    d_query, d_key, d_value, w_joined, sums_in, sequence, grad_one, pack, moved_1, moved_2, moved_3,
+    home, shard, joined, sums,
+    token_v, one_v, part_v, project_v, own_v, tp_sent, tp_got, pair_sent, pair_got, final_v,
+    summed_v, end_got, inner_v, mid_got, total_v, joined_v, quarter_got, cross_sent, cross_got, full_v,
+    step_v, step_got,
+    load_sem, tp_send, tp_recv, pair_send, pair_recv, home_send, home_recv, home_pass, home_took, home_local,
+    end_send, end_recv, mid_send, mid_recv, back_send, back_recv, shard_sem,
+    quarter_send, quarter_recv, cross_send, cross_recv, half_send, half_recv, half_local, step_send, step_recv,
+):
+    place, stage, core = lax.axis_index("fsdp"), lax.axis_index("ctx"), lax.axis_index("tp")
+    seq, half = stage // 2, stage % 2
+    bf16, f32 = jnp.bfloat16, jnp.float32
+    pieces = summed_v.shape[0]
+    piece = summed_v.shape[2]
+    quarter = joined_v.shape[0] // 4
+    width = d_query.shape[2]
+
+    barrier = pltpu.get_barrier_semaphore()
+    peers = [(place ^ other, stage, core) for other in (1, 2, 3)]
+    peers += [(place, lax.rem(stage + shift, 4), core) for shift in (1, 2, 3)]
+    peers += [(place, stage, 1 - core)]
+    for peer in peers:
+        pl.semaphore_signal(barrier, inc=1, device_id=peer, device_id_type=MESH)
+    pl.semaphore_wait(barrier, len(peers))
+
+    def remote(source, target, send, recv, device):
+        return pltpu.make_async_remote_copy(
+            source, target, send, recv, device_id=device, device_id_type=MESH
+        )
+
+    other_core = (place, stage, 1 - core)
+    partner = (place, stage ^ 1, core)
+    at_end = (stage == 0) | (stage == 3)
+    across = (place, jnp.where(at_end, stage, 3 - stage), core)
+    inward = (place, jnp.where(stage < 2, 1, 2), core)
+    outward = (place, jnp.where(stage < 2, 0, 3), core)
+
+    loads = [
+        pltpu.make_async_copy(source, part_v.at[index], load_sem.at[index])
+        for index, source in enumerate((pack.at[0], moved_1, moved_2, moved_3))
+    ]
+    loads.append(pltpu.make_async_copy(sequence, token_v, load_sem.at[4]))
+    loads.append(pltpu.make_async_copy(grad_one, one_v, load_sem.at[5]))
+    for load in loads:
+        load.start()
+
+    def input_share(chunk):
+        rows = jnp.concatenate([d_query[chunk], d_key[chunk], d_value[chunk]], 1)
+        project_v[chunk] = rows
+        return dot(rows, w_joined[...], ((1,), (1,)))
+
+    def block_of(i):
+        return jnp.where(i < 2, 2 * (1 - half) + i, 2 * half + i - 2)
+
+    def tp_copy(i):
+        return remote(tp_sent.at[i], tp_got.at[i], tp_send.at[i], tp_recv.at[i], other_core)
+
+    @pl.loop(0, 4)
+    def _(i):
+        block = block_of(i)
+        tp_sent[i] = input_share(2 * block + 1 - core).astype(bf16)
+        tp_copy(i).start()
+        own_v[i] = input_share(2 * block + core)
+
+    def pair_copy(i):
+        return remote(pair_sent.at[i], pair_got.at[i], pair_send.at[i], pair_recv.at[i], partner)
+
+    @pl.loop(0, 2)
+    def _(i):
+        tp_copy(i).wait_recv()
+        pair_sent[i] = (own_v[i] + tp_got[i].astype(f32)).astype(bf16)
+        pair_copy(i).start()
+
+    def end_copy(j):
+        return remote(summed_v.at[j], end_got.at[j], end_send.at[j], end_recv.at[j], inward)
+
+    def mid_copy(j):
+        return remote(inner_v.at[j], mid_got.at[j], mid_send.at[j], mid_recv.at[j], across)
+
+    def columns(j):
+        return pl.ds(j * piece, piece)
+
+    def back_copy(j):
+        return remote(total_v.at[j], shard.at[:, columns(j)], back_send.at[j], back_recv.at[j], outward)
+
+    def shard_copy(j):
+        return pltpu.make_async_copy(total_v.at[j], shard.at[:, columns(j)], shard_sem.at[j])
+
+    for load in loads[:4]:
+        load.wait()
+    for j in range(pieces):
+        terms = [part_v[index, :, j * piece : (j + 1) * piece].astype(f32) for index in range(4)]
+        summed_v[j] = (terms[0] + terms[1] + (terms[2] + terms[3])).astype(bf16)
+
+        @pl.when(at_end)
+        def _():
+            end_copy(j).start()
+
+    loads[4].wait()
+    tokens = token_v[...].reshape(-1, token_v.shape[2])
+    project = project_v[...].reshape(-1, project_v.shape[2])
+    strip = 256
+    for row in range(0, joined_v.shape[0], strip):
+        joined_v[row : row + strip, :] = dot(
+            tokens[:, row : row + strip], project, ((0,), (0,))
+        ).astype(bf16)
+
+    def quarter_copy(other):
+        rows = pl.ds(pl.multiple_of((place ^ other) * quarter, quarter), quarter)
+        return remote(
+            joined_v.at[rows], quarter_got.at[other - 1], quarter_send.at[other - 1], quarter_recv.at[other - 1],
+            (place ^ other, stage, core),
+        )
+
+    for other in (1, 2, 3):
+        quarter_copy(other).start()
+
+    def column_sum(grads):
+        return jnp.sum(grads[...].reshape(-1, width).astype(f32), 0, keepdims=True)
+
+    bias_parts = []
+    for total in (column_sum(d_query), column_sum(d_value)):
+        for which in (0, 1):
+            bias_parts.append(jnp.where(half == which, total, 0.0))
+    bias = jnp.concatenate(bias_parts, 1)
+    step_v[0] = sums_in[...]
+    step_v[0, 6:7, :] = bias
+    steps = [(place ^ 1, stage, core), (place ^ 2, stage, core), partner, (place, stage ^ 2, core)]
+
+    def step_copy(index):
+        return remote(
+            step_v.at[index], step_got.at[index], step_send.at[index], step_recv.at[index], steps[index]
+        )
+
+    def step_on(index):
+        step_copy(index).wait_recv()
+        step_v[index + 1] = step_v[index] + step_got[index]
+        if index < 3:
+            step_copy(index + 1).start()
+
+    step_copy(0).start()
+
+    loads[5].wait()
+
+    def home_copy(i):
+        return remote(
+            final_v.at[i], home.at[seq, core], home_send.at[i], home_recv.at[seq], (place, 2 * half + i, core)
+        )
+
+    def home_direct(i):
+        return remote(final_v.at[i], home.at[seq, core], home_send.at[i], home_took.at[seq], other_core)
+
+    def home_here(i):
+        return pltpu.make_async_copy(final_v.at[i], home.at[seq, core], home_local)
+
+    for i in range(2):
+        tp_copy(i + 2).wait_recv()
+        pair_copy(i).wait_recv()
+        final_v[i] = (
+            own_v[i + 2] + tp_got[i + 2].astype(f32) + pair_got[i].astype(f32) + one_v[2 * i + core]
+        ).astype(bf16)
+
+        @pl.when(2 * half + i == stage)
+        def _():
+            home_direct(i).start()
+            home_here(i).start()
+
+        @pl.when(2 * half + i != stage)
+        def _():
+            home_copy(i).start()
+
+    step_on(0)
+    for other in (1, 2, 3):
+        quarter_copy(other).wait_recv()
+    own_rows = pl.ds(pl.multiple_of(place * quarter, quarter), quarter)
+    cross_sent[...] = (
+        joined_v[own_rows, :].astype(f32)
+        + quarter_got[0].astype(f32)
+        + (quarter_got[1].astype(f32) + quarter_got[2].astype(f32))
+    ).astype(bf16)
+    cross_copy = remote(cross_sent, cross_got, cross_send, cross_recv, (place, stage ^ 2, core))
+    cross_copy.start()
+    step_on(1)
+
+    def from_end(j):
+        end_copy(j).wait_recv()
+        inner_v[j] = (summed_v[j].astype(f32) + end_got[j].astype(f32)).astype(bf16)
+        mid_copy(j).start()
+
+    def from_mid(j):
+        mid_copy(j).wait_recv()
+        total_v[j] = (inner_v[j].astype(f32) + mid_got[j].astype(f32)).astype(bf16)
+        back_copy(j).start()
+        shard_copy(j).start()
+
+    @pl.when(~at_end)
+    def _():
+        from_end(0)
+        for j in range(1, pieces):
+            from_end(j)
+            from_mid(j - 1)
+
+    step_on(2)
+    cross_copy.wait_recv()
+    full_v[...] = (cross_sent[...].astype(f32) + cross_got[...].astype(f32)).astype(bf16)
+    half_copy = remote(full_v, joined.at[half], half_send, half_recv, partner)
+    half_copy.start()
+    half_here = pltpu.make_async_copy(full_v, joined.at[half], half_local)
+    half_here.start()
+    step_on(3)
+    sums[...] = step_v[4]
+
+    def home_arrival(which):
+        return remote(
+            home.at[which, core], home.at[which, core], home_pass.at[which], home_recv.at[which], other_core
+        )
+
+    def home_share(which, whose):
+        return remote(
+            home.at[which, whose], home.at[which, whose], home_pass.at[which], home_took.at[which], other_core
+        )
+
+    for which in (0, 1):
+
+        @pl.when(2 * which + stage // 2 != stage)
+        def _():
+            home_arrival(which).wait_recv()
+            home_share(which, core).start()
+
+    @pl.when(~at_end)
+    def _():
+        from_mid(pieces - 1)
+        for j in range(pieces):
+            mid_copy(j).wait_send()
+            back_copy(j).wait_send()
+            shard_copy(j).wait()
+
+    @pl.when(at_end)
+    def _():
+        for j in range(pieces):
+            end_copy(j).wait_send()
+            back_copy(j).wait_recv()
+
+    for i in range(4):
+        tp_copy(i).wait_send()
+        step_copy(i).wait_send()
+    for i in range(2):
+        pair_copy(i).wait_send()
+
+        @pl.when(2 * half + i == stage)
+        def _():
+            home_direct(i).wait_send()
+            home_here(i).wait()
+
+        @pl.when(2 * half + i != stage)
+        def _():
+            home_copy(i).wait_send()
+
+    for which in (0, 1):
+
+        @pl.when(2 * which + stage // 2 != stage)
+        def _():
+            home_share(which, core).wait_send()
+
+        home_share(which, 1 - core).wait_recv()
+    for other in (1, 2, 3):
+        quarter_copy(other).wait_send()
+    cross_copy.wait_send()
+    half_here.wait()
+    half_copy.wait_send()
+    remote(full_v, joined.at[1 - half], half_send, half_recv, partner).wait_recv()
+
+
+def tail(d_query, d_key, d_value, w_joined, sums, sequence, grad_one, pack, moved):
+    rows, width = sequence.shape[1:]
+    columns, quarter = pack.shape[2], pack.shape[1]
+    joined = w_joined.shape[1]
+    pieces = 3
+    dma, bf16, f32 = pltpu.SemaphoreType.DMA, jnp.bfloat16, jnp.float32
+
+    def vmem(shape, dtype=bf16):
+        return pltpu.VMEM(shape, dtype)
+
+    any_spec, vmem_spec = pl.BlockSpec(memory_space=pl.ANY), pl.BlockSpec(memory_space=pltpu.VMEM)
+    cut = (pieces, quarter, columns // pieces)
+    one, two, three, four = dma, dma((2,)), dma((3,)), dma((4,))
+    return pl.pallas_call(
+        tail_kernel,
+        in_specs=[vmem_spec] * 5 + [any_spec] * 6,
+        out_specs=[any_spec] * 3 + [vmem_spec],
+        out_shape=[
+            jax.ShapeDtypeStruct((2, 2, rows, width), bf16),
+            jax.ShapeDtypeStruct((quarter, columns), bf16),
+            jax.ShapeDtypeStruct((2, quarter, joined), bf16),
+            jax.ShapeDtypeStruct(sums.shape, f32),
+        ],
+        scratch_shapes=[
+            vmem(sequence.shape), vmem(grad_one.shape, f32), vmem((4, quarter, columns)),
+            vmem((8, rows, joined)), vmem((4, rows, width), f32),
+            vmem((4, rows, width)), vmem((4, rows, width)), vmem((2, rows, width)), vmem((2, rows, width)),
+            vmem((2, rows, width)),
+            vmem(cut), vmem(cut), vmem(cut), vmem(cut), vmem(cut),
+            vmem((width, joined)), vmem((3, quarter, joined)), vmem((quarter, joined)), vmem((quarter, joined)),
+            vmem((quarter, joined)),
+            vmem((5,) + sums.shape, f32), vmem((4,) + sums.shape, f32),
+            dma((6,)), four, four, two, two, two, two, two, two, one,
+            three, three, three, three, three, three, three,
+            three, three, one, one, one, one, one, four, four,
+        ],
+        compiler_params=pltpu.CompilerParams(
+            collective_id=2, has_side_effects=True, vmem_limit_bytes=60 << 20
+        ),
+        cost_estimate=pl.CostEstimate(flops=80 << 30, bytes_accessed=32 << 20, transcendentals=0),
+        name="tail",
+    )(d_query, d_key, d_value, w_joined, sums, sequence, grad_one, pack, *moved)
 
 
 def pick(pair, index):
     return lax.dynamic_index_in_dim(pair, index, 0, keepdims=False)
-
-
-def home_blocks(blocks, stage):
-    odd = stage % 2 == 1
-    far = lax.ppermute(
-        jnp.where(stage < 2, blocks[1], blocks[0]), "ctx", [(1, 3), (2, 0), (0, 1), (3, 2)]
-    )
-    near = jnp.where(stage < 2, blocks[0], blocks[1])
-    crossed = lax.ppermute(near, "ctx", MID_SWAP)
-    near = jnp.where((stage == 1) | (stage == 2), crossed, near)
-    return jnp.stack([jnp.where(odd, far, near), jnp.where(odd, near, far)])
-
-
-def away_blocks(pair, stage):
-    odd = stage % 2 == 1
-    far = lax.ppermute(
-        jnp.where(odd, pair[0], pair[1]), "ctx", [(3, 1), (0, 2), (1, 0), (2, 3)]
-    )
-    near = jnp.where(odd, pair[1], pair[0])
-    crossed = lax.ppermute(near, "ctx", MID_SWAP)
-    near = jnp.where((stage == 1) | (stage == 2), crossed, near)
-    return jnp.stack([jnp.where(stage < 2, near, far), jnp.where(stage < 2, far, near)])
 
 
 def per_device_paired(
@@ -813,7 +1604,6 @@
     stage = lax.axis_index("ctx")
     core = lax.axis_index("tp")
     seq, half = stage // 2, stage % 2
-    inner = (stage == 1) | (stage == 2)
 
     def core_half(array):
         return lax.dynamic_slice_in_dim(array, core * half_rows, half_rows, 1)
@@ -821,38 +1611,12 @@
     def own_columns(array):
         return lax.dynamic_slice_in_dim(array, half * width, width, array.ndim - 1)
 
-    token_half = core_half(tokens)
-    ours, theirs = pick(token_half, seq), pick(token_half, 1 - seq)
-    from_pair = lax.ppermute(ours, "ctx", PAIR_SWAP)
-    crossed = lax.ppermute(theirs, "ctx", MID_SWAP)
-    relayed = lax.ppermute(crossed, "ctx", [(1, 0), (2, 3)])
-    far_inner = lax.ppermute(theirs, "ctx", [(3, 1), (0, 2)])
-    far_outer = lax.ppermute(theirs, "ctx", [(3, 0), (0, 3)])
-    arrived = jnp.stack(
-        [from_pair, jnp.where(inner, crossed, relayed), jnp.where(inner, far_inner, far_outer)]
-    )
-    arrived_other = lax.ppermute(arrived, "tp", TP_SWAP)
-    block_at = (stage ^ 1, jnp.where(seq == 0, 2, 1), jnp.where(seq == 0, 3, 0))
-    sequence = jnp.zeros((4, 2, half_rows, model_width), jnp.bfloat16)
-    sequence = lax.dynamic_update_slice(
-        sequence,
-        pick(tokens, seq).reshape(1, 2, half_rows, model_width),
-        (stage, 0, 0, 0),
-    )
-    for slot in range(3):
-        sequence = lax.dynamic_update_slice(
-            sequence, arrived[slot][None, None], (block_at[slot], core, 0, 0)
-        )
-        sequence = lax.dynamic_update_slice(
-            sequence, arrived_other[slot][None, None], (block_at[slot], 1 - core, 0, 0)
-        )
+    w_joined = jnp.concatenate([own_columns(w_query), own_columns(w_key), own_columns(w_value)], -1)
+    sequence, keep_all, full_joined, full_out, full_down = start(tokens, keep, w_joined, w_out, w_down)
     sequence = sequence.reshape(length, model_width)
-
-    keep_all = jnp.zeros((4,) + keep.shape, jnp.int32)
-    keep_all = lax.dynamic_update_slice(keep_all, keep[None], (stage, 0, 0))
-    for shift in range(1, 4):
-        moved = lax.ppermute(keep, "ctx", [(i, (i + shift) % 4) for i in range(4)])
-        keep_all = lax.dynamic_update_slice(keep_all, moved[None], ((stage - shift) % 4, 0, 0))
+    full_joined = full_joined.reshape(model_width, 3 * width)
+    full_out = full_out.reshape(model_width, 2 * width)
+    full_down = full_down.reshape(model_width, -1)
     keep_row = lax.dynamic_index_in_dim(keep_all, seq, 1, keepdims=False).reshape(length)
 
     bounds = jnp.cumsum(pick(doc_lengths, seq))
@@ -890,11 +1654,8 @@
         query_feat = jnp.where(rows == LINE_ROW + term, line_terms[term], query_feat)
     query_feat = query_feat.astype(jnp.bfloat16)
 
-    w_joined = jnp.concatenate([own_columns(w_query), own_columns(w_key), own_columns(w_value)], -1)
-    full_joined = gather_rows(w_joined, place)
-    full_out = gather_rows(w_out, place)
-    full_up = gather_rows(w_up, place)
-    full_down = gather_rows(w_down, place)
+    up_own, full_joined = lax.optimization_barrier((w_up.reshape(w_up.shape[0], -1), full_joined))
+    up_shards = [up_own] + [lax.ppermute(up_own, "fsdp", swap) for swap in (X_SWAP, Y_SWAP, D_SWAP)]
 
     bias = jnp.concatenate([own_columns(b_query), jnp.zeros((width,), jnp.float32), own_columns(b_value)])
     pad = -3 * width % LANES
@@ -909,118 +1670,49 @@
     attended_all, attended_t, lse = attend(spans, slopes, query_t, keys, values_t)
 
     row_count = length // 2
-
-    def own_half(array):
-        return lax.dynamic_slice_in_dim(array, half * row_count, row_count, 0)
-
-    def other_half(array):
-        return lax.dynamic_slice_in_dim(array, (1 - half) * row_count, row_count, 0)
-
-    mine = own_half(attended_all)
-    recv = lax.ppermute(other_half(attended_all), "ctx", PAIR_SWAP)
-    attended = jnp.concatenate(
-        [jnp.where(half == 0, mine, recv), jnp.where(half == 0, recv, mine)], -1
-    )
-    token_rows = own_half(sequence)
-    cotangent_half = away_blocks(core_half(cotangent), stage)
-    grad_in = join_cores(cotangent_half, core, 1).reshape(row_count, model_width).astype(jnp.float32)
-
-    branch_att = tp_sum(dot(attended, full_out, ((1,), (1,)))) + b_out
-    first_out, normed_one, inv_one = layer_norm(
-        token_rows.astype(jnp.float32) + branch_att, gain_one, shift_one
-    )
-    first_low = first_out.astype(jnp.bfloat16)
-    gate_up = jnp.einsum("rd,dcf->rcf", first_low, full_up, preferred_element_type=jnp.float32)
-    product, gelu_back = jax.vjp(
-        lambda gate_part, up_part: jax.nn.gelu(gate_part, approximate=False) * up_part,
-        gate_up[:, 0],
-        gate_up[:, 1],
-    )
-    hidden = product.astype(jnp.bfloat16)
-    branch_ffn = tp_sum(dot(hidden, full_down, ((1,), (1,)))) + b_down
-    result, normed_two, inv_two = layer_norm(first_out + branch_ffn, gain_two, shift_two)
-    grad_two, d_gain_two, d_shift_two = norm_back(grad_in, normed_two, inv_two, gain_two)
-    grad_ffn = grad_two.astype(jnp.bfloat16)
-    d_b_down = jnp.sum(grad_ffn.astype(jnp.float32), 0)
-    d_w_down = dot(grad_ffn, hidden, ((0,), (0,)))
-    grad_hidden = dot(grad_ffn, full_down)
-    grad_gate, grad_up = gelu_back(grad_hidden)
-    grad_gate_up = jnp.stack([grad_gate, grad_up], 1).astype(jnp.bfloat16)
-    d_w_up = jnp.einsum("rd,rcf->dcf", first_low, grad_gate_up, preferred_element_type=jnp.float32)
-    first_part = jnp.einsum(
-        "rcf,dcf->rd", grad_gate_up, full_up, preferred_element_type=jnp.float32
-    )
-    grad_first = grad_two + tp_sum(first_part)
-    grad_one, d_gain_one, d_shift_one = norm_back(grad_first, normed_one, inv_one, gain_one)
-    grad_att = grad_one.astype(jnp.bfloat16)
-    d_b_out = jnp.sum(grad_att.astype(jnp.float32), 0)
-    d_w_out = dot(grad_att, attended, ((0,), (0,)))
-    grad_attended = dot(grad_att, full_out).astype(jnp.bfloat16)
-
-    mine = own_columns(grad_attended)
-    away = lax.dynamic_slice_in_dim(grad_attended, (1 - half) * width, width, 1)
-    recv = lax.ppermute(away, "ctx", PAIR_SWAP)
-    grad_heads = jnp.concatenate(
-        [jnp.where(half == 0, mine, recv), jnp.where(half == 0, recv, mine)], 0
-    )
+    vectors = jnp.stack([b_out, gain_one, shift_one, b_down, gain_two, shift_two, b_out, b_out])
+    out, grad_one, grad_heads, pack, sums = middle(
+        attended_all.reshape(8, half_rows, width),
+        sequence.reshape(8, half_rows, model_width),
+        cotangent.reshape(2, 2, half_rows, model_width),
+        full_out,
+        full_down,
+        up_shards,
+        vectors,
+    )
+    out = out.reshape(2, block_rows, model_width)
+    grad_heads = grad_heads.reshape(length, width)
+    moved = [
+        lax.ppermute(pack[other], "fsdp", swap)
+        for other, swap in ((1, X_SWAP), (2, Y_SWAP), (3, D_SWAP))
+    ]
     d_query, d_key, d_value = attend_back(
         spans, slopes, query_t, queries, keys, keys_t, values, grad_heads, attended_t, lse
     )
-    grad_project = jnp.concatenate([d_query, d_key, d_value], -1)
-    d_joined = dot(sequence, grad_project, ((0,), (0,)))
-    input_part = dot(grad_project, full_joined, ((1,), (1,))).astype(jnp.bfloat16)
-    input_part = input_part.reshape(4, 2, half_rows, model_width)
-    over_tp = lax.ppermute(
-        lax.dynamic_index_in_dim(input_part, 1 - core, 1, keepdims=False), "tp", TP_SWAP
-    )
-    input_half = lax.dynamic_index_in_dim(input_part, core, 1, keepdims=False).astype(
-        jnp.float32
-    ) + over_tp.astype(jnp.float32)
-    away = lax.dynamic_slice_in_dim(input_half, 2 * (1 - half), 2, 0).astype(jnp.bfloat16)
-    d_rows = (
-        lax.dynamic_slice_in_dim(input_half, 2 * half, 2, 0)
-        + lax.ppermute(away, "ctx", PAIR_SWAP).astype(jnp.float32)
-        + core_half(grad_one.reshape(2, block_rows, model_width))
-    )
-    d_tokens = join_cores(home_blocks(d_rows.astype(jnp.bfloat16), stage), core, 1).astype(jnp.float32)
-    out = join_cores(
-        home_blocks(
-            core_half(result.reshape(2, block_rows, model_width)).astype(jnp.bfloat16), stage
-        ),
-        core,
-        1,
-    )
-
-    sum_out = line_sum(scatter_rows(d_w_out, place), stage)
-    sum_up = line_sum(scatter_rows(d_w_up, place), stage)
-    sum_down = line_sum(scatter_rows(d_w_down, place), stage)
-    joined = scatter_rows(d_joined, place).astype(jnp.bfloat16)
-    joined = joined + lax.ppermute(joined, "ctx", CROSS_SWAP)
-    joined_other = lax.ppermute(joined, "ctx", PAIR_SWAP)
-    low_half = jnp.where(half == 0, joined, joined_other).astype(jnp.float32)
-    high_half = jnp.where(half == 0, joined_other, joined).astype(jnp.float32)
+    d_tokens, shard, joined, sums = tail(
+        d_query.reshape(8, half_rows, width),
+        d_key.reshape(8, half_rows, width),
+        d_value.reshape(8, half_rows, width),
+        full_joined,
+        sums,
+        sequence.reshape(8, half_rows, model_width),
+        grad_one,
+        pack,
+        moved,
+    )
+    d_tokens = d_tokens.reshape(2, block_rows, model_width).astype(jnp.float32)
+    shard = shard.astype(jnp.float32)
+    sum_out, sum_down, sum_up = jnp.split(shard, (2 * width, 2 * width + w_down.shape[1]), 1)
+    sum_up = sum_up.reshape(w_up.shape)
+    joined = joined.astype(jnp.float32)
 
     def both_halves(first):
         return jnp.concatenate(
-            [low_half[..., first : first + width], high_half[..., first : first + width]], -1
-        )
-
-    d_bias = jnp.concatenate([d_query, d_value], -1).astype(jnp.float32).sum(0).reshape(2, 1, width)
-    d_bias = lax.dynamic_update_slice(
-        jnp.zeros((2, 2, width), jnp.float32), d_bias, (0, half, 0)
-    ).reshape(2, 2 * width)
-    (
-        total_bias,
-        total_b_out,
-        total_b_down,
-        total_gain_one,
-        total_shift_one,
-        total_gain_two,
-        total_shift_two,
-    ) = lax.psum(
-        (d_bias, d_b_out, d_b_down, d_gain_one, d_shift_one, d_gain_two, d_shift_two),
-        ("fsdp", "ctx"),
-    )
+            [joined[0, :, first : first + width], joined[1, :, first : first + width]], -1
+        )
+
+    total_gain_two, total_shift_two, total_b_down, total_gain_one, total_shift_one, total_b_out = sums[:6]
+    total_bias = sums[6].reshape(2, 2 * width)
     return (
         out,
         d_tokens,

time: 600 us -> 410 us (0.68)
  Pallas kernels: 106 us -> 324 us
  waiting for transfers between devices: 158 us -> 38.1 us
  starting transfers between devices: 90.8 us -> 7.12 us
  blocking collectives: 74.7 us -> 0 us
  other arithmetic: 73.4 us -> 11.2 us
  matrix products: 44.1 us -> 0 us
  local copies, waits for them, and re-layouts: 44.3 us -> 28.3 us
    pallas_call x0 -> x3, Pallas kernels: none -> 239 us  [the longest x1 105 us: tail(): pl.pallas_call(tail_kernel, in_specs=[vmem_spec] * 5 + [any_spec] * 6, ou...]
    ppermute x60 -> x6, waiting for transfers between devices: 158 us -> 38.1 us  [the longest x3 38.1 us: per_device_paired(): lax.ppermute(pack[other], 'fsdp', swap)]
    ppermute x60 -> x6, starting transfers between devices: 90.8 us -> 7.12 us  [the longest x3 3.57 us: per_device_paired(): lax.ppermute(pack[other], 'fsdp', swap)]
    psum x1 -> x0, blocking collectives: 74.7 us -> none  [per_device_paired(): lax.psum((d_bias, d_b_out, d_b_down, d_gain_one, d_shift_one, d_gain_two,...]
    dot_general x11 -> x0, matrix products: 44.1 us -> none  [the longest x8 21.2 us: dot(): lax.dot_general(left, right, (dims, ((), ())), preferred_element_type=jnp...]
    convert_element_type x11 -> x2, other arithmetic: 23.7 us -> 3.41 us  [the longest x1 3.35 us: per_device_paired(): d_tokens = d_tokens.reshape(2, block_rows, model_width).astype(jnp.float32)]
    dynamic_update_slice x25 -> x0, local copies, waits for them, and re-layouts: 15 us -> none  [the longest x15 10.2 us: gather_rows(): lax.dynamic_update_slice_in_dim(full, part, (place ^ other) * rows, 0)]
    reduce_sum x10 -> x0, other arithmetic: 12.6 us -> none  [the longest x3 4.46 us: norm_back(): return (grad_in, jnp.sum(grad_out * normed, 0), jnp.sum(grad_out, 0))]
  transfers between devices with their start and end apart: 60 -> 6, of which waited for: 19 -> 1; matrix products, arithmetic and copies ran while one was open for 15% -> 2% of each run, Pallas kernels for 18% -> 21%
where the time goes in v2:
time: 410 us
  Pallas kernels  324 us (79%)
  waiting for transfers between devices  38.1 us (9%)
  local copies, waits for them, and re-layouts  28.3 us (7%)
  other arithmetic  11.2 us (3%)
  starting transfers between devices  7.12 us (2%)
    pallas_call x1, Pallas kernels, tail(): pl.pallas_call(tail_kernel, in_specs=[vmem_spec] * 5 + [any_spec] * 6, ou...  105 us
    pallas_call x1, Pallas kernels, middle(): pl.pallas_call(middle_kernel, in_specs=[pl.BlockSpec(memory_space=pl.ANY)...  74 us
    pallas_call x1, Pallas kernels, start(): pl.pallas_call(start_kernel, in_specs=[pl.BlockSpec(memory_space=pl.ANY)]...  60.4 us
    pallas_call x1, Pallas kernels, attend_back(): pl.pallas_call(attend_back_kernel, grid_spec=pltpu.PrefetchScalarGridSpec...  41.6 us
    ppermute x3, waiting for transfers between devices, per_device_paired(): lax.ppermute(pack[other], 'fsdp', swap)  38.1 us
    pallas_call x1, Pallas kernels, attend(): pl.pallas_call(attend_kernel, grid_spec=pltpu.PrefetchScalarGridSpec(num_...  37.8 us
    unnamed x60, local copies, waits for them, and re-layouts  11.6 us
  transfers between devices with their start and end apart: 6, of which 1 were waited for; matrix products, arithmetic and copies ran while one was open for 2% of the time, Pallas kernels for 21%

profile of v2, /device:TPU:0, one launch (start us, length us, event | category | flops | bytes accessed | tf_op | source)
XLA Modules:
  0.0 409.5 jit_solution(11090822758085342836)
XLA Ops:
  0.7 1.5 copy.34
  2.2 0.1 constant_dynamic-slice_fusion.2
  2.3 0.1 constant_dynamic-slice_fusion
  2.5 0.8 pad_maximum_fusion.3.w_joined
  3.4 60.4 %start.1 = (bf16[4,2,256,768]{3,2,1,0:T(8,128)(2,1)}, s32[4,2,512]{2,1,0:T(2,128)}, bf16[4,192,576]{2,1,0:T(8,128)(2,1)}, bf16[4,192,384]{2,1,0:T(8,128)(2,1)}, bf16[4,192,1536]{2,1,0:T(8,128)(2,1)}) custom-call(bf16[2,512,768]{2,1,0:T(8,128)(2,1)} %tokens.1, s32[2,512]{1,0:T(2,128)} %keep.1, bf16[192,576]{1,0:T(8,128)(2,1)} %pad_maximum_fusion.3.w_joined, ...), custom_call_target="tpu_custom_call" | custom-call | flops 42949672960 | bytes 16777216 | tf_op jit(solution)/shard_map/start/pallas_call | solution.py:844
  63.7 2.5 collective-permute-start.2
  66.3 0.5 collective-permute-start.1
  66.8 0.5 collective-permute-start
  67.5 0.2 reduce-window.4
  68.3 0.2 select_reduce_fusion
  68.5 0.7 compare_select_fusion
  69.3 0.2 select_reduce_fusion.1
  69.5 0.1 subtract_reduce-precision_fusion
  69.6 0.2 select_select_fusion
  69.8 1.3 pad.8.w_ref
  71.1 0.7 stack.35.vectors
  71.7 1.9 select_convert_fusion.1.key_feat_ref
  73.6 0.7 select_convert_fusion.query_feat_ref
  74.4 1.9 copy-done.2
  76.2 5.0 %project.1 = (bf16[3,128,2048]{2,1,0:T(8,128)(2,1)S(1)}, bf16[3,2048,64]{2,1,0:T(8,128)(2,1)S(1)}, bf16[3,2048,128]{2,1,0:T(8,128)(2,1)S(1)}, bf16[3,64,2048]{2,...) custom-call(bf16[2048,768]{1,0:T(8,128)(2,1)S(1)} %bitcast.59, ...), custom_call_target="tpu_custom_call" | custom-call | flops 2013265920 | bytes 12582912 | tf_op jit(solution)/shard_map/project/pallas_call | solution.py:440
  81.3 1.1 copy-done.8
  82.4 37.8 %attend.1 = (bf16[2048,192]{1,0:T(8,128)(2,1)S(1)}, f32[3,64,2048]{2,1,0:T(8,128)S(1)}, f32[3,1,2048]{2,1,0:T(1,128)S(1)}) custom-call(s32[2,8]{1,0:T(2,128)S(1)} %pad_add_fusion.span_ref, f32[3]{0:T(128)S(1)} %get-tuple-element.94.slope_ref, bf16[3,128,2048]{2,1,0:T(8,128)(2,1)S(1)} %get-tuple-element.48.qt_ref, ...), custom_call_target="tpu_custom_call" | custom-call | flops 3221225472 | bytes 6291456 | tf_op jit(solution)/shard_map/attend/pallas_call | solution.py:540
  120.3 1.0 copy-done.6
  121.2 1.2 copy-done.11
  122.4 74.0 %middle.1 = (bf16[2,2,256,768]{3,2,1,0:T(8,128)(2,1)}, f32[4,256,768]{2,1,0:T(8,128)}, bf16[8,256,192]{2,1,0:T(8,128)(2,1)}, bf16[4,192,4992]{2,1,0:T(8,128)(2,1)}, f32[8,768]{1,0:T(8,128)}) custom-call(bf16[8,256,192]{2,1,0:T(8,128)(2,1)} %bitcast.63, bf16[8,256,768]{2,1,0:T(8,128)(2,1)} %bitcast.57, bf16[2,2,256,768]{3,2,1,0:T(8,128)(2,1)} %bitcast.75, ...), custom_call_target="tpu_custom_call" | custom-call | flops 53687091200 | bytes 33554432 | tf_op jit(solution)/shard_map/middle/pallas_call | solution.py:1224
  196.5 3.1 slice_bitcast_fusion
  199.5 1.6 collective-permute-start.5
  201.1 0.5 collective-permute-start.4
  201.6 1.5 collective-permute-start.3
  203.1 41.6 %attend_back.1 = (bf16[2048,192]{1,0:T(8,128)(2,1)S(1)}, bf16[2048,192]{1,0:T(8,128)(2,1)S(1)}, bf16[2048,192]{1,0:T(8,128)(2,1)S(1)}) custom-call(s32[2,8]{1,0:T(2,128)S(1)} %pad_add_fusion.span_ref, f32[3]{0:T(128)S(1)} %get-tuple-element.94.slope_ref, bf16[3,128,2048]{2,1,0:T(8,128)(2,1)} %copy-done.7, bf16[3,2048,64]{2,1,0:T(8,128)(2,1)} %copy-done.8, ...), custom_call_target="tpu_custom_call" | custom-call | flops 8053063680 | bytes 12582912 | tf_op jit(solution)/shard_map/attend_back/pallas_call | solution.py:669
  244.8 1.0 copy-done.3
  245.7 1.0 copy-done.4
  246.7 1.0 copy-done.5
  247.7 38.0 %collective-permute-done.4.moved_2 = bf16[192,4992]{1,0:T(8,128)(2,1)} collective-permute-done((bf16[192,4992]{1,0:T(8,128)(2,1)S(1)}, bf16[192,4992]{1,0:T(8,128)(2,1)}, u32[]{:S(2)}, u32[]{:S(2)}) %collective-permute-start.4) | collective-permute-done | bytes 1916960 | tf_op jit(solution)/shard_map/ppermute | solution.py:1686
  285.7 104.8 %tail.1 = (bf16[2,2,256,768]{3,2,1,0:T(8,128)(2,1)}, bf16[192,4992]{1,0:T(8,128)(2,1)}, bf16[2,192,576]{2,1,0:T(8,128)(2,1)}, f32[8,768]{1,0:T(8,128)}) custom-call(bf16[8,256,192]{2,1,0:T(8,128)(2,1)} %bitcast.60, bf16[8,256,192]{2,1,0:T(8,128)(2,1)} %bitcast.61, bf16[8,256,192]{2,1,0:T(8,128)(2,1)} %bitcast.62, bf16[768,576]{1,0:T(8,128)(2,1)} %bitcast.71, ...), custom_call_target="tpu_custom_call" | custom-call | flops 85899345920 | bytes 33554432 | tf_op jit(solution)/shard_map/tail/pallas_call | solution.py:1542
  390.6 1.5 slice_reduce_fusion.6
  392.0 1.7 slice_reduce_fusion
  393.7 1.6 split.12
  395.4 2.2 split.14
  397.6 0.3 split.13
  397.9 0.8 copy-done.16
  398.7 0.8 slice_bitcast_fusion.4
  399.5 3.0 reshape.486
  402.5 3.3 bitcast_convert_fusion
  405.9 0.8 pad_maximum_fusion.2
  406.7 0.8 pad_maximum_fusion.1
  407.5 0.8 pad_maximum_fusion
  408.4 1.1 copy.36
  (88 shorter events, 0.9 us)
Async XLA Ops:
  0.6 1.6 copy-start
  0.7 1.7 copy-start.17
  0.7 1.7 copy-start.18
  2.2 64.6 %copy-start.14 = (bf16[24,8,2,1536]{3,1,2,0:T(8,128)(2,1)}, bf16[24,8,2,1536]{3,1,2,0:T(8,128)(2,1)S(1)}, u32[]{:S(2)}) copy-start(bf16[24,8,2,1536]{3,1,2,0:T(8,128)(2,1)S(1)} %copy.34) | copy-start | bytes 3538948
  3.3 64.1 %copy-start.28 = (s32[2,8]{1,0:T(2,128)S(1)}, s32[2,8]{1,0:T(2,128)}, u32[]{:S(2)}) copy-start(s32[2,8]{1,0:T(2,128)} %param.19) | copy-start | bytes 196
  3.3 64.6 %copy-start.25 = (f32[384]{0:T(512)S(1)}, f32[384]{0:T(512)}, u32[]{:S(2)}) copy-start(f32[384]{0:T(512)} %param.22) | copy-start | bytes 4612
  3.3 64.7 %copy-start.26 = (f32[384]{0:T(512)S(1)}, f32[384]{0:T(512)}, u32[]{:S(2)}) copy-start(f32[384]{0:T(512)} %param.25) | copy-start | bytes 4612
  3.3 64.9 %copy-start.19 = (f32[768]{0:T(1024)S(1)}, f32[768]{0:T(1024)}, u32[]{:S(2)}) copy-start(f32[768]{0:T(1024)} %param.27) | copy-start | bytes 9220
  3.3 64.9 %copy-start.20 = (f32[768]{0:T(1024)S(1)}, f32[768]{0:T(1024)}, u32[]{:S(2)}) copy-start(f32[768]{0:T(1024)} %param.28) | copy-start | bytes 9220
  3.3 64.9 %copy-start.21 = (f32[768]{0:T(1024)S(1)}, f32[768]{0:T(1024)}, u32[]{:S(2)}) copy-start(f32[768]{0:T(1024)} %param.29) | copy-start | bytes 9220
  3.3 64.9 %copy-start.22 = (f32[768]{0:T(1024)S(1)}, f32[768]{0:T(1024)}, u32[]{:S(2)}) copy-start(f32[768]{0:T(1024)} %param.32) | copy-start | bytes 9220
  3.4 64.9 %copy-start.23 = (f32[768]{0:T(1024)S(1)}, f32[768]{0:T(1024)}, u32[]{:S(2)}) copy-start(f32[768]{0:T(1024)} %param.33) | copy-start | bytes 9220
  3.4 64.9 %copy-start.24 = (f32[768]{0:T(1024)S(1)}, f32[768]{0:T(1024)}, u32[]{:S(2)}) copy-start(f32[768]{0:T(1024)} %param.34) | copy-start | bytes 9220
  63.7 58.7 %collective-permute-start.2 = (bf16[192,3072]{1,0:T(8,128)(2,1)S(1)}, bf16[192,3072]{1,0:T(8,128)(2,1)}, u32[]{:S(2)}, u32[]{:S(2)}) collective-permute-start(bf16[192,3072]{1,0:T(8,128)(2,1)S(1)} %bitcast.66), channel_id=1, source_target_pairs={{0,24},{24,0},{8,16},{16,8},{1,25},{25,1},{9,17},{17,9},{2,26},{26... | collective-permute-start | bytes 3538952 | tf_op jit(solution)/shard_map/ppermute | solution.py:1658
  66.3 56.2 %collective-permute-start.1 = (bf16[192,3072]{1,0:T(8,128)(2,1)S(1)}, bf16[192,3072]{1,0:T(8,128)(2,1)}, u32[]{:S(2)}, u32[]{:S(2)}) collective-permute-start(bf16[192,3072]{1,0:T(8,128)(2,1)S(1)} %bitcast.67), channel_id=1, source_target_pairs={{0,16},{16,0},{8,24},{24,8},{1,17},{17,1},{9,25},{25,9},{2,18},{18... | collective-permute-start | bytes 3538952 | tf_op jit(solution)/shard_map/ppermute | solution.py:1658
  66.8 55.7 %collective-permute-start = (bf16[192,3072]{1,0:T(8,128)(2,1)S(1)}, bf16[192,3072]{1,0:T(8,128)(2,1)}, u32[]{:S(2)}, u32[]{:S(2)}) collective-permute-start(bf16[192,3072]{1,0:T(8,128)(2,1)S(1)} %bitcast.68), channel_id=1, source_target_pairs={{0,8},{8,0},{16,24},{24,16},{1,9},{9,1},{17,25},{25,17},{2,10},{10... | collective-permute-start | bytes 3538952 | tf_op jit(solution)/shard_map/ppermute | solution.py:1658
  74.3 1.9 copy-start.2
  81.3 1.1 copy-start.8
  82.4 37.8 %copy-start.7 = (bf16[3,128,2048]{2,1,0:T(8,128)(2,1)}, bf16[3,128,2048]{2,1,0:T(8,128)(2,1)S(1)}, u32[]{:S(2)}) copy-start(bf16[3,128,2048]{2,1,0:T(8,128)(2,1)S(1)} %get-tuple-element.48.qt_ref) | copy-start | bytes 4718596
  82.4 37.8 %copy-start.9 = (bf16[3,2048,128]{2,1,0:T(8,128)(2,1)}, bf16[3,2048,128]{2,1,0:T(8,128)(2,1)S(1)}, u32[]{:S(2)}) copy-start(bf16[3,2048,128]{2,1,0:T(8,128)(2,1)S(1)} %get-tuple-element.49.k_ref) | copy-start | bytes 4718596
  82.4 37.8 %copy-start.10 = (bf16[3,2048,128]{2,1,0:T(8,128)(2,1)}, bf16[3,2048,128]{2,1,0:T(8,128)(2,1)S(1)}, u32[]{:S(2)}) copy-start(bf16[3,2048,128]{2,1,0:T(8,128)(2,1)S(1)} %get-tuple-element.58.v_ref) | copy-start | bytes 4718596
  120.3 1.0 copy-start.6
  121.2 1.2 copy-start.11
  199.5 48.1 %collective-permute-start.5 = (bf16[192,4992]{1,0:T(8,128)(2,1)S(1)}, bf16[192,4992]{1,0:T(8,128)(2,1)S(1)}, u32[]{:S(2)}, u32[]{:S(2)}) collective-permute-start(bf16[192,4992]{1,0:T(8,128)(2,1)S(1)} %get-tuple-element.80), channel_id=1, source_target_pairs={{0,24},{24,0},{8,16},{16,8},{1,25},{25,1},{9,17},{17,9},{2,26},{26... | collective-permute-start | bytes 5750792 | tf_op jit(solution)/shard_map/ppermute | solution.py:1686
  201.1 84.6 %collective-permute-start.4 = (bf16[192,4992]{1,0:T(8,128)(2,1)S(1)}, bf16[192,4992]{1,0:T(8,128)(2,1)}, u32[]{:S(2)}, u32[]{:S(2)}) collective-permute-start(bf16[192,4992]{1,0:T(8,128)(2,1)S(1)} %get-tuple-element.81), channel_id=1, source_target_pairs={{0,16},{16,0},{8,24},{24,8},{1,17},{17,1},{9,25},{25,9},{2,18},{18... | collective-permute-start | bytes 5750792 | tf_op jit(solution)/shard_map/ppermute | solution.py:1686
  201.6 84.1 %collective-permute-start.3 = (bf16[192,4992]{1,0:T(8,128)(2,1)S(1)}, bf16[192,4992]{1,0:T(8,128)(2,1)}, u32[]{:S(2)}, u32[]{:S(2)}) collective-permute-start(bf16[192,4992]{1,0:T(8,128)(2,1)S(1)} %get-tuple-element.82), channel_id=1, source_target_pairs={{0,8},{8,0},{16,24},{24,16},{1,9},{9,1},{17,25},{25,17},{2,10},{10... | collective-permute-start | bytes 5750792 | tf_op jit(solution)/shard_map/ppermute | solution.py:1686
  244.8 1.0 copy-start.3
  245.7 1.0 copy-start.4
  246.7 1.0 copy-start.5
  247.7 38.1 %copy-start.27 = (bf16[192,4992]{1,0:T(8,128)(2,1)}, bf16[192,4992]{1,0:T(8,128)(2,1)S(1)}, u32[]{:S(2)}) copy-start(bf16[192,4992]{1,0:T(8,128)(2,1)S(1)} %collective-permute-done.5.moved_3) | copy-start | bytes 5750788
  390.6 7.0 %copy-start.12 = (bf16[192,4992]{1,0:T(8,128)(2,1)S(1)}, bf16[192,4992]{1,0:T(8,128)(2,1)}, u32[]{:S(2)}) copy-start(bf16[192,4992]{1,0:T(8,128)(2,1)} %get-tuple-element.71) | copy-start | bytes 5750788
  397.6 1.0 copy-start.16
  402.5 3.4 copy-start.15
  405.9 2.5 copy-start.13
  408.4 1.1 copy-start.1

commit v3 on v2

--- a/solution.py
+++ b/solution.py
@@ -488,13 +488,25 @@
     return jnp.where(apart == 0, dot(keys, query_t * bare), full)
 
 
+def sweep(first, last, step, most=2):
+    many = (last - first) // most
+
+    @pl.loop(0, many)
+    def _(i):
+        step(first + i * most, most)
+
+    @pl.loop(first + many * most, last)
+    def _(tile):
+        step(tile, 1)
+
+
 def attend_kernel(span_ref, slope_ref, qt_ref, k_ref, vt_ref, o_ref, ot_ref, lse_ref, max_ref, acc_ref):
     heads = qt_ref.shape[0]
     block = pl.program_id(0)
     after, same, bare = side_signs(TILE)
 
-    def tile_rows(tile):
-        return pl.ds(pl.multiple_of(tile * TILE, TILE), TILE)
+    def tile_rows(tile, count=1):
+        return pl.ds(pl.multiple_of(tile * TILE, TILE), count * TILE)
 
     own = tile_rows(block)
     for head in range(heads):
@@ -504,25 +516,23 @@
         max_ref[head] = top
         acc_ref[head] = dot(vt_ref[head, :, own], weights)
 
-    def step(tile, sign):
-        for head in range(heads):
-            query_t = qt_ref[head] if sign is None else qt_ref[head] * sign
-            scores = dot(k_ref[head, tile_rows(tile), :], query_t)
-            old = max_ref[head]
-            top = jnp.maximum(old, jnp.max(scores, 0, keepdims=True))
-            weights = jnp.exp(scores - top).astype(jnp.bfloat16)
-            max_ref[head] = top
-            acc_ref[head] = acc_ref[head] * jnp.exp(old - top) + dot(
-                vt_ref[head, :, tile_rows(tile)], weights
-            )
-
-    @pl.loop(span_ref[0, block], block)
-    def _(tile):
-        step(tile, None)
-
-    @pl.loop(block + 1, span_ref[1, block])
-    def _(tile):
-        step(tile, after)
+    def step(tile, count, sign):
+        each = range(heads)
+        keys = [k_ref[head, tile_rows(tile, count), :] for head in each]
+        values = [vt_ref[head, :, tile_rows(tile, count)] for head in each]
+        queries = [qt_ref[head] if sign is None else qt_ref[head] * sign for head in each]
+        old = [max_ref[head] for head in each]
+        acc = [acc_ref[head] for head in each]
+        scores = [dot(keys[head], queries[head]) for head in each]
+        top = [jnp.maximum(old[head], jnp.max(scores[head], 0, keepdims=True)) for head in each]
+        weights = [jnp.exp(scores[head] - top[head]).astype(jnp.bfloat16) for head in each]
+        parts = [dot(values[head], weights[head]) for head in each]
+        for head in each:
+            max_ref[head] = top[head]
+            acc_ref[head] = acc[head] * jnp.exp(old[head] - top[head]) + parts[head]
+
+    sweep(span_ref[0, block], block, lambda tile, count: step(tile, count, None))
+    sweep(block + 1, span_ref[1, block], lambda tile, count: step(tile, count, after))
 
     parts = []
     for head in range(heads):
@@ -583,8 +593,8 @@
     def low(value):
         return value.astype(jnp.bfloat16).astype(jnp.float32)
 
-    def tile_rows(tile):
-        return pl.ds(pl.multiple_of(tile * TILE, TILE), TILE)
+    def tile_rows(tile, count=1):
+        return pl.ds(pl.multiple_of(tile * TILE, TILE), count * TILE)
 
     @pl.when(block == 0)
     def _():
@@ -613,38 +623,48 @@
                 query = jnp.where(sub == LOG_ROW + 2, third, query)
                 qt_log[head, :, rows] = query.astype(jnp.bfloat16)
 
-    def accumulate(head, tile, scores, first):
-        rows = tile_rows(tile)
-        probs = jnp.exp(scores)
-        grad_probs = dot(v_ref[head], grad_t[head, :, rows])
-        grad_scores = (probs * grad_probs).astype(jnp.bfloat16)
-        value_part = dot(probs.astype(jnp.bfloat16), grad_heads[head, rows, :])
-        key_part = dot(grad_scores, q_ref[head, rows, :])
-        query_acc[head, :, rows] += dot(kt_ref[head], grad_scores)
-        if first:
-            value_acc[head] = value_part
-            key_acc[head] = key_part
-        else:
-            value_acc[head] += value_part
-            key_acc[head] += key_part
-
-    for head in range(heads):
-        accumulate(
-            head,
-            block,
-            diagonal_scores(k_ref[head], qt_log[head, :, tile_rows(block)], same, bare, slope_ref[head]),
-            True,
-        )
-
-    @pl.loop(span_ref[0, block], block)
-    def _(tile):
-        for head in range(heads):
-            accumulate(head, tile, dot(k_ref[head], qt_log[head, :, tile_rows(tile)] * after), False)
-
-    @pl.loop(block + 1, span_ref[1, block])
-    def _(tile):
-        for head in range(heads):
-            accumulate(head, tile, dot(k_ref[head], qt_log[head, :, tile_rows(tile)]), False)
+    def accumulate(tile, scores, first, count=1):
+        each = range(heads)
+        rows = tile_rows(tile, count)
+        values = [v_ref[head] for head in each]
+        turned = [grad_t[head, :, rows] for head in each]
+        grads = [grad_heads[head, rows, :] for head in each]
+        queries = [q_ref[head, rows, :] for head in each]
+        keys_t = [kt_ref[head] for head in each]
+        probs = [jnp.exp(scores[head]) for head in each]
+        grad_probs = [dot(values[head], turned[head]) for head in each]
+        grad_scores = [(probs[head] * grad_probs[head]).astype(jnp.bfloat16) for head in each]
+        value_part = [dot(probs[head].astype(jnp.bfloat16), grads[head]) for head in each]
+        key_part = [dot(grad_scores[head], queries[head]) for head in each]
+        query_part = [dot(keys_t[head], grad_scores[head]) for head in each]
+        for head in each:
+            if first:
+                value_acc[head] = value_part[head]
+                key_acc[head] = key_part[head]
+            else:
+                value_acc[head] += value_part[head]
+                key_acc[head] += key_part[head]
+            query_acc[head, :, rows] += query_part[head]
+
+    own = [qt_log[head, :, tile_rows(block)] for head in range(heads)]
+    accumulate(
+        block,
+        [
+            diagonal_scores(k_ref[head], own[head], same, bare, slope_ref[head])
+            for head in range(heads)
+        ],
+        True,
+    )
+    after_wide = side_signs(2 * TILE)[0]
+
+    def step(tile, count, sign):
+        queries = [qt_log[head, :, tile_rows(tile, count)] for head in range(heads)]
+        if sign is not None:
+            queries = [query * sign[:, : count * TILE] for query in queries]
+        accumulate(tile, [dot(k_ref[head], queries[head]) for head in range(heads)], False, count)
+
+    sweep(span_ref[0, block], block, lambda tile, count: step(tile, count, after_wide))
+    sweep(block + 1, span_ref[1, block], lambda tile, count: step(tile, count, None))
 
     dk_ref[...] = jnp.concatenate([key_acc[head] for head in range(heads)], 1).astype(jnp.bfloat16)
     dv_ref[...] = jnp.concatenate([value_acc[head] for head in range(heads)], 1).astype(jnp.bfloat16)
@@ -876,13 +896,13 @@
 
 def middle_kernel(
     attended, sequence, cotangent, w_out, w_down, up_0, up_1, up_2, up_3, vectors,
-    out_home, grad_one, grad_heads, pack, sums,
+    out_home, grad_one, grad_heads, early, late, down_sum, sums,
     token_v, mine_v, theirs_v, both_v, cot_v, out_w, down_w, up_w,
     send_a, recv_a, send_b, recv_b, send_c, recv_c,
     normed_v, inv_v, low_v, hidden_v, gate_v, lift_v, grad_v, ffn_v, att_v, result_v, keep_v, away_v, tile_v,
-    load_sem, pair_send, pair_recv, cot_send, cot_recv, cot_pass, cot_took,
+    down_v, down_got, load_sem, pair_send, pair_recv, cot_send, cot_recv, cot_pass, cot_took,
     a_send, a_recv, b_send, b_recv, c_send, c_recv, out_send, out_recv, out_pass, out_took,
-    one_sem, keep_sem, away_send, away_recv, tile_sem,
+    one_sem, keep_sem, away_send, away_recv, tile_sem, down_send, down_recv, down_sem,
 ):
     place, stage, core = lax.axis_index("fsdp"), lax.axis_index("ctx"), lax.axis_index("tp")
     seq, half = stage // 2, stage % 2
@@ -893,7 +913,8 @@
     quarter = up_0.shape[0]
 
     barrier = pltpu.get_barrier_semaphore()
-    peers = [(place, lax.rem(stage + shift, 4), core) for shift in (1, 2, 3)]
+    peers = [(place ^ other, stage, core) for other in (1, 2, 3)]
+    peers += [(place, lax.rem(stage + shift, 4), core) for shift in (1, 2, 3)]
     peers += [(place, stage, 1 - core)]
     for peer in peers:
         pl.semaphore_signal(barrier, inc=1, device_id=peer, device_id_type=MESH)
@@ -1081,6 +1102,32 @@
             dot(gate_v[c], up_w[:, :units], ((1,), (1,))) + dot(lift_v[c], up_w[:, units:], ((1,), (1,)))
         ).astype(jnp.bfloat16)
         exchange(c, send_c, recv_c, c_send, c_recv).start()
+
+    tile = tile_v.shape[2]
+
+    def columns(index):
+        return pl.ds(pl.multiple_of(index * tile, tile), tile)
+
+    def weight_part(left, right):
+        rows = left.shape[0] * left.shape[1]
+        return dot(
+            left[...].reshape(rows, left.shape[2]), right.reshape(rows, tile), ((0,), (0,))
+        ).astype(jnp.bfloat16)
+
+    unit_tiles = units // tile
+
+    def down_copy(i, other):
+        rows = pl.ds(pl.multiple_of((place ^ other) * quarter, quarter), quarter)
+        return remote(
+            down_v.at[rows, columns(i)], down_got.at[other - 1, :, columns(i)],
+            down_send.at[i, other - 1], down_recv.at[i, other - 1], (place ^ other, stage, core),
+        )
+
+    @pl.loop(0, unit_tiles)
+    def _(i):
+        down_v[:, columns(i)] = weight_part(ffn_v, hidden_v[:, :, columns(i)])
+        for other in (1, 2, 3):
+            down_copy(i, other).start()
 
     def one_copy(c):
         return pltpu.make_async_copy(grad_v.at[c], grad_one.at[c], one_sem.at[c])
@@ -1113,56 +1160,58 @@
         away_copy(c, half).start()
         keep_copy(c).start()
 
-    tile = tile_v.shape[2]
-
-    def tile_copy(slot, row, column):
+    early_tiles = early.shape[2] // tile
+
+    def tile_copy(slot, row, index):
+        target, column = index
         return pltpu.make_async_copy(
             tile_v.at[slot, pl.ds(row * quarter, quarter)],
-            pack.at[place ^ row, :, pl.ds(pl.multiple_of(column * tile, tile), tile)],
+            target.at[place ^ row, :, columns(column)],
             tile_sem.at[slot, row],
         )
 
-    def weight_tile(column, left, right):
-        slot = lax.rem(column, 2)
-
-        @pl.when(column >= 2)
+    def weight_tile(count, target, column, left, right):
+        slot = lax.rem(count, 2)
+
+        @pl.when(count >= 2)
         def _():
             for row in range(4):
-                tile_copy(slot, row, column - 2).wait()
-
-        rows = left.shape[0] * left.shape[1]
-        tile_v[slot] = dot(
-            left[...].reshape(rows, left.shape[2]), right.reshape(rows, tile), ((0,), (0,))
-        ).astype(jnp.bfloat16)
+                tile_copy(slot, row, (target, column)).wait()
+
+        tile_v[slot] = weight_part(left, right)
         for row in range(4):
-            tile_copy(slot, row, column).start()
-
-    out_tiles = both_v.shape[2] // tile
-    unit_tiles = units // tile
-
-    def columns(index):
-        return pl.ds(pl.multiple_of(index * tile, tile), tile)
-
-    @pl.loop(0, out_tiles)
-    def _(i):
-        weight_tile(i, att_v, both_v[:, :, columns(i)])
+            tile_copy(slot, row, (target, column)).start()
 
     @pl.loop(0, unit_tiles)
     def _(i):
-        weight_tile(out_tiles + i, ffn_v, hidden_v[:, :, columns(i)])
-
-    @pl.loop(0, unit_tiles)
+        weight_tile(i, early, i, low_v, gate_v[:, :, columns(i)])
+
+    @pl.loop(unit_tiles, early_tiles)
     def _(i):
-        weight_tile(out_tiles + unit_tiles + i, low_v, gate_v[:, :, columns(i)])
-
-    @pl.loop(0, unit_tiles)
+        weight_tile(i, early, i, low_v, lift_v[:, :, columns(i - unit_tiles)])
+
+    late_units = 2 * unit_tiles - early_tiles
+
+    @pl.loop(0, late_units)
     def _(i):
-        weight_tile(out_tiles + 2 * unit_tiles + i, low_v, lift_v[:, :, columns(i)])
-
-    last = out_tiles + 3 * unit_tiles
-    for column in (last - 2, last - 1):
+        weight_tile(early_tiles + i, late, i, low_v, lift_v[:, :, columns(early_tiles - unit_tiles + i)])
+
+    weight_tile(2 * unit_tiles, late, late_units, att_v, both_v[...])
+    for slot in (0, 1):
         for row in range(4):
-            tile_copy(column % 2, row, column).wait()
+            tile_copy(slot, row, (late, 0)).wait()
+
+    for i in range(unit_tiles):
+        for other in (1, 2, 3):
+            down_copy(i, other).wait_recv()
+    own_rows = pl.ds(pl.multiple_of(place * quarter, quarter), quarter)
+    down_got[0] = (
+        down_v[own_rows, :].astype(jnp.float32)
+        + down_got[0].astype(jnp.float32)
+        + (down_got[1].astype(jnp.float32) + down_got[2].astype(jnp.float32))
+    ).astype(jnp.bfloat16)
+    down_out = pltpu.make_async_copy(down_got.at[0], down_sum, down_sem)
+    down_out.start()
 
     def out_arrival(which):
         return remote(
@@ -1180,6 +1229,11 @@
         def _():
             out_arrival(which).wait_recv()
             out_share(which, core).start()
+
+    down_out.wait()
+    for i in range(unit_tiles):
+        for other in (1, 2, 3):
+            down_copy(i, other).wait_send()
 
     @pl.loop(0, chunks)
     def _(c):
@@ -1211,7 +1265,8 @@
 def middle(attended, sequence, cotangent, w_out, w_down, up_shards, vectors):
     chunks, rows, width = 4, sequence.shape[1], sequence.shape[2]
     head_width, units = w_out.shape[1], w_down.shape[1]
-    columns = head_width + 3 * units
+    tile = head_width
+    early, late = 6 * tile, 2 * units + head_width - 6 * tile
     dma, bf16, f32 = pltpu.SemaphoreType.DMA, jnp.bfloat16, jnp.float32
 
     def vmem(shape, dtype=bf16):
@@ -1224,12 +1279,14 @@
     return pl.pallas_call(
         middle_kernel,
         in_specs=[pl.BlockSpec(memory_space=pl.ANY)] * 9 + [pl.BlockSpec(memory_space=pltpu.VMEM)],
-        out_specs=[pl.BlockSpec(memory_space=pl.ANY)] * 4 + [pl.BlockSpec(memory_space=pltpu.VMEM)],
+        out_specs=[pl.BlockSpec(memory_space=pl.ANY)] * 6 + [pl.BlockSpec(memory_space=pltpu.VMEM)],
         out_shape=[
             jax.ShapeDtypeStruct((2, 2, rows, width), bf16),
             jax.ShapeDtypeStruct(wide, f32),
             jax.ShapeDtypeStruct((2 * chunks, rows, head_width // 2), bf16),
-            jax.ShapeDtypeStruct((4, width // 4, columns), bf16),
+            jax.ShapeDtypeStruct((4, width // 4, early), bf16),
+            jax.ShapeDtypeStruct((4, width // 4, late), bf16),
+            jax.ShapeDtypeStruct((width // 4, units), bf16),
             jax.ShapeDtypeStruct((8, width), f32),
         ],
         scratch_shapes=[
@@ -1239,10 +1296,10 @@
             vmem(wide, f32), vmem((chunks, rows, 1), f32), vmem(wide),
             vmem(inner), vmem(inner), vmem(inner),
             vmem(wide, f32), vmem(wide), vmem(wide), vmem(wide), vmem(narrow_rows), vmem(narrow_rows),
-            vmem((2, width, 384)),
+            vmem((2, width, tile)), vmem((width, units)), vmem((3, width // 4, units)),
             dma((8,)), four, four, two, two, two, two,
             four, four, four, four, four, four, four, two, two, two,
-            four, four, four, four, dma((2, 4)),
+            four, four, four, four, dma((2, 4)), dma((units // tile, 3)), dma((units // tile, 3)), dma,
         ],
         compiler_params=pltpu.CompilerParams(
             collective_id=1, has_side_effects=True, vmem_limit_bytes=60 << 20
@@ -1253,12 +1310,12 @@
 
 
 def tail_kernel(
-    d_query, d_key, d_value, w_joined, sums_in, sequence, grad_one, pack, moved_1, moved_2, moved_3,
+    d_query, d_key, d_value, w_joined, sums_in, sequence, grad_one, early, late, moved_1, moved_2, moved_3,
     home, shard, joined, sums,
-    token_v, one_v, part_v, project_v, own_v, tp_sent, tp_got, pair_sent, pair_got, final_v,
+    token_v, one_v, part_v, late_v, project_v, own_v, tp_sent, tp_got, pair_sent, pair_got, final_v,
     summed_v, end_got, inner_v, mid_got, total_v, joined_v, quarter_got, cross_sent, cross_got, full_v,
     step_v, step_got,
-    load_sem, tp_send, tp_recv, pair_send, pair_recv, home_send, home_recv, home_pass, home_took, home_local,
+    load_sem, late_send, late_recv, tp_send, tp_recv, pair_send, pair_recv, home_send, home_recv, home_pass, home_took, home_local,
     end_send, end_recv, mid_send, mid_recv, back_send, back_recv, shard_sem,
     quarter_send, quarter_recv, cross_send, cross_recv, half_send, half_recv, half_local, step_send, step_recv,
 ):
@@ -1292,10 +1349,20 @@
 
     loads = [
         pltpu.make_async_copy(source, part_v.at[index], load_sem.at[index])
-        for index, source in enumerate((pack.at[0], moved_1, moved_2, moved_3))
+        for index, source in enumerate((early.at[0], moved_1, moved_2, moved_3))
     ]
     loads.append(pltpu.make_async_copy(sequence, token_v, load_sem.at[4]))
     loads.append(pltpu.make_async_copy(grad_one, one_v, load_sem.at[5]))
+    loads.append(pltpu.make_async_copy(late.at[0], late_v.at[0], load_sem.at[6]))
+
+    def late_copy(other):
+        return remote(
+            late.at[other], late_v.at[other], late_send.at[other - 1], late_recv.at[other - 1],
+            (place ^ other, stage, core),
+        )
+
+    for other in (1, 2, 3):
+        late_copy(other).start()
     for load in loads:
         load.start()
 
@@ -1341,15 +1408,18 @@
     def shard_copy(j):
         return pltpu.make_async_copy(total_v.at[j], shard.at[:, columns(j)], shard_sem.at[j])
 
+    def sum_piece(j, parts, first):
+        terms = [parts[index, :, first : first + piece].astype(f32) for index in range(4)]
+        summed_v[j] = (terms[0] + terms[1] + (terms[2] + terms[3])).astype(bf16)
+
+        @pl.when(at_end)
+        def _():
+            end_copy(j).start()
+
     for load in loads[:4]:
         load.wait()
-    for j in range(pieces):
-        terms = [part_v[index, :, j * piece : (j + 1) * piece].astype(f32) for index in range(4)]
-        summed_v[j] = (terms[0] + terms[1] + (terms[2] + terms[3])).astype(bf16)
-
-        @pl.when(at_end)
-        def _():
-            end_copy(j).start()
+    for j in range(pieces - 1):
+        sum_piece(j, part_v, j * piece)
 
     loads[4].wait()
     tokens = token_v[...].reshape(-1, token_v.shape[2])
@@ -1394,6 +1464,10 @@
             step_copy(index + 1).start()
 
     step_copy(0).start()
+    loads[6].wait()
+    for other in (1, 2, 3):
+        late_copy(other).wait_recv()
+    sum_piece(pieces - 1, late_v, 0)
 
     loads[5].wait()
 
@@ -1520,28 +1594,30 @@
         home_share(which, 1 - core).wait_recv()
     for other in (1, 2, 3):
         quarter_copy(other).wait_send()
+        late_copy(other).wait_send()
     cross_copy.wait_send()
     half_here.wait()
     half_copy.wait_send()
     remote(full_v, joined.at[1 - half], half_send, half_recv, partner).wait_recv()
 
 
-def tail(d_query, d_key, d_value, w_joined, sums, sequence, grad_one, pack, moved):
+def tail(d_query, d_key, d_value, w_joined, sums, sequence, grad_one, early, late, moved):
     rows, width = sequence.shape[1:]
-    columns, quarter = pack.shape[2], pack.shape[1]
+    quarter, piece = late.shape[1:]
+    columns = early.shape[2] + piece
     joined = w_joined.shape[1]
-    pieces = 3
+    pieces = columns // piece
     dma, bf16, f32 = pltpu.SemaphoreType.DMA, jnp.bfloat16, jnp.float32
 
     def vmem(shape, dtype=bf16):
         return pltpu.VMEM(shape, dtype)
 
     any_spec, vmem_spec = pl.BlockSpec(memory_space=pl.ANY), pl.BlockSpec(memory_space=pltpu.VMEM)
-    cut = (pieces, quarter, columns // pieces)
+    cut = (pieces, quarter, piece)
     one, two, three, four = dma, dma((2,)), dma((3,)), dma((4,))
     return pl.pallas_call(
         tail_kernel,
-        in_specs=[vmem_spec] * 5 + [any_spec] * 6,
+        in_specs=[vmem_spec] * 5 + [any_spec] * 7,
         out_specs=[any_spec] * 3 + [vmem_spec],
         out_shape=[
             jax.ShapeDtypeStruct((2, 2, rows, width), bf16),
@@ -1550,7 +1626,7 @@
             jax.ShapeDtypeStruct(sums.shape, f32),
         ],
         scratch_shapes=[
-            vmem(sequence.shape), vmem(grad_one.shape, f32), vmem((4, quarter, columns)),
+            vmem(sequence.shape), vmem(grad_one.shape, f32), vmem(early.shape), vmem(late.shape),
             vmem((8, rows, joined)), vmem((4, rows, width), f32),
             vmem((4, rows, width)), vmem((4, rows, width)), vmem((2, rows, width)), vmem((2, rows, width)),
             vmem((2, rows, width)),
@@ -1558,7 +1634,7 @@
             vmem((width, joined)), vmem((3, quarter, joined)), vmem((quarter, joined)), vmem((quarter, joined)),
             vmem((quarter, joined)),
             vmem((5,) + sums.shape, f32), vmem((4,) + sums.shape, f32),
-            dma((6,)), four, four, two, two, two, two, two, two, one,
+            dma((7,)), three, three, four, four, two, two, two, two, two, two, one,
             three, three, three, three, three, three, three,
             three, three, one, one, one, one, one, four, four,
         ],
@@ -1567,7 +1643,7 @@
         ),
         cost_estimate=pl.CostEstimate(flops=80 << 30, bytes_accessed=32 << 20, transcendentals=0),
         name="tail",
-    )(d_query, d_key, d_value, w_joined, sums, sequence, grad_one, pack, *moved)
+    )(d_query, d_key, d_value, w_joined, sums, sequence, grad_one, early, late, *moved)
 
 
 def pick(pair, index):
@@ -1671,7 +1747,7 @@
 
     row_count = length // 2
     vectors = jnp.stack([b_out, gain_one, shift_one, b_down, gain_two, shift_two, b_out, b_out])
-    out, grad_one, grad_heads, pack, sums = middle(
+    out, grad_one, grad_heads, early, late, down_sum, sums = middle(
         attended_all.reshape(8, half_rows, width),
         sequence.reshape(8, half_rows, model_width),
         cotangent.reshape(2, 2, half_rows, model_width),
@@ -1683,7 +1759,7 @@
     out = out.reshape(2, block_rows, model_width)
     grad_heads = grad_heads.reshape(length, width)
     moved = [
-        lax.ppermute(pack[other], "fsdp", swap)
+        lax.ppermute(early[other], "fsdp", swap)
         for other, swap in ((1, X_SWAP), (2, Y_SWAP), (3, D_SWAP))
     ]
     d_query, d_key, d_value = attend_back(
@@ -1697,13 +1773,14 @@
         sums,
         sequence.reshape(8, half_rows, model_width),
         grad_one,
-        pack,
+        early,
+        late,
         moved,
     )
     d_tokens = d_tokens.reshape(2, block_rows, model_width).astype(jnp.float32)
-    shard = shard.astype(jnp.float32)
-    sum_out, sum_down, sum_up = jnp.split(shard, (2 * width, 2 * width + w_down.shape[1]), 1)
+    sum_up, sum_out = jnp.split(shard.astype(jnp.float32), (2 * w_up.shape[2],), 1)
     sum_up = sum_up.reshape(w_up.shape)
+    sum_down = lax.psum(down_sum, "ctx").astype(jnp.float32)
     joined = joined.astype(jnp.float32)
 
     def both_halves(first):

time: 410 us -> 370 us (0.902)
  waiting for transfers between devices: 38.1 us -> 5.99 us
  Pallas kernels: 324 us -> 302 us
  between operations: 1.17 us -> 14.6 us
    ppermute x3, waiting for transfers between devices: 38.1 us -> 0.01 us  [per_device_paired(): lax.ppermute(early[other], 'fsdp', swap)]
    pallas_call x1, Pallas kernels: 37.8 us -> 27 us  [attend(): pl.pallas_call(attend_kernel, grid_spec=pltpu.PrefetchScalarGridSpec(num_...]
    ppermute x3, waiting for transfers between devices: 0.01 us -> 5.96 us  [per_device_paired(): lax.ppermute(up_own, 'fsdp', swap)]
    pallas_call x1, Pallas kernels: 105 us -> 99.1 us  [tail(): pl.pallas_call(tail_kernel, in_specs=[vmem_spec] * 5 + [any_spec] * 7, ou...]
    unnamed x60 -> x56, local copies, waits for them, and re-layouts: 11.6 us -> 10.8 us
  transfers between devices with their start and end apart: 6 -> 7, of which waited for: 1 -> 2; matrix products, arithmetic and copies ran while one was open for 2% -> 2% of each run, Pallas kernels for 21% -> 19%
where the time goes in v3:
time: 370 us; the launch traced here: 369 us
  Pallas kernels  302 us (82%)
  local copies, waits for them, and re-layouts  26.2 us (7%)
  between operations  14.6 us (4%)
  other arithmetic  13.4 us (4%)
  starting transfers between devices  7.09 us (2%)
  waiting for transfers between devices  5.99 us (2%)
    pallas_call x1, Pallas kernels, tail(): pl.pallas_call(tail_kernel, in_specs=[vmem_spec] * 5 + [any_spec] * 7, ou...  99.1 us
    pallas_call x1, Pallas kernels, middle(): pl.pallas_call(middle_kernel, in_specs=[pl.BlockSpec(memory_space=pl.ANY)...  72.5 us
    pallas_call x1, Pallas kernels, start(): pl.pallas_call(start_kernel, in_specs=[pl.BlockSpec(memory_space=pl.ANY)]...  60.4 us
    pallas_call x1, Pallas kernels, attend_back(): pl.pallas_call(attend_back_kernel, grid_spec=pltpu.PrefetchScalarGridSpec...  38.1 us
    pallas_call x1, Pallas kernels, attend(): pl.pallas_call(attend_kernel, grid_spec=pltpu.PrefetchScalarGridSpec(num_...  27 us
    unnamed x56, local copies, waits for them, and re-layouts  10.8 us
  transfers between devices with their start and end apart: 7, of which 2 were waited for; matrix products, arithmetic and copies ran while one was open for 2% of the time, Pallas kernels for 19%

profile of v3, /device:TPU:0, one launch (start us, length us, event | category | flops | bytes accessed | tf_op | source)
XLA Modules:
  0.0 369.4 jit_solution(17768912168896551695)
XLA Ops:
  7.3 1.5 copy.34
  8.8 0.1 constant_dynamic-slice_fusion.2
  9.0 0.1 constant_dynamic-slice_fusion
  9.1 0.8 pad_maximum_fusion.3.w_joined
  10.0 60.4 %start.1 = (bf16[4,2,256,768]{3,2,1,0:T(8,128)(2,1)}, s32[4,2,512]{2,1,0:T(2,128)}, bf16[4,192,576]{2,1,0:T(8,128)(2,1)}, bf16[4,192,384]{2,1,0:T(8,128)(2,1)}, bf16[4,192,1536]{2,1,0:T(8,128)(2,1)}) custom-call(bf16[2,512,768]{2,1,0:T(8,128)(2,1)} %tokens.1, s32[2,512]{1,0:T(2,128)} %keep.1, bf16[192,576]{1,0:T(8,128)(2,1)} %pad_maximum_fusion.3.w_joined, ...), custom_call_target="tpu_custom_call" | custom-call | flops 42949672960 | bytes 16777216 | tf_op jit(solution)/shard_map/start/pallas_call | solution.py:864
  70.4 2.5 collective-permute-start.2
  72.9 0.5 collective-permute-start.1
  73.4 0.5 collective-permute-start
  74.1 0.2 reduce-window.4
  74.9 0.2 select_reduce_fusion
  75.1 0.7 compare_select_fusion
  75.9 0.2 select_reduce_fusion.1
  76.1 0.1 subtract_reduce-precision_fusion
  76.2 0.2 select_select_fusion
  76.4 1.3 pad.8.w_ref
  77.7 0.7 stack.35.vectors
  78.4 1.9 select_convert_fusion.1.key_feat_ref
  80.3 0.7 select_convert_fusion.query_feat_ref
  81.0 1.9 copy-done.2
  82.9 5.0 %project.1 = (bf16[3,128,2048]{2,1,0:T(8,128)(2,1)S(1)}, bf16[3,2048,64]{2,1,0:T(8,128)(2,1)S(1)}, bf16[3,2048,128]{2,1,0:T(8,128)(2,1)S(1)}, bf16[3,64,2048]{2,...) custom-call(bf16[2048,768]{1,0:T(8,128)(2,1)S(1)} %bitcast.59, ...), custom_call_target="tpu_custom_call" | custom-call | flops 2013265920 | bytes 12582912 | tf_op jit(solution)/shard_map/project/pallas_call | solution.py:440
  87.9 1.1 copy-done.8
  89.1 27.0 %attend.1 = (bf16[2048,192]{1,0:T(8,128)(2,1)S(1)}, f32[3,64,2048]{2,1,0:T(8,128)S(1)}, f32[3,1,2048]{2,1,0:T(1,128)S(1)}) custom-call(s32[2,8]{1,0:T(2,128)S(1)} %pad_add_fusion.span_ref, f32[3]{0:T(128)S(1)} %get-tuple-element.98.slope_ref, bf16[3,128,2048]{2,1,0:T(8,128)(2,1)S(1)} %get-tuple-element.50.qt_ref, ...), custom_call_target="tpu_custom_call" | custom-call | flops 3221225472 | bytes 6291456 | tf_op jit(solution)/shard_map/attend/pallas_call | solution.py:550
  116.1 0.9 copy-done.6
  117.1 1.2 copy-done.11
  118.3 5.9 %collective-permute-done.1.up_2 = bf16[192,3072]{1,0:T(8,128)(2,1)} collective-permute-done((bf16[192,3072]{1,0:T(8,128)(2,1)S(1)}, bf16[192,3072]{1,0:T(8,128)(2,1)}, u32[]{:S(2)}, u32[]{:S(2)}) %collective-permute-start.1) | collective-permute-done | bytes 1179680 | tf_op jit(solution)/shard_map/ppermute | solution.py:1734
  124.1 0.1 collective-permute-done.up_1
  124.2 72.5 %middle.1 = (bf16[2,2,256,768]{3,2,1,0:T(8,128)(2,1)}, f32[4,256,768]{2,1,0:T(8,128)}, bf16[8,256,192]{2,1,0:T(8,128)(2,1)}, bf16[4,192,2304]{2,1,0:T(8,128)(2,1...) custom-call(bf16[8,256,192]{2,1,0:T(8,128)(2,1)} %bitcast.63, ...), custom_call_target="tpu_custom_call" | custom-call | flops 53687091200 | bytes 33554432 | tf_op jit(solution)/shard_map/middle/pallas_call | solution.py:1279
  196.8 2.8 slice_bitcast_fusion
  199.6 1.8 collective-permute-start.5
  201.4 0.8 collective-permute-start.4
  202.2 0.9 collective-permute-start.3
  203.1 38.1 %attend_back.1 = (bf16[2048,192]{1,0:T(8,128)(2,1)S(1)}, bf16[2048,192]{1,0:T(8,128)(2,1)S(1)}, bf16[2048,192]{1,0:T(8,128)(2,1)S(1)}) custom-call(s32[2,8]{1,0:T(2,128)S(1)} %pad_add_fusion.span_ref, f32[3]{0:T(128)S(1)} %get-tuple-element.98.slope_ref, bf16[3,128,2048]{2,1,0:T(8,128)(2,1)} %copy-done.7, bf16[3,2048,64]{2,1,0:T(8,128)(2,1)} %copy-done.8, ...), custom_call_target="tpu_custom_call" | custom-call | flops 8053063680 | bytes 12582912 | tf_op jit(solution)/shard_map/attend_back/pallas_call | solution.py:689
  241.2 1.0 copy-done.3
  242.1 1.0 copy-done.4
  243.1 1.0 copy-done.5
  244.1 2.2 convert_element_type.76
  246.3 99.1 %tail.1 = (bf16[2,2,256,768]{3,2,1,0:T(8,128)(2,1)}, bf16[192,3456]{1,0:T(8,128)(2,1)}, bf16[2,192,576]{2,1,0:T(8,128)(2,1)}, f32[8,768]{1,0:T(8,128)}) custom-call(bf16[8,256,192]{2,1,0:T(8,128)(2,1)} %bitcast.60, bf16[8,256,192]{2,1,0:T(8,128)(2,1)} %bitcast.61, bf16[8,256,192]{2,1,0:T(8,128)(2,1)} %bitcast.62, bf16[768,576]{1,0:T(8,128)(2,1)} %bitcast.71, ...), custom_call_target="tpu_custom_call" | custom-call | flops 85899345920 | bytes 33554432 | tf_op jit(solution)/shard_map/tail/pallas_call | solution.py:1618
  345.4 1.3 slice_reduce_fusion.6
  346.8 1.6 slice_reduce_fusion
  348.4 1.6 split.8
  350.0 1.6 split.9
  351.7 0.8 slice_bitcast_fusion.4
  352.5 3.0 reshape.486
  355.5 3.3 bitcast_convert_fusion
  358.9 0.8 pad_maximum_fusion.2
  359.7 0.8 pad_maximum_fusion.1
  360.5 0.8 pad_maximum_fusion
  361.4 1.1 copy.37
  (87 shorter events, 1.0 us)
Async XLA Ops:
  7.2 1.7 copy-start
  7.2 1.8 copy-start.16
  7.2 1.8 copy-start.17
  7.2 236.9 %all-reduce.4.cloned.1.call-start = ((), (), s32[]{:S(2)}) async-start(), calls=%async_computation | async-start | bytes 1179648 | tf_op jit(solution)/shard_map/psum | solution.py:1783
  8.8 64.6 %copy-start.13 = (bf16[24,8,2,1536]{3,1,2,0:T(8,128)(2,1)}, bf16[24,8,2,1536]{3,1,2,0:T(8,128)(2,1)S(1)}, u32[]{:S(2)}) copy-start(bf16[24,8,2,1536]{3,1,2,0:T(8,128)(2,1)S(1)} %copy.34) | copy-start | bytes 3538948
  9.9 64.1 %copy-start.26 = (s32[2,8]{1,0:T(2,128)S(1)}, s32[2,8]{1,0:T(2,128)}, u32[]{:S(2)}) copy-start(s32[2,8]{1,0:T(2,128)} %param.19) | copy-start | bytes 196
  9.9 64.6 %copy-start.24 = (f32[384]{0:T(512)S(1)}, f32[384]{0:T(512)}, u32[]{:S(2)}) copy-start(f32[384]{0:T(512)} %param.22) | copy-start | bytes 4612
  9.9 64.7 %copy-start.25 = (f32[384]{0:T(512)S(1)}, f32[384]{0:T(512)}, u32[]{:S(2)}) copy-start(f32[384]{0:T(512)} %param.25) | copy-start | bytes 4612
  9.9 64.9 %copy-start.18 = (f32[768]{0:T(1024)S(1)}, f32[768]{0:T(1024)}, u32[]{:S(2)}) copy-start(f32[768]{0:T(1024)} %param.27) | copy-start | bytes 9220
  9.9 64.9 %copy-start.19 = (f32[768]{0:T(1024)S(1)}, f32[768]{0:T(1024)}, u32[]{:S(2)}) copy-start(f32[768]{0:T(1024)} %param.28) | copy-start | bytes 9220
  10.0 64.9 %copy-start.20 = (f32[768]{0:T(1024)S(1)}, f32[768]{0:T(1024)}, u32[]{:S(2)}) copy-start(f32[768]{0:T(1024)} %param.29) | copy-start | bytes 9220
  10.0 64.9 %copy-start.21 = (f32[768]{0:T(1024)S(1)}, f32[768]{0:T(1024)}, u32[]{:S(2)}) copy-start(f32[768]{0:T(1024)} %param.32) | copy-start | bytes 9220
  10.0 64.9 %copy-start.22 = (f32[768]{0:T(1024)S(1)}, f32[768]{0:T(1024)}, u32[]{:S(2)}) copy-start(f32[768]{0:T(1024)} %param.33) | copy-start | bytes 9220
  10.0 64.9 %copy-start.23 = (f32[768]{0:T(1024)S(1)}, f32[768]{0:T(1024)}, u32[]{:S(2)}) copy-start(f32[768]{0:T(1024)} %param.34) | copy-start | bytes 9220
  70.4 47.9 %collective-permute-start.2 = (bf16[192,3072]{1,0:T(8,128)(2,1)S(1)}, bf16[192,3072]{1,0:T(8,128)(2,1)}, u32[]{:S(2)}, u32[]{:S(2)}) collective-permute-start(bf16[192,3072]{1,0:T(8,128)(2,1)S(1)} %bitcast.66), channel_id=1, source_target_pairs={{0,24},{24,0},{8,16},{16,8},{1,25},{25,1},{9,17},{17,9},{2,26},{26... | collective-permute-start | bytes 3538952 | tf_op jit(solution)/shard_map/ppermute | solution.py:1734
  72.9 51.3 %collective-permute-start.1 = (bf16[192,3072]{1,0:T(8,128)(2,1)S(1)}, bf16[192,3072]{1,0:T(8,128)(2,1)}, u32[]{:S(2)}, u32[]{:S(2)}) collective-permute-start(bf16[192,3072]{1,0:T(8,128)(2,1)S(1)} %bitcast.67), channel_id=1, source_target_pairs={{0,16},{16,0},{8,24},{24,8},{1,17},{17,1},{9,25},{25,9},{2,18},{18... | collective-permute-start | bytes 3538952 | tf_op jit(solution)/shard_map/ppermute | solution.py:1734
  73.4 50.9 %collective-permute-start = (bf16[192,3072]{1,0:T(8,128)(2,1)S(1)}, bf16[192,3072]{1,0:T(8,128)(2,1)}, u32[]{:S(2)}, u32[]{:S(2)}) collective-permute-start(bf16[192,3072]{1,0:T(8,128)(2,1)S(1)} %bitcast.68), channel_id=1, source_target_pairs={{0,8},{8,0},{16,24},{24,16},{1,9},{9,1},{17,25},{25,17},{2,10},{10... | collective-permute-start | bytes 3538952 | tf_op jit(solution)/shard_map/ppermute | solution.py:1734
  81.0 1.9 copy-start.2
  87.9 1.1 copy-start.8
  89.1 27.0 %copy-start.7 = (bf16[3,128,2048]{2,1,0:T(8,128)(2,1)}, bf16[3,128,2048]{2,1,0:T(8,128)(2,1)S(1)}, u32[]{:S(2)}) copy-start(bf16[3,128,2048]{2,1,0:T(8,128)(2,1)S(1)} %get-tuple-element.50.qt_ref) | copy-start | bytes 4718596
  89.1 27.0 %copy-start.9 = (bf16[3,2048,128]{2,1,0:T(8,128)(2,1)}, bf16[3,2048,128]{2,1,0:T(8,128)(2,1)S(1)}, u32[]{:S(2)}) copy-start(bf16[3,2048,128]{2,1,0:T(8,128)(2,1)S(1)} %get-tuple-element.51.k_ref) | copy-start | bytes 4718596
  89.1 27.1 %copy-start.10 = (bf16[3,2048,128]{2,1,0:T(8,128)(2,1)}, bf16[3,2048,128]{2,1,0:T(8,128)(2,1)S(1)}, u32[]{:S(2)}) copy-start(bf16[3,2048,128]{2,1,0:T(8,128)(2,1)S(1)} %get-tuple-element.60.v_ref) | copy-start | bytes 4718596
  116.1 1.0 copy-start.6
  117.1 1.2 copy-start.11
  199.6 46.7 %collective-permute-start.5 = (bf16[192,2304]{1,0:T(8,128)(2,1)}, bf16[192,2304]{1,0:T(8,128)(2,1)}, u32[]{:S(2)}, u32[]{:S(2)}) collective-permute-start(bf16[192,2304]{1,0:T(8,128)(2,1)} %get-tuple-element.84), channel_id=1, source_target_pairs={{0,24},{24,0},{8,16},{16,8},{1,25},{25,1},{9,17},{17,9},{2,26},{26... | collective-permute-start | bytes 2654216 | tf_op jit(solution)/shard_map/ppermute | solution.py:1762
  201.4 44.9 %collective-permute-start.4 = (bf16[192,2304]{1,0:T(8,128)(2,1)S(1)}, bf16[192,2304]{1,0:T(8,128)(2,1)}, u32[]{:S(2)}, u32[]{:S(2)}) collective-permute-start(bf16[192,2304]{1,0:T(8,128)(2,1)S(1)} %get-tuple-element.85), channel_id=1, source_target_pairs={{0,16},{16,0},{8,24},{24,8},{1,17},{17,1},{9,25},{25,9},{2,18},{18... | collective-permute-start | bytes 2654216 | tf_op jit(solution)/shard_map/ppermute | solution.py:1762
  202.2 44.1 %collective-permute-start.3 = (bf16[192,2304]{1,0:T(8,128)(2,1)S(1)}, bf16[192,2304]{1,0:T(8,128)(2,1)}, u32[]{:S(2)}, u32[]{:S(2)}) collective-permute-start(bf16[192,2304]{1,0:T(8,128)(2,1)S(1)} %get-tuple-element.86), channel_id=1, source_target_pairs={{0,8},{8,0},{16,24},{24,16},{1,9},{9,1},{17,25},{25,17},{2,10},{10... | collective-permute-start | bytes 2654216 | tf_op jit(solution)/shard_map/ppermute | solution.py:1762
  241.2 1.0 copy-start.3
  242.1 1.0 copy-start.4
  243.1 1.0 copy-start.5
  350.0 1.6 copy-start.15
  355.5 3.4 copy-start.14
  358.9 2.5 copy-start.12
  361.4 1.1 copy-start.1
Sparse Core Ops, SparseCore 0:
  203.2 38.7 all-reduce.3

commit v4 on v3

--- a/solution.py
+++ b/solution.py
@@ -726,7 +726,7 @@
 
 def start_kernel(
     tokens, keep, w_joined, w_out, w_down, sequence, keep_all, full_joined, full_out, full_down,
-    z_send, z_recv, tp_send, tp_recv, w_send, w_recv, keep_send, keep_recv, local_sem,
+    z_send, z_recv, tp_send, tp_recv, w_send, w_recv, down_send, down_recv, keep_send, keep_recv, local_sem,
 ):
     place, stage, core = lax.axis_index("fsdp"), lax.axis_index("ctx"), lax.axis_index("tp")
     seq = stage // 2
@@ -784,9 +784,7 @@
             send(theirs, own, near, 2).start()
 
     weights = []
-    for index, (shard, full) in enumerate(
-        ((w_joined, full_joined), (w_out, full_out), (w_down, full_down))
-    ):
+    for index, (shard, full) in enumerate(((w_joined, full_joined), (w_out, full_out))):
         for other in (1, 2, 3):
             sem = 3 * index + other - 1
             weights.append(
@@ -796,6 +794,23 @@
                 )
             )
             weights[-1].start()
+
+    units = w_down.shape[1] // 2
+
+    def down_copy(owner, other, which, sem):
+        columns = pl.ds(which * units, units)
+        source = w_down if owner is place else full_down.at[owner]
+        return pltpu.make_async_remote_copy(
+            source.at[:, columns], full_down.at[owner, :, columns], down_send.at[sem], down_recv.at[sem],
+            device_id=(place ^ other, stage, core), device_id_type=MESH,
+        )
+
+    halves = [
+        down_copy(place, other, which, 2 * which + other - 1)
+        for other, which in ((1, 0), (2, 1), (1, 1), (2, 0))
+    ]
+    for copy in halves:
+        copy.start()
     flags = []
     for shift in (1, 2, 3):
         flags.append(
@@ -818,6 +833,11 @@
     ):
         local.append(pltpu.make_async_copy(source, target, local_sem.at[index]))
         local[-1].start()
+
+    on = [down_copy(place ^ 1, 2, 0, 4), down_copy(place ^ 2, 1, 1, 5)]
+    for first_half, second in zip(halves[:2], on):
+        first_half.wait_recv()
+        second.start()
 
     for own, near, end in mids:
         far = 3 - end
@@ -852,8 +872,10 @@
                 shared(block).wait_recv()
 
     first.wait_send()
-    for copy in weights + flags:
+    for copy in weights + flags + halves[2:] + on:
         copy.wait()
+    for copy in halves[:2]:
+        copy.wait_send()
     for copy in local:
         copy.wait()
 
@@ -863,7 +885,7 @@
     dma = pltpu.SemaphoreType.DMA
     return pl.pallas_call(
         start_kernel,
-        in_specs=[pl.BlockSpec(memory_space=pl.ANY)] * 5,
+        in_specs=[pl.BlockSpec(memory_space=pltpu.VMEM)] * 5,
         out_specs=[pl.BlockSpec(memory_space=pl.ANY)] * 5,
         out_shape=[
             jax.ShapeDtypeStruct((4, 2, block_rows // 2, width), tokens.dtype),
@@ -873,7 +895,7 @@
             jax.ShapeDtypeStruct((4,) + w_down.shape, w_down.dtype),
         ],
         scratch_shapes=[
-            dma((3,)), dma((4,)), dma((4,)), dma((4,)), dma((9,)), dma((9,)), dma((3,)), dma((3,)), dma((6,)),
+            dma((3,)), dma((4,)), dma((4,)), dma((4,)), dma((6,)), dma((6,)), dma((6,)), dma((6,)), dma((3,)), dma((3,)), dma((6,)),
         ],
         compiler_params=pltpu.CompilerParams(collective_id=0, has_side_effects=True),
         cost_estimate=pl.CostEstimate(flops=40 << 30, bytes_accessed=16 << 20, transcendentals=0),
@@ -895,12 +917,12 @@
 
 
 def middle_kernel(
-    attended, sequence, cotangent, w_out, w_down, up_0, up_1, up_2, up_3, vectors,
+    attended, sequence, cotangent, w_out, w_down, up_0, up_1, up_2, vectors,
     out_home, grad_one, grad_heads, early, late, down_sum, sums,
     token_v, mine_v, theirs_v, both_v, cot_v, out_w, down_w, up_w,
     send_a, recv_a, send_b, recv_b, send_c, recv_c,
     normed_v, inv_v, low_v, hidden_v, gate_v, lift_v, grad_v, ffn_v, att_v, result_v, keep_v, away_v, tile_v,
-    down_v, down_got, load_sem, pair_send, pair_recv, cot_send, cot_recv, cot_pass, cot_took,
+    down_v, down_got, load_sem, far_send, far_recv, pair_send, pair_recv, cot_send, cot_recv, cot_pass, cot_took,
     a_send, a_recv, b_send, b_recv, c_send, c_recv, out_send, out_recv, out_pass, out_took,
     one_sem, keep_sem, away_send, away_recv, tile_sem, down_send, down_recv, down_sem,
 ):
@@ -936,6 +958,18 @@
     for c in range(chunks):
         pair_copy(c).start()
 
+    def far_copy(which):
+        source, over = ((up_1, 2), (up_2, 1))[which]
+        columns = pl.ds(which * units, units)
+        rows = pl.ds(pl.multiple_of((place ^ 3 ^ over) * quarter, quarter), quarter)
+        return remote(
+            source.at[:, columns], up_w.at[rows, columns], far_send.at[which], far_recv.at[which],
+            (place ^ over, stage, core),
+        )
+
+    for which in (0, 1):
+        far_copy(which).start()
+
     def cot_owner(which):
         return 2 * which + stage // 2
 
@@ -974,7 +1008,7 @@
         pltpu.make_async_copy(sequence.at[pl.ds(half * chunks, chunks)], token_v, load_sem.at[2]),
         pltpu.make_async_copy(w_down, down_w, load_sem.at[3]),
     ]
-    for other, shard in enumerate((up_0, up_1, up_2, up_3)):
+    for other, shard in enumerate((up_0, up_1, up_2)):
         rows = pl.ds(pl.multiple_of((place ^ other) * quarter, quarter), quarter)
         loads.append(pltpu.make_async_copy(shard, up_w.at[rows], load_sem.at[4 + other]))
     for load in loads:
@@ -1011,6 +1045,8 @@
 
     for load in loads[2:]:
         load.wait()
+    for which in (0, 1):
+        far_copy(which).wait_recv()
 
     @pl.loop(0, chunks)
     def _(c):
@@ -1094,6 +1130,35 @@
         grad_ffn = grad_two.astype(jnp.bfloat16)
         ffn_v[c] = grad_ffn
         add_sum(2, grad_ffn.astype(jnp.float32))
+
+    tile = tile_v.shape[2]
+
+    def columns(index):
+        return pl.ds(pl.multiple_of(index * tile, tile), tile)
+
+    def weight_part(left, right):
+        rows = left.shape[0] * left.shape[1]
+        return dot(
+            left[...].reshape(rows, left.shape[2]), right.reshape(rows, tile), ((0,), (0,))
+        ).astype(jnp.bfloat16)
+
+    unit_tiles = units // tile
+
+    def down_copy(i, other):
+        rows = pl.ds(pl.multiple_of((place ^ other) * quarter, quarter), quarter)
+        return remote(
+            down_v.at[rows, columns(i)], down_got.at[other - 1, :, columns(i)],
+            down_send.at[i, other - 1], down_recv.at[i, other - 1], (place ^ other, stage, core),
+        )
+
+    @pl.loop(0, unit_tiles)
+    def _(i):
+        down_v[:, columns(i)] = weight_part(ffn_v, hidden_v[:, :, columns(i)])
+        for other in (1, 2, 3):
+            down_copy(i, other).start()
+
+    @pl.loop(0, chunks)
+    def _(c):
         for n in range(0, units, wide):
             grad_hidden = dot(ffn_v[c], down_w[:, n : n + wide])
             gate_v[c, :, n : n + wide] = (grad_hidden * gate_v[c, :, n : n + wide]).astype(jnp.bfloat16)
@@ -1102,32 +1167,6 @@
             dot(gate_v[c], up_w[:, :units], ((1,), (1,))) + dot(lift_v[c], up_w[:, units:], ((1,), (1,)))
         ).astype(jnp.bfloat16)
         exchange(c, send_c, recv_c, c_send, c_recv).start()
-
-    tile = tile_v.shape[2]
-
-    def columns(index):
-        return pl.ds(pl.multiple_of(index * tile, tile), tile)
-
-    def weight_part(left, right):
-        rows = left.shape[0] * left.shape[1]
-        return dot(
-            left[...].reshape(rows, left.shape[2]), right.reshape(rows, tile), ((0,), (0,))
-        ).astype(jnp.bfloat16)
-
-    unit_tiles = units // tile
-
-    def down_copy(i, other):
-        rows = pl.ds(pl.multiple_of((place ^ other) * quarter, quarter), quarter)
-        return remote(
-            down_v.at[rows, columns(i)], down_got.at[other - 1, :, columns(i)],
-            down_send.at[i, other - 1], down_recv.at[i, other - 1], (place ^ other, stage, core),
-        )
-
-    @pl.loop(0, unit_tiles)
-    def _(i):
-        down_v[:, columns(i)] = weight_part(ffn_v, hidden_v[:, :, columns(i)])
-        for other in (1, 2, 3):
-            down_copy(i, other).start()
 
     def one_copy(c):
         return pltpu.make_async_copy(grad_v.at[c], grad_one.at[c], one_sem.at[c])
@@ -1231,6 +1270,8 @@
             out_share(which, core).start()
 
     down_out.wait()
+    for which in (0, 1):
+        far_copy(which).wait_send()
     for i in range(unit_tiles):
         for other in (1, 2, 3):
             down_copy(i, other).wait_send()
@@ -1278,7 +1319,7 @@
     four, two = dma((chunks,)), dma((2,))
     return pl.pallas_call(
         middle_kernel,
-        in_specs=[pl.BlockSpec(memory_space=pl.ANY)] * 9 + [pl.BlockSpec(memory_space=pltpu.VMEM)],
+        in_specs=[pl.BlockSpec(memory_space=pl.ANY)] * 8 + [pl.BlockSpec(memory_space=pltpu.VMEM)],
         out_specs=[pl.BlockSpec(memory_space=pl.ANY)] * 6 + [pl.BlockSpec(memory_space=pltpu.VMEM)],
         out_shape=[
             jax.ShapeDtypeStruct((2, 2, rows, width), bf16),
@@ -1297,7 +1338,7 @@
             vmem(inner), vmem(inner), vmem(inner),
             vmem(wide, f32), vmem(wide), vmem(wide), vmem(wide), vmem(narrow_rows), vmem(narrow_rows),
             vmem((2, width, tile)), vmem((width, units)), vmem((3, width // 4, units)),
-            dma((8,)), four, four, two, two, two, two,
+            dma((7,)), two, two, four, four, two, two, two, two,
             four, four, four, four, four, four, four, two, two, two,
             four, four, four, four, dma((2, 4)), dma((units // tile, 3)), dma((units // tile, 3)), dma,
         ],
@@ -1731,7 +1772,7 @@
     query_feat = query_feat.astype(jnp.bfloat16)
 
     up_own, full_joined = lax.optimization_barrier((w_up.reshape(w_up.shape[0], -1), full_joined))
-    up_shards = [up_own] + [lax.ppermute(up_own, "fsdp", swap) for swap in (X_SWAP, Y_SWAP, D_SWAP)]
+    up_shards = [up_own] + [lax.ppermute(up_own, "fsdp", swap) for swap in (X_SWAP, Y_SWAP)]
 
     bias = jnp.concatenate([own_columns(b_query), jnp.zeros((width,), jnp.float32), own_columns(b_value)])
     pad = -3 * width % LANES

time: 370 us -> 338 us (0.914)
  Pallas kernels: 302 us -> 277 us
  waiting for transfers between devices: 5.99 us -> 0.03 us
    pallas_call x1, Pallas kernels: 60.4 us -> 45.1 us  [start(): pl.pallas_call(start_kernel, in_specs=[pl.BlockSpec(memory_space=pltpu.VM...]
    pallas_call x1, Pallas kernels: 72.5 us -> 63.3 us  [middle(): pl.pallas_call(middle_kernel, in_specs=[pl.BlockSpec(memory_space=pl.ANY)...]
    ppermute x3 -> x2, waiting for transfers between devices: 5.96 us -> 0.01 us  [per_device_paired(): lax.ppermute(up_own, 'fsdp', swap)]
  transfers between devices with their start and end apart: 7 -> 6, of which waited for: 2 -> 0; matrix products, arithmetic and copies ran while one was open for 2% -> 3% of each run, Pallas kernels for 19% -> 21%
where the time goes in v4:
time: 338 us; the launch traced here: 337 us
  Pallas kernels  277 us (82%)
  local copies, waits for them, and re-layouts  26.2 us (8%)
  between operations  14.6 us (4%)
  other arithmetic  13.4 us (4%)
  starting transfers between devices  5.66 us (2%)
    pallas_call x1, Pallas kernels, tail(): pl.pallas_call(tail_kernel, in_specs=[vmem_spec] * 5 + [any_spec] * 7, ou...  98.5 us
    pallas_call x1, Pallas kernels, middle(): pl.pallas_call(middle_kernel, in_specs=[pl.BlockSpec(memory_space=pl.ANY)...  63.3 us
    pallas_call x1, Pallas kernels, start(): pl.pallas_call(start_kernel, in_specs=[pl.BlockSpec(memory_space=pltpu.VM...  45.1 us
    pallas_call x1, Pallas kernels, attend_back(): pl.pallas_call(attend_back_kernel, grid_spec=pltpu.PrefetchScalarGridSpec...  38.1 us
    pallas_call x1, Pallas kernels, attend(): pl.pallas_call(attend_kernel, grid_spec=pltpu.PrefetchScalarGridSpec(num_...  27 us
    unnamed x56, local copies, waits for them, and re-layouts  10.9 us
  transfers between devices with their start and end apart: 6, of which 0 were waited for; matrix products, arithmetic and copies ran while one was open for 3% of the time, Pallas kernels for 21%

profile of v4, /device:TPU:0, one launch (start us, length us, event | category | flops | bytes accessed | tf_op | source)
XLA Modules:
  0.0 337.0 jit_solution(7209740422396914433)
XLA Ops:
  7.3 1.5 copy.34
  8.8 0.1 constant_dynamic-slice_fusion.2
  9.0 0.1 constant_dynamic-slice_fusion
  9.1 0.8 pad_maximum_fusion.3.w_joined
  10.0 45.1 %start.1 = (bf16[4,2,256,768]{3,2,1,0:T(8,128)(2,1)}, s32[4,2,512]{2,1,0:T(2,128)}, bf16[4,192,576]{2,1,0:T(8,128)(2,1)}, bf16[4,192,384]{2,1,0:T(8,128)(2,1)}, bf16[4,192,1536]{2,1,0:T(8,128)(2,1)}) custom-call(bf16[2,512,768]{2,1,0:T(8,128)(2,1)} %tokens.1, s32[2,512]{1,0:T(2,128)} %keep.1, bf16[192,576]{1,0:T(8,128)(2,1)} %pad_maximum_fusion.3.w_joined, ...), custom_call_target="tpu_custom_call" | custom-call | flops 42949672960 | bytes 16777216 | tf_op jit(solution)/shard_map/start/pallas_call | solution.py:886
  55.2 1.6 collective-permute-start.1
  56.7 0.5 collective-permute-start
  57.4 0.2 reduce-window.4
  57.6 0.1 convert_reduce_fusion
  57.7 0.1 slice.60
  57.8 0.1 slice.57
  58.3 0.2 select_reduce_fusion
  58.5 0.7 compare_select_fusion
  59.3 0.2 select_reduce_fusion.1
  59.5 0.1 subtract_reduce-precision_fusion
  59.6 0.2 select_select_fusion
  59.8 1.3 pad.8.w_ref
  61.1 0.7 stack.35.vectors
  61.7 1.9 select_convert_fusion.1.key_feat_ref
  63.6 0.7 select_convert_fusion.query_feat_ref
  64.3 1.9 copy-done.2
  66.2 5.0 %project.1 = (bf16[3,128,2048]{2,1,0:T(8,128)(2,1)S(1)}, bf16[3,2048,64]{2,1,0:T(8,128)(2,1)S(1)}, bf16[3,2048,128]{2,1,0:T(8,128)(2,1)S(1)}, bf16[3,64,2048]{2,...) custom-call(bf16[2048,768]{1,0:T(8,128)(2,1)S(1)} %bitcast.59, ...), custom_call_target="tpu_custom_call" | custom-call | flops 2013265920 | bytes 12582912 | tf_op jit(solution)/shard_map/project/pallas_call | solution.py:440
  71.3 1.1 copy-done.8
  72.4 27.0 %attend.1 = (bf16[2048,192]{1,0:T(8,128)(2,1)S(1)}, f32[3,64,2048]{2,1,0:T(8,128)S(1)}, f32[3,1,2048]{2,1,0:T(1,128)S(1)}) custom-call(s32[2,8]{1,0:T(2,128)S(1)} %pad_add_fusion.span_ref, f32[3]{0:T(128)S(1)} %get-tuple-element.98.slope_ref, bf16[3,128,2048]{2,1,0:T(8,128)(2,1)S(1)} %get-tuple-element.50.qt_ref, ...), custom_call_target="tpu_custom_call" | custom-call | flops 3221225472 | bytes 6291456 | tf_op jit(solution)/shard_map/attend/pallas_call | solution.py:550
  99.5 1.0 copy-done.6
  100.5 1.2 copy-done.11
  101.7 63.3 %middle.1 = (bf16[2,2,256,768]{3,2,1,0:T(8,128)(2,1)}, f32[4,256,768]{2,1,0:T(8,128)}, bf16[8,256,192]{2,1,0:T(8,128)(2,1)}, bf16[4,192,2304]{2,1,0:T(8,128)(2,1...) custom-call(bf16[8,256,192]{2,1,0:T(8,128)(2,1)} %bitcast.63, ...), custom_call_target="tpu_custom_call" | custom-call | flops 53687091200 | bytes 33554432 | tf_op jit(solution)/shard_map/middle/pallas_call | solution.py:1320
  165.0 2.8 slice_bitcast_fusion
  167.8 1.5 collective-permute-start.4
  169.3 1.3 collective-permute-start.3
  170.6 0.7 collective-permute-start.2
  171.4 38.1 %attend_back.1 = (bf16[2048,192]{1,0:T(8,128)(2,1)S(1)}, bf16[2048,192]{1,0:T(8,128)(2,1)S(1)}, bf16[2048,192]{1,0:T(8,128)(2,1)S(1)}) custom-call(s32[2,8]{1,0:T(2,128)S(1)} %pad_add_fusion.span_ref, f32[3]{0:T(128)S(1)} %get-tuple-element.98.slope_ref, bf16[3,128,2048]{2,1,0:T(8,128)(2,1)} %copy-done.7, bf16[3,2048,64]{2,1,0:T(8,128)(2,1)} %copy-done.8, ...), custom_call_target="tpu_custom_call" | custom-call | flops 8053063680 | bytes 12582912 | tf_op jit(solution)/shard_map/attend_back/pallas_call | solution.py:689
  209.4 1.0 copy-done.3
  210.4 1.0 copy-done.4
  211.4 1.0 copy-done.5
  212.3 2.2 convert_element_type.76
  214.6 98.5 %tail.1 = (bf16[2,2,256,768]{3,2,1,0:T(8,128)(2,1)}, bf16[192,3456]{1,0:T(8,128)(2,1)}, bf16[2,192,576]{2,1,0:T(8,128)(2,1)}, f32[8,768]{1,0:T(8,128)}) custom-call(bf16[8,256,192]{2,1,0:T(8,128)(2,1)} %bitcast.60, bf16[8,256,192]{2,1,0:T(8,128)(2,1)} %bitcast.61, bf16[8,256,192]{2,1,0:T(8,128)(2,1)} %bitcast.62, bf16[768,576]{1,0:T(8,128)(2,1)} %bitcast.70, ...), custom_call_target="tpu_custom_call" | custom-call | flops 85899345920 | bytes 33554432 | tf_op jit(solution)/shard_map/tail/pallas_call | solution.py:1659
  313.0 1.3 slice_reduce_fusion.6
  314.4 1.6 slice_reduce_fusion
  316.0 1.6 split.8
  317.6 1.6 split.9
  319.3 0.8 slice_bitcast_fusion.4
  320.1 3.0 reshape.486
  323.1 3.3 bitcast_convert_fusion
  326.5 0.8 pad_maximum_fusion.2
  327.3 0.8 pad_maximum_fusion.1
  328.1 0.8 pad_maximum_fusion
  329.0 1.1 copy.37
  (85 shorter events, 0.7 us)
Async XLA Ops:
  7.2 1.7 copy-start
  7.2 1.8 copy-start.16
  7.2 1.8 copy-start.17
  7.2 205.1 %all-reduce.4.cloned.1.call-start = ((), (), s32[]{:S(2)}) async-start(), calls=%async_computation | async-start | bytes 1179648 | tf_op jit(solution)/shard_map/psum | solution.py:1824
  8.8 47.9 %copy-start.13 = (bf16[24,8,2,1536]{3,1,2,0:T(8,128)(2,1)}, bf16[24,8,2,1536]{3,1,2,0:T(8,128)(2,1)S(1)}, u32[]{:S(2)}) copy-start(bf16[24,8,2,1536]{3,1,2,0:T(8,128)(2,1)S(1)} %copy.34) | copy-start | bytes 3538948
  9.9 47.5 %copy-start.26 = (s32[2,8]{1,0:T(2,128)S(1)}, s32[2,8]{1,0:T(2,128)}, u32[]{:S(2)}) copy-start(s32[2,8]{1,0:T(2,128)} %param.19) | copy-start | bytes 196
  9.9 48.0 %copy-start.24 = (f32[384]{0:T(512)S(1)}, f32[384]{0:T(512)}, u32[]{:S(2)}) copy-start(f32[384]{0:T(512)} %param.22) | copy-start | bytes 4612
  9.9 48.1 %copy-start.25 = (f32[384]{0:T(512)S(1)}, f32[384]{0:T(512)}, u32[]{:S(2)}) copy-start(f32[384]{0:T(512)} %param.25) | copy-start | bytes 4612
  9.9 48.2 %copy-start.18 = (f32[768]{0:T(1024)S(1)}, f32[768]{0:T(1024)}, u32[]{:S(2)}) copy-start(f32[768]{0:T(1024)} %param.27) | copy-start | bytes 9220
  9.9 48.2 %copy-start.19 = (f32[768]{0:T(1024)S(1)}, f32[768]{0:T(1024)}, u32[]{:S(2)}) copy-start(f32[768]{0:T(1024)} %param.28) | copy-start | bytes 9220
  10.0 48.2 %copy-start.20 = (f32[768]{0:T(1024)S(1)}, f32[768]{0:T(1024)}, u32[]{:S(2)}) copy-start(f32[768]{0:T(1024)} %param.29) | copy-start | bytes 9220
  10.0 48.3 %copy-start.21 = (f32[768]{0:T(1024)S(1)}, f32[768]{0:T(1024)}, u32[]{:S(2)}) copy-start(f32[768]{0:T(1024)} %param.32) | copy-start | bytes 9220
  10.0 48.3 %copy-start.22 = (f32[768]{0:T(1024)S(1)}, f32[768]{0:T(1024)}, u32[]{:S(2)}) copy-start(f32[768]{0:T(1024)} %param.33) | copy-start | bytes 9220
  10.0 48.3 %copy-start.23 = (f32[768]{0:T(1024)S(1)}, f32[768]{0:T(1024)}, u32[]{:S(2)}) copy-start(f32[768]{0:T(1024)} %param.34) | copy-start | bytes 9220
  55.2 46.5 %collective-permute-start.1 = (bf16[192,3072]{1,0:T(8,128)(2,1)S(1)}, bf16[192,3072]{1,0:T(8,128)(2,1)}, u32[]{:S(2)}, u32[]{:S(2)}) collective-permute-start(bf16[192,3072]{1,0:T(8,128)(2,1)S(1)} %bitcast.66), channel_id=1, source_target_pairs={{0,16},{16,0},{8,24},{24,8},{1,17},{17,1},{9,25},{25,9},{2,18},{18... | collective-permute-start | bytes 3538952 | tf_op jit(solution)/shard_map/ppermute | solution.py:1775
  56.7 44.9 %collective-permute-start = (bf16[192,3072]{1,0:T(8,128)(2,1)S(1)}, bf16[192,3072]{1,0:T(8,128)(2,1)}, u32[]{:S(2)}, u32[]{:S(2)}) collective-permute-start(bf16[192,3072]{1,0:T(8,128)(2,1)S(1)} %bitcast.67), channel_id=1, source_target_pairs={{0,8},{8,0},{16,24},{24,16},{1,9},{9,1},{17,25},{25,17},{2,10},{10... | collective-permute-start | bytes 3538952 | tf_op jit(solution)/shard_map/ppermute | solution.py:1775
  64.3 1.9 copy-start.2
  71.3 1.1 copy-start.8
  72.4 27.0 %copy-start.7 = (bf16[3,128,2048]{2,1,0:T(8,128)(2,1)}, bf16[3,128,2048]{2,1,0:T(8,128)(2,1)S(1)}, u32[]{:S(2)}) copy-start(bf16[3,128,2048]{2,1,0:T(8,128)(2,1)S(1)} %get-tuple-element.50.qt_ref) | copy-start | bytes 4718596
  72.4 27.0 %copy-start.9 = (bf16[3,2048,128]{2,1,0:T(8,128)(2,1)}, bf16[3,2048,128]{2,1,0:T(8,128)(2,1)S(1)}, u32[]{:S(2)}) copy-start(bf16[3,2048,128]{2,1,0:T(8,128)(2,1)S(1)} %get-tuple-element.51.k_ref) | copy-start | bytes 4718596
  72.4 27.1 %copy-start.10 = (bf16[3,2048,128]{2,1,0:T(8,128)(2,1)}, bf16[3,2048,128]{2,1,0:T(8,128)(2,1)S(1)}, u32[]{:S(2)}) copy-start(bf16[3,2048,128]{2,1,0:T(8,128)(2,1)S(1)} %get-tuple-element.60.v_ref) | copy-start | bytes 4718596
  99.5 1.0 copy-start.6
  100.5 1.2 copy-start.11
  167.8 46.7 %collective-permute-start.4 = (bf16[192,2304]{1,0:T(8,128)(2,1)}, bf16[192,2304]{1,0:T(8,128)(2,1)}, u32[]{:S(2)}, u32[]{:S(2)}) collective-permute-start(bf16[192,2304]{1,0:T(8,128)(2,1)} %get-tuple-element.84), channel_id=1, source_target_pairs={{0,24},{24,0},{8,16},{16,8},{1,25},{25,1},{9,17},{17,9},{2,26},{26... | collective-permute-start | bytes 2654216 | tf_op jit(solution)/shard_map/ppermute | solution.py:1803
  169.3 45.2 %collective-permute-start.3 = (bf16[192,2304]{1,0:T(8,128)(2,1)S(1)}, bf16[192,2304]{1,0:T(8,128)(2,1)}, u32[]{:S(2)}, u32[]{:S(2)}) collective-permute-start(bf16[192,2304]{1,0:T(8,128)(2,1)S(1)} %get-tuple-element.85), channel_id=1, source_target_pairs={{0,16},{16,0},{8,24},{24,8},{1,17},{17,1},{9,25},{25,9},{2,18},{18... | collective-permute-start | bytes 2654216 | tf_op jit(solution)/shard_map/ppermute | solution.py:1803
  170.6 43.9 %collective-permute-start.2 = (bf16[192,2304]{1,0:T(8,128)(2,1)S(1)}, bf16[192,2304]{1,0:T(8,128)(2,1)}, u32[]{:S(2)}, u32[]{:S(2)}) collective-permute-start(bf16[192,2304]{1,0:T(8,128)(2,1)S(1)} %get-tuple-element.86), channel_id=1, source_target_pairs={{0,8},{8,0},{16,24},{24,16},{1,9},{9,1},{17,25},{25,17},{2,10},{10... | collective-permute-start | bytes 2654216 | tf_op jit(solution)/shard_map/ppermute | solution.py:1803
  209.4 1.0 copy-start.3
  210.4 1.0 copy-start.4
  211.4 1.0 copy-start.5
  317.6 1.6 copy-start.15
  323.1 3.4 copy-start.14
  326.5 2.5 copy-start.12
  329.0 1.1 copy-start.1
Sparse Core Ops, SparseCore 0:
  171.5 38.7 all-reduce.3

commit v5 on v4

--- a/solution.py
+++ b/solution.py
@@ -385,6 +385,7 @@
 
 
 LANES = 128
+VMEM_BYTES = 60 << 20
 MESH = pl.DeviceIdType.MESH
 TILE = 256
 DOC_ROW, KEEP_ROW, POS_ROW, LINE_ROW, LOG_ROW, FEAT_END = 64, 72, 73, 79, 82, 85
@@ -401,74 +402,6 @@
     high = low(value)
     middle = low(value - high)
     return high, middle, low(value - high - middle)
-
-
-def narrow(value):
-    return lax.reduce_precision(value, 8, 7)
-
-
-def project_kernel(x_ref, w_ref, bias_ref, key_feat_ref, query_feat_ref, qt_ref, q_ref, k_ref, kt_ref, v_ref, vt_ref):
-    heads = q_ref.shape[0]
-    rows = x_ref.shape[0]
-    y = dot(x_ref[...], w_ref[...]) + bias_ref[...]
-    y = y.astype(jnp.bfloat16).astype(jnp.float32)
-    lane = lax.broadcasted_iota(jnp.int32, (rows, LANES), 1)
-    sub = lax.broadcasted_iota(jnp.int32, (LANES, rows), 0)
-
-    def head_part(index):
-        pair = y[:, index // 2 * LANES : (index // 2 + 1) * LANES]
-        if index % 2:
-            pair = pltpu.roll(pair, HEAD, 1)
-        return jnp.where(lane < HEAD, pair, 0.0)
-
-    for head in range(heads):
-        query = head_part(head) * 0.125
-        q_ref[head] = query[:, :HEAD].astype(jnp.bfloat16)
-        qt_ref[head] = (query.T + query_feat_ref[head].astype(jnp.float32)).astype(jnp.bfloat16)
-        key = head_part(heads + head)
-        k_ref[head] = (key + key_feat_ref[...].astype(jnp.float32)).astype(jnp.bfloat16)
-        kt_ref[head] = key.T[:HEAD].astype(jnp.bfloat16)
-        value = head_part(2 * heads + head)
-        ones = (lane >= HEAD) & (lane < HEAD + 3)
-        v_ref[head] = jnp.where(ones, 1.0, value).astype(jnp.bfloat16)
-        vt_ref[head] = jnp.where(sub == HEAD, 1.0, value.T)[:80].astype(jnp.bfloat16)
-
-
-def project(x, weight, bias, key_feat, query_feat, heads):
-    length, width = x.shape
-    rows = 2 * TILE
-    return pl.pallas_call(
-        project_kernel,
-        grid=(length // rows,),
-        in_specs=[
-            pl.BlockSpec((rows, width), lambda i: (i, 0)),
-            pl.BlockSpec(weight.shape, lambda i: (0, 0)),
-            pl.BlockSpec(bias.shape, lambda i: (0, 0)),
-            pl.BlockSpec((rows, LANES), lambda i: (i, 0)),
-            pl.BlockSpec((heads, LANES, rows), lambda i: (0, 0, i)),
-        ],
-        out_specs=[
-            pl.BlockSpec((heads, LANES, rows), lambda i: (0, 0, i)),
-            pl.BlockSpec((heads, rows, HEAD), lambda i: (0, i, 0)),
-            pl.BlockSpec((heads, rows, LANES), lambda i: (0, i, 0)),
-            pl.BlockSpec((heads, HEAD, rows), lambda i: (0, 0, i)),
-            pl.BlockSpec((heads, rows, LANES), lambda i: (0, i, 0)),
-            pl.BlockSpec((heads, 80, rows), lambda i: (0, 0, i)),
-        ],
-        out_shape=[
-            jax.ShapeDtypeStruct((heads, LANES, length), jnp.bfloat16),
-            jax.ShapeDtypeStruct((heads, length, HEAD), jnp.bfloat16),
-            jax.ShapeDtypeStruct((heads, length, LANES), jnp.bfloat16),
-            jax.ShapeDtypeStruct((heads, HEAD, length), jnp.bfloat16),
-            jax.ShapeDtypeStruct((heads, length, LANES), jnp.bfloat16),
-            jax.ShapeDtypeStruct((heads, 80, length), jnp.bfloat16),
-        ],
-        compiler_params=pltpu.CompilerParams(vmem_limit_bytes=40 << 20),
-        cost_estimate=pl.CostEstimate(
-            flops=2 * length * width * weight.shape[1], bytes_accessed=12 << 20, transcendentals=0
-        ),
-        name="project",
-    )(x, weight, bias, key_feat, query_feat)
 
 
 def side_signs(rows):
@@ -500,9 +433,340 @@
         step(tile, 1)
 
 
-def attend_kernel(span_ref, slope_ref, qt_ref, k_ref, vt_ref, o_ref, ot_ref, lse_ref, max_ref, acc_ref):
+def doc_bounds(docs_ref, seq):
+    bounds, total = [], 0
+    for index in range(docs_ref.shape[1]):
+        total = total + docs_ref[seq, index]
+        bounds.append(total)
+    return bounds
+
+
+def tile_span(docs_ref, seq, block):
+    first, last = block * TILE, block * TILE + TILE - 1
+    begin = end = start = 0
+    for bound in doc_bounds(docs_ref, seq):
+        begin = jnp.where(bound <= first, bound, begin)
+        end = jnp.where(start <= last, bound, end)
+        start = bound
+    return lax.div(begin, TILE), lax.div(end + TILE - 1, TILE)
+
+
+def start_kernel(
+    docs, slopes, tokens, keep, w_query, w_key, w_value, w_out, w_down, b_query, b_value, w_up,
+    sequence, full_joined, full_out, full_down, up_flat, query_t, queries, keys, keys_t, values, values_t,
+    tokens_v, own_v, joined_v, keep_v, up_v, qt_v, q_v, k_v, kt_v, v_v, vt_v,
+    z_send, z_recv, tp_send, tp_recv, w_send, w_recv, down_send, down_recv, keep_send, keep_recv, local_sem,
+    block_sem, joined_sem, up_sem, out_sem,
+):
+    place, stage, core = lax.axis_index("fsdp"), lax.axis_index("ctx"), lax.axis_index("tp")
+    seq, half = stage // 2, stage % 2
+    half_rows, model_width = sequence.shape[2:]
+    rows_of = 2 * half_rows
+    heads = qt_v.shape[1]
+    width = heads * HEAD
+    f32, bf16 = jnp.float32, jnp.bfloat16
+    barrier = pltpu.get_barrier_semaphore()
+    peers = [(place ^ other, stage, core) for other in (1, 2, 3)]
+    peers += [(place, lax.rem(stage + shift, 4), core) for shift in (1, 2, 3)]
+    peers += [(place, stage, 1 - core)]
+    for peer in peers:
+        pl.semaphore_signal(barrier, inc=1, device_id=peer, device_id_type=MESH)
+
+    def columns_of(weight):
+        return jnp.where(half == 0, weight[:, :width], weight[:, width:])
+
+    own_v[...] = jnp.concatenate([columns_of(w[...]) for w in (w_query, w_key, w_value)], 1)
+    joined_v[place] = own_v[...]
+    tokens_v[stage] = tokens[seq].reshape(2, half_rows, model_width)
+    keep_v[stage] = keep[...]
+    pl.semaphore_wait(barrier, len(peers))
+
+    def remote(source, target, send, recv, device):
+        return pltpu.make_async_remote_copy(
+            source, target, send, recv, device_id=device, device_id_type=MESH
+        )
+
+    rows = pl.ds(pl.multiple_of(core * half_rows, half_rows), half_rows)
+    ours, theirs = tokens.at[seq, rows], tokens.at[1 - seq, rows]
+    other_core = (place, stage, 1 - core)
+    inner = (stage == 1) | (stage == 2)
+    facing, opposite = 3 - stage, stage ^ 2
+
+    def send(source, block, target, slot):
+        return remote(source, tokens_v.at[block, core], z_send.at[slot], z_recv.at[block], (place, target, core))
+
+    def arrival(block):
+        return remote(ours, tokens_v.at[block, core], z_send.at[0], z_recv.at[block], other_core)
+
+    def share(block, whose):
+        half_block = tokens_v.at[block, whose]
+        return remote(half_block, half_block, tp_send.at[block], tp_recv.at[block], other_core)
+
+    to_pair = send(ours, stage, stage ^ 1, 0)
+    to_facing = send(theirs, stage, facing, 1)
+    to_opposite = send(theirs, stage, opposite, 2)
+    to_facing.start()
+    to_pair.start()
+
+    @pl.when(~inner)
+    def _():
+        to_opposite.start()
+
+    weights = [
+        remote(
+            own_v, joined_v.at[place], w_send.at[other - 1], w_recv.at[other - 1], (place ^ other, stage, core)
+        )
+        for other in (1, 2, 3)
+    ]
+    flags = [
+        remote(
+            keep, keep_v.at[stage], keep_send.at[shift - 1], keep_recv.at[shift - 1],
+            (place, lax.rem(stage + shift, 4), core),
+        )
+        for shift in (1, 2, 3)
+    ]
+    outs = [
+        remote(
+            w_out, full_out.at[place], w_send.at[other + 2], w_recv.at[other + 2], (place ^ other, stage, core)
+        )
+        for other in (1, 2, 3)
+    ]
+
+    units = w_down.shape[1] // 2
+
+    def down_copy(owner, other, which, sem):
+        columns = pl.ds(which * units, units)
+        source = w_down if owner is place else full_down.at[owner]
+        return remote(
+            source.at[:, columns], full_down.at[owner, :, columns], down_send.at[sem], down_recv.at[sem],
+            (place ^ other, stage, core),
+        )
+
+    halves = [
+        down_copy(place, other, which, 2 * which + other - 1)
+        for other, which in ((1, 0), (2, 1), (1, 1), (2, 0))
+    ]
+    on = [down_copy(place ^ 1, 2, 0, 4), down_copy(place ^ 2, 1, 1, 5)]
+    for copy in weights + flags + outs + halves:
+        copy.start()
+    local = [
+        pltpu.make_async_copy(w_out, full_out.at[place], local_sem.at[0]),
+        pltpu.make_async_copy(w_down, full_down.at[place], local_sem.at[1]),
+    ]
+    for copy in local:
+        copy.start()
+
+    for part in (0, 1):
+        up_v[:, pl.ds(part * w_up.shape[2], w_up.shape[2])] = w_up[:, part, :]
+    up_out = pltpu.make_async_copy(up_v, up_flat, up_sem)
+    up_out.start()
+
+    bounds = doc_bounds(docs, seq)
+    third, fourth = 3 - stage, 3 - (stage ^ 1)
+
+    def out_copies(slot, block):
+        at = pl.ds(pl.multiple_of(block * rows_of, rows_of), rows_of)
+        pairs = (
+            (qt_v.at[slot], query_t.at[:, :, at]),
+            (q_v.at[slot], queries.at[:, at, :]),
+            (k_v.at[slot], keys.at[:, at, :]),
+            (kt_v.at[slot], keys_t.at[:, :, at]),
+            (v_v.at[slot], values.at[:, at, :]),
+            (vt_v.at[slot], values_t.at[:, :, at]),
+        )
+        return [
+            pltpu.make_async_copy(source, target, block_sem.at[slot, index])
+            for index, (source, target) in enumerate(pairs)
+        ]
+
+    def sequence_copy(block):
+        return pltpu.make_async_copy(tokens_v.at[block], sequence.at[block], out_sem.at[block])
+
+    def low(value):
+        return value.astype(bf16).astype(f32)
+
+    def project(slot, block):
+        x = tokens_v[block].reshape(rows_of, model_width)
+        y = dot(x, joined_v[...].reshape(model_width, 3 * width))
+        zero = jnp.zeros((1, width), f32)
+        biases = [
+            jnp.where(half == 0, b[:, :width], b[:, width:])
+            for b in (b_query[...].reshape(1, -1), b_value[...].reshape(1, -1))
+        ]
+        y = low(y + jnp.concatenate([biases[0], zero, biases[1]], 1))
+        fill = -y.shape[1] % LANES
+        if fill:
+            y = jnp.concatenate([y, jnp.zeros((rows_of, fill), f32)], 1)
+        lane = lax.broadcasted_iota(jnp.int32, (rows_of, LANES), 1)
+        sub = lax.broadcasted_iota(jnp.int32, (LANES, rows_of), 0)
+        first = block * rows_of
+        key_pos = first + lax.broadcasted_iota(jnp.int32, (rows_of, LANES), 0)
+        query_pos = first + lax.broadcasted_iota(jnp.int32, (LANES, rows_of), 1)
+
+        def segments(positions):
+            return sum((bound <= positions).astype(jnp.int32) for bound in bounds)
+
+        flag = keep_v[block, pl.ds(seq, 1), :].astype(f32)
+        flag = jnp.broadcast_to(flag, (LANES, rows_of)).T
+        key_feat = jnp.where(lane < DOC_ROW, 0.0, 1.0)
+        key_doc = jnp.where(segments(key_pos) == lane - DOC_ROW, 0.0, MASKED)
+        key_feat = jnp.where((lane >= DOC_ROW) & (lane < DOC_ROW + len(bounds)), key_doc, key_feat)
+        key_feat = jnp.where(lane == KEEP_ROW, jnp.where(flag > 0.5, 0.0, MASKED), key_feat)
+        pos_low = key_pos & 255
+        key_feat = jnp.where(
+            (lane >= POS_ROW) & (lane < POS_ROW + 3), (key_pos - pos_low).astype(f32), key_feat
+        )
+        key_feat = jnp.where((lane >= POS_ROW + 3) & (lane < LINE_ROW), pos_low.astype(f32), key_feat)
+        key_feat = jnp.where(lane >= FEAT_END, 0.0, key_feat)
+        doc_feat = jnp.where(segments(query_pos) == sub - DOC_ROW, 1.0, 0.0)
+        doc_feat = jnp.where(sub == KEEP_ROW, 1.0, doc_feat)
+
+        def head_part(index):
+            pair = y[:, index // 2 * LANES : (index // 2 + 1) * LANES]
+            if index % 2:
+                pair = pltpu.roll(pair, HEAD, 1)
+            return jnp.where(lane < HEAD, pair, 0.0)
+
+        for head in range(heads):
+            query_feat = doc_feat
+            slope = jnp.full((1, rows_of), slopes[head], f32)
+            slope_terms = three_terms(slope, low)
+            line_terms = three_terms(-slope * query_pos[:1].astype(f32), low)
+            for term in range(3):
+                here = (sub == POS_ROW + term) | (sub == POS_ROW + 3 + term)
+                query_feat = jnp.where(here, slope_terms[term], query_feat)
+                query_feat = jnp.where(sub == LINE_ROW + term, line_terms[term], query_feat)
+            query = head_part(head) * 0.125
+            q_v[slot, head] = query[:, :HEAD].astype(bf16)
+            qt_v[slot, head] = (query.T + query_feat).astype(bf16)
+            key = head_part(heads + head)
+            k_v[slot, head] = (key + key_feat).astype(bf16)
+            kt_v[slot, head] = key.T[:HEAD].astype(bf16)
+            value = head_part(2 * heads + head)
+            ones = (lane >= HEAD) & (lane < HEAD + 3)
+            v_v[slot, head] = jnp.where(ones, 1.0, value).astype(bf16)
+            vt_v[slot, head] = jnp.where(sub == HEAD, 1.0, value.T)[:80].astype(bf16)
+
+    for copy in weights + flags:
+        copy.wait_recv()
+    joined_out = pltpu.make_async_copy(joined_v, full_joined, joined_sem)
+    joined_out.start()
+
+    @pl.loop(0, 4)
+    def _(i):
+        pair = stage ^ 1
+        block = jnp.where(i == 0, stage, jnp.where(i == 1, pair, jnp.where(i == 2, third, fourth)))
+        slot = lax.rem(i, 2)
+
+        @pl.when(i == 1)
+        def _():
+            arrival(pair).wait_recv()
+            share(pair, core).start()
+            arrival(third).wait_recv()
+
+            @pl.when(inner)
+            def _():
+                send(tokens_v.at[third, core], third, pair, 2).start()
+
+            share(third, core).start()
+            for near, far in zip(halves[:2], on):
+                near.wait_recv()
+                far.start()
+
+        @pl.when(i == 3)
+        def _():
+            arrival(fourth).wait_recv()
+            share(fourth, core).start()
+
+        @pl.when(i >= 1)
+        def _():
+            share(block, 1 - core).wait_recv()
+
+        @pl.when(i >= 2)
+        def _():
+            for copy in out_copies(slot, block):
+                copy.wait()
+
+        sequence_copy(block).start()
+        project(slot, block)
+        for copy in out_copies(slot, block):
+            copy.start()
+
+    to_pair.wait_send()
+    to_facing.wait_send()
+    to_opposite.wait_send()
+    for block in (stage ^ 1, third, fourth):
+        share(block, core).wait_send()
+    for copy in outs + halves[2:] + on:
+        copy.wait()
+    for copy in weights + flags + halves[:2]:
+        copy.wait_send()
+    for copy in local + [joined_out, up_out]:
+        copy.wait()
+    for block in range(4):
+        sequence_copy(block).wait()
+    for slot in (0, 1):
+        for copy in out_copies(slot, 0):
+            copy.wait()
+
+
+def start(docs, slopes, tokens, keep, w_query, w_key, w_value, w_out, w_down, b_query, b_value, w_up):
+    _, block_rows, model_width = tokens.shape
+    heads = slopes.shape[0]
+    width, length = heads * HEAD, 4 * block_rows
+    dma, bf16 = pltpu.SemaphoreType.DMA, jnp.bfloat16
+    half_rows, quarter = block_rows // 2, w_query.shape[0]
+    any_spec = pl.BlockSpec(memory_space=pl.ANY)
+    vmem_spec = pl.BlockSpec(memory_space=pltpu.VMEM)
+    smem_spec = pl.BlockSpec(memory_space=pltpu.SMEM)
+
+    def parts(rows):
+        return [
+            (heads, LANES, rows),
+            (heads, rows, HEAD),
+            (heads, rows, LANES),
+            (heads, HEAD, rows),
+            (heads, rows, LANES),
+            (heads, 80, rows),
+        ]
+
+    three, four, six = dma((3,)), dma((4,)), dma((6,))
+    return pl.pallas_call(
+        start_kernel,
+        in_specs=[smem_spec] * 2 + [vmem_spec] * 10,
+        out_specs=[any_spec] * 11,
+        out_shape=[
+            jax.ShapeDtypeStruct(shape, bf16)
+            for shape in [
+                (4, 2, half_rows, model_width),
+                (4, quarter, 3 * width),
+                (4,) + w_out.shape,
+                (4,) + w_down.shape,
+                (quarter, 2 * w_up.shape[2]),
+            ]
+            + parts(length)
+        ],
+        scratch_shapes=[
+            pltpu.VMEM((4, 2, half_rows, model_width), bf16),
+            pltpu.VMEM((quarter, 3 * width), bf16),
+            pltpu.VMEM((4, quarter, 3 * width), bf16),
+            pltpu.VMEM((4,) + keep.shape, keep.dtype),
+            pltpu.VMEM((quarter, 2 * w_up.shape[2]), bf16),
+            *[pltpu.VMEM((2,) + shape, bf16) for shape in parts(block_rows)],
+            three, four, four, four, six, six, six, six, three, three, dma((2,)), dma((2, 6)), dma, dma, four,
+        ],
+        compiler_params=pltpu.CompilerParams(
+            collective_id=0, has_side_effects=True, vmem_limit_bytes=VMEM_BYTES
+        ),
+        cost_estimate=pl.CostEstimate(flops=40 << 30, bytes_accessed=16 << 20, transcendentals=0),
+        name="start",
+    )(docs, slopes, tokens, keep, w_query, w_key, w_value, w_out, w_down, b_query, b_value, w_up)
+
+
+def attend_kernel(docs_ref, slope_ref, qt_ref, k_ref, vt_ref, o_ref, ot_ref, lse_ref, max_ref, acc_ref):
     heads = qt_ref.shape[0]
     block = pl.program_id(0)
+    first_tile, last_tile = tile_span(docs_ref, lax.axis_index("ctx") // 2, block)
     after, same, bare = side_signs(TILE)
 
     def tile_rows(tile, count=1):
@@ -531,8 +795,8 @@
             max_ref[head] = top[head]
             acc_ref[head] = acc[head] * jnp.exp(old[head] - top[head]) + parts[head]
 
-    sweep(span_ref[0, block], block, lambda tile, count: step(tile, count, None))
-    sweep(block + 1, span_ref[1, block], lambda tile, count: step(tile, count, after))
+    sweep(first_tile, block, lambda tile, count: step(tile, count, None))
+    sweep(block + 1, last_tile, lambda tile, count: step(tile, count, after))
 
     parts = []
     for head in range(heads):
@@ -544,7 +808,7 @@
     o_ref[...] = jnp.concatenate(parts, 0).T.astype(jnp.bfloat16)
 
 
-def attend(spans, slopes, query_t, keys, value_t):
+def attend(docs, slopes, query_t, keys, value_t):
     heads, _, length = query_t.shape
     blocks = length // TILE
     return pl.pallas_call(
@@ -572,22 +836,23 @@
             jax.ShapeDtypeStruct((heads, HEAD, length), jnp.float32),
             jax.ShapeDtypeStruct((heads, 1, length), jnp.float32),
         ],
-        compiler_params=pltpu.CompilerParams(vmem_limit_bytes=40 << 20),
+        compiler_params=pltpu.CompilerParams(vmem_limit_bytes=VMEM_BYTES),
         cost_estimate=pl.CostEstimate(
             flops=heads * length * length * 256, bytes_accessed=6 << 20, transcendentals=heads * length * length
         ),
         name="attend",
-    )(spans, slopes, query_t, keys, value_t)
+    )(docs, slopes, query_t, keys, value_t)
 
 
 def attend_back_kernel(
-    span_ref, slope_ref, qt_ref, q_ref, k_ref, kt_ref, v_ref, g_ref, ot_ref, lse_ref,
+    docs_ref, slope_ref, qt_ref, q_ref, k_ref, kt_ref, v_ref, g_ref, ot_ref, lse_ref,
     dq_ref, dk_ref, dv_ref, qt_log, grad_heads, grad_t, query_acc, key_acc, value_acc,
 ):
     heads = qt_ref.shape[0]
     blocks = pl.num_programs(0)
     block = pl.program_id(0)
     length = qt_ref.shape[2]
+    first_tile, last_tile = tile_span(docs_ref, lax.axis_index("ctx") // 2, block)
     after, same, bare = side_signs(TILE)
 
     def low(value):
@@ -663,8 +928,8 @@
             queries = [query * sign[:, : count * TILE] for query in queries]
         accumulate(tile, [dot(k_ref[head], queries[head]) for head in range(heads)], False, count)
 
-    sweep(span_ref[0, block], block, lambda tile, count: step(tile, count, after_wide))
-    sweep(block + 1, span_ref[1, block], lambda tile, count: step(tile, count, None))
+    sweep(first_tile, block, lambda tile, count: step(tile, count, after_wide))
+    sweep(block + 1, last_tile, lambda tile, count: step(tile, count, None))
 
     dk_ref[...] = jnp.concatenate([key_acc[head] for head in range(heads)], 1).astype(jnp.bfloat16)
     dv_ref[...] = jnp.concatenate([value_acc[head] for head in range(heads)], 1).astype(jnp.bfloat16)
@@ -678,7 +943,7 @@
             dq_ref[rows, :] = (turned.T * 0.125).astype(jnp.bfloat16)
 
 
-def attend_back(spans, slopes, query_t, queries, keys, keys_t, values, grads, out_t, lse):
+def attend_back(docs, slopes, query_t, queries, keys, keys_t, values, grads, out_t, lse):
     heads, _, length = query_t.shape
     blocks = length // TILE
     width = heads * HEAD
@@ -716,191 +981,12 @@
             ],
         ),
         out_shape=[jax.ShapeDtypeStruct((length, width), jnp.bfloat16)] * 3,
-        compiler_params=pltpu.CompilerParams(vmem_limit_bytes=50 << 20),
+        compiler_params=pltpu.CompilerParams(vmem_limit_bytes=VMEM_BYTES),
         cost_estimate=pl.CostEstimate(
             flops=heads * length * length * 640, bytes_accessed=12 << 20, transcendentals=heads * length * length
         ),
         name="attend_back",
-    )(spans, slopes, query_t, queries, keys, keys_t, values, grads, out_t, lse)
-
-
-def start_kernel(
-    tokens, keep, w_joined, w_out, w_down, sequence, keep_all, full_joined, full_out, full_down,
-    z_send, z_recv, tp_send, tp_recv, w_send, w_recv, down_send, down_recv, keep_send, keep_recv, local_sem,
-):
-    place, stage, core = lax.axis_index("fsdp"), lax.axis_index("ctx"), lax.axis_index("tp")
-    seq = stage // 2
-    half_rows = sequence.shape[2]
-    barrier = pltpu.get_barrier_semaphore()
-    peers = [(place ^ other, stage, core) for other in (1, 2, 3)]
-    peers += [(place, lax.rem(stage + shift, 4), core) for shift in (1, 2, 3)]
-    peers += [(place, stage, 1 - core)]
-    for peer in peers:
-        pl.semaphore_signal(barrier, inc=1, device_id=peer, device_id_type=MESH)
-    pl.semaphore_wait(barrier, len(peers))
-
-    rows = pl.ds(pl.multiple_of(core * half_rows, half_rows), half_rows)
-    ours, theirs = tokens.at[seq, rows], tokens.at[1 - seq, rows]
-
-    def send(source, block, target, slot):
-        return pltpu.make_async_remote_copy(
-            source, sequence.at[block, core], z_send.at[slot], z_recv.at[block],
-            device_id=(place, target, core), device_id_type=MESH,
-        )
-
-    def arrival(block):
-        return pltpu.make_async_remote_copy(
-            ours, sequence.at[block, core], z_send.at[0], z_recv.at[block],
-            device_id=(place, stage, 1 - core), device_id_type=MESH,
-        )
-
-    def share(block):
-        return pltpu.make_async_remote_copy(
-            sequence.at[block, core], sequence.at[block, core], tp_send.at[block], tp_recv.at[block],
-            device_id=(place, stage, 1 - core), device_id_type=MESH,
-        )
-
-    def shared(block):
-        return pltpu.make_async_remote_copy(
-            sequence.at[block, 1 - core], sequence.at[block, 1 - core], tp_send.at[block], tp_recv.at[block],
-            device_id=(place, stage, 1 - core), device_id_type=MESH,
-        )
-
-    first = send(ours, stage, stage ^ 1, 0)
-    ends = ((0, 2, 3), (3, 1, 0))
-    mids = ((1, 2, 0), (2, 1, 3))
-    for own, near, _ in mids:
-
-        @pl.when(stage == own)
-        def _():
-            send(theirs, own, near, 1).start()
-
-    first.start()
-    for own, near, far in ends:
-
-        @pl.when(stage == own)
-        def _():
-            send(theirs, own, far, 1).start()
-            send(theirs, own, near, 2).start()
-
-    weights = []
-    for index, (shard, full) in enumerate(((w_joined, full_joined), (w_out, full_out))):
-        for other in (1, 2, 3):
-            sem = 3 * index + other - 1
-            weights.append(
-                pltpu.make_async_remote_copy(
-                    shard, full.at[place], w_send.at[sem], w_recv.at[sem],
-                    device_id=(place ^ other, stage, core), device_id_type=MESH,
-                )
-            )
-            weights[-1].start()
-
-    units = w_down.shape[1] // 2
-
-    def down_copy(owner, other, which, sem):
-        columns = pl.ds(which * units, units)
-        source = w_down if owner is place else full_down.at[owner]
-        return pltpu.make_async_remote_copy(
-            source.at[:, columns], full_down.at[owner, :, columns], down_send.at[sem], down_recv.at[sem],
-            device_id=(place ^ other, stage, core), device_id_type=MESH,
-        )
-
-    halves = [
-        down_copy(place, other, which, 2 * which + other - 1)
-        for other, which in ((1, 0), (2, 1), (1, 1), (2, 0))
-    ]
-    for copy in halves:
-        copy.start()
-    flags = []
-    for shift in (1, 2, 3):
-        flags.append(
-            pltpu.make_async_remote_copy(
-                keep, keep_all.at[stage], keep_send.at[shift - 1], keep_recv.at[shift - 1],
-                device_id=(place, lax.rem(stage + shift, 4), core), device_id_type=MESH,
-            )
-        )
-        flags[-1].start()
-    local = []
-    for index, (source, target) in enumerate(
-        (
-            (tokens.at[seq, pl.ds(0, half_rows)], sequence.at[stage, 0]),
-            (tokens.at[seq, pl.ds(half_rows, half_rows)], sequence.at[stage, 1]),
-            (keep, keep_all.at[stage]),
-            (w_joined, full_joined.at[place]),
-            (w_out, full_out.at[place]),
-            (w_down, full_down.at[place]),
-        )
-    ):
-        local.append(pltpu.make_async_copy(source, target, local_sem.at[index]))
-        local[-1].start()
-
-    on = [down_copy(place ^ 1, 2, 0, 4), down_copy(place ^ 2, 1, 1, 5)]
-    for first_half, second in zip(halves[:2], on):
-        first_half.wait_recv()
-        second.start()
-
-    for own, near, end in mids:
-        far = 3 - end
-
-        @pl.when(stage == own)
-        def _():
-            arrival(near).wait_recv()
-            send(sequence.at[near, core], near, end, 2).start()
-            share(near).start()
-            arrival(end).wait_recv()
-            share(end).start()
-            arrival(far).wait_recv()
-            share(far).start()
-            send(theirs, own, near, 1).wait_send()
-            send(sequence.at[near, core], near, end, 2).wait_send()
-            for block in (near, end, far):
-                share(block).wait_send()
-                shared(block).wait_recv()
-
-    for own, near, far in ends:
-
-        @pl.when(stage == own)
-        def _():
-            inner = 3 - near
-            for block in (inner, far, near):
-                arrival(block).wait_recv()
-                share(block).start()
-            send(theirs, own, near, 1).wait_send()
-            send(theirs, own, near, 2).wait_send()
-            for block in (inner, far, near):
-                share(block).wait_send()
-                shared(block).wait_recv()
-
-    first.wait_send()
-    for copy in weights + flags + halves[2:] + on:
-        copy.wait()
-    for copy in halves[:2]:
-        copy.wait_send()
-    for copy in local:
-        copy.wait()
-
-
-def start(tokens, keep, w_joined, w_out, w_down):
-    _, block_rows, width = tokens.shape
-    dma = pltpu.SemaphoreType.DMA
-    return pl.pallas_call(
-        start_kernel,
-        in_specs=[pl.BlockSpec(memory_space=pltpu.VMEM)] * 5,
-        out_specs=[pl.BlockSpec(memory_space=pl.ANY)] * 5,
-        out_shape=[
-            jax.ShapeDtypeStruct((4, 2, block_rows // 2, width), tokens.dtype),
-            jax.ShapeDtypeStruct((4,) + keep.shape, keep.dtype),
-            jax.ShapeDtypeStruct((4,) + w_joined.shape, w_joined.dtype),
-            jax.ShapeDtypeStruct((4,) + w_out.shape, w_out.dtype),
-            jax.ShapeDtypeStruct((4,) + w_down.shape, w_down.dtype),
-        ],
-        scratch_shapes=[
-            dma((3,)), dma((4,)), dma((4,)), dma((4,)), dma((6,)), dma((6,)), dma((6,)), dma((6,)), dma((3,)), dma((3,)), dma((6,)),
-        ],
-        compiler_params=pltpu.CompilerParams(collective_id=0, has_side_effects=True),
-        cost_estimate=pl.CostEstimate(flops=40 << 30, bytes_accessed=16 << 20, transcendentals=0),
-        name="start",
-    )(tokens, keep, w_joined, w_out, w_down)
+    )(docs, slopes, query_t, queries, keys, keys_t, values, grads, out_t, lse)
 
 
 def rows_norm(residual):
@@ -917,15 +1003,18 @@
 
 
 def middle_kernel(
-    attended, sequence, cotangent, w_out, w_down, up_0, up_1, up_2, vectors,
-    out_home, grad_one, grad_heads, early, late, down_sum, sums,
-    token_v, mine_v, theirs_v, both_v, cot_v, out_w, down_w, up_w,
-    send_a, recv_a, send_b, recv_b, send_c, recv_c,
-    normed_v, inv_v, low_v, hidden_v, gate_v, lift_v, grad_v, ffn_v, att_v, result_v, keep_v, away_v, tile_v,
-    down_v, down_got, load_sem, far_send, far_recv, pair_send, pair_recv, cot_send, cot_recv, cot_pass, cot_took,
-    a_send, a_recv, b_send, b_recv, c_send, c_recv, out_send, out_recv, out_pass, out_took,
-    one_sem, keep_sem, away_send, away_recv, tile_sem, down_send, down_recv, down_sem,
+    attended, sequence, cotangent, w_out, w_down, up_0, up_1, up_2, *rest,
 ):
+    vectors, rest = rest[:6], rest[6:]
+    (
+        out_home, grad_one, grad_heads, early_0, early_1, early_2, early_3, late, down_sum, sums,
+        token_v, mine_v, theirs_v, both_v, cot_v, out_w, down_w, up_w,
+        send_a, recv_a, send_b, recv_b, send_c, recv_c,
+        normed_v, inv_v, low_v, hidden_v, gate_v, lift_v, grad_v, ffn_v, att_v, result_v, keep_v, away_v, tile_v,
+        down_v, down_got, load_sem, far_send, far_recv, pair_send, pair_recv, cot_send, cot_recv, cot_pass, cot_took,
+        a_send, a_recv, b_send, b_recv, c_send, c_recv, out_send, out_recv, out_pass, out_took,
+        one_sem, keep_sem, away_send, away_recv, tile_sem, down_send, down_recv, down_sem,
+    ) = rest
     place, stage, core = lax.axis_index("fsdp"), lax.axis_index("ctx"), lax.axis_index("tp")
     seq, half = stage // 2, stage % 2
     pair = stage ^ 1
@@ -1014,10 +1103,7 @@
     for load in loads:
         load.start()
 
-    def vector(index):
-        return vectors[index : index + 1, :]
-
-    b_out, gain_one, shift_one, b_down, gain_two, shift_two = (vector(i) for i in range(6))
+    b_out, gain_one, shift_one, b_down, gain_two, shift_two = (v[...].reshape(1, -1) for v in vectors)
     sums[...] = jnp.zeros_like(sums)
 
     def add_sum(index, rows):
@@ -1199,14 +1285,15 @@
         away_copy(c, half).start()
         keep_copy(c).start()
 
-    early_tiles = early.shape[2] // tile
-
-    def tile_copy(slot, row, index):
+    early = (early_0, early_1, early_2, early_3)
+    early_tiles = early_0.shape[1] // tile
+
+    def tile_copy(slot, other, index):
         target, column = index
+        rows = pl.ds(pl.multiple_of((place ^ other) * quarter, quarter), quarter)
+        place_of = target[other] if isinstance(target, tuple) else target.at[other]
         return pltpu.make_async_copy(
-            tile_v.at[slot, pl.ds(row * quarter, quarter)],
-            target.at[place ^ row, :, columns(column)],
-            tile_sem.at[slot, row],
+            tile_v.at[slot, rows], place_of.at[:, columns(column)], tile_sem.at[slot, other]
         )
 
     def weight_tile(count, target, column, left, right):
@@ -1319,13 +1406,13 @@
     four, two = dma((chunks,)), dma((2,))
     return pl.pallas_call(
         middle_kernel,
-        in_specs=[pl.BlockSpec(memory_space=pl.ANY)] * 8 + [pl.BlockSpec(memory_space=pltpu.VMEM)],
-        out_specs=[pl.BlockSpec(memory_space=pl.ANY)] * 6 + [pl.BlockSpec(memory_space=pltpu.VMEM)],
+        in_specs=[pl.BlockSpec(memory_space=pl.ANY)] * 8 + [pl.BlockSpec(memory_space=pltpu.VMEM)] * 6,
+        out_specs=[pl.BlockSpec(memory_space=pl.ANY)] * 9 + [pl.BlockSpec(memory_space=pltpu.VMEM)],
         out_shape=[
             jax.ShapeDtypeStruct((2, 2, rows, width), bf16),
             jax.ShapeDtypeStruct(wide, f32),
             jax.ShapeDtypeStruct((2 * chunks, rows, head_width // 2), bf16),
-            jax.ShapeDtypeStruct((4, width // 4, early), bf16),
+            *[jax.ShapeDtypeStruct((width // 4, early), bf16)] * 4,
             jax.ShapeDtypeStruct((4, width // 4, late), bf16),
             jax.ShapeDtypeStruct((width // 4, units), bf16),
             jax.ShapeDtypeStruct((8, width), f32),
@@ -1343,28 +1430,29 @@
             four, four, four, four, dma((2, 4)), dma((units // tile, 3)), dma((units // tile, 3)), dma,
         ],
         compiler_params=pltpu.CompilerParams(
-            collective_id=1, has_side_effects=True, vmem_limit_bytes=60 << 20
+            collective_id=1, has_side_effects=True, vmem_limit_bytes=VMEM_BYTES
         ),
         cost_estimate=pl.CostEstimate(flops=50 << 30, bytes_accessed=32 << 20, transcendentals=0),
         name="middle",
-    )(attended, sequence, cotangent, w_out, w_down, *up_shards, vectors)
+    )(attended, sequence, cotangent, w_out, w_down, *up_shards, *vectors)
 
 
 def tail_kernel(
     d_query, d_key, d_value, w_joined, sums_in, sequence, grad_one, early, late, moved_1, moved_2, moved_3,
     home, shard, joined, sums,
-    token_v, one_v, part_v, late_v, project_v, own_v, tp_sent, tp_got, pair_sent, pair_got, final_v,
-    summed_v, end_got, inner_v, mid_got, total_v, joined_v, quarter_got, cross_sent, cross_got, full_v,
-    step_v, step_got,
-    load_sem, late_send, late_recv, tp_send, tp_recv, pair_send, pair_recv, home_send, home_recv, home_pass, home_took, home_local,
-    end_send, end_recv, mid_send, mid_recv, back_send, back_recv, shard_sem,
-    quarter_send, quarter_recv, cross_send, cross_recv, half_send, half_recv, half_local, step_send, step_recv,
+    query_v, key_v, value_v, token_v, one_v, part_v, late_v, project_v, own_v, tp_sent, tp_got, pair_sent, pair_got,
+    final_v, summed_v, end_got, inner_v, mid_got, total_v, joined_v, quarter_got, both_sent, both_end, both_inner,
+    both_mid, both_total, step_v, step_got,
+    load_sem, late_send, late_recv, tp_send, tp_recv, pair_send, pair_recv, home_send, home_recv, home_pass,
+    home_took, home_local, end_send, end_recv, mid_send, mid_recv, back_send, back_recv, shard_sem,
+    quarter_send, quarter_recv, both_send, both_recv, both_local, step_send, step_recv,
 ):
     place, stage, core = lax.axis_index("fsdp"), lax.axis_index("ctx"), lax.axis_index("tp")
     seq, half = stage // 2, stage % 2
     bf16, f32 = jnp.bfloat16, jnp.float32
     pieces = summed_v.shape[0]
     piece = summed_v.shape[2]
+    early_pieces = early.shape[1] // piece
     quarter = joined_v.shape[0] // 4
     width = d_query.shape[2]
 
@@ -1374,6 +1462,26 @@
     peers += [(place, stage, 1 - core)]
     for peer in peers:
         pl.semaphore_signal(barrier, inc=1, device_id=peer, device_id_type=MESH)
+
+    loads = [
+        pltpu.make_async_copy(source, target, load_sem.at[index])
+        for index, (source, target) in enumerate(
+            (
+                (early, part_v.at[0]),
+                (moved_1, part_v.at[1]),
+                (moved_2, part_v.at[2]),
+                (moved_3, part_v.at[3]),
+                (d_query, query_v),
+                (d_key, key_v),
+                (d_value, value_v),
+                (late.at[0], late_v.at[0]),
+                (sequence, token_v),
+                (grad_one, one_v),
+            )
+        )
+    ]
+    for load in loads:
+        load.start()
     pl.semaphore_wait(barrier, len(peers))
 
     def remote(source, target, send, recv, device):
@@ -1384,17 +1492,9 @@
     other_core = (place, stage, 1 - core)
     partner = (place, stage ^ 1, core)
     at_end = (stage == 0) | (stage == 3)
-    across = (place, jnp.where(at_end, stage, 3 - stage), core)
-    inward = (place, jnp.where(stage < 2, 1, 2), core)
-    outward = (place, jnp.where(stage < 2, 0, 3), core)
-
-    loads = [
-        pltpu.make_async_copy(source, part_v.at[index], load_sem.at[index])
-        for index, source in enumerate((early.at[0], moved_1, moved_2, moved_3))
-    ]
-    loads.append(pltpu.make_async_copy(sequence, token_v, load_sem.at[4]))
-    loads.append(pltpu.make_async_copy(grad_one, one_v, load_sem.at[5]))
-    loads.append(pltpu.make_async_copy(late.at[0], late_v.at[0], load_sem.at[6]))
+    inward = (place, stage ^ 1, core)
+    outward = (place, stage ^ 1, core)
+    across = (place, 3 - stage, core)
 
     def late_copy(other):
         return remote(
@@ -1404,11 +1504,48 @@
 
     for other in (1, 2, 3):
         late_copy(other).start()
-    for load in loads:
-        load.start()
+
+    def columns(j):
+        return pl.ds(j * piece, piece)
+
+    def end_copy(j):
+        return remote(summed_v.at[j], end_got.at[j], end_send.at[j], end_recv.at[j], inward)
+
+    def mid_copy(j):
+        return remote(inner_v.at[j], mid_got.at[j], mid_send.at[j], mid_recv.at[j], across)
+
+    def back_copy(j):
+        return remote(total_v.at[j], shard.at[:, columns(j)], back_send.at[j], back_recv.at[j], outward)
+
+    def shard_copy(j):
+        return pltpu.make_async_copy(total_v.at[j], shard.at[:, columns(j)], shard_sem.at[j])
+
+    def sum_piece(j, parts, first):
+        terms = [parts[index, :, first : first + piece].astype(f32) for index in range(4)]
+        summed_v[j] = (terms[0] + terms[1] + (terms[2] + terms[3])).astype(bf16)
+
+        @pl.when(at_end)
+        def _():
+            end_copy(j).start()
+
+    def from_end(j):
+        end_copy(j).wait_recv()
+        inner_v[j] = (summed_v[j].astype(f32) + end_got[j].astype(f32)).astype(bf16)
+        mid_copy(j).start()
+
+    def from_mid(j):
+        mid_copy(j).wait_recv()
+        total_v[j] = (inner_v[j].astype(f32) + mid_got[j].astype(f32)).astype(bf16)
+        back_copy(j).start()
+        shard_copy(j).start()
+
+    for load in loads[:4]:
+        load.wait()
+    for j in range(early_pieces):
+        sum_piece(j, part_v, j * piece)
 
     def input_share(chunk):
-        rows = jnp.concatenate([d_query[chunk], d_key[chunk], d_value[chunk]], 1)
+        rows = jnp.concatenate([query_v[chunk], key_v[chunk], value_v[chunk]], 1)
         project_v[chunk] = rows
         return dot(rows, w_joined[...], ((1,), (1,)))
 
@@ -1417,6 +1554,9 @@
 
     def tp_copy(i):
         return remote(tp_sent.at[i], tp_got.at[i], tp_send.at[i], tp_recv.at[i], other_core)
+
+    for load in loads[4:7]:
+        load.wait()
 
     @pl.loop(0, 4)
     def _(i):
@@ -1434,35 +1574,12 @@
         pair_sent[i] = (own_v[i] + tp_got[i].astype(f32)).astype(bf16)
         pair_copy(i).start()
 
-    def end_copy(j):
-        return remote(summed_v.at[j], end_got.at[j], end_send.at[j], end_recv.at[j], inward)
-
-    def mid_copy(j):
-        return remote(inner_v.at[j], mid_got.at[j], mid_send.at[j], mid_recv.at[j], across)
-
-    def columns(j):
-        return pl.ds(j * piece, piece)
-
-    def back_copy(j):
-        return remote(total_v.at[j], shard.at[:, columns(j)], back_send.at[j], back_recv.at[j], outward)
-
-    def shard_copy(j):
-        return pltpu.make_async_copy(total_v.at[j], shard.at[:, columns(j)], shard_sem.at[j])
-
-    def sum_piece(j, parts, first):
-        terms = [parts[index, :, first : first + piece].astype(f32) for index in range(4)]
-        summed_v[j] = (terms[0] + terms[1] + (terms[2] + terms[3])).astype(bf16)
-
-        @pl.when(at_end)
-        def _():
-            end_copy(j).start()
-
-    for load in loads[:4]:
-        load.wait()
-    for j in range(pieces - 1):
-        sum_piece(j, part_v, j * piece)
-
-    loads[4].wait()
+    @pl.when(~at_end)
+    def _():
+        for j in range(early_pieces // 2):
+            from_end(j)
+
+    loads[8].wait()
     tokens = token_v[...].reshape(-1, token_v.shape[2])
     project = project_v[...].reshape(-1, project_v.shape[2])
     strip = 256
@@ -1485,7 +1602,7 @@
         return jnp.sum(grads[...].reshape(-1, width).astype(f32), 0, keepdims=True)
 
     bias_parts = []
-    for total in (column_sum(d_query), column_sum(d_value)):
+    for total in (column_sum(query_v), column_sum(value_v)):
         for which in (0, 1):
             bias_parts.append(jnp.where(half == which, total, 0.0))
     bias = jnp.concatenate(bias_parts, 1)
@@ -1505,12 +1622,48 @@
             step_copy(index + 1).start()
 
     step_copy(0).start()
-    loads[6].wait()
+
+    @pl.when(~at_end)
+    def _():
+        for j in range(early_pieces // 2, early_pieces):
+            from_end(j)
+            from_mid(j - early_pieces // 2)
+
+    loads[7].wait()
     for other in (1, 2, 3):
         late_copy(other).wait_recv()
-    sum_piece(pieces - 1, late_v, 0)
-
-    loads[5].wait()
+    for j in range(early_pieces, pieces):
+        sum_piece(j, late_v, (j - early_pieces) * piece)
+    step_on(0)
+
+    def both_end_copy():
+        return remote(both_sent, both_end, both_send.at[0], both_recv.at[0], inward)
+
+    def both_mid_copy():
+        return remote(both_inner, both_mid, both_send.at[1], both_recv.at[1], across)
+
+    def both_back_copy():
+        return remote(both_total, joined, both_send.at[2], both_recv.at[2], outward)
+
+    def both_here():
+        return pltpu.make_async_copy(both_total, joined, both_local)
+
+    for other in (1, 2, 3):
+        quarter_copy(other).wait_recv()
+    own_rows = pl.ds(pl.multiple_of(place * quarter, quarter), quarter)
+    both_sent[...] = (
+        joined_v[own_rows, :].astype(f32)
+        + quarter_got[0].astype(f32)
+        + (quarter_got[1].astype(f32) + quarter_got[2].astype(f32))
+    ).astype(bf16)
+
+    @pl.when(at_end)
+    def _():
+        both_end_copy().start()
+
+    step_on(1)
+
+    loads[9].wait()
 
     def home_copy(i):
         return remote(
@@ -1539,44 +1692,23 @@
         def _():
             home_copy(i).start()
 
-    step_on(0)
-    for other in (1, 2, 3):
-        quarter_copy(other).wait_recv()
-    own_rows = pl.ds(pl.multiple_of(place * quarter, quarter), quarter)
-    cross_sent[...] = (
-        joined_v[own_rows, :].astype(f32)
-        + quarter_got[0].astype(f32)
-        + (quarter_got[1].astype(f32) + quarter_got[2].astype(f32))
-    ).astype(bf16)
-    cross_copy = remote(cross_sent, cross_got, cross_send, cross_recv, (place, stage ^ 2, core))
-    cross_copy.start()
-    step_on(1)
-
-    def from_end(j):
-        end_copy(j).wait_recv()
-        inner_v[j] = (summed_v[j].astype(f32) + end_got[j].astype(f32)).astype(bf16)
-        mid_copy(j).start()
-
-    def from_mid(j):
-        mid_copy(j).wait_recv()
-        total_v[j] = (inner_v[j].astype(f32) + mid_got[j].astype(f32)).astype(bf16)
-        back_copy(j).start()
-        shard_copy(j).start()
-
     @pl.when(~at_end)
     def _():
-        from_end(0)
-        for j in range(1, pieces):
+        for j in range(early_pieces, pieces):
             from_end(j)
-            from_mid(j - 1)
+            from_mid(j - early_pieces // 2)
+        both_end_copy().wait_recv()
+        both_inner[half] = both_sent[...]
+        both_inner[1 - half] = both_end[...]
+        both_mid_copy().start()
+        for j in range(pieces - early_pieces // 2, pieces):
+            from_mid(j)
+        both_mid_copy().wait_recv()
+        both_total[...] = (both_inner[...].astype(f32) + both_mid[...].astype(f32)).astype(bf16)
+        both_back_copy().start()
+        both_here().start()
 
     step_on(2)
-    cross_copy.wait_recv()
-    full_v[...] = (cross_sent[...].astype(f32) + cross_got[...].astype(f32)).astype(bf16)
-    half_copy = remote(full_v, joined.at[half], half_send, half_recv, partner)
-    half_copy.start()
-    half_here = pltpu.make_async_copy(full_v, joined.at[half], half_local)
-    half_here.start()
     step_on(3)
     sums[...] = step_v[4]
 
@@ -1599,17 +1731,21 @@
 
     @pl.when(~at_end)
     def _():
-        from_mid(pieces - 1)
         for j in range(pieces):
             mid_copy(j).wait_send()
             back_copy(j).wait_send()
             shard_copy(j).wait()
+        both_mid_copy().wait_send()
+        both_back_copy().wait_send()
+        both_here().wait()
 
     @pl.when(at_end)
     def _():
         for j in range(pieces):
             end_copy(j).wait_send()
             back_copy(j).wait_recv()
+        both_end_copy().wait_send()
+        both_back_copy().wait_recv()
 
     for i in range(4):
         tp_copy(i).wait_send()
@@ -1636,17 +1772,14 @@
     for other in (1, 2, 3):
         quarter_copy(other).wait_send()
         late_copy(other).wait_send()
-    cross_copy.wait_send()
-    half_here.wait()
-    half_copy.wait_send()
-    remote(full_v, joined.at[1 - half], half_send, half_recv, partner).wait_recv()
 
 
 def tail(d_query, d_key, d_value, w_joined, sums, sequence, grad_one, early, late, moved):
     rows, width = sequence.shape[1:]
-    quarter, piece = late.shape[1:]
-    columns = early.shape[2] + piece
+    quarter = early.shape[0]
     joined = w_joined.shape[1]
+    piece = 3 * LANES
+    columns = early.shape[1] + late.shape[2]
     pieces = columns // piece
     dma, bf16, f32 = pltpu.SemaphoreType.DMA, jnp.bfloat16, jnp.float32
 
@@ -1655,32 +1788,34 @@
 
     any_spec, vmem_spec = pl.BlockSpec(memory_space=pl.ANY), pl.BlockSpec(memory_space=pltpu.VMEM)
     cut = (pieces, quarter, piece)
-    one, two, three, four = dma, dma((2,)), dma((3,)), dma((4,))
+    both = (2, quarter, joined)
+    one, two, three, four, many = dma, dma((2,)), dma((3,)), dma((4,)), dma((pieces,))
     return pl.pallas_call(
         tail_kernel,
-        in_specs=[vmem_spec] * 5 + [any_spec] * 7,
+        in_specs=[any_spec] * 3 + [vmem_spec] * 2 + [any_spec] * 7,
         out_specs=[any_spec] * 3 + [vmem_spec],
         out_shape=[
             jax.ShapeDtypeStruct((2, 2, rows, width), bf16),
             jax.ShapeDtypeStruct((quarter, columns), bf16),
-            jax.ShapeDtypeStruct((2, quarter, joined), bf16),
+            jax.ShapeDtypeStruct(both, bf16),
             jax.ShapeDtypeStruct(sums.shape, f32),
         ],
         scratch_shapes=[
-            vmem(sequence.shape), vmem(grad_one.shape, f32), vmem(early.shape), vmem(late.shape),
+            vmem(d_query.shape), vmem(d_query.shape), vmem(d_query.shape),
+            vmem(sequence.shape), vmem(grad_one.shape, f32), vmem((4,) + early.shape), vmem(late.shape),
             vmem((8, rows, joined)), vmem((4, rows, width), f32),
             vmem((4, rows, width)), vmem((4, rows, width)), vmem((2, rows, width)), vmem((2, rows, width)),
             vmem((2, rows, width)),
             vmem(cut), vmem(cut), vmem(cut), vmem(cut), vmem(cut),
             vmem((width, joined)), vmem((3, quarter, joined)), vmem((quarter, joined)), vmem((quarter, joined)),
-            vmem((quarter, joined)),
+            vmem(both), vmem(both), vmem(both),
             vmem((5,) + sums.shape, f32), vmem((4,) + sums.shape, f32),
-            dma((7,)), three, three, four, four, two, two, two, two, two, two, one,
-            three, three, three, three, three, three, three,
-            three, three, one, one, one, one, one, four, four,
+            dma((10,)), three, three, four, four, two, two, two, two, two, two, one,
+            many, many, many, many, many, many, many,
+            three, three, three, three, one, four, four,
         ],
         compiler_params=pltpu.CompilerParams(
-            collective_id=2, has_side_effects=True, vmem_limit_bytes=60 << 20
+            collective_id=2, has_side_effects=True, vmem_limit_bytes=VMEM_BYTES
         ),
         cost_estimate=pl.CostEstimate(flops=80 << 30, bytes_accessed=32 << 20, transcendentals=0),
         name="tail",
@@ -1689,6 +1824,70 @@
 
 def pick(pair, index):
     return lax.dynamic_index_in_dim(pair, index, 0, keepdims=False)
+
+
+def finish_kernel(
+    tokens_ref, shard_ref, joined_ref, down_ref, sums_ref,
+    d_tokens, d_query, d_key, d_value, d_out, d_up, d_down, *vectors,
+):
+    f32 = jnp.float32
+    for index in range(6):
+        vectors[index][...] = sums_ref[index]
+    biases = sums_ref[6]
+    vectors[6][...] = biases[: biases.shape[0] // 2]
+    vectors[7][...] = biases[biases.shape[0] // 2 :]
+    d_tokens[...] = tokens_ref[...].astype(f32)
+    units = d_up.shape[2]
+    d_up[:, 0, :] = shard_ref[:, :units].astype(f32)
+    d_up[:, 1, :] = shard_ref[:, units : 2 * units].astype(f32)
+    d_out[...] = shard_ref[:, 2 * units :].astype(f32)
+    d_down[...] = down_ref[...].astype(f32)
+    width = d_query.shape[1] // 2
+    for index, target in enumerate((d_query, d_key, d_value)):
+        columns = slice(index * width, (index + 1) * width)
+        target[...] = jnp.concatenate(
+            [joined_ref[0, :, columns], joined_ref[1, :, columns]], 1
+        ).astype(f32)
+
+
+def finish(tokens, shard, joined, down, sums):
+    steps = 4
+    quarter, units = down.shape
+    head_width = shard.shape[1] - 2 * units
+    row, some = tokens.shape[0] // steps, quarter // steps
+    sizes = [sums.shape[1]] * 6 + [head_width] * 2
+    f32 = jnp.float32
+
+    def rows(width):
+        return pl.BlockSpec((some, width), lambda i: (i, 0))
+
+    return pl.pallas_call(
+        finish_kernel,
+        grid=(steps,),
+        in_specs=[
+            pl.BlockSpec((row, tokens.shape[1]), lambda i: (i, 0)),
+            rows(shard.shape[1]),
+            pl.BlockSpec((2, some, joined.shape[2]), lambda i: (0, i, 0)),
+            rows(units),
+            pl.BlockSpec(sums.shape, lambda i: (0, 0)),
+        ],
+        out_specs=[
+            pl.BlockSpec((row, tokens.shape[1]), lambda i: (i, 0)),
+            rows(head_width), rows(head_width), rows(head_width), rows(head_width),
+            pl.BlockSpec((some, 2, units), lambda i: (i, 0, 0)),
+            rows(units),
+            *[pl.BlockSpec((size,), lambda i: (0,)) for size in sizes],
+        ],
+        out_shape=[
+            jax.ShapeDtypeStruct(tokens.shape, f32),
+            *[jax.ShapeDtypeStruct((quarter, head_width), f32)] * 4,
+            jax.ShapeDtypeStruct((quarter, 2, units), f32),
+            jax.ShapeDtypeStruct((quarter, units), f32),
+            *[jax.ShapeDtypeStruct((size,), f32) for size in sizes],
+        ],
+        compiler_params=pltpu.CompilerParams(vmem_limit_bytes=VMEM_BYTES),
+        name="finish",
+    )(tokens, shard, joined, down, sums)
 
 
 def per_device_paired(
@@ -1717,78 +1916,23 @@
     local_heads = b_query.shape[0] // HEAD
     heads = local_heads // 2
     width = heads * HEAD
-    place = lax.axis_index("fsdp")
-    stage = lax.axis_index("ctx")
+    half = lax.axis_index("ctx") % 2
     core = lax.axis_index("tp")
-    seq, half = stage // 2, stage % 2
-
-    def core_half(array):
-        return lax.dynamic_slice_in_dim(array, core * half_rows, half_rows, 1)
-
-    def own_columns(array):
-        return lax.dynamic_slice_in_dim(array, half * width, width, array.ndim - 1)
-
-    w_joined = jnp.concatenate([own_columns(w_query), own_columns(w_key), own_columns(w_value)], -1)
-    sequence, keep_all, full_joined, full_out, full_down = start(tokens, keep, w_joined, w_out, w_down)
-    sequence = sequence.reshape(length, model_width)
+    slopes = head_slopes(core * local_heads + half * heads, heads)
+    (
+        sequence, full_joined, full_out, full_down, up_own, query_t, queries, keys, keys_t, values, values_t,
+    ) = start(
+        doc_lengths, slopes, tokens, keep, w_query, w_key, w_value, w_out, w_down,
+        b_query, b_value, w_up,
+    )
     full_joined = full_joined.reshape(model_width, 3 * width)
     full_out = full_out.reshape(model_width, 2 * width)
     full_down = full_down.reshape(model_width, -1)
-    keep_row = lax.dynamic_index_in_dim(keep_all, seq, 1, keepdims=False).reshape(length)
-
-    bounds = jnp.cumsum(pick(doc_lengths, seq))
-    docs = bounds.shape[0]
-    positions = jnp.arange(length, dtype=jnp.int32)
-    segments = jnp.sum((bounds[None, :] <= positions[:, None]).astype(jnp.int32), -1)
-    starts = jnp.concatenate([jnp.zeros((1,), jnp.int32), bounds[:-1]])
-    firsts = segments[:: TILE]
-    lasts = segments[TILE - 1 :: TILE]
-    doc_index = jnp.arange(docs, dtype=jnp.int32)
-    span_from = jnp.sum(jnp.where(firsts[:, None] == doc_index, starts, 0), -1) // TILE
-    span_to = (jnp.sum(jnp.where(lasts[:, None] == doc_index, bounds, 0), -1) + TILE - 1) // TILE
-    spans = jnp.stack([span_from, span_to]).astype(jnp.int32)
-    slopes = head_slopes(core * local_heads + half * heads, heads)
-    feature = jnp.arange(LANES, dtype=jnp.int32)
-    key_doc = jnp.where(segments[:, None] == feature - DOC_ROW, 0.0, MASKED)
-    pos_high = (positions // 256 * 256).astype(jnp.float32)[:, None]
-    pos_low = (positions % 256).astype(jnp.float32)[:, None]
-    key_feat = jnp.where(feature < DOC_ROW, 0.0, 1.0)[None, :]
-    key_feat = jnp.where((feature >= DOC_ROW) & (feature < DOC_ROW + docs), key_doc, key_feat)
-    key_feat = jnp.where(feature == KEEP_ROW, jnp.where(keep_row == 1, 0.0, MASKED)[:, None], key_feat)
-    key_feat = jnp.where((feature >= POS_ROW) & (feature < POS_ROW + 3), pos_high, key_feat)
-    key_feat = jnp.where((feature >= POS_ROW + 3) & (feature < LINE_ROW), pos_low, key_feat)
-    key_feat = jnp.where(feature >= FEAT_END, 0.0, key_feat).astype(jnp.bfloat16)
-    rows = feature[None, :, None]
-    query_feat = jnp.where(segments[None, None, :] == rows - DOC_ROW, 1.0, 0.0)
-    query_feat = jnp.where(rows == KEEP_ROW, 1.0, query_feat)
-    slope_terms = three_terms(slopes[:, None, None], narrow)
-    line_terms = three_terms(
-        -slopes[:, None, None] * positions.astype(jnp.float32)[None, None, :], narrow
-    )
-    for term in range(3):
-        here = (rows == POS_ROW + term) | (rows == POS_ROW + 3 + term)
-        query_feat = jnp.where(here, slope_terms[term], query_feat)
-        query_feat = jnp.where(rows == LINE_ROW + term, line_terms[term], query_feat)
-    query_feat = query_feat.astype(jnp.bfloat16)
-
-    up_own, full_joined = lax.optimization_barrier((w_up.reshape(w_up.shape[0], -1), full_joined))
     up_shards = [up_own] + [lax.ppermute(up_own, "fsdp", swap) for swap in (X_SWAP, Y_SWAP)]
-
-    bias = jnp.concatenate([own_columns(b_query), jnp.zeros((width,), jnp.float32), own_columns(b_value)])
-    pad = -3 * width % LANES
-    query_t, queries, keys, keys_t, values, values_t = project(
-        sequence,
-        jnp.pad(full_joined, ((0, 0), (0, pad))),
-        jnp.pad(bias, (0, pad))[None],
-        key_feat,
-        query_feat,
-        heads,
-    )
-    attended_all, attended_t, lse = attend(spans, slopes, query_t, keys, values_t)
-
-    row_count = length // 2
-    vectors = jnp.stack([b_out, gain_one, shift_one, b_down, gain_two, shift_two, b_out, b_out])
-    out, grad_one, grad_heads, early, late, down_sum, sums = middle(
+    attended_all, attended_t, lse = attend(doc_lengths, slopes, query_t, keys, values_t)
+
+    vectors = (b_out, gain_one, shift_one, b_down, gain_two, shift_two)
+    out, grad_one, grad_heads, *early, late, down_sum, sums = middle(
         attended_all.reshape(8, half_rows, width),
         sequence.reshape(8, half_rows, model_width),
         cotangent.reshape(2, 2, half_rows, model_width),
@@ -1804,7 +1948,7 @@
         for other, swap in ((1, X_SWAP), (2, Y_SWAP), (3, D_SWAP))
     ]
     d_query, d_key, d_value = attend_back(
-        spans, slopes, query_t, queries, keys, keys_t, values, grad_heads, attended_t, lse
+        doc_lengths, slopes, query_t, queries, keys, keys_t, values, grad_heads, attended_t, lse
     )
     d_tokens, shard, joined, sums = tail(
         d_query.reshape(8, half_rows, width),
@@ -1814,31 +1958,26 @@
         sums,
         sequence.reshape(8, half_rows, model_width),
         grad_one,
-        early,
+        early[0],
         late,
         moved,
     )
-    d_tokens = d_tokens.reshape(2, block_rows, model_width).astype(jnp.float32)
-    sum_up, sum_out = jnp.split(shard.astype(jnp.float32), (2 * w_up.shape[2],), 1)
-    sum_up = sum_up.reshape(w_up.shape)
-    sum_down = lax.psum(down_sum, "ctx").astype(jnp.float32)
-    joined = joined.astype(jnp.float32)
-
-    def both_halves(first):
-        return jnp.concatenate(
-            [joined[0, :, first : first + width], joined[1, :, first : first + width]], -1
-        )
-
-    total_gain_two, total_shift_two, total_b_down, total_gain_one, total_shift_one, total_b_out = sums[:6]
-    total_bias = sums[6].reshape(2, 2 * width)
+    (
+        d_tokens, d_w_query, d_w_key, d_w_value, sum_out, sum_up, sum_down,
+        total_gain_two, total_shift_two, total_b_down, total_gain_one, total_shift_one, total_b_out,
+        total_b_query, total_b_value,
+    ) = finish(
+        d_tokens.reshape(2 * block_rows, model_width), shard, joined, lax.psum(down_sum, "ctx"), sums
+    )
+    d_tokens = d_tokens.reshape(2, block_rows, model_width)
     return (
         out,
         d_tokens,
-        both_halves(0),
-        total_bias[0],
-        both_halves(width),
-        both_halves(2 * width),
-        total_bias[1],
+        d_w_query,
+        total_b_query,
+        d_w_key,
+        d_w_value,
+        total_b_value,
         sum_out,
         total_b_out,
         total_gain_one,

time: 338 us -> 300 us (0.89)
  local copies, waits for them, and re-layouts: 26.2 us -> 3.99 us
  other arithmetic: 13.4 us -> 0.53 us
    convert_element_type x7 -> x0, other arithmetic: 8.18 us -> none  [the longest x1 3.35 us: per_device_paired(): d_tokens = d_tokens.reshape(2, block_rows, model_width).astype(jnp.float32)]
    pallas_call x3, Pallas kernels: 149 us -> 142 us  [the longest x1 86.8 us: tail(): pl.pallas_call(tail_kernel, in_specs=[any_spec] * 3 + [vmem_spec] * 2 + [...]
    unnamed x56 -> x13, local copies, waits for them, and re-layouts: 10.9 us -> 3.99 us
    squeeze x2 -> x0, local copies, waits for them, and re-layouts: 3.62 us -> none  [the longest x1 2.82 us: per_device_paired(): early[other]]
    concatenate x6 -> x0, other arithmetic: 3.48 us -> none  [the longest x3 2.5 us: both_halves(): jnp.concatenate([joined[0, :, first:first + width], joined[1, :, first:fi...]
  transfers between devices with their start and end apart: 6 -> 6, of which waited for: 0 -> 0; matrix products, arithmetic and copies ran while one was open for 3% -> 0% of each run, Pallas kernels for 21% -> 52%
where the time goes in v5:
time: 300 us
  Pallas kernels  276 us (92%)
  between operations  14.2 us (5%)
  starting transfers between devices  5.71 us (2%)
  local copies, waits for them, and re-layouts  3.99 us (1%)
    pallas_call x1, Pallas kernels, tail(): pl.pallas_call(tail_kernel, in_specs=[any_spec] * 3 + [vmem_spec] * 2 + [...  86.8 us
    pallas_call x1, Pallas kernels, middle(): pl.pallas_call(middle_kernel, in_specs=[pl.BlockSpec(memory_space=pl.ANY)...  65 us
    pallas_call x1, Pallas kernels, start(): pl.pallas_call(start_kernel, in_specs=[smem_spec] * 2 + [vmem_spec] * 10,...  49.2 us
    pallas_call x1, Pallas kernels, attend_back(): pl.pallas_call(attend_back_kernel, grid_spec=pltpu.PrefetchScalarGridSpec...  39.6 us
    pallas_call x1, Pallas kernels, attend(): pl.pallas_call(attend_kernel, grid_spec=pltpu.PrefetchScalarGridSpec(num_...  29.4 us
  transfers between devices with their start and end apart: 6, of which 0 were waited for; matrix products, arithmetic and copies ran while one was open for 0% of the time, Pallas kernels for 52%

profile of v5, /device:TPU:0, one launch (start us, length us, event | category | flops | bytes accessed | tf_op | source)
XLA Modules:
  0.0 300.2 jit_solution(14450867432509357623)
XLA Ops:
  7.2 0.0 all-reduce.2.cloned.1.call-start
  7.2 0.5 compare_select_fusion.slopes.slope_ref
  7.8 49.2 %start.1 = (bf16[4,2,256,768]{3,2,1,0:T(8,128)(2,1)}, bf16[4,192,576]{2,1,0:T(8,128)(2,1)}, bf16[4,192,384]{2,1,0:T(8,128)(2,1)}, bf16[4,192,1536]{2,1,0:T(8,128...) custom-call(s32[2,8]{1,0:T(2,128)} %docs_ref.3, ...), custom_call_target="tpu_custom_call" | custom-call | flops 42949672960 | bytes 16777216 | tf_op jit(solution)/shard_map/start/pallas_call | solution.py:734
  57.0 0.6 collective-permute-start.1
  57.6 1.5 collective-permute-start
  59.1 29.4 %attend.1 = (bf16[2048,192]{1,0:T(8,128)(2,1)}, f32[3,64,2048]{2,1,0:T(8,128)}, f32[3,1,2048]{2,1,0:T(1,128)}) custom-call(s32[2,8]{1,0:T(2,128)} %docs_ref.3, f32[3]{0:T(128)} %compare_select_fusion.slopes.slope_ref, bf16[3,128,2048]{2,1,0:T(8,128)(2,1)} %get-tuple-element.62.qt_ref, bf16[3,2048,128]{2,1,0:T(8,128)(2,1)} %get-tuple-element.63.k_ref, ...), custom_call_target="tpu_custom_call" | custom-call | flops 3221225472 | bytes 6291456 | tf_op jit(solution)/shard_map/attend/pallas_call | solution.py:814
  88.5 0.0 collective-permute-done.1.up_2
  88.5 0.0 copy-start.1
  88.5 0.0 collective-permute-done.up_1
  88.5 0.0 copy-start.2
  88.5 1.0 copy-done.1
  89.5 0.4 copy-done.2
  89.9 65.0 %middle.1 = (bf16[2,2,256,768]{3,2,1,0:T(8,128)(2,1)}, f32[4,256,768]{2,1,0:T(8,128)}, bf16[8,256,192]{2,1,0:T(8,128)(2,1)}, bf16[192,2304]{1,0:T(8,128)(2,1)}, ...) custom-call(bf16[8,256,192]{2,1,0:T(8,128)(2,1)} %bitcast.24, ...), custom_call_target="tpu_custom_call" | custom-call | flops 53687091200 | bytes 33554432 | tf_op jit(solution)/shard_map/middle/pallas_call | solution.py:1407
  154.9 1.6 collective-permute-start.2
  156.4 0.5 collective-permute-start.3
  157.0 1.5 collective-permute-start.4
  158.4 0.0 all-reduce.2.cloned.1.call-update
  158.5 39.6 %attend_back.1 = (bf16[2048,192]{1,0:T(8,128)(2,1)}, bf16[2048,192]{1,0:T(8,128)(2,1)}, bf16[2048,192]{1,0:T(8,128)(2,1)}) custom-call(s32[2,8]{1,0:T(2,128)} %docs_ref.3, f32[3]{0:T(128)} %compare_select_fusion.slopes.slope_ref, bf16[3,128,2048]{2,1,0:T(8,128)(2,1)} %get-tuple-element.62.qt_ref, bf16[3,2048,64]{2,1,0:T(8,128)(2,1)} %get-tuple-element.71.q_ref, ...), custom_call_target="tpu_custom_call" | custom-call | flops 8053063680 | bytes 12582912 | tf_op jit(solution)/shard_map/attend_back/pallas_call | solution.py:954
  198.0 0.0 collective-permute-done.2.moved_1
  198.1 0.0 copy-start.3
  198.1 0.0 collective-permute-done.3.moved_2
  198.1 0.0 copy-start.4
  198.1 0.0 collective-permute-done.4.moved_3
  198.1 0.0 copy-start.5
  198.1 0.9 copy-done.3
  199.0 0.3 copy-done.4
  199.3 0.3 copy-done.5
  199.6 86.8 %tail.1 = (bf16[2,2,256,768]{3,2,1,0:T(8,128)(2,1)}, bf16[192,3456]{1,0:T(8,128)(2,1)}, bf16[2,192,576]{2,1,0:T(8,128)(2,1)}, f32[8,768]{1,0:T(8,128)}) custom-call(bf16[8,256,192]{2,1,0:T(8,128)(2,1)} %bitcast.21, bf16[8,256,192]{2,1,0:T(8,128)(2,1)} %bitcast.22, bf16[8,256,192]{2,1,0:T(8,128)(2,1)} %bitcast.23, bf16[768,576]{1,0:T(8,128)(2,1)} %bitcast.25, ...), custom_call_target="tpu_custom_call" | custom-call | flops 85899345920 | bytes 33554432 | tf_op jit(solution)/shard_map/tail/pallas_call | solution.py:1793
  286.4 0.0 all-reduce.2.cloned.1.call-done.down_ref
  286.4 0.0 copy-start
  286.4 5.7 %finish.1 = (f32[1024,768]{1,0:T(8,128)}, f32[192,384]{1,0:T(8,128)}, f32[192,384]{1,0:T(8,128)}, f32[192,384]{1,0:T(8,128)}, f32[192,384]{1,0:T(8,128)}, /*inde...) custom-call(bf16[1024,768]{1,0:T(8,128)(2,1)} %bitcast.14, ...), custom_call_target="tpu_custom_call" | custom-call | tf_op jit(solution)/shard_map/finish/pallas_call | solution.py:1864
  292.2 0.0 copy-done
  292.2 1.1 copy.36
Async XLA Ops:
  7.2 279.2 %all-reduce.2.cloned.1.call-start = ((), (), s32[]{:S(2)}) async-start(), calls=%async_computation | async-start | bytes 1179648 | tf_op jit(solution)/shard_map/psum | solution.py:1970
  57.0 31.5 %collective-permute-start.1 = (bf16[192,3072]{1,0:T(8,128)(2,1)}, bf16[192,3072]{1,0:T(8,128)(2,1)S(1)}, u32[]{:S(2)}, u32[]{:S(2)}) collective-permute-start(bf16[192,3072]{1,0:T(8,128)(2,1)} %get-tuple-element.69.up_0), channel_id=1, source_target_pairs={{0,16},{16,0},{8,24},{24,8},{1,17},{17,1},{9,25},{25,9},{2,18},{18... | collective-permute-start | bytes 3538952 | tf_op jit(solution)/shard_map/ppermute | solution.py:1931
  57.6 30.9 %collective-permute-start = (bf16[192,3072]{1,0:T(8,128)(2,1)}, bf16[192,3072]{1,0:T(8,128)(2,1)S(1)}, u32[]{:S(2)}, u32[]{:S(2)}) collective-permute-start(bf16[192,3072]{1,0:T(8,128)(2,1)} %get-tuple-element.69.up_0), channel_id=1, source_target_pairs={{0,8},{8,0},{16,24},{24,16},{1,9},{9,1},{17,25},{25,17},{2,10},{10... | collective-permute-start | bytes 3538952 | tf_op jit(solution)/shard_map/ppermute | solution.py:1931
  88.5 1.0 copy-start.1
  88.5 1.4 copy-start.2
  154.9 43.2 %collective-permute-start.2 = (bf16[192,2304]{1,0:T(8,128)(2,1)}, bf16[192,2304]{1,0:T(8,128)(2,1)S(1)}, u32[]{:S(2)}, u32[]{:S(2)}) collective-permute-start(bf16[192,2304]{1,0:T(8,128)(2,1)} %get-tuple-element.85), channel_id=1, source_target_pairs={{0,8},{8,0},{16,24},{24,16},{1,9},{9,1},{17,25},{25,17},{2,10},{10... | collective-permute-start | bytes 2654216 | tf_op jit(solution)/shard_map/ppermute | solution.py:1947
  156.4 41.6 %collective-permute-start.3 = (bf16[192,2304]{1,0:T(8,128)(2,1)}, bf16[192,2304]{1,0:T(8,128)(2,1)S(1)}, u32[]{:S(2)}, u32[]{:S(2)}) collective-permute-start(bf16[192,2304]{1,0:T(8,128)(2,1)} %get-tuple-element.86), channel_id=1, source_target_pairs={{0,16},{16,0},{8,24},{24,8},{1,17},{17,1},{9,25},{25,9},{2,18},{18... | collective-permute-start | bytes 2654216 | tf_op jit(solution)/shard_map/ppermute | solution.py:1947
  157.0 41.1 %collective-permute-start.4 = (bf16[192,2304]{1,0:T(8,128)(2,1)}, bf16[192,2304]{1,0:T(8,128)(2,1)S(1)}, u32[]{:S(2)}, u32[]{:S(2)}) collective-permute-start(bf16[192,2304]{1,0:T(8,128)(2,1)} %get-tuple-element.87), channel_id=1, source_target_pairs={{0,24},{24,0},{8,16},{16,8},{1,25},{25,1},{9,17},{17,9},{2,26},{26... | collective-permute-start | bytes 2654216 | tf_op jit(solution)/shard_map/ppermute | solution.py:1947
  198.1 0.9 copy-start.3
  198.1 1.2 copy-start.4
  198.1 1.5 copy-start.5
  286.4 5.8 %copy-start = (bf16[2,2,256,768]{3,2,1,0:T(8,128)(2,1)S(1)}, bf16[2,2,256,768]{3,2,1,0:T(8,128)(2,1)}, u32[]{:S(2)}) copy-start(bf16[2,2,256,768]{3,2,1,0:T(8,128)(2,1)} %get-tuple-element.70) | copy-start | bytes 4718596
Sparse Core Ops, SparseCore 0:
  158.6 37.3 all-reduce.1

commit v6 on v5

--- a/solution.py
+++ b/solution.py
@@ -413,12 +413,17 @@
     return after, same, bare
 
 
-def diagonal_scores(keys, query_t, same, bare, slope):
+def diagonal_scores(keys, queries_t, same, bare, slopes):
     rows = lax.broadcasted_iota(jnp.int32, (TILE, TILE), 0)
     cols = lax.broadcasted_iota(jnp.int32, (TILE, TILE), 1)
-    apart = jnp.abs(rows - cols)
-    full = dot(keys, query_t * same) - slope * apart.astype(jnp.float32)
-    return jnp.where(apart == 0, dot(keys, query_t * bare), full)
+    apart = jnp.abs(rows - cols).astype(jnp.float32)
+    own = rows == cols
+    full = [dot(key, query_t * same) for key, query_t in zip(keys, queries_t)]
+    alone = [dot(key, query_t * bare) for key, query_t in zip(keys, queries_t)]
+    return [
+        jnp.where(own, single, scores - slope * apart)
+        for scores, single, slope in zip(full, alone, slopes)
+    ]
 
 
 def sweep(first, last, step, most=2):
@@ -452,11 +457,11 @@
 
 
 def start_kernel(
-    docs, slopes, tokens, keep, w_query, w_key, w_value, w_out, w_down, b_query, b_value, w_up,
-    sequence, full_joined, full_out, full_down, up_flat, query_t, queries, keys, keys_t, values, values_t,
-    tokens_v, own_v, joined_v, keep_v, up_v, qt_v, q_v, k_v, kt_v, v_v, vt_v,
-    z_send, z_recv, tp_send, tp_recv, w_send, w_recv, down_send, down_recv, keep_send, keep_recv, local_sem,
-    block_sem, joined_sem, up_sem, out_sem,
+    docs, slopes, tokens, keep, w_query, w_key, w_value, w_out, w_up, b_query, b_value, cotangent,
+    sequence, full_joined, full_out, full_gate, up_lift, cot_far, cot_near, query_t, queries, keys, keys_t, values, values_t,
+    tokens_v, own_v, joined_v, keep_v, gate_v, lift_v, qt_v, q_v, k_v, kt_v, v_v, vt_v,
+    z_send, z_recv, tp_send, tp_recv, w_send, w_recv, gate_send, gate_recv, keep_send, keep_recv, local_sem,
+    block_sem, joined_sem, lift_sem, gate_sem, cot_sem, out_sem,
 ):
     place, stage, core = lax.axis_index("fsdp"), lax.axis_index("ctx"), lax.axis_index("tp")
     seq, half = stage // 2, stage % 2
@@ -491,6 +496,7 @@
     other_core = (place, stage, 1 - core)
     inner = (stage == 1) | (stage == 2)
     facing, opposite = 3 - stage, stage ^ 2
+    third, fourth = jnp.where(inner, facing, opposite), jnp.where(inner, opposite, facing)
 
     def send(source, block, target, slot):
         return remote(source, tokens_v.at[block, core], z_send.at[slot], z_recv.at[block], (place, target, core))
@@ -503,14 +509,12 @@
         return remote(half_block, half_block, tp_send.at[block], tp_recv.at[block], other_core)
 
     to_pair = send(ours, stage, stage ^ 1, 0)
-    to_facing = send(theirs, stage, facing, 1)
-    to_opposite = send(theirs, stage, opposite, 2)
-    to_facing.start()
+    to_across = send(theirs, stage, third, 1)
     to_pair.start()
 
-    @pl.when(~inner)
+    @pl.when(inner)
     def _():
-        to_opposite.start()
+        to_across.start()
 
     weights = [
         remote(
@@ -532,37 +536,36 @@
         for other in (1, 2, 3)
     ]
 
-    units = w_down.shape[1] // 2
-
-    def down_copy(owner, other, which, sem):
-        columns = pl.ds(which * units, units)
-        source = w_down if owner is place else full_down.at[owner]
-        return remote(
-            source.at[:, columns], full_down.at[owner, :, columns], down_send.at[sem], down_recv.at[sem],
-            (place ^ other, stage, core),
-        )
+    units = w_up.shape[2] // 2
+
+    def gate_copy(owner, other, which, sem):
+        block = gate_v.at[owner, :, pl.ds(which * units, units)]
+        return remote(block, block, gate_send.at[sem], gate_recv.at[sem], (place ^ other, stage, core))
 
     halves = [
-        down_copy(place, other, which, 2 * which + other - 1)
+        gate_copy(place, other, which, 2 * which + other - 1)
         for other, which in ((1, 0), (2, 1), (1, 1), (2, 0))
     ]
-    on = [down_copy(place ^ 1, 2, 0, 4), down_copy(place ^ 2, 1, 1, 5)]
-    for copy in weights + flags + outs + halves:
+    on = [gate_copy(place ^ 1, 2, 0, 4), gate_copy(place ^ 2, 1, 1, 5)]
+    for copy in weights + flags + outs:
         copy.start()
-    local = [
-        pltpu.make_async_copy(w_out, full_out.at[place], local_sem.at[0]),
-        pltpu.make_async_copy(w_down, full_down.at[place], local_sem.at[1]),
+    gate_v[place] = w_up[:, 0, :]
+    for copy in halves:
+        copy.start()
+    lift_v[...] = w_up[:, 1, :]
+    lift_out = pltpu.make_async_copy(lift_v, up_lift, lift_sem)
+    lift_out.start()
+    own_out = pltpu.make_async_copy(w_out, full_out.at[place], local_sem)
+    own_out.start()
+    odd = stage % 2
+    cot_outs = [
+        pltpu.make_async_copy(cotangent.at[1 - odd, core], cot_far, cot_sem.at[0]),
+        pltpu.make_async_copy(cotangent.at[odd, core], cot_near, cot_sem.at[1]),
     ]
-    for copy in local:
+    for copy in cot_outs:
         copy.start()
 
-    for part in (0, 1):
-        up_v[:, pl.ds(part * w_up.shape[2], w_up.shape[2])] = w_up[:, part, :]
-    up_out = pltpu.make_async_copy(up_v, up_flat, up_sem)
-    up_out.start()
-
     bounds = doc_bounds(docs, seq)
-    third, fourth = 3 - stage, 3 - (stage ^ 1)
 
     def out_copies(slot, block):
         at = pl.ds(pl.multiple_of(block * rows_of, rows_of), rows_of)
@@ -652,6 +655,11 @@
     joined_out = pltpu.make_async_copy(joined_v, full_joined, joined_sem)
     joined_out.start()
 
+    @pl.when(~inner)
+    def _():
+        to_pair.wait_send()
+        to_across.start()
+
     @pl.loop(0, 4)
     def _(i):
         pair = stage ^ 1
@@ -676,6 +684,11 @@
         @pl.when(i == 3)
         def _():
             arrival(fourth).wait_recv()
+
+            @pl.when(inner)
+            def _():
+                send(tokens_v.at[fourth, core], fourth, pair, 3).start()
+
             share(fourth, core).start()
 
         @pl.when(i >= 1)
@@ -692,16 +705,26 @@
         for copy in out_copies(slot, block):
             copy.start()
 
-    to_pair.wait_send()
-    to_facing.wait_send()
-    to_opposite.wait_send()
+    @pl.when(inner)
+    def _():
+        to_pair.wait_send()
+
+    to_across.wait_send()
+
+    @pl.when(inner)
+    def _():
+        for block, slot in ((third, 2), (fourth, 3)):
+            send(tokens_v.at[block, core], block, stage ^ 1, slot).wait_send()
+
     for block in (stage ^ 1, third, fourth):
         share(block, core).wait_send()
     for copy in outs + halves[2:] + on:
         copy.wait()
+    gate_out = pltpu.make_async_copy(gate_v, full_gate, gate_sem)
+    gate_out.start()
     for copy in weights + flags + halves[:2]:
         copy.wait_send()
-    for copy in local + [joined_out, up_out]:
+    for copy in [own_out, joined_out, lift_out, gate_out] + cot_outs:
         copy.wait()
     for block in range(4):
         sequence_copy(block).wait()
@@ -710,7 +733,7 @@
             copy.wait()
 
 
-def start(docs, slopes, tokens, keep, w_query, w_key, w_value, w_out, w_down, b_query, b_value, w_up):
+def start(docs, slopes, tokens, keep, w_query, w_key, w_value, w_out, w_up, b_query, b_value, cotangent):
     _, block_rows, model_width = tokens.shape
     heads = slopes.shape[0]
     width, length = heads * HEAD, 4 * block_rows
@@ -734,15 +757,17 @@
     return pl.pallas_call(
         start_kernel,
         in_specs=[smem_spec] * 2 + [vmem_spec] * 10,
-        out_specs=[any_spec] * 11,
+        out_specs=[any_spec] * 13,
         out_shape=[
             jax.ShapeDtypeStruct(shape, bf16)
             for shape in [
                 (4, 2, half_rows, model_width),
                 (4, quarter, 3 * width),
                 (4,) + w_out.shape,
-                (4,) + w_down.shape,
-                (quarter, 2 * w_up.shape[2]),
+                (4, quarter, w_up.shape[2]),
+                (quarter, w_up.shape[2]),
+                (half_rows, model_width),
+                (half_rows, model_width),
             ]
             + parts(length)
         ],
@@ -751,16 +776,17 @@
             pltpu.VMEM((quarter, 3 * width), bf16),
             pltpu.VMEM((4, quarter, 3 * width), bf16),
             pltpu.VMEM((4,) + keep.shape, keep.dtype),
-            pltpu.VMEM((quarter, 2 * w_up.shape[2]), bf16),
+            pltpu.VMEM((4, quarter, w_up.shape[2]), bf16),
+            pltpu.VMEM((quarter, w_up.shape[2]), bf16),
             *[pltpu.VMEM((2,) + shape, bf16) for shape in parts(block_rows)],
-            three, four, four, four, six, six, six, six, three, three, dma((2,)), dma((2, 6)), dma, dma, four,
+            four, four, four, four, six, six, six, six, three, three, dma, dma((2, 6)), dma, dma, dma, dma((2,)), four,
         ],
         compiler_params=pltpu.CompilerParams(
             collective_id=0, has_side_effects=True, vmem_limit_bytes=VMEM_BYTES
         ),
         cost_estimate=pl.CostEstimate(flops=40 << 30, bytes_accessed=16 << 20, transcendentals=0),
         name="start",
-    )(docs, slopes, tokens, keep, w_query, w_key, w_value, w_out, w_down, b_query, b_value, w_up)
+    )(docs, slopes, tokens, keep, w_query, w_key, w_value, w_out, w_up, b_query, b_value, cotangent)
 
 
 def attend_kernel(docs_ref, slope_ref, qt_ref, k_ref, vt_ref, o_ref, ot_ref, lse_ref, max_ref, acc_ref):
@@ -773,12 +799,17 @@
         return pl.ds(pl.multiple_of(tile * TILE, TILE), count * TILE)
 
     own = tile_rows(block)
-    for head in range(heads):
-        scores = diagonal_scores(k_ref[head, own, :], qt_ref[head], same, bare, slope_ref[head])
-        top = jnp.max(scores, 0, keepdims=True)
-        weights = jnp.exp(scores - top).astype(jnp.bfloat16)
-        max_ref[head] = top
-        acc_ref[head] = dot(vt_ref[head, :, own], weights)
+    each = range(heads)
+    scores = diagonal_scores(
+        [k_ref[head, own, :] for head in each], [qt_ref[head] for head in each], same, bare,
+        [slope_ref[head] for head in each],
+    )
+    tops = [jnp.max(scores[head], 0, keepdims=True) for head in each]
+    weights = [jnp.exp(scores[head] - tops[head]).astype(jnp.bfloat16) for head in each]
+    parts = [dot(vt_ref[head, :, own], weights[head]) for head in each]
+    for head in each:
+        max_ref[head] = tops[head]
+        acc_ref[head] = parts[head]
 
     def step(tile, count, sign):
         each = range(heads)
@@ -914,10 +945,10 @@
     own = [qt_log[head, :, tile_rows(block)] for head in range(heads)]
     accumulate(
         block,
-        [
-            diagonal_scores(k_ref[head], own[head], same, bare, slope_ref[head])
-            for head in range(heads)
-        ],
+        diagonal_scores(
+            [k_ref[head] for head in range(heads)], own, same, bare,
+            [slope_ref[head] for head in range(heads)],
+        ),
         True,
     )
     after_wide = side_signs(2 * TILE)[0]
@@ -1003,7 +1034,7 @@
 
 
 def middle_kernel(
-    attended, sequence, cotangent, w_out, w_down, up_0, up_1, up_2, *rest,
+    attended, sequence, cotangent, cot_far, cot_near, w_out, gate_full, w_down, lift_0, lift_1, lift_2, lift_3, *rest,
 ):
     vectors, rest = rest[:6], rest[6:]
     (
@@ -1011,9 +1042,9 @@
         token_v, mine_v, theirs_v, both_v, cot_v, out_w, down_w, up_w,
         send_a, recv_a, send_b, recv_b, send_c, recv_c,
         normed_v, inv_v, low_v, hidden_v, gate_v, lift_v, grad_v, ffn_v, att_v, result_v, keep_v, away_v, tile_v,
-        down_v, down_got, load_sem, far_send, far_recv, pair_send, pair_recv, cot_send, cot_recv, cot_pass, cot_took,
+        down_v, down_got, home_v, load_sem, near_send, near_recv, pair_send, pair_recv, cot_send, cot_pass, cot_took,
         a_send, a_recv, b_send, b_recv, c_send, c_recv, out_send, out_recv, out_pass, out_took,
-        one_sem, keep_sem, away_send, away_recv, tile_sem, down_send, down_recv, down_sem,
+        one_sem, keep_sem, away_send, away_recv, tile_sem, down_send, down_recv, down_sem, home_sem,
     ) = rest
     place, stage, core = lax.axis_index("fsdp"), lax.axis_index("ctx"), lax.axis_index("tp")
     seq, half = stage // 2, stage % 2
@@ -1021,7 +1052,7 @@
     chunks = token_v.shape[0]
     units = hidden_v.shape[2]
     wide = 512
-    quarter = up_0.shape[0]
+    quarter = lift_0.shape[0]
 
     barrier = pltpu.get_barrier_semaphore()
     peers = [(place ^ other, stage, core) for other in (1, 2, 3)]
@@ -1047,44 +1078,41 @@
     for c in range(chunks):
         pair_copy(c).start()
 
-    def far_copy(which):
-        source, over = ((up_1, 2), (up_2, 1))[which]
-        columns = pl.ds(which * units, units)
-        rows = pl.ds(pl.multiple_of((place ^ 3 ^ over) * quarter, quarter), quarter)
-        return remote(
-            source.at[:, columns], up_w.at[rows, columns], far_send.at[which], far_recv.at[which],
-            (place ^ over, stage, core),
-        )
-
-    for which in (0, 1):
-        far_copy(which).start()
+    def rows_of(owner):
+        return pl.ds(pl.multiple_of(owner * quarter, quarter), quarter)
+
+    def near_copy(owner, other, which, sem):
+        columns = pl.ds(which * (units // 2), units // 2)
+        block = down_w.at[rows_of(owner), columns]
+        source = w_down.at[:, columns] if owner is place else block
+        return remote(source, block, near_send.at[sem], near_recv.at[sem], (place ^ other, stage, core))
+
+    halves = [
+        near_copy(place, other, which, 2 * which + other - 1)
+        for other, which in ((1, 0), (2, 1), (1, 1), (2, 0))
+    ]
+    on = [near_copy(place ^ 1, 2, 0, 4), near_copy(place ^ 2, 1, 1, 5)]
+    for copy in halves:
+        copy.start()
 
     def cot_owner(which):
         return 2 * which + stage // 2
 
-    def cot_copy(which):
-        return remote(
-            cotangent.at[which, core], cot_v.at[stage % 2, core],
-            cot_send.at[which], cot_recv.at[stage % 2], (place, cot_owner(which), core),
-        )
-
-    def cot_local(which):
-        return pltpu.make_async_copy(cotangent.at[which], cot_v.at[stage % 2], cot_send.at[which])
-
-    for which in (0, 1):
-
-        @pl.when(cot_owner(which) == stage)
-        def _():
-            cot_local(which).start()
-
-        @pl.when(cot_owner(which) != stage)
-        def _():
-            cot_copy(which).start()
-
-    def cot_arrival(block):
-        return remote(
-            cot_v.at[block, core], cot_v.at[block, core], cot_pass.at[block], cot_recv.at[block], other_core
-        )
+    near_block = jnp.where(stage < 2, 0, 1)
+    far_block = 1 - near_block
+    facing = (stage == 1) | (stage == 2)
+    far_load = pltpu.make_async_copy(cot_far, cot_v.at[far_block, core], cot_send.at[0])
+    near_load = pltpu.make_async_copy(cot_near, cot_v.at[near_block, core], cot_send.at[1])
+    own_load = pltpu.make_async_copy(cotangent.at[stage // 2], cot_v.at[near_block], cot_send.at[1])
+    far_load.start()
+
+    @pl.when(facing)
+    def _():
+        near_load.start()
+
+    @pl.when(~facing)
+    def _():
+        own_load.start()
 
     def cot_share(block, whose):
         return remote(
@@ -1095,11 +1123,12 @@
         pltpu.make_async_copy(attended.at[pl.ds(half * chunks, chunks)], mine_v, load_sem.at[0]),
         pltpu.make_async_copy(w_out, out_w, load_sem.at[1]),
         pltpu.make_async_copy(sequence.at[pl.ds(half * chunks, chunks)], token_v, load_sem.at[2]),
-        pltpu.make_async_copy(w_down, down_w, load_sem.at[3]),
+        pltpu.make_async_copy(w_down, down_w.at[rows_of(place)], load_sem.at[3]),
+        pltpu.make_async_copy(gate_full, up_w.at[:, pl.ds(0, units)], load_sem.at[4]),
     ]
-    for other, shard in enumerate((up_0, up_1, up_2)):
-        rows = pl.ds(pl.multiple_of((place ^ other) * quarter, quarter), quarter)
-        loads.append(pltpu.make_async_copy(shard, up_w.at[rows], load_sem.at[4 + other]))
+    for other, shard in enumerate((lift_0, lift_1, lift_2, lift_3)):
+        target = up_w.at[rows_of(place ^ other), pl.ds(units, units)]
+        loads.append(pltpu.make_async_copy(shard, target, load_sem.at[5 + other]))
     for load in loads:
         load.start()
 
@@ -1118,8 +1147,7 @@
     loads[0].wait()
     loads[1].wait()
 
-    @pl.loop(0, chunks)
-    def _(c):
+    def attention_branch(c):
         pair_copy(c).wait_recv()
         first, second = mine_v[c], theirs_v[c]
         both = jnp.where(
@@ -1129,23 +1157,34 @@
         send_a[c] = dot(both, out_w[...], ((1,), (1,))).astype(jnp.bfloat16)
         exchange(c, send_a, recv_a, a_send, a_recv).start()
 
+    attention_branch(0)
+    far_load.wait()
+    cot_share(far_block, core).start()
+
+    @pl.when(facing)
+    def _():
+        near_load.wait()
+        cot_share(near_block, core).start()
+
+    @pl.when(~facing)
+    def _():
+        own_load.wait()
+
     for load in loads[2:]:
         load.wait()
-    for which in (0, 1):
-        far_copy(which).wait_recv()
-
     @pl.loop(0, chunks)
     def _(c):
+        @pl.when(c + 1 < chunks)
+        def _():
+            attention_branch(c + 1)
+
+        @pl.when(c == 1)
+        def _():
+            for near, far in zip(halves[:2], on):
+                near.wait_recv()
+                far.start()
+
         exchange(c, send_a, recv_a, a_send, a_recv).wait_recv()
-
-        @pl.when(c == chunks - 1)
-        def _():
-            for block in (0, 1):
-
-                @pl.when(2 * half + block != stage)
-                def _():
-                    cot_arrival(block).wait_recv()
-                    cot_share(block, core).start()
 
         residual = token_v[c].astype(jnp.float32) + (total(c, send_a, recv_a) + b_out)
         normed, inv_scale = rows_norm(residual)
@@ -1161,32 +1200,28 @@
             hidden_v[c, :, n : n + wide] = (gelu * lift).astype(jnp.bfloat16)
             gate_v[c, :, n : n + wide] = (lift * (chance + gate * density)).astype(jnp.bfloat16)
             lift_v[c, :, n : n + wide] = gelu.astype(jnp.bfloat16)
+
+    for copy in halves[2:] + on:
+        copy.wait_recv()
+    @pl.loop(0, chunks)
+    def _(c):
         send_b[c] = dot(hidden_v[c], down_w[...], ((1,), (1,))).astype(jnp.bfloat16)
         exchange(c, send_b, recv_b, b_send, b_recv).start()
 
-    for block in (0, 1):
-
-        @pl.when(2 * half + block != stage)
-        def _():
-            cot_share(block, core).wait_send()
-            cot_share(block, 1 - core).wait_recv()
-
-    for which in (0, 1):
-
-        @pl.when(cot_owner(which) == stage)
-        def _():
-            cot_local(which).wait()
-
-        @pl.when(cot_owner(which) != stage)
-        def _():
-            cot_copy(which).wait_send()
+    cot_share(far_block, core).wait_send()
+    cot_share(far_block, 1 - core).wait_recv()
+
+    @pl.when(facing)
+    def _():
+        cot_share(near_block, core).wait_send()
+        cot_share(near_block, 1 - core).wait_recv()
 
     def home(c):
         return 2 * half + c // 2
 
     def out_copy(c):
         return remote(
-            result_v.at[c], out_home.at[seq, core], out_send.at[c], out_recv.at[seq], (place, home(c), core)
+            result_v.at[c], home_v.at[seq], out_send.at[c], out_recv.at[seq], (place, home(c), core)
         )
 
     def out_local(c):
@@ -1341,13 +1376,16 @@
 
     def out_arrival(which):
         return remote(
-            out_home.at[which, core], out_home.at[which, core], out_pass.at[which], out_recv.at[which], other_core
+            home_v.at[which], home_v.at[which], out_pass.at[which], out_recv.at[which], other_core
         )
 
     def out_share(which, whose):
         return remote(
-            out_home.at[which, whose], out_home.at[which, whose], out_pass.at[which], out_took.at[which], other_core
-        )
+            home_v.at[which], out_home.at[which, whose], out_pass.at[which], out_took.at[which], other_core
+        )
+
+    def out_here(which):
+        return pltpu.make_async_copy(home_v.at[which], out_home.at[which, core], home_sem.at[which])
 
     for which in (0, 1):
 
@@ -1355,10 +1393,11 @@
         def _():
             out_arrival(which).wait_recv()
             out_share(which, core).start()
+            out_here(which).start()
 
     down_out.wait()
-    for which in (0, 1):
-        far_copy(which).wait_send()
+    for copy in halves + on:
+        copy.wait_send()
     for i in range(unit_tiles):
         for other in (1, 2, 3):
             down_copy(i, other).wait_send()
@@ -1388,9 +1427,10 @@
         def _():
             out_share(which, core).wait_send()
             out_share(which, 1 - core).wait_recv()
-
-
-def middle(attended, sequence, cotangent, w_out, w_down, up_shards, vectors):
+            out_here(which).wait()
+
+
+def middle(attended, sequence, cotangents, w_out, w_gate, w_down, lift_shards, vectors):
     chunks, rows, width = 4, sequence.shape[1], sequence.shape[2]
     head_width, units = w_out.shape[1], w_down.shape[1]
     tile = head_width
@@ -1406,7 +1446,7 @@
     four, two = dma((chunks,)), dma((2,))
     return pl.pallas_call(
         middle_kernel,
-        in_specs=[pl.BlockSpec(memory_space=pl.ANY)] * 8 + [pl.BlockSpec(memory_space=pltpu.VMEM)] * 6,
+        in_specs=[pl.BlockSpec(memory_space=pl.ANY)] * 12 + [pl.BlockSpec(memory_space=pltpu.VMEM)] * 6,
         out_specs=[pl.BlockSpec(memory_space=pl.ANY)] * 9 + [pl.BlockSpec(memory_space=pltpu.VMEM)],
         out_shape=[
             jax.ShapeDtypeStruct((2, 2, rows, width), bf16),
@@ -1424,28 +1464,29 @@
             vmem(wide, f32), vmem((chunks, rows, 1), f32), vmem(wide),
             vmem(inner), vmem(inner), vmem(inner),
             vmem(wide, f32), vmem(wide), vmem(wide), vmem(wide), vmem(narrow_rows), vmem(narrow_rows),
-            vmem((2, width, tile)), vmem((width, units)), vmem((3, width // 4, units)),
-            dma((7,)), two, two, four, four, two, two, two, two,
+            vmem((2, width, tile)), vmem((width, units)), vmem((3, width // 4, units)), vmem((2, rows, width)),
+            dma((9,)), dma((6,)), dma((6,)), four, four, two, two, two,
             four, four, four, four, four, four, four, two, two, two,
-            four, four, four, four, dma((2, 4)), dma((units // tile, 3)), dma((units // tile, 3)), dma,
+            four, four, four, four, dma((2, 4)), dma((units // tile, 3)), dma((units // tile, 3)), dma, two,
         ],
         compiler_params=pltpu.CompilerParams(
             collective_id=1, has_side_effects=True, vmem_limit_bytes=VMEM_BYTES
         ),
         cost_estimate=pl.CostEstimate(flops=50 << 30, bytes_accessed=32 << 20, transcendentals=0),
         name="middle",
-    )(attended, sequence, cotangent, w_out, w_down, *up_shards, *vectors)
+    )(attended, sequence, *cotangents, w_out, w_gate, w_down, *lift_shards, *vectors)
 
 
 def tail_kernel(
     d_query, d_key, d_value, w_joined, sums_in, sequence, grad_one, early, late, moved_1, moved_2, moved_3,
-    home, shard, joined, sums,
+    down_own, down_in,
+    home, shard, joined, down, sums,
     query_v, key_v, value_v, token_v, one_v, part_v, late_v, project_v, own_v, tp_sent, tp_got, pair_sent, pair_got,
     final_v, summed_v, end_got, inner_v, mid_got, total_v, joined_v, quarter_got, both_sent, both_end, both_inner,
-    both_mid, both_total, step_v, step_got,
+    both_mid, both_total, step_v, step_got, home_v, down_v, down_inner, down_got, down_total,
     load_sem, late_send, late_recv, tp_send, tp_recv, pair_send, pair_recv, home_send, home_recv, home_pass,
     home_took, home_local, end_send, end_recv, mid_send, mid_recv, back_send, back_recv, shard_sem,
-    quarter_send, quarter_recv, both_send, both_recv, both_local, step_send, step_recv,
+    quarter_send, quarter_recv, both_send, both_recv, both_local, step_send, step_recv, home_sem, down_sem, down_mid_send, down_mid_recv, down_back_send, down_back_recv,
 ):
     place, stage, core = lax.axis_index("fsdp"), lax.axis_index("ctx"), lax.axis_index("tp")
     seq, half = stage // 2, stage % 2
@@ -1480,7 +1521,11 @@
             )
         )
     ]
-    for load in loads:
+    down_loads = [
+        pltpu.make_async_copy(source, down_v.at[index], down_sem.at[index])
+        for index, source in enumerate((down_own, down_in))
+    ]
+    for load in down_loads + loads:
         load.start()
     pl.semaphore_wait(barrier, len(peers))
 
@@ -1539,6 +1584,43 @@
         back_copy(j).start()
         shard_copy(j).start()
 
+    down_pieces = down_mid_send.shape[0]
+    down_size = down_v.shape[2] // down_pieces
+
+    def down_part(ref, j):
+        return ref.at[:, pl.ds(j * down_size, down_size)]
+
+    def down_mid(j):
+        return remote(
+            down_part(down_inner, j), down_part(down_got, j), down_mid_send.at[j], down_mid_recv.at[j], across
+        )
+
+    def down_back(j):
+        return remote(
+            down_part(down_total, j), down_part(down, j), down_back_send.at[j], down_back_recv.at[j], outward
+        )
+
+    def down_here(j):
+        return pltpu.make_async_copy(down_part(down_total, j), down_part(down, j), down_sem.at[j])
+
+    def down_from_mid(j):
+        down_mid(j).wait_recv()
+        part = slice(j * down_size, (j + 1) * down_size)
+        down_total[:, part] = (
+            down_inner[:, part].astype(f32) + down_got[:, part].astype(f32)
+        ).astype(bf16)
+        down_back(j).start()
+        down_here(j).start()
+
+    for load in down_loads:
+        load.wait()
+
+    @pl.when(~at_end)
+    def _():
+        down_inner[...] = (down_v[0].astype(f32) + down_v[1].astype(f32)).astype(bf16)
+        for j in range(down_pieces):
+            down_mid(j).start()
+
     for load in loads[:4]:
         load.wait()
     for j in range(early_pieces):
@@ -1578,6 +1660,11 @@
     def _():
         for j in range(early_pieces // 2):
             from_end(j)
+
+    @pl.when(~at_end)
+    def _():
+        for j in range(down_pieces):
+            down_from_mid(j)
 
     loads[8].wait()
     tokens = token_v[...].reshape(-1, token_v.shape[2])
@@ -1667,7 +1754,7 @@
 
     def home_copy(i):
         return remote(
-            final_v.at[i], home.at[seq, core], home_send.at[i], home_recv.at[seq], (place, 2 * half + i, core)
+            final_v.at[i], home_v.at[seq], home_send.at[i], home_recv.at[seq], (place, 2 * half + i, core)
         )
 
     def home_direct(i):
@@ -1714,13 +1801,16 @@
 
     def home_arrival(which):
         return remote(
-            home.at[which, core], home.at[which, core], home_pass.at[which], home_recv.at[which], other_core
+            home_v.at[which], home_v.at[which], home_pass.at[which], home_recv.at[which], other_core
         )
 
     def home_share(which, whose):
         return remote(
-            home.at[which, whose], home.at[which, whose], home_pass.at[which], home_took.at[which], other_core
-        )
+            home_v.at[which], home.at[which, whose], home_pass.at[which], home_took.at[which], other_core
+        )
+
+    def home_keep(which):
+        return pltpu.make_async_copy(home_v.at[which], home.at[which, core], home_sem.at[which])
 
     for which in (0, 1):
 
@@ -1728,6 +1818,7 @@
         def _():
             home_arrival(which).wait_recv()
             home_share(which, core).start()
+            home_keep(which).start()
 
     @pl.when(~at_end)
     def _():
@@ -1739,8 +1830,17 @@
         both_back_copy().wait_send()
         both_here().wait()
 
+    @pl.when(~at_end)
+    def _():
+        for j in range(down_pieces):
+            down_mid(j).wait_send()
+            down_back(j).wait_send()
+            down_here(j).wait()
+
     @pl.when(at_end)
     def _():
+        for j in range(down_pieces):
+            down_back(j).wait_recv()
         for j in range(pieces):
             end_copy(j).wait_send()
             back_copy(j).wait_recv()
@@ -1767,6 +1867,7 @@
         @pl.when(2 * which + stage // 2 != stage)
         def _():
             home_share(which, core).wait_send()
+            home_keep(which).wait()
 
         home_share(which, 1 - core).wait_recv()
     for other in (1, 2, 3):
@@ -1774,7 +1875,7 @@
         late_copy(other).wait_send()
 
 
-def tail(d_query, d_key, d_value, w_joined, sums, sequence, grad_one, early, late, moved):
+def tail(d_query, d_key, d_value, w_joined, sums, sequence, grad_one, early, late, moved, downs):
     rows, width = sequence.shape[1:]
     quarter = early.shape[0]
     joined = w_joined.shape[1]
@@ -1792,12 +1893,13 @@
     one, two, three, four, many = dma, dma((2,)), dma((3,)), dma((4,)), dma((pieces,))
     return pl.pallas_call(
         tail_kernel,
-        in_specs=[any_spec] * 3 + [vmem_spec] * 2 + [any_spec] * 7,
-        out_specs=[any_spec] * 3 + [vmem_spec],
+        in_specs=[any_spec] * 3 + [vmem_spec] * 2 + [any_spec] * 9,
+        out_specs=[any_spec] * 4 + [vmem_spec],
         out_shape=[
             jax.ShapeDtypeStruct((2, 2, rows, width), bf16),
             jax.ShapeDtypeStruct((quarter, columns), bf16),
             jax.ShapeDtypeStruct(both, bf16),
+            jax.ShapeDtypeStruct(downs[0].shape, bf16),
             jax.ShapeDtypeStruct(sums.shape, f32),
         ],
         scratch_shapes=[
@@ -1809,17 +1911,18 @@
             vmem(cut), vmem(cut), vmem(cut), vmem(cut), vmem(cut),
             vmem((width, joined)), vmem((3, quarter, joined)), vmem((quarter, joined)), vmem((quarter, joined)),
             vmem(both), vmem(both), vmem(both),
-            vmem((5,) + sums.shape, f32), vmem((4,) + sums.shape, f32),
+            vmem((5,) + sums.shape, f32), vmem((4,) + sums.shape, f32), vmem((2, rows, width)),
+            vmem((2,) + downs[0].shape), vmem(downs[0].shape), vmem(downs[0].shape), vmem(downs[0].shape),
             dma((10,)), three, three, four, four, two, two, two, two, two, two, one,
             many, many, many, many, many, many, many,
-            three, three, three, three, one, four, four,
+            three, three, three, three, one, four, four, two, two, two, two, two, two,
         ],
         compiler_params=pltpu.CompilerParams(
             collective_id=2, has_side_effects=True, vmem_limit_bytes=VMEM_BYTES
         ),
         cost_estimate=pl.CostEstimate(flops=80 << 30, bytes_accessed=32 << 20, transcendentals=0),
         name="tail",
-    )(d_query, d_key, d_value, w_joined, sums, sequence, grad_one, early, late, *moved)
+    )(d_query, d_key, d_value, w_joined, sums, sequence, grad_one, early, late, *moved, *downs)
 
 
 def pick(pair, index):
@@ -1916,29 +2019,38 @@
     local_heads = b_query.shape[0] // HEAD
     heads = local_heads // 2
     width = heads * HEAD
+    cotangent = cotangent.reshape(2, 2, half_rows, model_width)
     half = lax.axis_index("ctx") % 2
     core = lax.axis_index("tp")
     slopes = head_slopes(core * local_heads + half * heads, heads)
     (
-        sequence, full_joined, full_out, full_down, up_own, query_t, queries, keys, keys_t, values, values_t,
+        sequence, full_joined, full_out, full_gate, up_lift, cot_far, cot_near, query_t, queries, keys, keys_t, values, values_t,
     ) = start(
-        doc_lengths, slopes, tokens, keep, w_query, w_key, w_value, w_out, w_down,
-        b_query, b_value, w_up,
+        doc_lengths, slopes, tokens, keep, w_query, w_key, w_value, w_out, w_up, b_query, b_value,
+        cotangent,
     )
     full_joined = full_joined.reshape(model_width, 3 * width)
     full_out = full_out.reshape(model_width, 2 * width)
-    full_down = full_down.reshape(model_width, -1)
-    up_shards = [up_own] + [lax.ppermute(up_own, "fsdp", swap) for swap in (X_SWAP, Y_SWAP)]
+    full_gate = full_gate.reshape(model_width, -1)
+    lift_shards = [up_lift] + [
+        lax.ppermute(up_lift, "fsdp", swap) for swap in (X_SWAP, Y_SWAP, D_SWAP)
+    ]
+    cotangents = (
+        cotangent,
+        lax.ppermute(cot_far, "ctx", [(3, 1), (0, 2), (1, 0), (2, 3)]),
+        lax.ppermute(cot_near, "ctx", [(1, 2), (2, 1)]),
+    )
     attended_all, attended_t, lse = attend(doc_lengths, slopes, query_t, keys, values_t)
 
     vectors = (b_out, gain_one, shift_one, b_down, gain_two, shift_two)
     out, grad_one, grad_heads, *early, late, down_sum, sums = middle(
         attended_all.reshape(8, half_rows, width),
         sequence.reshape(8, half_rows, model_width),
-        cotangent.reshape(2, 2, half_rows, model_width),
+        cotangents,
         full_out,
-        full_down,
-        up_shards,
+        full_gate,
+        w_down,
+        lift_shards,
         vectors,
     )
     out = out.reshape(2, block_rows, model_width)
@@ -1947,10 +2059,11 @@
         lax.ppermute(early[other], "fsdp", swap)
         for other, swap in ((1, X_SWAP), (2, Y_SWAP), (3, D_SWAP))
     ]
+    downs = (down_sum, lax.ppermute(down_sum, "ctx", [(0, 1), (3, 2)]))
     d_query, d_key, d_value = attend_back(
         doc_lengths, slopes, query_t, queries, keys, keys_t, values, grad_heads, attended_t, lse
     )
-    d_tokens, shard, joined, sums = tail(
+    d_tokens, shard, joined, down, sums = tail(
         d_query.reshape(8, half_rows, width),
         d_key.reshape(8, half_rows, width),
         d_value.reshape(8, half_rows, width),
@@ -1961,13 +2074,14 @@
         early[0],
         late,
         moved,
+        downs,
     )
     (
         d_tokens, d_w_query, d_w_key, d_w_value, sum_out, sum_up, sum_down,
         total_gain_two, total_shift_two, total_b_down, total_gain_one, total_shift_one, total_b_out,
         total_b_query, total_b_value,
     ) = finish(
-        d_tokens.reshape(2 * block_rows, model_width), shard, joined, lax.psum(down_sum, "ctx"), sums
+        d_tokens.reshape(2 * block_rows, model_width), shard, joined, down, sums
     )
     d_tokens = d_tokens.reshape(2, block_rows, model_width)
     return (

time: 300 us -> 295 us (0.983)
  between operations: 14.2 us -> 0.86 us
  starting transfers between devices: 5.71 us -> 11 us
    ppermute x2 -> x6, starting transfers between devices: 2.12 us -> 7.48 us  [the longest x3 3.55 us: per_device_paired(): lax.ppermute(up_lift, 'fsdp', swap)]
    pallas_call x1, Pallas kernels: 86.8 us -> 90.7 us  [tail(): pl.pallas_call(tail_kernel, in_specs=[any_spec] * 3 + [vmem_spec] * 2 + [...]
  transfers between devices with their start and end apart: 6 -> 9, of which waited for: 0 -> 0; matrix products, arithmetic and copies ran while one was open for 0% -> 0% of each run, Pallas kernels for 52% -> 23%
where the time goes in v6:
time: 295 us
  Pallas kernels  278 us (94%)
  starting transfers between devices  11 us (4%)
  local copies, waits for them, and re-layouts  4.16 us (1%)
    pallas_call x1, Pallas kernels, tail(): pl.pallas_call(tail_kernel, in_specs=[any_spec] * 3 + [vmem_spec] * 2 + [...  90.7 us
    pallas_call x1, Pallas kernels, middle(): pl.pallas_call(middle_kernel, in_specs=[pl.BlockSpec(memory_space=pl.ANY)...  66.3 us
    pallas_call x1, Pallas kernels, start(): pl.pallas_call(start_kernel, in_specs=[smem_spec] * 2 + [vmem_spec] * 10,...  48.7 us
    pallas_call x1, Pallas kernels, attend_back(): pl.pallas_call(attend_back_kernel, grid_spec=pltpu.PrefetchScalarGridSpec...  39.7 us
    pallas_call x1, Pallas kernels, attend(): pl.pallas_call(attend_kernel, grid_spec=pltpu.PrefetchScalarGridSpec(num_...  27 us
  transfers between devices with their start and end apart: 9, of which 0 were waited for; matrix products, arithmetic and copies ran while one was open for 0% of the time, Pallas kernels for 23%

profile of v6, /device:TPU:0, one launch (start us, length us, event | category | flops | bytes accessed | tf_op | source)
XLA Modules:
  0.0 294.7 jit_solution(18082777322859892120)
XLA Ops:
  0.7 0.5 compare_select_fusion.slopes.slope_ref
  1.2 48.7 %start.1 = (bf16[4,2,256,768]{3,2,1,0:T(8,128)(2,1)}, bf16[4,192,576]{2,1,0:T(8,128)(2,1)}, bf16[4,192,384]{2,1,0:T(8,128)(2,1)}, bf16[4,192,1536]{2,1,0:T(8,128...) custom-call(s32[2,8]{1,0:T(2,128)} %docs_ref.3, ...), custom_call_target="tpu_custom_call" | custom-call | flops 42949672960 | bytes 16777216 | tf_op jit(solution)/shard_map/start/pallas_call | solution.py:757
  49.8 1.6 collective-permute-start.4
  51.4 1.4 collective-permute-start.3
  52.8 0.6 collective-permute-start.2
  53.4 0.0 collective-permute-start
  53.4 0.9 collective-permute-start.1
  54.3 27.0 %attend.1 = (bf16[2048,192]{1,0:T(8,128)(2,1)}, f32[3,64,2048]{2,1,0:T(8,128)}, f32[3,1,2048]{2,1,0:T(1,128)}) custom-call(s32[2,8]{1,0:T(2,128)} %docs_ref.3, f32[3]{0:T(128)} %compare_select_fusion.slopes.slope_ref, bf16[3,128,2048]{2,1,0:T(8,128)(2,1)} %get-tuple-element.65.qt_ref, bf16[3,2048,128]{2,1,0:T(8,128)(2,1)} %get-tuple-element.66.k_ref, ...), custom_call_target="tpu_custom_call" | custom-call | flops 3221225472 | bytes 6291456 | tf_op jit(solution)/shard_map/attend/pallas_call | solution.py:845
  81.2 0.0 collective-permute-done.cot_far
  81.2 0.0 copy-start.8
  81.2 0.0 collective-permute-done.1.cot_near
  81.2 0.0 copy-start.9
  81.3 0.0 collective-permute-done.4.lift_3
  81.3 0.0 copy-start.4
  81.3 0.0 collective-permute-done.3.lift_2
  81.3 0.0 copy-start.5
  81.3 0.0 collective-permute-done.2.lift_1
  81.3 0.0 copy-start.7
  81.3 0.7 copy-done.8
  82.0 0.1 copy-done.9
  82.1 0.2 copy-done.4
  82.3 0.2 copy-done.5
  82.5 0.2 copy-done.7
  82.7 66.3 %middle.1 = (bf16[2,2,256,768]{3,2,1,0:T(8,128)(2,1)}, f32[4,256,768]{2,1,0:T(8,128)}, bf16[8,256,192]{2,1,0:T(8,128)(2,1)}, bf16[192,2304]{1,0:T(8,128)(2,1)}, ...) custom-call(bf16[8,256,192]{2,1,0:T(8,128)(2,1)} %bitcast.25, ...), custom_call_target="tpu_custom_call" | custom-call | flops 53687091200 | bytes 33554432 | tf_op jit(solution)/shard_map/middle/pallas_call | solution.py:1447
  149.0 0.7 collective-permute-start.5
  149.7 1.4 collective-permute-start.6
  151.1 1.5 collective-permute-start.7
  152.6 3.1 %collective-permute-start.8 = (bf16[192,1536]{1,0:T(8,128)(2,1)}, bf16[192,1536]{1,0:T(8,128)(2,1)S(1)}, u32[]{:S(2)}, u32[]{:S(2)}) collective-permute-start(bf16[192,1536]{1,0:T(8,128)(2,1)} %get-tuple-element.93.down_own), channel_id=1, source_target_pairs={{0,2},{6,4},{1,3},{7,5},{8,10},{14,12},{9,11},{15,13},{16,18},{22,... | collective-permute-start | bytes 1769480 | tf_op jit(solution)/shard_map/ppermute | solution.py:2062
  155.7 39.7 %attend_back.1 = (bf16[2048,192]{1,0:T(8,128)(2,1)}, bf16[2048,192]{1,0:T(8,128)(2,1)}, bf16[2048,192]{1,0:T(8,128)(2,1)}) custom-call(s32[2,8]{1,0:T(2,128)} %docs_ref.3, f32[3]{0:T(128)} %compare_select_fusion.slopes.slope_ref, bf16[3,128,2048]{2,1,0:T(8,128)(2,1)} %get-tuple-element.65.qt_ref, bf16[3,2048,64]{2,1,0:T(8,128)(2,1)} %get-tuple-element.76.q_ref, ...), custom_call_target="tpu_custom_call" | custom-call | flops 8053063680 | bytes 12582912 | tf_op jit(solution)/shard_map/attend_back/pallas_call | solution.py:985
  195.4 0.0 collective-permute-done.8.down_in
  195.4 0.0 copy-start.6
  195.4 0.0 collective-permute-done.5.moved_1
  195.4 0.0 copy-start.1
  195.4 0.0 collective-permute-done.6.moved_2
  195.4 0.0 copy-start.2
  195.4 0.0 collective-permute-done.7.moved_3
  195.4 0.0 copy-start.3
  195.4 0.8 copy-done.6
  196.3 0.2 copy-done.1
  196.5 0.3 copy-done.2
  196.8 0.3 copy-done.3
  197.1 90.7 %tail.1 = (bf16[2,2,256,768]{3,2,1,0:T(8,128)(2,1)}, bf16[192,3456]{1,0:T(8,128)(2,1)}, bf16[2,192,576]{2,1,0:T(8,128)(2,1)}, bf16[192,1536]{1,0:T(8,128)(2,1)}, f32[8,768]{1,0:T(8,128)}) custom-call(bf16[8,256,192]{2,1,0:T(8,128)(2,1)} %bitcast.22, bf16[8,256,192]{2,1,0:T(8,128)(2,1)} %bitcast.23, bf16[8,256,192]{2,1,0:T(8,128)(2,1)} %bitcast.24, ...), custom_call_target="tpu_custom_call" | custom-call | flops 85899345920 | bytes 33554432 | tf_op jit(solution)/shard_map/tail/pallas_call | solution.py:1894
  287.8 0.0 copy-start
  287.8 5.7 %finish.1 = (f32[1024,768]{1,0:T(8,128)}, f32[192,384]{1,0:T(8,128)}, f32[192,384]{1,0:T(8,128)}, f32[192,384]{1,0:T(8,128)}, f32[192,384]{1,0:T(8,128)}, /*inde...) custom-call(bf16[1024,768]{1,0:T(8,128)(2,1)} %bitcast.14, ...), custom_call_target="tpu_custom_call" | custom-call | tf_op jit(solution)/shard_map/finish/pallas_call | solution.py:1967
  293.6 0.0 copy-done
  293.6 1.1 copy.35
Async XLA Ops:
  49.8 31.4 %collective-permute-start.4 = (bf16[192,1536]{1,0:T(8,128)(2,1)}, bf16[192,1536]{1,0:T(8,128)(2,1)S(1)}, u32[]{:S(2)}, u32[]{:S(2)}) collective-permute-start(bf16[192,1536]{1,0:T(8,128)(2,1)} %get-tuple-element.74.lift_0), channel_id=1, source_target_pairs={{0,24},{24,0},{8,16},{16,8},{1,25},{25,1},{9,17},{17,9},{2,26},{26... | collective-permute-start | bytes 1769480 | tf_op jit(solution)/shard_map/ppermute | solution.py:2036
  51.4 29.9 %collective-permute-start.3 = (bf16[192,1536]{1,0:T(8,128)(2,1)}, bf16[192,1536]{1,0:T(8,128)(2,1)S(1)}, u32[]{:S(2)}, u32[]{:S(2)}) collective-permute-start(bf16[192,1536]{1,0:T(8,128)(2,1)} %get-tuple-element.74.lift_0), channel_id=1, source_target_pairs={{0,16},{16,0},{8,24},{24,8},{1,17},{17,1},{9,25},{25,9},{2,18},{18... | collective-permute-start | bytes 1769480 | tf_op jit(solution)/shard_map/ppermute | solution.py:2036
  52.8 28.5 %collective-permute-start.2 = (bf16[192,1536]{1,0:T(8,128)(2,1)}, bf16[192,1536]{1,0:T(8,128)(2,1)S(1)}, u32[]{:S(2)}, u32[]{:S(2)}) collective-permute-start(bf16[192,1536]{1,0:T(8,128)(2,1)} %get-tuple-element.74.lift_0), channel_id=1, source_target_pairs={{0,8},{8,0},{16,24},{24,16},{1,9},{9,1},{17,25},{25,17},{2,10},{10... | collective-permute-start | bytes 1769480 | tf_op jit(solution)/shard_map/ppermute | solution.py:2036
  53.4 27.8 %collective-permute-start = (bf16[256,768]{1,0:T(8,128)(2,1)}, bf16[256,768]{1,0:T(8,128)(2,1)S(1)}, u32[]{:S(2)}, u32[]{:S(2)}) collective-permute-start(bf16[256,768]{1,0:T(8,128)(2,1)} %get-tuple-element.70), channel_id=1, source_target_pairs={{6,2},{0,4},{2,0},{4,6},{7,3},{1,5},{3,1},{5,7},{14,10},{8,12},{10... | collective-permute-start | bytes 1179656 | tf_op jit(solution)/shard_map/ppermute | solution.py:2040
  53.4 27.8 %collective-permute-start.1 = (bf16[256,768]{1,0:T(8,128)(2,1)}, bf16[256,768]{1,0:T(8,128)(2,1)S(1)}, u32[]{:S(2)}, u32[]{:S(2)}) collective-permute-start(bf16[256,768]{1,0:T(8,128)(2,1)} %get-tuple-element.71), channel_id=1, source_target_pairs={{2,4},{4,2},{3,5},{5,3},{10,12},{12,10},{11,13},{13,11},{18,20},{2... | collective-permute-start | bytes 1179656 | tf_op jit(solution)/shard_map/ppermute | solution.py:2041
  81.2 0.8 copy-start.8
  81.2 0.9 copy-start.9
  81.3 1.0 copy-start.4
  81.3 1.2 copy-start.5
  81.3 1.4 copy-start.7
  149.0 46.4 %collective-permute-start.5 = (bf16[192,2304]{1,0:T(8,128)(2,1)}, bf16[192,2304]{1,0:T(8,128)(2,1)S(1)}, u32[]{:S(2)}, u32[]{:S(2)}) collective-permute-start(bf16[192,2304]{1,0:T(8,128)(2,1)} %get-tuple-element.90), channel_id=1, source_target_pairs={{0,8},{8,0},{16,24},{24,16},{1,9},{9,1},{17,25},{25,17},{2,10},{10... | collective-permute-start | bytes 2654216 | tf_op jit(solution)/shard_map/ppermute | solution.py:2059
  149.7 45.7 %collective-permute-start.6 = (bf16[192,2304]{1,0:T(8,128)(2,1)}, bf16[192,2304]{1,0:T(8,128)(2,1)S(1)}, u32[]{:S(2)}, u32[]{:S(2)}) collective-permute-start(bf16[192,2304]{1,0:T(8,128)(2,1)} %get-tuple-element.91), channel_id=1, source_target_pairs={{0,16},{16,0},{8,24},{24,8},{1,17},{17,1},{9,25},{25,9},{2,18},{18... | collective-permute-start | bytes 2654216 | tf_op jit(solution)/shard_map/ppermute | solution.py:2059
  151.1 44.3 %collective-permute-start.7 = (bf16[192,2304]{1,0:T(8,128)(2,1)}, bf16[192,2304]{1,0:T(8,128)(2,1)S(1)}, u32[]{:S(2)}, u32[]{:S(2)}) collective-permute-start(bf16[192,2304]{1,0:T(8,128)(2,1)} %get-tuple-element.92), channel_id=1, source_target_pairs={{0,24},{24,0},{8,16},{16,8},{1,25},{25,1},{9,17},{17,9},{2,26},{26... | collective-permute-start | bytes 2654216 | tf_op jit(solution)/shard_map/ppermute | solution.py:2059
  152.6 42.8 %collective-permute-start.8 = (bf16[192,1536]{1,0:T(8,128)(2,1)}, bf16[192,1536]{1,0:T(8,128)(2,1)S(1)}, u32[]{:S(2)}, u32[]{:S(2)}) collective-permute-start(bf16[192,1536]{1,0:T(8,128)(2,1)} %get-tuple-element.93.down_own), channel_id=1, source_target_pairs={{0,2},{6,4},{1,3},{7,5},{8,10},{14,12},{9,11},{15,13},{16,18},{22,... | collective-permute-start | bytes 1769480 | tf_op jit(solution)/shard_map/ppermute | solution.py:2062
  195.4 0.9 copy-start.6
  195.4 1.1 copy-start.1
  195.4 1.4 copy-start.2
  195.4 1.6 copy-start.3
  287.8 5.8 %copy-start = (bf16[2,2,256,768]{3,2,1,0:T(8,128)(2,1)S(1)}, bf16[2,2,256,768]{3,2,1,0:T(8,128)(2,1)}, u32[]{:S(2)}) copy-start(bf16[2,2,256,768]{3,2,1,0:T(8,128)(2,1)} %get-tuple-element.75) | copy-start | bytes 4718596

commit v7 on v6

--- a/solution.py
+++ b/solution.py
@@ -1632,7 +1632,9 @@
         return dot(rows, w_joined[...], ((1,), (1,)))
 
     def block_of(i):
-        return jnp.where(i < 2, 2 * (1 - half) + i, 2 * half + i - 2)
+        left = jnp.where(stage == 0, 3 - i, jnp.where(i == 0, 0, 4 - i))
+        right = jnp.where(stage == 3, i, jnp.where(i == 0, 3, i - 1))
+        return jnp.where(stage < 2, left, right)
 
     def tp_copy(i):
         return remote(tp_sent.at[i], tp_got.at[i], tp_send.at[i], tp_recv.at[i], other_core)
@@ -1650,11 +1652,24 @@
     def pair_copy(i):
         return remote(pair_sent.at[i], pair_got.at[i], pair_send.at[i], pair_recv.at[i], partner)
 
-    @pl.loop(0, 2)
-    def _(i):
-        tp_copy(i).wait_recv()
-        pair_sent[i] = (own_v[i] + tp_got[i].astype(f32)).astype(bf16)
-        pair_copy(i).start()
+    def share_of(i):
+        return own_v[i] + tp_got[i].astype(f32)
+
+    def residual(i):
+        return one_v[2 * (block_of(i) - 2 * half) + core]
+
+    tp_copy(0).wait_recv()
+    pair_sent[0] = share_of(0).astype(bf16)
+    pair_copy(0).start()
+    loads[9].wait()
+
+    @pl.when(at_end)
+    def _():
+        for i in (1, 2):
+            tp_copy(i).wait_recv()
+            part = share_of(i) + residual(i) if i == 2 else share_of(i)
+            pair_sent[i] = part.astype(bf16)
+            pair_copy(i).start()
 
     @pl.when(~at_end)
     def _():
@@ -1716,6 +1731,19 @@
             from_end(j)
             from_mid(j - early_pieces // 2)
 
+    def home_copy(i):
+        return remote(
+            final_v.at[i - 1], home_v, home_send.at[i - 1], home_recv, (place, block_of(i), core)
+        )
+
+    @pl.when(~at_end)
+    def _():
+        for i in (1, 2):
+            tp_copy(i).wait_recv()
+            pair_copy(i - 1).wait_recv()
+            final_v[i - 1] = (share_of(i) + pair_got[i - 1].astype(f32) + residual(i)).astype(bf16)
+            home_copy(i).start()
+
     loads[7].wait()
     for other in (1, 2, 3):
         late_copy(other).wait_recv()
@@ -1750,34 +1778,22 @@
 
     step_on(1)
 
-    loads[9].wait()
-
-    def home_copy(i):
-        return remote(
-            final_v.at[i], home_v.at[seq], home_send.at[i], home_recv.at[seq], (place, 2 * half + i, core)
-        )
-
-    def home_direct(i):
-        return remote(final_v.at[i], home.at[seq, core], home_send.at[i], home_took.at[seq], other_core)
-
-    def home_here(i):
-        return pltpu.make_async_copy(final_v.at[i], home.at[seq, core], home_local)
-
-    for i in range(2):
-        tp_copy(i + 2).wait_recv()
-        pair_copy(i).wait_recv()
-        final_v[i] = (
-            own_v[i + 2] + tp_got[i + 2].astype(f32) + pair_got[i].astype(f32) + one_v[2 * i + core]
-        ).astype(bf16)
-
-        @pl.when(2 * half + i == stage)
-        def _():
-            home_direct(i).start()
-            home_here(i).start()
-
-        @pl.when(2 * half + i != stage)
-        def _():
-            home_copy(i).start()
+    tp_copy(3).wait_recv()
+
+    @pl.when(at_end)
+    def _():
+        pair_copy(0).wait_recv()
+        final_v[2] = (share_of(3) + pair_got[0].astype(f32) + residual(3)).astype(bf16)
+
+    @pl.when(~at_end)
+    def _():
+        pair_copy(2).wait_recv()
+        final_v[2] = (share_of(3) + pair_got[2].astype(f32)).astype(bf16)
+
+    home_direct = remote(final_v.at[2], home.at[seq, core], home_send.at[2], home_took.at[seq], other_core)
+    home_here = pltpu.make_async_copy(final_v.at[2], home.at[seq, core], home_local)
+    home_direct.start()
+    home_here.start()
 
     @pl.when(~at_end)
     def _():
@@ -1799,26 +1815,13 @@
     step_on(3)
     sums[...] = step_v[4]
 
-    def home_arrival(which):
-        return remote(
-            home_v.at[which], home_v.at[which], home_pass.at[which], home_recv.at[which], other_core
-        )
-
-    def home_share(which, whose):
-        return remote(
-            home_v.at[which], home.at[which, whose], home_pass.at[which], home_took.at[which], other_core
-        )
-
-    def home_keep(which):
-        return pltpu.make_async_copy(home_v.at[which], home.at[which, core], home_sem.at[which])
-
-    for which in (0, 1):
-
-        @pl.when(2 * which + stage // 2 != stage)
-        def _():
-            home_arrival(which).wait_recv()
-            home_share(which, core).start()
-            home_keep(which).start()
+    def home_share(whose):
+        return remote(home_v, home.at[1 - seq, whose], home_pass, home_took.at[1 - seq], other_core)
+
+    home_keep = pltpu.make_async_copy(home_v, home.at[1 - seq, core], home_sem)
+    remote(home_v, home_v, home_pass, home_recv, other_core).wait_recv()
+    home_share(core).start()
+    home_keep.start()
 
     @pl.when(~at_end)
     def _():
@@ -1850,26 +1853,24 @@
     for i in range(4):
         tp_copy(i).wait_send()
         step_copy(i).wait_send()
-    for i in range(2):
-        pair_copy(i).wait_send()
-
-        @pl.when(2 * half + i == stage)
-        def _():
-            home_direct(i).wait_send()
-            home_here(i).wait()
-
-        @pl.when(2 * half + i != stage)
-        def _():
+    pair_copy(0).wait_send()
+
+    @pl.when(at_end)
+    def _():
+        for i in (1, 2):
+            pair_copy(i).wait_send()
+
+    @pl.when(~at_end)
+    def _():
+        for i in (1, 2):
             home_copy(i).wait_send()
 
-    for which in (0, 1):
-
-        @pl.when(2 * which + stage // 2 != stage)
-        def _():
-            home_share(which, core).wait_send()
-            home_keep(which).wait()
-
-        home_share(which, 1 - core).wait_recv()
+    home_direct.wait_send()
+    home_here.wait()
+    home_share(core).wait_send()
+    home_keep.wait()
+    home_share(1 - core).wait_recv()
+    remote(final_v.at[2], home.at[seq, 1 - core], home_send.at[2], home_took.at[seq], other_core).wait_recv()
     for other in (1, 2, 3):
         quarter_copy(other).wait_send()
         late_copy(other).wait_send()
@@ -1906,16 +1907,16 @@
             vmem(d_query.shape), vmem(d_query.shape), vmem(d_query.shape),
             vmem(sequence.shape), vmem(grad_one.shape, f32), vmem((4,) + early.shape), vmem(late.shape),
             vmem((8, rows, joined)), vmem((4, rows, width), f32),
-            vmem((4, rows, width)), vmem((4, rows, width)), vmem((2, rows, width)), vmem((2, rows, width)),
-            vmem((2, rows, width)),
+            vmem((4, rows, width)), vmem((4, rows, width)), vmem((3, rows, width)), vmem((3, rows, width)),
+            vmem((3, rows, width)),
             vmem(cut), vmem(cut), vmem(cut), vmem(cut), vmem(cut),
             vmem((width, joined)), vmem((3, quarter, joined)), vmem((quarter, joined)), vmem((quarter, joined)),
             vmem(both), vmem(both), vmem(both),
-            vmem((5,) + sums.shape, f32), vmem((4,) + sums.shape, f32), vmem((2, rows, width)),
+            vmem((5,) + sums.shape, f32), vmem((4,) + sums.shape, f32), vmem((rows, width)),
             vmem((2,) + downs[0].shape), vmem(downs[0].shape), vmem(downs[0].shape), vmem(downs[0].shape),
-            dma((10,)), three, three, four, four, two, two, two, two, two, two, one,
+            dma((10,)), three, three, four, four, three, three, three, one, one, two, one,
             many, many, many, many, many, many, many,
-            three, three, three, three, one, four, four, two, two, two, two, two, two,
+            three, three, three, three, one, four, four, one, two, two, two, two, two,
         ],
         compiler_params=pltpu.CompilerParams(
             collective_id=2, has_side_effects=True, vmem_limit_bytes=VMEM_BYTES

time: 295 us -> 294 us (level)
  no operation moved by 1% of the time
where the time goes in v7:
time: 294 us; the launch traced here: 295 us
  Pallas kernels  278 us (95%)
  starting transfers between devices  11 us (4%)
  local copies, waits for them, and re-layouts  4.16 us (1%)
    pallas_call x1, Pallas kernels, tail(): pl.pallas_call(tail_kernel, in_specs=[any_spec] * 3 + [vmem_spec] * 2 + [...  90.5 us
    pallas_call x1, Pallas kernels, middle(): pl.pallas_call(middle_kernel, in_specs=[pl.BlockSpec(memory_space=pl.ANY)...  66.4 us
    pallas_call x1, Pallas kernels, start(): pl.pallas_call(start_kernel, in_specs=[smem_spec] * 2 + [vmem_spec] * 10,...  48.7 us
    pallas_call x1, Pallas kernels, attend_back(): pl.pallas_call(attend_back_kernel, grid_spec=pltpu.PrefetchScalarGridSpec...  39.7 us
    pallas_call x1, Pallas kernels, attend(): pl.pallas_call(attend_kernel, grid_spec=pltpu.PrefetchScalarGridSpec(num_...  27 us
  transfers between devices with their start and end apart: 9, of which 0 were waited for; matrix products, arithmetic and copies ran while one was open for 0% of the time, Pallas kernels for 23%

profile of v7, /device:TPU:0, one launch (start us, length us, event | category | flops | bytes accessed | tf_op | source)
XLA Modules:
  0.0 294.5 jit_solution(6932240604114676867)
XLA Ops:
  0.7 0.5 compare_select_fusion.slopes.slope_ref
  1.2 48.7 %start.1 = (bf16[4,2,256,768]{3,2,1,0:T(8,128)(2,1)}, bf16[4,192,576]{2,1,0:T(8,128)(2,1)}, bf16[4,192,384]{2,1,0:T(8,128)(2,1)}, bf16[4,192,1536]{2,1,0:T(8,128...) custom-call(s32[2,8]{1,0:T(2,128)} %docs_ref.3, ...), custom_call_target="tpu_custom_call" | custom-call | flops 42949672960 | bytes 16777216 | tf_op jit(solution)/shard_map/start/pallas_call | solution.py:757
  49.8 1.6 collective-permute-start.4
  51.4 1.4 collective-permute-start.3
  52.8 0.6 collective-permute-start.2
  53.4 0.0 collective-permute-start
  53.4 0.9 collective-permute-start.1
  54.3 27.0 %attend.1 = (bf16[2048,192]{1,0:T(8,128)(2,1)}, f32[3,64,2048]{2,1,0:T(8,128)}, f32[3,1,2048]{2,1,0:T(1,128)}) custom-call(s32[2,8]{1,0:T(2,128)} %docs_ref.3, f32[3]{0:T(128)} %compare_select_fusion.slopes.slope_ref, bf16[3,128,2048]{2,1,0:T(8,128)(2,1)} %get-tuple-element.65.qt_ref, bf16[3,2048,128]{2,1,0:T(8,128)(2,1)} %get-tuple-element.66.k_ref, ...), custom_call_target="tpu_custom_call" | custom-call | flops 3221225472 | bytes 6291456 | tf_op jit(solution)/shard_map/attend/pallas_call | solution.py:845
  81.2 0.0 collective-permute-done.cot_far
  81.2 0.0 copy-start.8
  81.2 0.0 collective-permute-done.1.cot_near
  81.2 0.0 copy-start.9
  81.3 0.0 collective-permute-done.4.lift_3
  81.3 0.0 copy-start.4
  81.3 0.0 collective-permute-done.3.lift_2
  81.3 0.0 copy-start.5
  81.3 0.0 collective-permute-done.2.lift_1
  81.3 0.0 copy-start.7
  81.3 0.7 copy-done.8
  82.0 0.1 copy-done.9
  82.1 0.2 copy-done.4
  82.3 0.2 copy-done.5
  82.5 0.2 copy-done.7
  82.7 66.4 %middle.1 = (bf16[2,2,256,768]{3,2,1,0:T(8,128)(2,1)}, f32[4,256,768]{2,1,0:T(8,128)}, bf16[8,256,192]{2,1,0:T(8,128)(2,1)}, bf16[192,2304]{1,0:T(8,128)(2,1)}, ...) custom-call(bf16[8,256,192]{2,1,0:T(8,128)(2,1)} %bitcast.25, ...), custom_call_target="tpu_custom_call" | custom-call | flops 53687091200 | bytes 33554432 | tf_op jit(solution)/shard_map/middle/pallas_call | solution.py:1447
  149.1 0.6 collective-permute-start.5
  149.7 1.5 collective-permute-start.6
  151.2 1.5 collective-permute-start.7
  152.7 3.0 %collective-permute-start.8 = (bf16[192,1536]{1,0:T(8,128)(2,1)}, bf16[192,1536]{1,0:T(8,128)(2,1)S(1)}, u32[]{:S(2)}, u32[]{:S(2)}) collective-permute-start(bf16[192,1536]{1,0:T(8,128)(2,1)} %get-tuple-element.93.down_own), channel_id=1, source_target_pairs={{0,2},{6,4},{1,3},{7,5},{8,10},{14,12},{9,11},{15,13},{16,18},{22,... | collective-permute-start | bytes 1769480 | tf_op jit(solution)/shard_map/ppermute | solution.py:2063
  155.7 39.7 %attend_back.1 = (bf16[2048,192]{1,0:T(8,128)(2,1)}, bf16[2048,192]{1,0:T(8,128)(2,1)}, bf16[2048,192]{1,0:T(8,128)(2,1)}) custom-call(s32[2,8]{1,0:T(2,128)} %docs_ref.3, f32[3]{0:T(128)} %compare_select_fusion.slopes.slope_ref, bf16[3,128,2048]{2,1,0:T(8,128)(2,1)} %get-tuple-element.65.qt_ref, bf16[3,2048,64]{2,1,0:T(8,128)(2,1)} %get-tuple-element.76.q_ref, ...), custom_call_target="tpu_custom_call" | custom-call | flops 8053063680 | bytes 12582912 | tf_op jit(solution)/shard_map/attend_back/pallas_call | solution.py:985
  195.4 0.0 collective-permute-done.8.down_in
  195.4 0.0 copy-start.6
  195.4 0.0 collective-permute-done.5.moved_1
  195.4 0.0 copy-start.1
  195.4 0.0 collective-permute-done.6.moved_2
  195.4 0.0 copy-start.2
  195.5 0.0 collective-permute-done.7.moved_3
  195.5 0.0 copy-start.3
  195.5 0.8 copy-done.6
  196.3 0.2 copy-done.1
  196.5 0.3 copy-done.2
  196.8 0.3 copy-done.3
  197.1 90.5 %tail.1 = (bf16[2,2,256,768]{3,2,1,0:T(8,128)(2,1)}, bf16[192,3456]{1,0:T(8,128)(2,1)}, bf16[2,192,576]{2,1,0:T(8,128)(2,1)}, bf16[192,1536]{1,0:T(8,128)(2,1)}, f32[8,768]{1,0:T(8,128)}) custom-call(bf16[8,256,192]{2,1,0:T(8,128)(2,1)} %bitcast.22, bf16[8,256,192]{2,1,0:T(8,128)(2,1)} %bitcast.23, bf16[8,256,192]{2,1,0:T(8,128)(2,1)} %bitcast.24, ...), custom_call_target="tpu_custom_call" | custom-call | flops 85899345920 | bytes 33554432 | tf_op jit(solution)/shard_map/tail/pallas_call | solution.py:1895
  287.6 0.0 copy-start
  287.6 5.7 %finish.1 = (f32[1024,768]{1,0:T(8,128)}, f32[192,384]{1,0:T(8,128)}, f32[192,384]{1,0:T(8,128)}, f32[192,384]{1,0:T(8,128)}, f32[192,384]{1,0:T(8,128)}, /*inde...) custom-call(bf16[1024,768]{1,0:T(8,128)(2,1)} %bitcast.14, ...), custom_call_target="tpu_custom_call" | custom-call | tf_op jit(solution)/shard_map/finish/pallas_call | solution.py:1968
  293.3 0.0 copy-done
  293.4 1.1 copy.35
Async XLA Ops:
  49.8 31.4 %collective-permute-start.4 = (bf16[192,1536]{1,0:T(8,128)(2,1)}, bf16[192,1536]{1,0:T(8,128)(2,1)S(1)}, u32[]{:S(2)}, u32[]{:S(2)}) collective-permute-start(bf16[192,1536]{1,0:T(8,128)(2,1)} %get-tuple-element.74.lift_0), channel_id=1, source_target_pairs={{0,24},{24,0},{8,16},{16,8},{1,25},{25,1},{9,17},{17,9},{2,26},{26... | collective-permute-start | bytes 1769480 | tf_op jit(solution)/shard_map/ppermute | solution.py:2037
  51.4 29.9 %collective-permute-start.3 = (bf16[192,1536]{1,0:T(8,128)(2,1)}, bf16[192,1536]{1,0:T(8,128)(2,1)S(1)}, u32[]{:S(2)}, u32[]{:S(2)}) collective-permute-start(bf16[192,1536]{1,0:T(8,128)(2,1)} %get-tuple-element.74.lift_0), channel_id=1, source_target_pairs={{0,16},{16,0},{8,24},{24,8},{1,17},{17,1},{9,25},{25,9},{2,18},{18... | collective-permute-start | bytes 1769480 | tf_op jit(solution)/shard_map/ppermute | solution.py:2037
  52.8 28.5 %collective-permute-start.2 = (bf16[192,1536]{1,0:T(8,128)(2,1)}, bf16[192,1536]{1,0:T(8,128)(2,1)S(1)}, u32[]{:S(2)}, u32[]{:S(2)}) collective-permute-start(bf16[192,1536]{1,0:T(8,128)(2,1)} %get-tuple-element.74.lift_0), channel_id=1, source_target_pairs={{0,8},{8,0},{16,24},{24,16},{1,9},{9,1},{17,25},{25,17},{2,10},{10... | collective-permute-start | bytes 1769480 | tf_op jit(solution)/shard_map/ppermute | solution.py:2037
  53.4 27.8 %collective-permute-start = (bf16[256,768]{1,0:T(8,128)(2,1)}, bf16[256,768]{1,0:T(8,128)(2,1)S(1)}, u32[]{:S(2)}, u32[]{:S(2)}) collective-permute-start(bf16[256,768]{1,0:T(8,128)(2,1)} %get-tuple-element.70), channel_id=1, source_target_pairs={{6,2},{0,4},{2,0},{4,6},{7,3},{1,5},{3,1},{5,7},{14,10},{8,12},{10... | collective-permute-start | bytes 1179656 | tf_op jit(solution)/shard_map/ppermute | solution.py:2041
  53.4 27.8 %collective-permute-start.1 = (bf16[256,768]{1,0:T(8,128)(2,1)}, bf16[256,768]{1,0:T(8,128)(2,1)S(1)}, u32[]{:S(2)}, u32[]{:S(2)}) collective-permute-start(bf16[256,768]{1,0:T(8,128)(2,1)} %get-tuple-element.71), channel_id=1, source_target_pairs={{2,4},{4,2},{3,5},{5,3},{10,12},{12,10},{11,13},{13,11},{18,20},{2... | collective-permute-start | bytes 1179656 | tf_op jit(solution)/shard_map/ppermute | solution.py:2042
  81.2 0.8 copy-start.8
  81.2 0.9 copy-start.9
  81.3 1.0 copy-start.4
  81.3 1.2 copy-start.5
  81.3 1.4 copy-start.7
  149.1 46.3 %collective-permute-start.5 = (bf16[192,2304]{1,0:T(8,128)(2,1)}, bf16[192,2304]{1,0:T(8,128)(2,1)S(1)}, u32[]{:S(2)}, u32[]{:S(2)}) collective-permute-start(bf16[192,2304]{1,0:T(8,128)(2,1)} %get-tuple-element.90), channel_id=1, source_target_pairs={{0,8},{8,0},{16,24},{24,16},{1,9},{9,1},{17,25},{25,17},{2,10},{10... | collective-permute-start | bytes 2654216 | tf_op jit(solution)/shard_map/ppermute | solution.py:2060
  149.7 45.8 %collective-permute-start.6 = (bf16[192,2304]{1,0:T(8,128)(2,1)}, bf16[192,2304]{1,0:T(8,128)(2,1)S(1)}, u32[]{:S(2)}, u32[]{:S(2)}) collective-permute-start(bf16[192,2304]{1,0:T(8,128)(2,1)} %get-tuple-element.91), channel_id=1, source_target_pairs={{0,16},{16,0},{8,24},{24,8},{1,17},{17,1},{9,25},{25,9},{2,18},{18... | collective-permute-start | bytes 2654216 | tf_op jit(solution)/shard_map/ppermute | solution.py:2060
  151.2 44.3 %collective-permute-start.7 = (bf16[192,2304]{1,0:T(8,128)(2,1)}, bf16[192,2304]{1,0:T(8,128)(2,1)S(1)}, u32[]{:S(2)}, u32[]{:S(2)}) collective-permute-start(bf16[192,2304]{1,0:T(8,128)(2,1)} %get-tuple-element.92), channel_id=1, source_target_pairs={{0,24},{24,0},{8,16},{16,8},{1,25},{25,1},{9,17},{17,9},{2,26},{26... | collective-permute-start | bytes 2654216 | tf_op jit(solution)/shard_map/ppermute | solution.py:2060
  152.7 42.7 %collective-permute-start.8 = (bf16[192,1536]{1,0:T(8,128)(2,1)}, bf16[192,1536]{1,0:T(8,128)(2,1)S(1)}, u32[]{:S(2)}, u32[]{:S(2)}) collective-permute-start(bf16[192,1536]{1,0:T(8,128)(2,1)} %get-tuple-element.93.down_own), channel_id=1, source_target_pairs={{0,2},{6,4},{1,3},{7,5},{8,10},{14,12},{9,11},{15,13},{16,18},{22,... | collective-permute-start | bytes 1769480 | tf_op jit(solution)/shard_map/ppermute | solution.py:2063
  195.4 0.9 copy-start.6
  195.4 1.1 copy-start.1
  195.4 1.4 copy-start.2
  195.5 1.6 copy-start.3
  287.6 5.8 %copy-start = (bf16[2,2,256,768]{3,2,1,0:T(8,128)(2,1)S(1)}, bf16[2,2,256,768]{3,2,1,0:T(8,128)(2,1)}, u32[]{:S(2)}) copy-start(bf16[2,2,256,768]{3,2,1,0:T(8,128)(2,1)} %get-tuple-element.75) | copy-start | bytes 4718596

commit v8 on v6

--- a/solution.py
+++ b/solution.py
@@ -1434,7 +1434,7 @@
     chunks, rows, width = 4, sequence.shape[1], sequence.shape[2]
     head_width, units = w_out.shape[1], w_down.shape[1]
     tile = head_width
-    early, late = 6 * tile, 2 * units + head_width - 6 * tile
+    early, late = 7 * tile, 2 * units + head_width - 7 * tile
     dma, bf16, f32 = pltpu.SemaphoreType.DMA, jnp.bfloat16, jnp.float32
 
     def vmem(shape, dtype=bf16):

time: 295 us -> 298 us (1.010)
  transfers between devices with their start and end apart: 9 -> 9, of which waited for: 0 -> 1; matrix products, arithmetic and copies ran while one was open for 0% -> 0% of each run, Pallas kernels for 23% -> 22%
where the time goes in v8:
time: 298 us; the launch traced here: 297 us
  Pallas kernels  280 us (94%)
  starting transfers between devices  11 us (4%)
  local copies, waits for them, and re-layouts  3.87 us (1%)
    pallas_call x1, Pallas kernels, tail(): pl.pallas_call(tail_kernel, in_specs=[any_spec] * 3 + [vmem_spec] * 2 + [...  92.2 us
    pallas_call x1, Pallas kernels, middle(): pl.pallas_call(middle_kernel, in_specs=[pl.BlockSpec(memory_space=pl.ANY)...  66.4 us
    pallas_call x1, Pallas kernels, start(): pl.pallas_call(start_kernel, in_specs=[smem_spec] * 2 + [vmem_spec] * 10,...  48.6 us
    pallas_call x1, Pallas kernels, attend_back(): pl.pallas_call(attend_back_kernel, grid_spec=pltpu.PrefetchScalarGridSpec...  39.7 us
    pallas_call x1, Pallas kernels, attend(): pl.pallas_call(attend_kernel, grid_spec=pltpu.PrefetchScalarGridSpec(num_...  27 us
  transfers between devices with their start and end apart: 9, of which 1 were waited for; matrix products, arithmetic and copies ran while one was open for 0% of the time, Pallas kernels for 22%

profile of v8, /device:TPU:0, one launch (start us, length us, event | category | flops | bytes accessed | tf_op | source)
XLA Modules:
  0.0 297.3 jit_solution(9303527444267670524)
XLA Ops:
  0.7 0.5 compare_select_fusion.slopes.slope_ref
  1.2 48.6 %start.1 = (bf16[4,2,256,768]{3,2,1,0:T(8,128)(2,1)}, bf16[4,192,576]{2,1,0:T(8,128)(2,1)}, bf16[4,192,384]{2,1,0:T(8,128)(2,1)}, bf16[4,192,1536]{2,1,0:T(8,128...) custom-call(s32[2,8]{1,0:T(2,128)} %docs_ref.3, ...), custom_call_target="tpu_custom_call" | custom-call | flops 42949672960 | bytes 16777216 | tf_op jit(solution)/shard_map/start/pallas_call | solution.py:757
  49.8 1.6 collective-permute-start.4
  51.4 1.4 collective-permute-start.3
  52.8 0.6 collective-permute-start.2
  53.4 0.0 collective-permute-start
  53.4 0.9 collective-permute-start.1
  54.2 27.0 %attend.1 = (bf16[2048,192]{1,0:T(8,128)(2,1)}, f32[3,64,2048]{2,1,0:T(8,128)}, f32[3,1,2048]{2,1,0:T(1,128)}) custom-call(s32[2,8]{1,0:T(2,128)} %docs_ref.3, f32[3]{0:T(128)} %compare_select_fusion.slopes.slope_ref, bf16[3,128,2048]{2,1,0:T(8,128)(2,1)} %get-tuple-element.65.qt_ref, bf16[3,2048,128]{2,1,0:T(8,128)(2,1)} %get-tuple-element.66.k_ref, ...), custom_call_target="tpu_custom_call" | custom-call | flops 3221225472 | bytes 6291456 | tf_op jit(solution)/shard_map/attend/pallas_call | solution.py:845
  81.2 0.0 collective-permute-done.cot_far
  81.2 0.0 copy-start.8
  81.2 0.0 collective-permute-done.1.cot_near
  81.2 0.0 copy-start.9
  81.2 0.0 collective-permute-done.4.lift_3
  81.2 0.0 copy-start.4
  81.3 0.0 collective-permute-done.3.lift_2
  81.3 0.0 copy-start.5
  81.3 0.0 collective-permute-done.2.lift_1
  81.3 0.0 copy-start.7
  81.3 0.7 copy-done.8
  82.0 0.1 copy-done.9
  82.1 0.2 copy-done.4
  82.3 0.2 copy-done.5
  82.5 0.2 copy-done.7
  82.7 66.4 %middle.1 = (bf16[2,2,256,768]{3,2,1,0:T(8,128)(2,1)}, f32[4,256,768]{2,1,0:T(8,128)}, bf16[8,256,192]{2,1,0:T(8,128)(2,1)}, bf16[192,2688]{1,0:T(8,128)(2,1)}, ...) custom-call(bf16[8,256,192]{2,1,0:T(8,128)(2,1)} %bitcast.25, ...), custom_call_target="tpu_custom_call" | custom-call | flops 53687091200 | bytes 33554432 | tf_op jit(solution)/shard_map/middle/pallas_call | solution.py:1447
  149.1 0.6 collective-permute-start.5
  149.6 1.5 collective-permute-start.6
  151.2 1.5 collective-permute-start.7
  152.6 3.1 %collective-permute-start.8 = (bf16[192,1536]{1,0:T(8,128)(2,1)}, bf16[192,1536]{1,0:T(8,128)(2,1)S(1)}, u32[]{:S(2)}, u32[]{:S(2)}) collective-permute-start(bf16[192,1536]{1,0:T(8,128)(2,1)} %get-tuple-element.93.down_own), channel_id=1, source_target_pairs={{0,2},{6,4},{1,3},{7,5},{8,10},{14,12},{9,11},{15,13},{16,18},{22,... | collective-permute-start | bytes 1769480 | tf_op jit(solution)/shard_map/ppermute | solution.py:2062
  155.7 39.7 %attend_back.1 = (bf16[2048,192]{1,0:T(8,128)(2,1)}, bf16[2048,192]{1,0:T(8,128)(2,1)}, bf16[2048,192]{1,0:T(8,128)(2,1)}) custom-call(s32[2,8]{1,0:T(2,128)} %docs_ref.3, f32[3]{0:T(128)} %compare_select_fusion.slopes.slope_ref, bf16[3,128,2048]{2,1,0:T(8,128)(2,1)} %get-tuple-element.65.qt_ref, bf16[3,2048,64]{2,1,0:T(8,128)(2,1)} %get-tuple-element.76.q_ref, ...), custom_call_target="tpu_custom_call" | custom-call | flops 8053063680 | bytes 12582912 | tf_op jit(solution)/shard_map/attend_back/pallas_call | solution.py:985
  195.4 0.0 collective-permute-done.8.down_in
  195.4 0.0 copy-start.6
  195.4 0.0 collective-permute-done.5.moved_1
  195.5 0.0 copy-start.1
  195.5 1.3 collective-permute-done.6.moved_2
  196.8 0.0 copy-start.2
  196.8 0.0 collective-permute-done.7.moved_3
  196.8 0.0 copy-start.3
  196.8 0.0 copy-done.6
  196.8 0.0 copy-done.1
  196.8 1.0 copy-done.2
  197.8 0.4 copy-done.3
  198.1 92.2 %tail.1 = (bf16[2,2,256,768]{3,2,1,0:T(8,128)(2,1)}, bf16[192,3456]{1,0:T(8,128)(2,1)}, bf16[2,192,576]{2,1,0:T(8,128)(2,1)}, bf16[192,1536]{1,0:T(8,128)(2,1)}, f32[8,768]{1,0:T(8,128)}) custom-call(bf16[8,256,192]{2,1,0:T(8,128)(2,1)} %bitcast.22, bf16[8,256,192]{2,1,0:T(8,128)(2,1)} %bitcast.23, bf16[8,256,192]{2,1,0:T(8,128)(2,1)} %bitcast.24, ...), custom_call_target="tpu_custom_call" | custom-call | flops 85899345920 | bytes 33554432 | tf_op jit(solution)/shard_map/tail/pallas_call | solution.py:1894
  290.4 0.0 copy-start
  290.4 5.7 %finish.1 = (f32[1024,768]{1,0:T(8,128)}, f32[192,384]{1,0:T(8,128)}, f32[192,384]{1,0:T(8,128)}, f32[192,384]{1,0:T(8,128)}, f32[192,384]{1,0:T(8,128)}, /*inde...) custom-call(bf16[1024,768]{1,0:T(8,128)(2,1)} %bitcast.14, ...), custom_call_target="tpu_custom_call" | custom-call | tf_op jit(solution)/shard_map/finish/pallas_call | solution.py:1967
  296.1 0.0 copy-done
  296.1 1.1 copy.35
Async XLA Ops:
  49.8 31.4 %collective-permute-start.4 = (bf16[192,1536]{1,0:T(8,128)(2,1)}, bf16[192,1536]{1,0:T(8,128)(2,1)S(1)}, u32[]{:S(2)}, u32[]{:S(2)}) collective-permute-start(bf16[192,1536]{1,0:T(8,128)(2,1)} %get-tuple-element.74.lift_0), channel_id=1, source_target_pairs={{0,24},{24,0},{8,16},{16,8},{1,25},{25,1},{9,17},{17,9},{2,26},{26... | collective-permute-start | bytes 1769480 | tf_op jit(solution)/shard_map/ppermute | solution.py:2036
  51.4 29.9 %collective-permute-start.3 = (bf16[192,1536]{1,0:T(8,128)(2,1)}, bf16[192,1536]{1,0:T(8,128)(2,1)S(1)}, u32[]{:S(2)}, u32[]{:S(2)}) collective-permute-start(bf16[192,1536]{1,0:T(8,128)(2,1)} %get-tuple-element.74.lift_0), channel_id=1, source_target_pairs={{0,16},{16,0},{8,24},{24,8},{1,17},{17,1},{9,25},{25,9},{2,18},{18... | collective-permute-start | bytes 1769480 | tf_op jit(solution)/shard_map/ppermute | solution.py:2036
  52.8 28.5 %collective-permute-start.2 = (bf16[192,1536]{1,0:T(8,128)(2,1)}, bf16[192,1536]{1,0:T(8,128)(2,1)S(1)}, u32[]{:S(2)}, u32[]{:S(2)}) collective-permute-start(bf16[192,1536]{1,0:T(8,128)(2,1)} %get-tuple-element.74.lift_0), channel_id=1, source_target_pairs={{0,8},{8,0},{16,24},{24,16},{1,9},{9,1},{17,25},{25,17},{2,10},{10... | collective-permute-start | bytes 1769480 | tf_op jit(solution)/shard_map/ppermute | solution.py:2036
  53.4 27.8 %collective-permute-start = (bf16[256,768]{1,0:T(8,128)(2,1)}, bf16[256,768]{1,0:T(8,128)(2,1)S(1)}, u32[]{:S(2)}, u32[]{:S(2)}) collective-permute-start(bf16[256,768]{1,0:T(8,128)(2,1)} %get-tuple-element.70), channel_id=1, source_target_pairs={{6,2},{0,4},{2,0},{4,6},{7,3},{1,5},{3,1},{5,7},{14,10},{8,12},{10... | collective-permute-start | bytes 1179656 | tf_op jit(solution)/shard_map/ppermute | solution.py:2040
  53.4 27.8 %collective-permute-start.1 = (bf16[256,768]{1,0:T(8,128)(2,1)}, bf16[256,768]{1,0:T(8,128)(2,1)S(1)}, u32[]{:S(2)}, u32[]{:S(2)}) collective-permute-start(bf16[256,768]{1,0:T(8,128)(2,1)} %get-tuple-element.71), channel_id=1, source_target_pairs={{2,4},{4,2},{3,5},{5,3},{10,12},{12,10},{11,13},{13,11},{18,20},{2... | collective-permute-start | bytes 1179656 | tf_op jit(solution)/shard_map/ppermute | solution.py:2041
  81.2 0.8 copy-start.8
  81.2 0.9 copy-start.9
  81.2 1.0 copy-start.4
  81.3 1.2 copy-start.5
  81.3 1.4 copy-start.7
  149.1 46.4 %collective-permute-start.5 = (bf16[192,2688]{1,0:T(8,128)(2,1)}, bf16[192,2688]{1,0:T(8,128)(2,1)S(1)}, u32[]{:S(2)}, u32[]{:S(2)}) collective-permute-start(bf16[192,2688]{1,0:T(8,128)(2,1)} %get-tuple-element.90), channel_id=1, source_target_pairs={{0,8},{8,0},{16,24},{24,16},{1,9},{9,1},{17,25},{25,17},{2,10},{10... | collective-permute-start | bytes 3096584 | tf_op jit(solution)/shard_map/ppermute | solution.py:2059
  149.6 47.1 %collective-permute-start.6 = (bf16[192,2688]{1,0:T(8,128)(2,1)}, bf16[192,2688]{1,0:T(8,128)(2,1)S(1)}, u32[]{:S(2)}, u32[]{:S(2)}) collective-permute-start(bf16[192,2688]{1,0:T(8,128)(2,1)} %get-tuple-element.91), channel_id=1, source_target_pairs={{0,16},{16,0},{8,24},{24,8},{1,17},{17,1},{9,25},{25,9},{2,18},{18... | collective-permute-start | bytes 3096584 | tf_op jit(solution)/shard_map/ppermute | solution.py:2059
  151.2 45.6 %collective-permute-start.7 = (bf16[192,2688]{1,0:T(8,128)(2,1)}, bf16[192,2688]{1,0:T(8,128)(2,1)S(1)}, u32[]{:S(2)}, u32[]{:S(2)}) collective-permute-start(bf16[192,2688]{1,0:T(8,128)(2,1)} %get-tuple-element.92), channel_id=1, source_target_pairs={{0,24},{24,0},{8,16},{16,8},{1,25},{25,1},{9,17},{17,9},{2,26},{26... | collective-permute-start | bytes 3096584 | tf_op jit(solution)/shard_map/ppermute | solution.py:2059
  152.6 42.8 %collective-permute-start.8 = (bf16[192,1536]{1,0:T(8,128)(2,1)}, bf16[192,1536]{1,0:T(8,128)(2,1)S(1)}, u32[]{:S(2)}, u32[]{:S(2)}) collective-permute-start(bf16[192,1536]{1,0:T(8,128)(2,1)} %get-tuple-element.93.down_own), channel_id=1, source_target_pairs={{0,2},{6,4},{1,3},{7,5},{8,10},{14,12},{9,11},{15,13},{16,18},{22,... | collective-permute-start | bytes 1769480 | tf_op jit(solution)/shard_map/ppermute | solution.py:2062
  195.4 1.3 copy-start.6
  195.5 1.3 copy-start.1
  196.8 1.0 copy-start.2
  196.8 1.3 copy-start.3
  290.4 5.8 %copy-start = (bf16[2,2,256,768]{3,2,1,0:T(8,128)(2,1)S(1)}, bf16[2,2,256,768]{3,2,1,0:T(8,128)(2,1)}, u32[]{:S(2)}) copy-start(bf16[2,2,256,768]{3,2,1,0:T(8,128)(2,1)} %get-tuple-element.75) | copy-start | bytes 4718596
